TPU v7x, 32 devices: a whole 2x2x4 slice. The times are simulated.
32 devices in a mesh: req: 16 (over z, x, core), tp: 2 (over y).
Axes of the slice: x: 2, y: 2, z: 4, core: 2. Of those that a mesh axis runs over, the one named last changes fastest.
Arguments:
- x_in: bfloat16 [2048, 8192], P('req', 'tp'), may hold values from -6 to 6
- z_gate: bfloat16 [2048, 8192], P('req', 'tp'), may hold values from -6 to 6
- conv_edge: bfloat16 [128, 3, 8192], P('req', None, 'tp'), may hold values from -6 to 6
- conv_weight: float32 [4, 8192], P(None, 'tp'), may hold values from -3 to 3
- conv_bias: float32 [8192], P('tp'), may hold values from -3 to 3
- x_proj_weight: bfloat16 [8192, 288], P('tp'), may hold values from -0.0625 to 0.0625
- dt_gain: float32 [256], replicated, may hold values from 0.5 to 1.5
- b_gain: float32 [16], replicated, may hold values from 0.5 to 1.5
- c_gain: float32 [16], replicated, may hold values from 0.5 to 1.5
- dt_proj_weight: bfloat16 [256, 8192], P(None, 'tp'), may hold values from -0.375 to 0.375
- dt_bias: float32 [8192], P('tp'), may hold values from -6 to -2
- a_log: float32 [16, 8192], P(None, 'tp'), may hold values from 0 to 3
- skip: float32 [8192], P('tp'), may hold values from 0.5 to 1.5
- ssm_state: bfloat16 [128, 16, 8192], P('req', None, 'tp'), may hold values from -6 to 6
- accepted: int32 [128], P('req'), may hold values from 0 to 16, as said below
- prompt_len: int32 [128], P('req'), may hold values from 1 to 8192, 131072 in all
- tenant_range: int32 [4, 2], replicated, may hold values from 0 to 128, as said below
- owner: int32 [128], replicated, may hold values from 0 to 15, as said below
Outputs:
- mixed_out: bfloat16 [2048, 8192], P('req', 'tp')
- owned_state: bfloat16 [192, 16, 8192], P('req', None, 'tp')
- owned_edge: bfloat16 [192, 3, 8192], P('req', None, 'tp')
- tenant_stats: float32 [4, 2], replicated
Inputs may be any that keep to these rules, and one draw needn't show every extreme that they name: `accepted`: accepted draft tokens; the largest value 16 occurs in every draw. `tenant_range`: the rows cover all requests in order, row k starting where row k - 1 ends; every tenant has at least one request. The 8 requests of one device go to 8 different owners; at most 12 requests go to one owner, and some owner receives exactly 12 in every draw.
All inputs are finite; a program needn't handle non-finite values. No bound on the sum of `prompt_len` on one device may be relied on, other than what follows from the above.
Results may differ from a plain program's by a relative error of at most 0.0085.
Values may be sent and summed in bfloat16 or wider, within the bound.
No kernel may reach another device: no remote copies, remote signals or barrier semaphores. Data moves between devices by JAX's collectives and lax.ppermute only.
A program may use at most 64 MiB of HBM per device.

v0:
```python
import jax
import jax.numpy as jnp
from jax import lax
from jax.sharding import PartitionSpec as P

STEPS = 16
PAIR_MOST = 1


EPSILON = 1e-06
SQUARE_FLOOR = 0.25


def rms_scaled(values, scale_gain, floor_value, eps_value):
    square = jnp.mean(values * values, axis=-1, keepdims=True)
    return values * lax.rsqrt(jnp.maximum(square, floor_value) + eps_value) * scale_gain


def normalize(projected, dt_gain, b_gain, c_gain):
    rank_cols = dt_gain.shape[0]
    state_cols = b_gain.shape[0]
    dt_low = rms_scaled(projected[:, :rank_cols], dt_gain, 0.0, EPSILON).astype(jnp.bfloat16)
    input_map = rms_scaled(
        projected[:, rank_cols : rank_cols + state_cols], b_gain, SQUARE_FLOOR, 0.0
    ).astype(jnp.bfloat16)
    output_map = rms_scaled(
        projected[:, rank_cols + state_cols :], c_gain, SQUARE_FLOOR, 0.0
    ).astype(jnp.bfloat16)
    return (dt_low, input_map, output_map)


def per_device(
    x_in,
    z_gate,
    conv_edge,
    conv_weight,
    conv_bias,
    x_proj_weight,
    dt_gain,
    b_gain,
    c_gain,
    dt_proj_weight,
    dt_bias,
    a_log,
    skip,
    ssm_state,
    accepted,
    prompt_len,
    tenant_range,
    owner,
):
    per_dev = ssm_state.shape[0]
    channels = x_in.shape[1]
    drafts = x_in.shape[0] // per_dev
    taps = conv_weight.shape[0]
    state_size = ssm_state.shape[1]
    owners = lax.axis_size("req")
    device = lax.axis_index("req")
    own_most = min(per_dev + per_dev // 2, owners)
    window = jnp.concatenate([conv_edge, x_in.reshape(per_dev, drafts, channels)], axis=1)
    lag_index = accepted[:, None] + jnp.arange(taps - 1, dtype=jnp.int32)[None, :]
    kept_edge = jnp.take_along_axis(window, lag_index[:, :, None], axis=1)
    my_owners = lax.dynamic_slice_in_dim(owner, device * per_dev, per_dev)
    local_ids = jnp.arange(per_dev, dtype=jnp.int32)
    earlier = jnp.sum(
        (my_owners[None, :] == my_owners[:, None]) & (local_ids[None, :] < local_ids[:, None]),
        axis=1,
    )
    send_slot = my_owners * PAIR_MOST + earlier

    def place_rows(payload):
        blank_rows = jnp.zeros((owners * PAIR_MOST,) + payload.shape[1:], payload.dtype)
        return blank_rows.at[send_slot].set(payload)

    route_table = owner.reshape(owners, per_dev)
    incoming = jnp.sum((route_table == device).astype(jnp.int32), axis=1)
    occupied = (jnp.arange(PAIR_MOST, dtype=jnp.int32)[None, :] < incoming[:, None]).reshape(-1)
    target = jnp.where(occupied, jnp.cumsum(occupied.astype(jnp.int32)) - 1, own_most)

    def settle_rows(payload):
        blank_rows = jnp.zeros((own_most,) + payload.shape[1:], payload.dtype)
        return blank_rows.at[target].set(payload, mode="drop")

    summed = jnp.zeros((per_dev, drafts, channels), jnp.float32) + conv_bias
    for offset in range(taps):
        summed = summed + conv_weight[offset] * window[:, offset : offset + drafts, :].astype(
            jnp.float32
        )
    conv_out = jax.nn.silu(summed).astype(jnp.bfloat16)
    flattened = conv_out.reshape(per_dev * drafts, channels)
    partial_proj = jnp.dot(flattened, x_proj_weight, preferred_element_type=jnp.float32)
    projected = lax.psum(partial_proj, "tp")
    dt_low, input_map, output_map = normalize(projected, dt_gain, b_gain, c_gain)
    step_size = jax.nn.softplus(
        jnp.dot(dt_low, dt_proj_weight, preferred_element_type=jnp.float32) + dt_bias
    )
    step_size = step_size.reshape(per_dev, drafts, channels)
    decay_rate = -jnp.exp(a_log)
    conv_float = conv_out.astype(jnp.float32)
    in_float = input_map.astype(jnp.float32).reshape(per_dev, drafts, state_size)
    out_float = output_map.astype(jnp.float32).reshape(per_dev, drafts, state_size)
    initial = ssm_state.astype(jnp.float32)
    kept_first = jnp.where((accepted == 0)[:, None, None], initial, jnp.zeros_like(initial))

    def advance(running, position):
        hidden, kept_state = running
        size_now = step_size[:, position, :]
        conv_now = conv_float[:, position, :]
        decay_now = jnp.exp(size_now[:, None, :] * decay_rate[None, :, :])
        hidden = (
            decay_now * hidden + (size_now * conv_now)[:, None, :] * in_float[:, position, :, None]
        )
        output_now = jnp.sum(out_float[:, position, :, None] * hidden, axis=1) + skip * conv_now
        kept_state = jnp.where((accepted == position + 1)[:, None, None], hidden, kept_state)
        return ((hidden, kept_state), output_now)

    (last_state, kept_state), per_step = lax.scan(
        advance, (initial, kept_first), jnp.arange(drafts, dtype=jnp.int32)
    )
    kept_state = kept_state.astype(jnp.bfloat16)
    received_state, received_edge = (
        lax.all_to_all(place_rows(kept_state), "req", split_axis=0, concat_axis=0, tiled=True),
        lax.all_to_all(place_rows(kept_edge), "req", split_axis=0, concat_axis=0, tiled=True),
    )
    scan_out = jnp.transpose(per_step, (1, 0, 2))
    gate_float = z_gate.reshape(per_dev, drafts, channels).astype(jnp.float32)
    mixed_out = (
        (scan_out * jax.nn.silu(gate_float))
        .astype(jnp.bfloat16)
        .reshape(per_dev * drafts, channels)
    )
    owned_state = settle_rows(received_state)
    owned_edge = settle_rows(received_edge)
    global_ids = device * per_dev + local_ids
    inside = (global_ids[None, :] >= tenant_range[:, 0:1]) & (
        global_ids[None, :] < tenant_range[:, 1:2]
    )
    accepted_float = accepted.astype(jnp.float32)
    new_length = (prompt_len + accepted + 1).astype(jnp.float32)
    accept_sum = jnp.sum(jnp.where(inside, accepted_float[None, :], 0.0), axis=1)
    length_sum = jnp.sum(jnp.where(inside, new_length[None, :], 0.0), axis=1)
    partial_sums = jnp.stack([accept_sum, length_sum], axis=1)
    totals = lax.psum(partial_sums, "req")
    members = (tenant_range[:, 1] - tenant_range[:, 0]).astype(jnp.float32)
    accept_rate = totals[:, 0] / (STEPS * members)
    length_load = totals[:, 1] / members / (jnp.sum(totals[:, 1]) / jnp.sum(members))
    tenant_stats = jnp.stack([accept_rate, length_load], axis=1)
    return (mixed_out, owned_state, owned_edge, tenant_stats)


def solution(mesh):
    placed = (
        P("req", "tp"),
        P("req", "tp"),
        P("req", None, "tp"),
        P(None, "tp"),
        P("tp"),
        P("tp", None),
        P(),
        P(),
        P(),
        P(None, "tp"),
        P("tp"),
        P(None, "tp"),
        P("tp"),
        P("req", None, "tp"),
        P("req"),
        P("req"),
        P(),
        P(),
    )
    return jax.shard_map(
        per_device,
        mesh=mesh,
        in_specs=placed,
        out_specs=(P("req", "tp"), P("req", None, "tp"), P("req", None, "tp"), P()),
        check_vma=False,
    )
```

profile of v0, /device:TPU:11, one launch (start us, length us, event | category | flops | bytes accessed | tf_op | source)
XLA Modules:
  0.0 361.3 jit_solution(11368662169548580320)
XLA Ops:
  9.4 1.8 copy_dynamic-update-slice_fusion
  11.2 2.7 fusion.16
  16.5 2.0 gather_fusion
  19.9 2.2 scatter_fusion.2
  22.1 6.5 %all-to-all-start.1 = ((bf16[16,3,4096]{2,1,0:T(4,128)(2,1)}), bf16[16,3,4096]{2,1,0:T(4,128)(2,1)}, u32[]{:S(2)}, u32[]{:S(2)}) async-start(bf16[16,3,4096]{2,1,0:T(4,128)(2,1)} %scatter_fusion.2), calls=%async_computation.1 | async-start | bytes 1048576 | tf_op jit(solution)/shard_map/all_to_all | solution.py:123
  28.7 2.9 broadcast_select_fusion.1
  32.4 6.4 %all-reduce.2.cloned.1.call-done = f32[128,288]{0,1:T(8,128)} async-done(((f32[128,288]{0,1:T(8,128)}), f32[128,288]{0,1:T(8,128)}) %all-reduce.2.cloned.1.call-update) | async-done | bytes 147472 | tf_op jit(solution)/shard_map/psum | solution.py:92
  42.3 4.5 %compare_select_fusion = f32[128,4096]{1,0:T(8,128)} fusion(bf16[256,4096]{1,0:T(8,128)(2,1)} %param.29, f32[4096]{0:T(1024)} %param.30, f32[128,288]{0,1:T(8,128)} %all-reduce.2.cloned.1.call-done, f32[256]{0:T(256)} %param.26, f32[128]{0:T(128)S(1)} %add_rsqrt_fusion), kind=kOutput, calls=%fused_computation.17 | convolution fusion | flops 272203776 | bytes 4343296 | tf_op jit(solution)/shard_map/dot_general | solution.py:95
  46.9 212.8 %while.14 = (s32[]{:T(128)}, f32[8,16,4096]{2,1,0:T(8,128)}, bf16[8,16,4096]{2,1,0:T(8,128)(2,1)S(1)}, f32[16,8,4096]{2,1,0:T(8,128)}, s32[16]{0:T(128)S(1)}, /*...) while((s32[]{:T(128)}, f32[8,16,4096]{2,1,0:T(8,128)}, ...), condition=%wide.region_6.7_spmd, body=%wide.region_4.6_spmd.sunk | while | flops 3735566 | bytes 10243851 | solution.py:117
  52.4 3.5 multiply_reduce_fusion.5
  58.2 1.9 broadcast_select_fusion.4
  65.7 3.5 multiply_reduce_fusion.5
  71.5 1.9 broadcast_select_fusion.4
  79.0 3.5 multiply_reduce_fusion.5
  84.8 1.9 broadcast_select_fusion.4
  92.3 3.5 multiply_reduce_fusion.5
  98.1 1.9 broadcast_select_fusion.4
  105.6 3.5 multiply_reduce_fusion.5
  111.4 1.9 broadcast_select_fusion.4
  118.9 3.5 multiply_reduce_fusion.5
  124.7 1.9 broadcast_select_fusion.4
  132.2 3.5 multiply_reduce_fusion.5
  138.0 1.9 broadcast_select_fusion.4
  145.5 3.5 multiply_reduce_fusion.5
  151.3 1.9 broadcast_select_fusion.4
  158.8 3.5 multiply_reduce_fusion.5
  164.6 1.9 broadcast_select_fusion.4
  172.1 3.5 multiply_reduce_fusion.5
  177.9 1.9 broadcast_select_fusion.4
  185.4 3.5 multiply_reduce_fusion.5
  191.2 1.9 broadcast_select_fusion.4
  198.7 3.5 multiply_reduce_fusion.5
  204.5 1.9 broadcast_select_fusion.4
  212.0 3.5 multiply_reduce_fusion.5
  217.8 1.9 broadcast_select_fusion.4
  225.3 3.5 multiply_reduce_fusion.5
  231.1 1.9 broadcast_select_fusion.4
  238.6 3.5 multiply_reduce_fusion.5
  244.4 1.9 broadcast_select_fusion.4
  251.9 3.5 multiply_reduce_fusion.5
  255.4 1.6 fusion.23
  257.7 1.9 broadcast_select_fusion.4
  261.2 2.9 scatter_fusion
  264.1 6.8 %all-to-all-start = ((bf16[16,16,4096]{2,1,0:T(8,128)(2,1)}), bf16[16,16,4096]{2,1,0:T(8,128)(2,1)}, u32[]{:S(2)}, u32[]{:S(2)}) async-start(bf16[16,16,4096]{2,1,0:T(8,128)(2,1)} %scatter_fusion), calls=%async_computation | async-start | bytes 4194304 | tf_op jit(solution)/shard_map/all_to_all | solution.py:122
  271.2 63.7 %psum.15 = f32[4,2]{0,1:T(2,128)S(1)} all-reduce(f32[4,2]{0,1:T(2,128)S(1)} %pad_maximum_fusion), channel_id=1, replica_groups=mesh['req'=16,'tp'=2] {'req'}, use_global_device_ids=true, to_apply=%region_16.17 | all-reduce | flops 8 | bytes 64 | tf_op jit(solution)/shard_map/psum | solution.py:143
  340.1 3.6 fusion.2
  345.4 2.1 scatter_fusion.3
  348.8 5.6 %scatter_fusion.1 = bf16[12,16,4096]{2,1,0:T(8,128)(2,1)} fusion(bf16[12,16,4096]{2,1,0:T(8,128)(2,1)} %broadcast_in_dim.97, s32[16]{0:T(128)S(1)} %fusion.5, bf16[16,16,4096]{2,1,0:T(8,128)(2,1)} %all-to-all-done), kind=kCustom, calls=%fused_computation.2 | custom fusion | bytes 6291520 | tf_op jit(solution)/shard_map/scatter | solution.py:82
  (177 shorter events, 100.9 us)
Async XLA Ops:
  7.2 7.3 %copy-start = (bf16[4096,288]{0,1:T(8,128)(2,1)S(1)}, bf16[4096,288]{0,1:T(8,128)(2,1)}, u32[]{:S(2)}) copy-start(bf16[4096,288]{0,1:T(8,128)(2,1)} %param.25) | copy-start | bytes 7077892
  7.2 4.0 %copy-start.2 = (bf16[128,4096]{1,0:T(8,128)(2,1)S(1)}, bf16[128,4096]{1,0:T(8,128)(2,1)}, u32[]{:S(2)}) copy-start(bf16[128,4096]{1,0:T(8,128)(2,1)} %param.20) | copy-start | bytes 3145732
  7.2 4.0 %copy-start.7 = (f32[4096]{0:T(1024)S(1)}, f32[4096]{0:T(1024)}, u32[]{:S(2)}) copy-start(f32[4096]{0:T(1024)} %param.24) | copy-start | bytes 49156
  7.2 31.6 %all-reduce.2.cloned.1.call-start = ((), (), s32[]{:S(2)}) async-start(), calls=%async_computation.2 | async-start | bytes 294912 | tf_op jit(solution)/shard_map/psum | solution.py:92
  11.2 2.7 copy-start.1
  14.4 1.5 copy-start.9
  14.5 1.7 copy-start.13
  22.1 242.0 %all-to-all-start.1 = ((bf16[16,3,4096]{2,1,0:T(4,128)(2,1)}), bf16[16,3,4096]{2,1,0:T(4,128)(2,1)}, u32[]{:S(2)}, u32[]{:S(2)}) async-start(bf16[16,3,4096]{2,1,0:T(4,128)(2,1)} %scatter_fusion.2), calls=%async_computation.1 | async-start | bytes 1048576 | tf_op jit(solution)/shard_map/all_to_all | solution.py:123
  28.7 2.9 copy-start.6
  28.7 10.8 %copy-start.10 = (f32[16]{0:T(128)S(1)}, f32[16]{0:T(128)}, u32[]{:S(2)}) copy-start(f32[16]{0:T(128)} %param.28) | copy-start | bytes 196
  28.7 10.8 %copy-start.11 = (f32[16]{0:T(128)S(1)}, f32[16]{0:T(128)}, u32[]{:S(2)}) copy-start(f32[16]{0:T(128)} %param.27) | copy-start | bytes 196
  42.3 4.6 %copy-start.5 = (f32[4096]{0:T(1024)S(1)}, f32[4096]{0:T(1024)}, u32[]{:S(2)}) copy-start(f32[4096]{0:T(1024)} %param.32) | copy-start | bytes 49156
  264.1 6.8 %copy-start.8 = (s32[4,2]{0,1:T(2,128)S(1)}, s32[4,2]{0,1:T(2,128)}, u32[]{:S(2)}) copy-start(s32[4,2]{0,1:T(2,128)} %param.36) | copy-start | bytes 100
  264.1 6.8 %copy-start.12 = (s32[8]{0:T(128)S(1)}, s32[8]{0:T(128)}, u32[]{:S(2)}) copy-start(s32[8]{0:T(128)} %param.35) | copy-start | bytes 100
  264.1 70.8 %copy-start.14 = (s32[128]{0:T(128)S(1)}, s32[128]{0:T(128)}, u32[]{:S(2)}) copy-start(s32[128]{0:T(128)} %param.37) | copy-start | bytes 1540
  264.1 71.3 %copy-start.4 = (bf16[128,4096]{1,0:T(8,128)(2,1)S(1)}, bf16[128,4096]{1,0:T(8,128)(2,1)}, u32[]{:S(2)}) copy-start(bf16[128,4096]{1,0:T(8,128)(2,1)} %param.21) | copy-start | bytes 3145732
  264.1 83.4 %all-to-all-start = ((bf16[16,16,4096]{2,1,0:T(8,128)(2,1)}), bf16[16,16,4096]{2,1,0:T(8,128)(2,1)}, u32[]{:S(2)}, u32[]{:S(2)}) async-start(bf16[16,16,4096]{2,1,0:T(8,128)(2,1)} %scatter_fusion), calls=%async_computation | async-start | bytes 4194304 | tf_op jit(solution)/shard_map/all_to_all | solution.py:122
  347.5 7.0 %copy-start.3 = (bf16[12,3,4096]{2,1,0:T(4,128)(2,1)}, bf16[12,3,4096]{2,1,0:T(4,128)(2,1)S(1)}, u32[]{:S(2)}) copy-start(bf16[12,3,4096]{2,1,0:T(4,128)(2,1)S(1)} %scatter_fusion.3) | copy-start | bytes 884740
Sparse Core Ops, SparseCore 0:
  16.1 22.6 all-reduce.1
where the time goes:
time: 367 us; the launch traced here: 361 us
  other arithmetic  146 us (40%)
  local copies, waits for them, and re-layouts  68.7 us (19%)
  blocking collectives  63.7 us (17%)
  loops' own time  41.6 us (11%)
  between operations  15.7 us (4%)
  starting transfers between devices  13.4 us (4%)
  waiting for transfers between devices  6.45 us (2%)
  matrix products  5.99 us (2%)
    psum x1, blocking collectives, per_device(): totals = lax.psum(partial_sums, 'req')  63.7 us
    reduce_sum x16, other arithmetic, advance(): jnp.sum(out_float[:, position, :, None] * hidden, axis=1) + skip * conv_now  56.6 us
    another operation x1, loops' own time, per_device(): lax.scan(advance, (initial, kept_first), jnp.arange(drafts, dtype=jnp.int...  41.6 us
    select_n x16, other arithmetic, advance(): jnp.where((accepted == position + 1)[:, None, None], hidden, kept_state)  31 us
    dynamic_update_slice x16, other arithmetic, per_device(): lax.scan(advance, (initial, kept_first), jnp.arange(drafts, dtype=jnp.int...  25.2 us
    dynamic_slice x16, local copies, waits for them, and re-layouts, advance(): size_now = step_size[:, position, :]  21.2 us
    mul x16, other arithmetic, advance(): decay_now = jnp.exp(size_now[:, None, :] * decay_rate[None, :, :])  16 us
    mul x16, local copies, waits for them, and re-layouts, advance(): out_float[:, position, :, None] * hidden  11.1 us
  transfers between devices with their start and end apart: 3, of which 1 were waited for; matrix products, arithmetic and copies ran while one was open for 57% of the time, Pallas kernels for 0%

commit v1 on v0

v1 whole, which is shorter than its diff:
```python
import functools

import jax
import jax.numpy as jnp
from jax import lax
from jax.experimental import pallas as pl
from jax.experimental.pallas import tpu as pltpu
from jax.sharding import PartitionSpec as P

EPSILON = 1e-06
SQUARE_FLOOR = 0.25
LOG2_E = 1.4426950408889634
LANES = 128
EDGE_ROWS = 4
DIGIT = 7
VMEM_BYTES = 48 * 1024 * 1024


def iota(shape, axis):
    return lax.broadcasted_iota(jnp.int32, shape, axis)


def one_hot(condition):
    return jnp.where(condition, 1.0, 0.0).astype(jnp.bfloat16)


def dot(lhs, rhs):
    return jnp.dot(lhs, rhs, preferred_element_type=jnp.float32)


def silu(value):
    return value / (1.0 + jnp.exp(-value))


def to_step_major(requests, steps):
    rows = requests * steps
    row, col = iota((rows, rows), 0), iota((rows, rows), 1)
    return one_hot(col == lax.rem(row, requests) * steps + lax.div(row, requests))


def to_request_major(requests, steps):
    rows = requests * steps
    row, col = iota((rows, rows), 0), iota((rows, rows), 1)
    return one_hot(row == lax.rem(col, requests) * steps + lax.div(col, requests))


def by_request(index, scalars):
    out = jnp.zeros_like(index)
    for request, scalar in enumerate(scalars):
        out = jnp.where(index == request, scalar, out)
    return out


def conv_kernel(
    place_ref, accepted_ref, length_ref, owner_ref,
    x_ref, edge_ref, weight_ref, bias_ref, proj_ref,
    conv_ref, partial_ref, slot_ref,
):
    requests, lags, block = edge_ref.shape
    taps = weight_ref.shape[0]
    steps = x_ref.shape[0] // requests
    slots = slot_ref.shape[0]
    base = place_ref[0] * requests
    accepted = [accepted_ref[r] for r in range(requests)]
    lengths = [length_ref[r] + accepted[r] + 1 for r in range(requests)]
    owners = [owner_ref[base + r] for r in range(requests)]

    stream = dot(to_step_major(requests, steps), x_ref[...])
    edge = edge_ref[...].astype(jnp.float32)
    window = [edge[:, k, :] for k in range(lags)]
    window += [stream[t * requests : (t + 1) * requests] for t in range(steps)]
    weight = [weight_ref[k : k + 1, :] for k in range(taps)]
    outs = []
    for t in range(steps):
        summed = bias_ref[...] + weight[0] * window[t]
        for k in range(1, taps):
            summed = summed + weight[k] * window[t + k]
        outs.append(silu(summed))
    conv_out = jnp.concatenate(outs, axis=0).astype(jnp.bfloat16)
    conv_ref[...] = conv_out
    partial = dot(conv_out, proj_ref[...])

    @pl.when(pl.program_id(0) == 0)
    def _():
        partial_ref[...] = partial

    @pl.when(pl.program_id(0) > 0)
    def _():
        partial_ref[...] += partial

    rows = jnp.concatenate(window, axis=0).astype(jnp.bfloat16)
    count = rows.shape[0]
    row, col = iota((slots * EDGE_ROWS, count), 0), iota((slots * EDGE_ROWS, count), 1)
    request = lax.rem(col, requests)
    lag = lax.rem(row, EDGE_ROWS)
    pick = (
        (lax.div(row, EDGE_ROWS) == by_request(request, owners))
        & (lax.div(col, requests) == by_request(request, accepted) + lag)
        & (lag < lags)
    )
    picked = dot(one_hot(pick), rows)
    lane = iota((slots * EDGE_ROWS, block), 1)
    low = [length & ((1 << DIGIT) - 1) for length in lengths]
    high = [length >> DIGIT for length in lengths]
    numbers = by_request(lane, accepted + low + high).astype(jnp.float32)
    last = lax.rem(iota((slots * EDGE_ROWS, block), 0), EDGE_ROWS) == lags
    picked = jnp.where(last, numbers, picked)
    for s in range(slots):
        slot_ref[s] = picked[s * EDGE_ROWS : (s + 1) * EDGE_ROWS].astype(jnp.bfloat16)


def conv_project(place, accepted, prompt_len, owner, x_in, conv_edge, conv_weight, conv_bias, proj, slots):
    rows, channels = x_in.shape
    requests, lags, _ = conv_edge.shape
    taps, width = conv_weight.shape[0], proj.shape[1]
    block = min(1024, channels)
    smem = pl.BlockSpec(memory_space=pltpu.SMEM)
    return pl.pallas_call(
        conv_kernel,
        grid=(channels // block,),
        in_specs=[
            smem, smem, smem, smem,
            pl.BlockSpec((rows, block), lambda j: (0, j)),
            pl.BlockSpec((requests, lags, block), lambda j: (0, 0, j)),
            pl.BlockSpec((taps, block), lambda j: (0, j)),
            pl.BlockSpec((1, block), lambda j: (0, j)),
            pl.BlockSpec((block, width), lambda j: (j, 0)),
        ],
        out_specs=[
            pl.BlockSpec((rows, block), lambda j: (0, j)),
            pl.BlockSpec((rows, width), lambda j: (0, 0)),
            pl.BlockSpec((slots, EDGE_ROWS, block), lambda j: (0, 0, j)),
        ],
        out_shape=[
            jax.ShapeDtypeStruct((rows, channels), jnp.bfloat16),
            jax.ShapeDtypeStruct((rows, width), jnp.float32),
            jax.ShapeDtypeStruct((slots, EDGE_ROWS, channels), jnp.bfloat16),
        ],
        compiler_params=pltpu.CompilerParams(
            dimension_semantics=("arbitrary",), vmem_limit_bytes=VMEM_BYTES
        ),
        name="conv_project",
    )(place, accepted, prompt_len, owner, x_in, conv_edge, conv_weight, conv_bias, proj)


def rms_scaled(values, gain, floor_value, eps_value):
    square = jnp.mean(values * values, axis=-1, keepdims=True)
    return (values * lax.rsqrt(jnp.maximum(square, floor_value) + eps_value) * gain).astype(jnp.bfloat16)


def scan_kernel(parts, *refs):
    place_ref, accepted_ref, owner_ref = refs[:3]
    part_refs = refs[3 : 3 + parts]
    (
        dt_gain_ref, b_gain_ref, c_gain_ref, dt_weight_ref, dt_bias_ref, a_log_ref, skip_ref,
        conv_ref, state_ref, z_ref, *_, mixed_ref, slot_ref,
        low_ref, in_ref, out_ref, size_ref, drive_ref, rate_ref, kept_ref, sum_ref,
    ) = refs[3 + parts :]
    rank, states = dt_gain_ref.shape[1], b_gain_ref.shape[1]
    requests = accepted_ref.shape[0]
    rows, block = conv_ref.shape
    steps = rows // requests
    slots = slot_ref.shape[0] // states

    @pl.when(pl.program_id(0) == 0)
    def _():
        total = part_refs[0][...]
        for part in part_refs[1:]:
            total = total + part[...]
        low_ref[...] = rms_scaled(total[:, :rank], dt_gain_ref[...], 0.0, EPSILON)
        in_map = rms_scaled(total[:, rank : rank + states], b_gain_ref[...], SQUARE_FLOOR, 0.0)
        out_map = rms_scaled(total[:, rank + states :], c_gain_ref[...], SQUARE_FLOOR, 0.0)
        wide = states * LANES
        spread = one_hot(lax.div(iota((states, wide), 1), LANES) == iota((states, wide), 0))
        in_ref[...] = dot(in_map, spread)
        out_ref[...] = dot(out_map, spread)

    conv = conv_ref[...].astype(jnp.float32)
    raw = dot(low_ref[...], dt_weight_ref[...]) + dt_bias_ref[...]
    size = jnp.maximum(raw, 0.0) + jnp.log1p(jnp.exp(-jnp.abs(raw)))
    size_ref[...] = size
    drive_ref[...] = size * conv
    kept_ref[...] = dot(to_step_major(requests, states), state_ref[...])
    rate = jnp.exp(a_log_ref[...]) * (-LOG2_E)
    for n in range(states):
        rate_ref[n * requests : (n + 1) * requests, :] = jnp.broadcast_to(
            rate[n : n + 1, :], (requests, block)
        )

    accepted = by_request(
        iota((requests, LANES), 0), [accepted_ref[r] for r in range(requests)]
    )
    pair = 2 if block % (2 * LANES) == 0 else 1

    def columns(c, carry):
        spans = [pl.ds(pl.multiple_of((c * pair + i) * LANES, LANES), LANES) for i in range(pair)]
        start = tuple(
            tuple(kept_ref[n * requests : (n + 1) * requests, s] for s in spans)
            for n in range(states)
        )

        def step(t, hidden):
            at = pl.ds(pl.multiple_of(t * requests, requests), requests)
            sizes = [size_ref[at, s] for s in spans]
            drives = [drive_ref[at, s] for s in spans]
            stop = accepted == t + 1
            sums = [None] * pair
            new = []
            for n in range(states):
                b = in_ref[at, n * LANES : (n + 1) * LANES]
                c_map = out_ref[at, n * LANES : (n + 1) * LANES]
                own = slice(n * requests, (n + 1) * requests)
                mine = []
                for i, s in enumerate(spans):
                    decay = jnp.exp2(sizes[i] * rate_ref[own, s])
                    h = decay * hidden[n][i] + drives[i] * b
                    pltpu.store(kept_ref.at[own, s], h, mask=stop)
                    term = c_map * h
                    sums[i] = term if sums[i] is None else sums[i] + term
                    mine.append(h)
                new.append(tuple(mine))
            for i, s in enumerate(spans):
                sum_ref[at, s] = sums[i]
            return tuple(new)

        lax.fori_loop(0, steps, step, start, unroll=2)
        return carry

    lax.fori_loop(0, block // (pair * LANES), columns, 0)

    gate = silu(dot(to_step_major(requests, steps), z_ref[...]))
    mixed = ((sum_ref[...] + skip_ref[...] * conv) * gate).astype(jnp.bfloat16)
    mixed_ref[...] = dot(to_request_major(requests, steps), mixed).astype(jnp.bfloat16)

    base = place_ref[0] * requests
    shape = (slots * states, states * requests)
    row, col = iota(shape, 0), iota(shape, 1)
    owners = by_request(lax.rem(col, requests), [owner_ref[base + r] for r in range(requests)])
    pick = (lax.rem(row, states) == lax.div(col, requests)) & (lax.div(row, states) == owners)
    slot_ref[...] = dot(one_hot(pick), kept_ref[...].astype(jnp.bfloat16)).astype(jnp.bfloat16)


def scan_chunk(first, width, scalars, partials, gains, dt_weight, channel_rows, conv, state, z_gate, mixed, slots):
    rows, channels = conv.shape
    dt_bias, a_log, skip = channel_rows
    states = a_log.shape[0]
    rank = dt_weight.shape[0]
    block = min(512, width)
    skipped = first // block
    smem = pl.BlockSpec(memory_space=pltpu.SMEM)

    def whole(array):
        return pl.BlockSpec(array.shape, lambda j: (0, 0))

    def columns(height):
        return pl.BlockSpec((height, block), lambda j: (0, j + skipped))

    operands = [*scalars, *partials, *gains, dt_weight, dt_bias, a_log, skip, conv, state, z_gate]
    in_specs = [smem] * len(scalars) + [whole(a) for a in (*partials, *gains)]
    in_specs += [columns(a.shape[0]) for a in operands[len(in_specs) :]]
    aliases = {}
    if mixed is not None:
        aliases[len(operands)] = 0
        operands.append(mixed)
        in_specs.append(pl.BlockSpec(memory_space=pl.ANY))
    return pl.pallas_call(
        functools.partial(scan_kernel, len(partials)),
        grid=(width // block,),
        in_specs=in_specs,
        out_specs=[
            columns(rows),
            pl.BlockSpec((slots * states, block), lambda j: (0, j)),
        ],
        out_shape=[
            jax.ShapeDtypeStruct((rows, channels), jnp.bfloat16),
            jax.ShapeDtypeStruct((slots * states, width), jnp.bfloat16),
        ],
        scratch_shapes=[
            pltpu.VMEM((rows, rank), jnp.bfloat16),
            pltpu.VMEM((rows, states * LANES), jnp.float32),
            pltpu.VMEM((rows, states * LANES), jnp.float32),
            pltpu.VMEM((rows, block), jnp.float32),
            pltpu.VMEM((rows, block), jnp.float32),
            pltpu.VMEM((states * scalars[1].shape[0], block), jnp.float32),
            pltpu.VMEM((states * scalars[1].shape[0], block), jnp.float32),
            pltpu.VMEM((rows, block), jnp.float32),
        ],
        input_output_aliases=aliases,
        compiler_params=pltpu.CompilerParams(
            dimension_semantics=("arbitrary",), vmem_limit_bytes=VMEM_BYTES
        ),
        name="scan_chunk",
    )(*operands)


def edge_kernel(steps, source_ref, count_ref, range_ref, got_ref, edge_ref, stats_ref):
    slots, _, channels = got_ref.shape
    own_most, lags, _ = edge_ref.shape
    for i in range(own_most):

        @pl.when(i < count_ref[0])
        def _():
            edge_ref[i] = got_ref[source_ref[i], :lags, :]

        @pl.when(i >= count_ref[0])
        def _():
            edge_ref[i] = jnp.zeros((lags, channels), jnp.bfloat16)

    requests = count_ref.shape[0] - 1
    numbers = got_ref[:, lags, :LANES].astype(jnp.float32)
    lane, slot = iota((slots, LANES), 1), iota((slots, LANES), 0)
    request = slot * requests + lax.rem(lane, requests)
    counts = jnp.where(lane < requests, numbers, 0.0)
    digit = lax.div(lane, requests)
    lengths = jnp.where(digit == 1, numbers, 0.0) + jnp.where(
        digit == 2, numbers * float(1 << DIGIT), 0.0
    )
    tenants = range_ref.shape[0]
    tiles = (tenants, 2)
    sums, loads, members = [], [], []
    for k in range(tenants):
        start, end = range_ref[k, 0], range_ref[k, 1]
        inside = (request >= start) & (request < end)
        sums.append(jnp.sum(jnp.where(inside, counts, 0.0), keepdims=True))
        loads.append(jnp.sum(jnp.where(inside, lengths, 0.0), keepdims=True))
        members.append(jnp.full((1, 1), 1, jnp.int32) * (end - start))
    members = [m.astype(jnp.float32) for m in members]
    mean = sum(loads[1:], loads[0]) / sum(members[1:], members[0])
    out = jnp.zeros(tiles, jnp.float32)
    row, col = iota(tiles, 0), iota(tiles, 1)
    for k in range(tenants):
        rate = sums[k] / (float(steps) * members[k])
        load = loads[k] / members[k] / mean
        out = jnp.where(row == k, jnp.where(col == 0, rate, load), out)
    stats_ref[...] = out


def settle_edges(source, count, tenant_range, got, own_most, lags, steps):
    smem = pl.BlockSpec(memory_space=pltpu.SMEM)
    vmem = pl.BlockSpec(memory_space=pltpu.VMEM)
    return pl.pallas_call(
        functools.partial(edge_kernel, steps),
        in_specs=[smem, smem, smem, vmem],
        out_specs=[vmem, vmem],
        out_shape=[
            jax.ShapeDtypeStruct((own_most, lags, got.shape[2]), jnp.bfloat16),
            jax.ShapeDtypeStruct((tenant_range.shape[0], 2), jnp.float32),
        ],
        compiler_params=pltpu.CompilerParams(vmem_limit_bytes=VMEM_BYTES),
        name="settle_edges",
    )(source, count, tenant_range, got)


def settle_kernel(first, source_ref, count_ref, got_ref, *refs):
    owned_ref, blank_ref, sems = refs[-3:]
    own_most = owned_ref.shape[0]
    width = got_ref.shape[2]
    blank_ref[...] = jnp.zeros_like(blank_ref)

    def copy(i, filled):
        origin = got_ref.at[source_ref[i]] if filled else blank_ref
        return pltpu.make_async_copy(
            origin, owned_ref.at[i, :, first : first + width], sems.at[i]
        )

    for act in ("start", "wait"):
        for i in range(own_most):
            for filled in (True, False):

                @pl.when((i < count_ref[0]) == filled)
                def _():
                    getattr(copy(i, filled), act)()


def settle_states(first, source, count, got, owned, shape):
    smem = pl.BlockSpec(memory_space=pltpu.SMEM)
    anywhere = pl.BlockSpec(memory_space=pl.ANY)
    before = () if owned is None else (owned,)
    return pl.pallas_call(
        functools.partial(settle_kernel, first),
        in_specs=[smem, smem, anywhere] + [anywhere] * len(before),
        out_specs=anywhere,
        out_shape=jax.ShapeDtypeStruct(shape, got.dtype),
        scratch_shapes=[
            pltpu.VMEM(got.shape[1:], got.dtype),
            pltpu.SemaphoreType.DMA((shape[0],)),
        ],
        input_output_aliases={3: 0} if before else {},
        compiler_params=pltpu.CompilerParams(vmem_limit_bytes=VMEM_BYTES),
        name="settle_states",
    )(source, count, got, *before)


def per_device(
    x_in, z_gate, conv_edge, conv_weight, conv_bias, x_proj_weight, dt_gain, b_gain, c_gain,
    dt_proj_weight, dt_bias, a_log, skip, ssm_state, accepted, prompt_len, tenant_range, owner,
):
    requests, states, channels = ssm_state.shape
    lags = conv_edge.shape[1]
    owners = lax.axis_size("req")
    own_most = min(requests + requests // 2, owners)
    place = lax.axis_index("req").astype(jnp.int32).reshape(1)

    conv, partial, edge_slots = conv_project(
        place, accepted, prompt_len, owner, x_in, conv_edge, conv_weight,
        conv_bias.reshape(1, -1), x_proj_weight, owners,
    )
    if lax.axis_size("tp") == 2:
        partials = (partial, lax.ppermute(partial, "tp", [(0, 1), (1, 0)]))
    else:
        partials = (lax.psum(partial, "tp"),)

    def exchange(slots):
        return lax.all_to_all(slots, "req", split_axis=0, concat_axis=0, tiled=True)

    got_edges = exchange(edge_slots)

    hits = jnp.any(owner.reshape(owners, requests) == place, axis=1)
    ids = jnp.arange(owners, dtype=jnp.int32)
    ranks = jnp.sum((hits[None, :] & (ids[None, :] < ids[:, None])).astype(jnp.int32), axis=1)
    at = hits[None, :] & (ranks[None, :] == jnp.arange(own_most, dtype=jnp.int32)[:, None])
    source = jnp.sum(jnp.where(at, ids[None, :], 0), axis=1)
    count = jnp.broadcast_to(jnp.sum(hits.astype(jnp.int32)), (requests + 1,))

    gains = (dt_gain.reshape(1, -1), b_gain.reshape(1, -1), c_gain.reshape(1, -1))
    rows = (dt_bias.reshape(1, -1), a_log, skip.reshape(1, -1))
    scalars = (place, accepted, owner)
    state = ssm_state.reshape(requests * states, channels)
    mixed, owned = None, None
    cut = channels // 4
    chunks = ((0, cut), (cut, channels - cut)) if cut % 512 == 0 else ((0, channels),)
    received = []
    for first, width in chunks:
        mixed, slots = scan_chunk(
            first, width, scalars, partials, gains, dt_proj_weight, rows, conv, state, z_gate,
            mixed, owners,
        )
        received.append((first, exchange(slots.reshape(owners, states, width))))
    owned_edge, tenant_stats = settle_edges(
        source, count, tenant_range, got_edges, own_most, lags, x_in.shape[0] // requests
    )
    for first, got in received:
        owned = settle_states(first, source, count, got, owned, (own_most, states, channels))
    return (mixed, owned, owned_edge, tenant_stats)


def solution(mesh):
    placed = (
        P("req", "tp"),
        P("req", "tp"),
        P("req", None, "tp"),
        P(None, "tp"),
        P("tp"),
        P("tp", None),
        P(),
        P(),
        P(),
        P(None, "tp"),
        P("tp"),
        P(None, "tp"),
        P("tp"),
        P("req", None, "tp"),
        P("req"),
        P("req"),
        P(),
        P(),
    )
    return jax.shard_map(
        per_device,
        mesh=mesh,
        in_specs=placed,
        out_specs=(P("req", "tp"), P("req", None, "tp"), P("req", None, "tp"), P()),
        check_vma=False,
    )
```

time: 367 us -> 107 us (0.29); the launches traced: 361 us -> 106 us
  other arithmetic: 146 us -> 0.99 us
  blocking collectives: 63.7 us -> 0 us
  local copies, waits for them, and re-layouts: 68.7 us -> 15.8 us
  loops' own time: 41.6 us -> 0 us
  Pallas kernels: 0 us -> 40.6 us
  waiting for transfers between devices: 6.45 us -> 27.1 us
  between operations: 15.7 us -> 0.84 us
  starting transfers between devices: 13.4 us -> 20.8 us
  matrix products: 5.99 us -> 0 us
    psum x1 -> x0, blocking collectives: 63.7 us -> none  [per_device(): totals = lax.psum(partial_sums, 'req')]
    reduce_sum x23 -> x3, other arithmetic: 60 us -> 0.87 us  [the longest x1 0.64 us: per_device(): count = jnp.broadcast_to(jnp.sum(hits.astype(jnp.int32)), (requests + 1,))]
    another operation x1 -> x0, loops' own time: 41.6 us -> none  [per_device(): lax.scan(advance, (initial, kept_first), jnp.arange(drafts, dtype=jnp.int...]
    pallas_call x0 -> x6, Pallas kernels: none -> 40.6 us  [the longest x2 22.1 us: scan_chunk(): pl.pallas_call(functools.partial(scan_kernel, len(partials)), grid=(width...]
    select_n x20 -> x0, other arithmetic: 34.3 us -> none  [the longest x16 31 us: advance(): jnp.where((accepted == position + 1)[:, None, None], hidden, kept_state)]
    dynamic_slice x33 -> x0, local copies, waits for them, and re-layouts: 31.1 us -> none  [the longest x16 21.2 us: advance(): size_now = step_size[:, position, :]]
    dynamic_update_slice x16 -> x0, other arithmetic: 25.2 us -> none  [per_device(): lax.scan(advance, (initial, kept_first), jnp.arange(drafts, dtype=jnp.int...]
    all_to_all x2 -> x3, waiting for transfers between devices: 0.01 us -> 21.9 us  [exchange(): return lax.all_to_all(slots, 'req', split_axis=0, concat_axis=0, tiled=True)]
  transfers between devices with their start and end apart: 3 -> 4, of which waited for: 1 -> 2; matrix products, arithmetic and copies ran while one was open for 57% -> 2% of each run, Pallas kernels for 0% -> 32%
where the time goes in v1:
time: 107 us; the launch traced here: 106 us
  Pallas kernels  40.6 us (38%)
  waiting for transfers between devices  27.1 us (25%)
  starting transfers between devices  20.8 us (19%)
  local copies, waits for them, and re-layouts  15.8 us (15%)
    pallas_call x2, Pallas kernels, scan_chunk(): pl.pallas_call(functools.partial(scan_kernel, len(partials)), grid=(width...  22.1 us
    all_to_all x3, waiting for transfers between devices, exchange(): return lax.all_to_all(slots, 'req', split_axis=0, concat_axis=0, tiled=True)  21.9 us
    all_to_all x3, starting transfers between devices, exchange(): return lax.all_to_all(slots, 'req', split_axis=0, concat_axis=0, tiled=True)  19.6 us
    unnamed x52, local copies, waits for them, and re-layouts  15 us
    pallas_call x2, Pallas kernels, settle_states(): pl.pallas_call(functools.partial(settle_kernel, first), in_specs=[smem, s...  11.4 us
    ppermute x1, waiting for transfers between devices, per_device(): partials = (partial, lax.ppermute(partial, 'tp', [(0, 1), (1, 0)]))  5.2 us
    pallas_call x1, Pallas kernels, conv_project(): pl.pallas_call(conv_kernel, grid=(channels // block,), in_specs=[smem, sm...  5.16 us
  transfers between devices with their start and end apart: 4, of which 2 were waited for; matrix products, arithmetic and copies ran while one was open for 2% of the time, Pallas kernels for 32%

profile of v1, /device:TPU:11, one launch (start us, length us, event | category | flops | bytes accessed | tf_op | source)
XLA Modules:
  0.0 106.1 jit_solution(9665438825908429391)
XLA Ops:
  0.6 1.8 %copy.32.edge_ref = bf16[8,3,4096]{2,1,0:T(4,128)(2,1)} copy(bf16[8,3,4096]{2,0,1:T(8,128)(2,1)} %param.20) | data formatting | bytes 393216 | tf_op args[2]
  2.4 0.0 copy-start.18
  2.5 0.0 copy-start.22
  2.5 4.6 %copy.33.proj_ref = bf16[4096,288]{1,0:T(8,128)(2,1)} copy(bf16[4096,288]{0,1:T(8,128)(2,1)} %param.23) | data formatting | bytes 4718592 | tf_op args[5]
  7.1 0.0 copy-done.16
  7.1 0.0 copy-start.4
  7.1 0.9 copy-done.4
  8.1 0.0 copy-start.19
  8.1 0.0 copy-start.20
  8.1 0.0 copy-start.21
  8.1 5.2 %conv_project.1 = (bf16[128,4096]{1,0:T(8,128)(2,1)S(1)}, f32[128,288]{1,0:T(8,128)S(1)}, bf16[16,4,4096]{2,1,0:T(4,128)(2,1)S(1)}) custom-call(s32[1]{0:T(128)} %bitcast.place_ref.refs_0_, s32[8]{0:T(128)S(1)} %copy-done.17, s32[8]{0:T(128)S(1)} %copy-done.22, s32[128]{0:T(128)S(1)} %copy-done.18, bf16[128,4096]{1,0:T(8,128)(2,1)S(1)} %copy-done.5, ...), custom_call_target="tpu_custom_call" | custom-call | tf_op jit(solution)/shard_map/conv_project/pallas_call | solution.py:118
  13.3 0.0 copy-start.6
  13.3 0.7 copy-done.6
  14.0 0.8 copy-done.11
  14.8 6.7 %all-to-all-start.2 = ((bf16[16,4,4096]{2,1,0:T(4,128)(2,1)}), bf16[16,4,4096]{2,1,0:T(4,128)(2,1)}, u32[]{:S(2)}, u32[]{:S(2)}) async-start(bf16[16,4,4096]{2,1,0:T(4,128)(2,1)} %copy-done.11), calls=%async_computation.2 | async-start | bytes 1048576 | tf_op jit(solution)/shard_map/all_to_all | solution.py:414
  21.4 1.2 %collective-permute-start = (f32[128,288]{1,0:T(8,128)}, f32[128,288]{1,0:T(8,128)S(1)}, u32[]{:S(2)}, u32[]{:S(2)}) collective-permute-start(f32[128,288]{1,0:T(8,128)} %copy-done.6), channel_id=1, source_target_pairs={{0,1},{1,0},{2,3},{3,2},{4,5},{5,4},{6,7},{7,6},{8,9},{9,8},{10,11... | collective-permute-start | bytes 442376 | tf_op jit(solution)/shard_map/ppermute | solution.py:409
  22.7 5.2 %collective-permute-done.refs_4_ = f32[128,288]{1,0:T(8,128)S(1)} collective-permute-done((f32[128,288]{1,0:T(8,128)}, f32[128,288]{1,0:T(8,128)S(1)}, u32[]{:S(2)}, u32[]{:S(2)}) %collective-permute-start) | collective-permute-done | bytes 147488 | tf_op jit(solution)/shard_map/ppermute | solution.py:409
  27.9 0.0 copy-done.15
  27.9 0.0 copy-done.19
  27.9 0.0 copy-done.20
  27.9 0.0 copy-done.21
  27.9 0.0 copy-done
  27.9 0.0 copy-start.7
  28.0 0.9 copy-done.7
  28.9 6.5 %scan_chunk.2 = (bf16[128,4096]{1,0:T(8,128)(2,1)}, bf16[256,1024]{1,0:T(8,128)(2,1)S(1)}) custom-call(s32[1]{0:T(128)} %bitcast.place_ref.refs_0_, s32[8]{0:T(128)S(1)} %copy-done.17, s32[128]{0:T(128)S(1)} %copy-done.18, f32[128,288]{1,0:T(8,128)S(1)} %copy-done.7, f32[128,288]{1,0:T(8,128)S(1)} %collective-permute-done.refs_4_, f32[1,256]{1,0:T(1,128)S(1)} %bitcast.19, ...), custom_call_target="tpu_custom_call" | custom-call | tf_op jit(solution)/shard_map/scan_chunk/pallas_call | solution.py:266
  35.4 0.7 copy-done.9
  36.0 0.8 copy-done.12
  36.8 0.0 all-to-all-done.2.got_ref
  36.8 6.7 %all-to-all-start.1 = ((bf16[16,16,1024]{2,1,0:T(8,128)(2,1)}), bf16[16,16,1024]{2,1,0:T(8,128)(2,1)}, u32[]{:S(2)}, u32[]{:S(2)}) async-start(bf16[16,16,1024]{2,1,0:T(8,128)(2,1)} %bitcast.13), calls=%async_computation.1 | async-start | bytes 1048576 | tf_op jit(solution)/shard_map/all_to_all | solution.py:414
  43.6 0.9 copy-done.8
  44.5 0.9 copy-done.10
  45.4 15.6 %scan_chunk.3 = (bf16[128,4096]{1,0:T(8,128)(2,1)}, bf16[256,3072]{1,0:T(8,128)(2,1)S(1)}) custom-call(s32[1]{0:T(128)} %bitcast.place_ref.refs_0_, s32[8]{0:T(128)S(1)} %copy-done.17, s32[128]{0:T(128)S(1)} %copy-done.18, f32[128,288]{1,0:T(8,128)S(1)} %copy-done.8, f32[128,288]{1,0:T(8,128)S(1)} %copy-done.10, ...), custom_call_target="tpu_custom_call", output_to_operand_aliasing={{0}: (15, {})} | custom-call | tf_op jit(solution)/shard_map/scan_chunk/pallas_call | solution.py:266
  61.0 1.2 %copy-done.2 = bf16[256,3072]{1,0:T(8,128)(2,1)} copy-done((bf16[256,3072]{1,0:T(8,128)(2,1)}, bf16[256,3072]{1,0:T(8,128)(2,1)S(1)}, u32[]{:S(2)}) %copy-start.2) | copy-done | bytes 1572888
  62.2 0.0 all-to-all-done.1.got_ref
  62.2 6.1 %all-to-all-start = ((bf16[16,16,3072]{2,1,0:T(8,128)(2,1)}), bf16[16,16,3072]{2,1,0:T(8,128)(2,1)S(1)}, u32[]{:S(2)}, u32[]{:S(2)}) async-start(bf16[16,16,3072]{2,1,0:T(8,128)(2,1)} %bitcast.12), calls=%async_computation | async-start | bytes 3145728 | tf_op jit(solution)/shard_map/all_to_all | solution.py:414
  68.3 0.1 eq.26
  68.4 0.0 copy-done.23
  68.4 0.1 copy.34.range_ref
  68.5 0.1 reduce_or.9
  68.6 0.6 convert_reduce_fusion.1
  69.3 0.1 convert_reduce_fusion
  69.4 0.1 select_reduce_fusion.source_ref
  69.5 0.7 broadcast_in_dim.24.count_ref
  70.2 2.0 %settle_edges.1 = (bf16[12,3,4096]{2,1,0:T(4,128)(2,1)}, f32[4,2]{1,0:T(4,128)S(1)}) custom-call(s32[12]{0:T(128)S(1)} %select_reduce_fusion.source_ref, s32[9]{0:T(128)S(1)} %broadcast_in_dim.24.count_ref, s32[4,2]{1,0:T(4,128)S(1)} %copy.34.range_ref, bf16[16,4,4096]{2,1,0:T(4,128)(2,1)} %all-to-all-done.2.got_ref), custom_call_target="tpu_custom_call" | custom-call | tf_op jit(solution)/shard_map/settle_edges/pallas_call | solution.py:341
  72.2 0.6 copy.35
  72.8 9.7 %settle_states.2.refs_0_ = bf16[12,16,4096]{2,1,0:T(8,128)(2,1)} custom-call(s32[12]{0:T(128)S(1)} %select_reduce_fusion.source_ref, s32[9]{0:T(128)S(1)} %broadcast_in_dim.24.count_ref, bf16[16,16,1024]{2,1,0:T(8,128)(2,1)} %all-to-all-done.1.got_ref), custom_call_target="tpu_custom_call" | custom-call | tf_op jit(solution)/shard_map/settle_states/pallas_call | solution.py:379
  82.6 21.9 %all-to-all-done.got_ref = bf16[16,16,3072]{2,1,0:T(8,128)(2,1)S(1)} async-done(((bf16[16,16,3072]{2,1,0:T(8,128)(2,1)}), bf16[16,16,3072]{2,1,0:T(8,128)(2,1)S(1)}, u32[]{:S(2)}, u32[]{:S(2)}) %all-to-all-start) | async-done | bytes 1572896 | tf_op jit(solution)/shard_map/all_to_all | solution.py:414
  104.5 1.6 %settle_states.3 = bf16[12,16,4096]{2,1,0:T(8,128)(2,1)} custom-call(s32[12]{0:T(128)S(1)} %select_reduce_fusion.source_ref, s32[9]{0:T(128)S(1)} %broadcast_in_dim.24.count_ref, bf16[16,16,3072]{2,1,0:T(8,128)(2,1)S(1)} %all-to-all-done.got_ref, bf16[12,16,4096]{2,1,0:T(8,128)(2,1)} %settle_states.2.refs_0_), custom_call_target="tpu_custom_call", output_to_operand_aliasing={{}: (3, {})} | custom-call | tf_op jit(solution)/shard_map/settle_states/pallas_call | solution.py:379
  (25 shorter events, 0.0 us)
Async XLA Ops:
  2.4 4.6 %copy-start.5 = (bf16[128,4096]{1,0:T(8,128)(2,1)S(1)}, bf16[128,4096]{1,0:T(8,128)(2,1)}, u32[]{:S(2)}) copy-start(bf16[128,4096]{1,0:T(8,128)(2,1)} %x_ref.1) | copy-start | bytes 3145732
  2.4 4.6 %copy-start.13 = (f32[4,4096]{1,0:T(4,128)S(1)}, f32[4,4096]{1,0:T(4,128)}, u32[]{:S(2)}) copy-start(f32[4,4096]{1,0:T(4,128)} %weight_ref.1) | copy-start | bytes 196612
  2.4 4.6 %copy-start.16 = (f32[4096]{0:T(1024)S(1)}, f32[4096]{0:T(1024)}, u32[]{:S(2)}) copy-start(f32[4096]{0:T(1024)} %param.22) | copy-start | bytes 49156
  2.4 4.6 %copy-start.17 = (s32[8]{0:T(128)S(1)}, s32[8]{0:T(128)}, u32[]{:S(2)}) copy-start(s32[8]{0:T(128)} %refs_1_.3) | copy-start | bytes 100
  2.4 4.6 %copy-start.18 = (s32[128]{0:T(128)S(1)}, s32[128]{0:T(128)}, u32[]{:S(2)}) copy-start(s32[128]{0:T(128)} %refs_2_.3) | copy-start | bytes 1540
  2.5 4.6 %copy-start.22 = (s32[8]{0:T(128)S(1)}, s32[8]{0:T(128)}, u32[]{:S(2)}) copy-start(s32[8]{0:T(128)} %length_ref.1) | copy-start | bytes 100
  7.1 1.0 copy-start.4
  8.1 19.8 %copy-start.1 = (bf16[128,4096]{1,0:T(8,128)(2,1)S(1)}, bf16[128,4096]{1,0:T(8,128)(2,1)}, u32[]{:S(2)}) copy-start(bf16[128,4096]{1,0:T(8,128)(2,1)} %refs_14_.3) | copy-start | bytes 3145732
  8.1 19.8 %copy-start.3 = (f32[16,4096]{1,0:T(8,128)S(1)}, f32[16,4096]{1,0:T(8,128)}, u32[]{:S(2)}) copy-start(f32[16,4096]{1,0:T(8,128)} %refs_10_.3) | copy-start | bytes 786436
  8.1 19.8 %copy-start.14 = (f32[4096]{0:T(1024)S(1)}, f32[4096]{0:T(1024)}, u32[]{:S(2)}) copy-start(f32[4096]{0:T(1024)} %param.28) | copy-start | bytes 49156
  8.1 19.8 %copy-start.15 = (f32[4096]{0:T(1024)S(1)}, f32[4096]{0:T(1024)}, u32[]{:S(2)}) copy-start(f32[4096]{0:T(1024)} %param.30) | copy-start | bytes 49156
  8.1 19.8 %copy-start.19 = (f32[256]{0:T(256)S(1)}, f32[256]{0:T(256)}, u32[]{:S(2)}) copy-start(f32[256]{0:T(256)} %param.24) | copy-start | bytes 3076
  8.1 19.8 %copy-start.20 = (f32[16]{0:T(128)S(1)}, f32[16]{0:T(128)}, u32[]{:S(2)}) copy-start(f32[16]{0:T(128)} %param.25) | copy-start | bytes 196
  8.1 19.8 %copy-start.21 = (f32[16]{0:T(128)S(1)}, f32[16]{0:T(128)}, u32[]{:S(2)}) copy-start(f32[16]{0:T(128)} %param.26) | copy-start | bytes 196
  13.3 0.7 copy-start.6
  14.0 0.8 copy-start.11
  14.8 13.2 %copy-start = (bf16[8,16,4096]{2,1,0:T(8,128)(2,1)S(1)}, bf16[8,16,4096]{2,1,0:T(8,128)(2,1)}, u32[]{:S(2)}) copy-start(bf16[8,16,4096]{2,1,0:T(8,128)(2,1)} %param.31) | copy-start | bytes 3145732
  14.8 22.1 %all-to-all-start.2 = ((bf16[16,4,4096]{2,1,0:T(4,128)(2,1)}), bf16[16,4,4096]{2,1,0:T(4,128)(2,1)}, u32[]{:S(2)}, u32[]{:S(2)}) async-start(bf16[16,4,4096]{2,1,0:T(4,128)(2,1)} %copy-done.11), calls=%async_computation.2 | async-start | bytes 1048576 | tf_op jit(solution)/shard_map/all_to_all | solution.py:414
  21.4 6.4 %collective-permute-start = (f32[128,288]{1,0:T(8,128)}, f32[128,288]{1,0:T(8,128)S(1)}, u32[]{:S(2)}, u32[]{:S(2)}) collective-permute-start(f32[128,288]{1,0:T(8,128)} %copy-done.6), channel_id=1, source_target_pairs={{0,1},{1,0},{2,3},{3,2},{4,5},{5,4},{6,7},{7,6},{8,9},{9,8},{10,11... | collective-permute-start | bytes 442376 | tf_op jit(solution)/shard_map/ppermute | solution.py:409
  27.9 0.9 copy-start.7
  35.3 0.7 copy-start.9
  36.0 0.8 copy-start.12
  36.8 25.3 %all-to-all-start.1 = ((bf16[16,16,1024]{2,1,0:T(8,128)(2,1)}), bf16[16,16,1024]{2,1,0:T(8,128)(2,1)}, u32[]{:S(2)}, u32[]{:S(2)}) async-start(bf16[16,16,1024]{2,1,0:T(8,128)(2,1)} %bitcast.13), calls=%async_computation.1 | async-start | bytes 1048576 | tf_op jit(solution)/shard_map/all_to_all | solution.py:414
  43.6 0.9 copy-start.8
  44.5 0.9 copy-start.10
  61.0 1.2 %copy-start.2 = (bf16[256,3072]{1,0:T(8,128)(2,1)}, bf16[256,3072]{1,0:T(8,128)(2,1)S(1)}, u32[]{:S(2)}) copy-start(bf16[256,3072]{1,0:T(8,128)(2,1)S(1)} %get-tuple-element.17) | copy-start | bytes 4718596
  62.2 6.2 %copy-start.23 = (s32[4,2]{0,1:T(2,128)S(1)}, s32[4,2]{0,1:T(2,128)}, u32[]{:S(2)}) copy-start(s32[4,2]{0,1:T(2,128)} %param.34) | copy-start | bytes 100
  62.2 42.3 %all-to-all-start = ((bf16[16,16,3072]{2,1,0:T(8,128)(2,1)}), bf16[16,16,3072]{2,1,0:T(8,128)(2,1)S(1)}, u32[]{:S(2)}, u32[]{:S(2)}) async-start(bf16[16,16,3072]{2,1,0:T(8,128)(2,1)} %bitcast.12), calls=%async_computation | async-start | bytes 3145728 | tf_op jit(solution)/shard_map/all_to_all | solution.py:414

commit v2 on v1

--- a/solution.py
+++ b/solution.py
@@ -14,6 +14,7 @@
 EDGE_ROWS = 4
 DIGIT = 7
 VMEM_BYTES = 48 * 1024 * 1024
+VECTOR_WEIGHT = 30000
 
 
 def iota(shape, axis):
@@ -26,6 +27,10 @@
 
 def dot(lhs, rhs):
     return jnp.dot(lhs, rhs, preferred_element_type=jnp.float32)
+
+
+def in_hbm(array):
+    return pltpu.with_memory_space_constraint(array, pltpu.HBM)
 
 
 def silu(value):
@@ -51,23 +56,12 @@
     return out
 
 
-def conv_kernel(
-    place_ref, accepted_ref, length_ref, owner_ref,
-    x_ref, edge_ref, weight_ref, bias_ref, proj_ref,
-    conv_ref, partial_ref, slot_ref,
-):
-    requests, lags, block = edge_ref.shape
+def conv_kernel(x_ref, edge_ref, weight_ref, bias_ref, proj_ref, conv_ref, partial_ref):
+    lags, requests, _ = edge_ref.shape
     taps = weight_ref.shape[0]
     steps = x_ref.shape[0] // requests
-    slots = slot_ref.shape[0]
-    base = place_ref[0] * requests
-    accepted = [accepted_ref[r] for r in range(requests)]
-    lengths = [length_ref[r] + accepted[r] + 1 for r in range(requests)]
-    owners = [owner_ref[base + r] for r in range(requests)]
-
     stream = dot(to_step_major(requests, steps), x_ref[...])
-    edge = edge_ref[...].astype(jnp.float32)
-    window = [edge[:, k, :] for k in range(lags)]
+    window = [edge_ref[k].astype(jnp.float32) for k in range(lags)]
     window += [stream[t * requests : (t + 1) * requests] for t in range(steps)]
     weight = [weight_ref[k : k + 1, :] for k in range(taps)]
     outs = []
@@ -78,7 +72,9 @@
         outs.append(silu(summed))
     conv_out = jnp.concatenate(outs, axis=0).astype(jnp.bfloat16)
     conv_ref[...] = conv_out
-    partial = dot(conv_out, proj_ref[...])
+    partial = lax.dot_general(
+        conv_out, proj_ref[...], (((1,), (1,)), ((), ())), preferred_element_type=jnp.float32
+    )
 
     @pl.when(pl.program_id(0) == 0)
     def _():
@@ -88,59 +84,97 @@
     def _():
         partial_ref[...] += partial
 
-    rows = jnp.concatenate(window, axis=0).astype(jnp.bfloat16)
-    count = rows.shape[0]
-    row, col = iota((slots * EDGE_ROWS, count), 0), iota((slots * EDGE_ROWS, count), 1)
-    request = lax.rem(col, requests)
-    lag = lax.rem(row, EDGE_ROWS)
-    pick = (
-        (lax.div(row, EDGE_ROWS) == by_request(request, owners))
-        & (lax.div(col, requests) == by_request(request, accepted) + lag)
-        & (lag < lags)
-    )
-    picked = dot(one_hot(pick), rows)
-    lane = iota((slots * EDGE_ROWS, block), 1)
-    low = [length & ((1 << DIGIT) - 1) for length in lengths]
-    high = [length >> DIGIT for length in lengths]
-    numbers = by_request(lane, accepted + low + high).astype(jnp.float32)
-    last = lax.rem(iota((slots * EDGE_ROWS, block), 0), EDGE_ROWS) == lags
-    picked = jnp.where(last, numbers, picked)
-    for s in range(slots):
-        slot_ref[s] = picked[s * EDGE_ROWS : (s + 1) * EDGE_ROWS].astype(jnp.bfloat16)
-
-
-def conv_project(place, accepted, prompt_len, owner, x_in, conv_edge, conv_weight, conv_bias, proj, slots):
+
+def conv_project(x_in, conv_edge, conv_weight, conv_bias, proj):
     rows, channels = x_in.shape
-    requests, lags, _ = conv_edge.shape
-    taps, width = conv_weight.shape[0], proj.shape[1]
+    lags, requests, _ = conv_edge.shape
+    taps, width = conv_weight.shape[0], proj.shape[0]
     block = min(1024, channels)
-    smem = pl.BlockSpec(memory_space=pltpu.SMEM)
     return pl.pallas_call(
         conv_kernel,
         grid=(channels // block,),
         in_specs=[
-            smem, smem, smem, smem,
             pl.BlockSpec((rows, block), lambda j: (0, j)),
-            pl.BlockSpec((requests, lags, block), lambda j: (0, 0, j)),
+            pl.BlockSpec((lags, requests, block), lambda j: (0, 0, j)),
             pl.BlockSpec((taps, block), lambda j: (0, j)),
             pl.BlockSpec((1, block), lambda j: (0, j)),
-            pl.BlockSpec((block, width), lambda j: (j, 0)),
+            pl.BlockSpec((width, block), lambda j: (0, j)),
         ],
         out_specs=[
             pl.BlockSpec((rows, block), lambda j: (0, j)),
             pl.BlockSpec((rows, width), lambda j: (0, 0)),
-            pl.BlockSpec((slots, EDGE_ROWS, block), lambda j: (0, 0, j)),
         ],
         out_shape=[
-            jax.ShapeDtypeStruct((rows, channels), jnp.bfloat16),
-            jax.ShapeDtypeStruct((rows, width), jnp.float32),
-            jax.ShapeDtypeStruct((slots, EDGE_ROWS, channels), jnp.bfloat16),
+            pltpu.HBM((rows, channels), jnp.bfloat16),
+            pltpu.HBM((rows, width), jnp.float32),
         ],
         compiler_params=pltpu.CompilerParams(
             dimension_semantics=("arbitrary",), vmem_limit_bytes=VMEM_BYTES
         ),
         name="conv_project",
-    )(place, accepted, prompt_len, owner, x_in, conv_edge, conv_weight, conv_bias, proj)
+    )(in_hbm(x_in), in_hbm(conv_edge), conv_weight, conv_bias, in_hbm(proj))
+
+
+def kept_edge_kernel(
+    place_ref, accepted_ref, length_ref, owner_ref, x_ref, edge_ref, _, slot_ref
+):
+    lags, requests, block = edge_ref.shape
+    steps = x_ref.shape[0] // requests
+    slots = slot_ref.shape[0]
+    base = place_ref[0] * requests
+    accepted = [accepted_ref[r] for r in range(requests)]
+    lengths = [length_ref[r] + accepted[r] + 1 for r in range(requests)]
+    owners = [owner_ref[base + r] for r in range(requests)]
+    height = slots * EDGE_ROWS
+
+    def pick(count, request_of, place_of):
+        row, col = iota((height, count), 0), iota((height, count), 1)
+        request, lag = request_of(col), lax.rem(row, EDGE_ROWS)
+        return one_hot(
+            (lax.div(row, EDGE_ROWS) == by_request(request, owners))
+            & (place_of(col) == by_request(request, accepted) + lag)
+            & (lag < lags)
+        )
+
+    picked = dot(
+        pick(requests * steps, lambda c: lax.div(c, steps), lambda c: lax.rem(c, steps) + lags),
+        x_ref[...],
+    )
+    edge = jnp.concatenate([edge_ref[k].astype(jnp.float32) for k in range(lags)], axis=0)
+    picked += dot(
+        pick(lags * requests, lambda c: lax.rem(c, requests), lambda c: lax.div(c, requests)),
+        edge.astype(jnp.bfloat16),
+    )
+    low = [length & ((1 << DIGIT) - 1) for length in lengths]
+    high = [length >> DIGIT for length in lengths]
+    numbers = by_request(iota((1, block), 1), accepted + low + high).astype(jnp.float32)
+    last = lax.rem(iota((height, block), 0), EDGE_ROWS) == lags
+    picked = jnp.where(last, jnp.broadcast_to(numbers, (height, block)), picked)
+    for s in range(slots):
+        slot_ref[s] = picked[s * EDGE_ROWS : (s + 1) * EDGE_ROWS].astype(jnp.bfloat16)
+
+
+def kept_edges(scalars, x_in, conv_edge, after, slots):
+    rows, channels = x_in.shape
+    lags, requests, _ = conv_edge.shape
+    block = min(1024, channels)
+    smem = pl.BlockSpec(memory_space=pltpu.SMEM)
+    return pl.pallas_call(
+        kept_edge_kernel,
+        grid=(channels // block,),
+        in_specs=[smem] * len(scalars)
+        + [
+            pl.BlockSpec((rows, block), lambda j: (0, j)),
+            pl.BlockSpec((lags, requests, block), lambda j: (0, 0, j)),
+            pl.BlockSpec(memory_space=pl.ANY),
+        ],
+        out_specs=pl.BlockSpec((slots, EDGE_ROWS, block), lambda j: (0, 0, j)),
+        out_shape=pltpu.HBM((slots, EDGE_ROWS, channels), jnp.bfloat16),
+        compiler_params=pltpu.CompilerParams(
+            dimension_semantics=("arbitrary",), vmem_limit_bytes=VMEM_BYTES
+        ),
+        name="kept_edges",
+    )(*scalars, in_hbm(x_in), in_hbm(conv_edge), in_hbm(after))
 
 
 def rms_scaled(values, gain, floor_value, eps_value):
@@ -255,7 +289,8 @@
     def columns(height):
         return pl.BlockSpec((height, block), lambda j: (0, j + skipped))
 
-    operands = [*scalars, *partials, *gains, dt_weight, dt_bias, a_log, skip, conv, state, z_gate]
+    operands = [*scalars, *partials, *gains, in_hbm(dt_weight), dt_bias, in_hbm(a_log), skip]
+    operands += [in_hbm(conv), in_hbm(state), in_hbm(z_gate)]
     in_specs = [smem] * len(scalars) + [whole(a) for a in (*partials, *gains)]
     in_specs += [columns(a.shape[0]) for a in operands[len(in_specs) :]]
     aliases = {}
@@ -273,7 +308,7 @@
         ],
         out_shape=[
             jax.ShapeDtypeStruct((rows, channels), jnp.bfloat16),
-            jax.ShapeDtypeStruct((slots * states, width), jnp.bfloat16),
+            pltpu.HBM((slots * states, width), jnp.bfloat16),
         ],
         scratch_shapes=[
             pltpu.VMEM((rows, rank), jnp.bfloat16),
@@ -288,6 +323,11 @@
         input_output_aliases=aliases,
         compiler_params=pltpu.CompilerParams(
             dimension_semantics=("arbitrary",), vmem_limit_bytes=VMEM_BYTES
+        ),
+        cost_estimate=pl.CostEstimate(
+            flops=VECTOR_WEIGHT * 8 * rows * states * width,
+            transcendentals=rows * states * width,
+            bytes_accessed=2 * width * (3 * rows + rank + states * slots),
         ),
         name="scan_chunk",
     )(*operands)
@@ -401,10 +441,11 @@
     own_most = min(requests + requests // 2, owners)
     place = lax.axis_index("req").astype(jnp.int32).reshape(1)
 
-    conv, partial, edge_slots = conv_project(
-        place, accepted, prompt_len, owner, x_in, conv_edge, conv_weight,
-        conv_bias.reshape(1, -1), x_proj_weight, owners,
-    )
+    by_lag = jnp.transpose(conv_edge, (1, 0, 2))
+    conv, partial = conv_project(
+        x_in, by_lag, conv_weight, conv_bias.reshape(1, -1), x_proj_weight.T
+    )
+    edge_slots = kept_edges((place, accepted, prompt_len, owner), x_in, by_lag, partial, owners)
     if lax.axis_size("tp") == 2:
         partials = (partial, lax.ppermute(partial, "tp", [(0, 1), (1, 0)]))
     else:

time: 107 us -> 98.7 us (0.922)
  local copies, waits for them, and re-layouts: 15.8 us -> 3.08 us
  Pallas kernels: 40.6 us -> 45.3 us
  starting transfers between devices: 20.8 us -> 19.2 us
  waiting for transfers between devices: 27.1 us -> 28.7 us
    unnamed x52 -> x26, local copies, waits for them, and re-layouts: 15 us -> 2.34 us
    all_to_all x3, waiting for transfers between devices: 21.9 us -> 28.7 us  [exchange(): return lax.all_to_all(slots, 'req', split_axis=0, concat_axis=0, tiled=True)]
    ppermute x1, waiting for transfers between devices: 5.2 us -> 0.01 us  [per_device(): partials = (partial, lax.ppermute(partial, 'tp', [(0, 1), (1, 0)]))]
    pallas_call x1 -> x2, Pallas kernels: 5.16 us -> 8.96 us  [the longest x1 5.22 us: conv_project(): pl.pallas_call(conv_kernel, grid=(channels // block,), in_specs=[pl.Block...]
    all_to_all x3, starting transfers between devices: 19.6 us -> 17.9 us  [exchange(): return lax.all_to_all(slots, 'req', split_axis=0, concat_axis=0, tiled=True)]
  transfers between devices with their start and end apart: 4 -> 4, of which waited for: 2 -> 2; matrix products, arithmetic and copies ran while one was open for 2% -> 3% of each run, Pallas kernels for 32% -> 39%
where the time goes in v2:
time: 98.7 us; the launch traced here: 98 us
  Pallas kernels  45.3 us (46%)
  waiting for transfers between devices  28.7 us (29%)
  starting transfers between devices  19.2 us (19%)
  local copies, waits for them, and re-layouts  3.08 us (3%)
  other arithmetic  0.99 us (1%)
    all_to_all x3, waiting for transfers between devices, exchange(): return lax.all_to_all(slots, 'req', split_axis=0, concat_axis=0, tiled=True)  28.7 us
    pallas_call x2, Pallas kernels, scan_chunk(): pl.pallas_call(functools.partial(scan_kernel, len(partials)), grid=(width...  23 us
    all_to_all x3, starting transfers between devices, exchange(): return lax.all_to_all(slots, 'req', split_axis=0, concat_axis=0, tiled=True)  17.9 us
    pallas_call x2, Pallas kernels, settle_states(): pl.pallas_call(functools.partial(settle_kernel, first), in_specs=[smem, s...  11.4 us
    pallas_call x1, Pallas kernels, conv_project(): pl.pallas_call(conv_kernel, grid=(channels // block,), in_specs=[pl.Block...  5.22 us
    pallas_call x1, Pallas kernels, kept_edges(): pl.pallas_call(kept_edge_kernel, grid=(channels // block,), in_specs=[sme...  3.74 us
    unnamed x26, local copies, waits for them, and re-layouts  2.34 us
    pallas_call x1, Pallas kernels, settle_edges(): pl.pallas_call(functools.partial(edge_kernel, steps), in_specs=[smem, sme...  2.04 us
  transfers between devices with their start and end apart: 4, of which 2 were waited for; matrix products, arithmetic and copies ran while one was open for 3% of the time, Pallas kernels for 39%

profile of v2, /device:TPU:11, one launch (start us, length us, event | category | flops | bytes accessed | tf_op | source)
XLA Modules:
  0.0 98.0 jit_solution(1996356820950581399)
XLA Ops:
  0.6 0.0 copy-start.1
  0.6 0.8 copy-done.1
  1.5 0.0 copy-start.2
  1.5 0.7 copy-done.2
  2.2 0.0 copy-start.3
  2.2 0.0 copy-start.4
  2.2 0.0 copy-start.5
  2.2 5.2 %conv_project.1 = (bf16[128,4096]{1,0:T(8,128)(2,1)}, f32[128,288]{1,0:T(8,128)}) custom-call(bf16[128,4096]{1,0:T(8,128)(2,1)} %x_ref.3, bf16[3,8,4096]{2,1,0:T(8,128)(2,1)} %bitcast.25, f32[4,4096]{1,0:T(4,128)S(1)} %copy-done.1, f32[1,4096]{1,0:T(1,128)S(1)} %bitcast.12, bf16[288,4096]{1,0:T(8,128)(2,1)} %bitcast.23), custom_call_target="tpu_custom_call" | custom-call | tf_op jit(solution)/shard_map/conv_project/pallas_call | solution.py:93
  7.4 0.0 copy-start
  7.4 0.0 copy-start.6
  7.4 0.0 copy-start.7
  7.4 0.0 copy-start.8
  7.5 0.0 copy-start.9
  7.5 0.0 copy-start.10
  7.5 1.3 %collective-permute-start = (f32[128,288]{1,0:T(8,128)}, f32[128,288]{1,0:T(8,128)S(1)}, u32[]{:S(2)}, u32[]{:S(2)}) collective-permute-start(f32[128,288]{1,0:T(8,128)} %get-tuple-element.12.refs_3_._), channel_id=1, source_target_pairs={{0,1},{1,0},{2,3},{3,2},{4,5},{5,4},{6,7},{7,6},{8,9},{9,8},{10,11... | collective-permute-start | bytes 442376 | tf_op jit(solution)/shard_map/ppermute | solution.py:450
  8.8 0.0 copy-done.3
  8.8 0.0 copy-done.4
  8.8 0.0 copy-done.5
  8.8 3.7 %kept_edges.1 = bf16[16,4,4096]{2,1,0:T(4,128)(2,1)} custom-call(s32[1]{0:T(128)} %bitcast.refs_0_.place_ref, s32[8]{0:T(128)S(1)} %copy-done.4, s32[8]{0:T(128)S(1)} %copy-done.3, s32[128]{0:T(128)S(1)} %copy-done.5, bf16[128,4096]{1,0:T(8,128)(2,1)} %x_ref.3, bf16[3,8,4096]{2,1,0:T(8,128)(2,1)} %bitcast.26, f32[128,288]{1,0:T(8,128)} %get-tuple-element.12.refs_3_._), custom_call_target="tpu_custom_call" | custom-call | tf_op jit(solution)/shard_map/kept_edges/pallas_call | solution.py:162
  12.5 6.8 %all-to-all-start.2 = ((bf16[16,4,4096]{2,1,0:T(4,128)(2,1)}), bf16[16,4,4096]{2,1,0:T(4,128)(2,1)}, u32[]{:S(2)}, u32[]{:S(2)}) async-start(bf16[16,4,4096]{2,1,0:T(4,128)(2,1)} %kept_edges.1), calls=%async_computation.2 | async-start | bytes 1048576 | tf_op jit(solution)/shard_map/all_to_all | solution.py:455
  19.4 0.0 collective-permute-done.refs_4_
  19.4 0.0 copy-done
  19.4 0.0 copy-done.6
  19.4 0.0 copy-done.7
  19.4 0.0 copy-done.8
  19.4 0.0 copy-done.9
  19.4 0.0 copy-done.10
  19.4 6.9 %scan_chunk.2 = (bf16[128,4096]{1,0:T(8,128)(2,1)}, bf16[256,1024]{1,0:T(8,128)(2,1)}) custom-call(s32[1]{0:T(128)} %bitcast.refs_0_.place_ref, s32[8]{0:T(128)S(1)} %copy-done.4, s32[128]{0:T(128)S(1)} %copy-done.5, f32[128,288]{1,0:T(8,128)S(1)} %copy-done, f32[128,288]{1,0:T(8,128)S(1)} %collective-permute-done.refs_4_, f32[1,256]{1,0:T(1,128)S(1)} %bitcast.17, ...), custom_call_target="tpu_custom_call" | custom-call | flops 503316480000 | bytes 1835008 | tf_op jit(solution)/shard_map/scan_chunk/pallas_call | solution.py:301
  26.3 6.7 %all-to-all-done.2.got_ref = bf16[16,4,4096]{2,1,0:T(4,128)(2,1)} async-done(((bf16[16,4,4096]{2,1,0:T(4,128)(2,1)}), bf16[16,4,4096]{2,1,0:T(4,128)(2,1)}, u32[]{:S(2)}, u32[]{:S(2)}) %all-to-all-start.2) | async-done | bytes 524320 | tf_op jit(solution)/shard_map/all_to_all | solution.py:455
  33.1 5.0 %all-to-all-start.1 = ((bf16[16,16,1024]{2,1,0:T(8,128)(2,1)}), bf16[16,16,1024]{2,1,0:T(8,128)(2,1)}, u32[]{:S(2)}, u32[]{:S(2)}) async-start(bf16[16,16,1024]{2,1,0:T(8,128)(2,1)} %bitcast.27), calls=%async_computation.1 | async-start | bytes 1048576 | tf_op jit(solution)/shard_map/all_to_all | solution.py:455
  38.0 16.1 %scan_chunk.3 = (bf16[128,4096]{1,0:T(8,128)(2,1)}, bf16[256,3072]{1,0:T(8,128)(2,1)}) custom-call(s32[1]{0:T(128)} %bitcast.refs_0_.place_ref, s32[8]{0:T(128)S(1)} %copy-done.4, s32[128]{0:T(128)S(1)} %copy-done.5, f32[128,288]{1,0:T(8,128)S(1)} %copy-done, f32[128,288]{1,0:T(8,128)S(1)} %collective-permute-done.refs_4_, ...), custom_call_target="tpu_custom_call", output_to_operand_aliasing={{0}: (15, {})} | custom-call | flops 1509949440000 | bytes 5505024 | tf_op jit(solution)/shard_map/scan_chunk/pallas_call | solution.py:301
  54.1 0.0 all-to-all-done.1.got_ref
  54.1 0.0 copy-start.11
  54.1 6.1 %all-to-all-start = ((bf16[16,16,3072]{2,1,0:T(8,128)(2,1)}), bf16[16,16,3072]{2,1,0:T(8,128)(2,1)S(1)}, u32[]{:S(2)}, u32[]{:S(2)}) async-start(bf16[16,16,3072]{2,1,0:T(8,128)(2,1)} %bitcast.24), calls=%async_computation | async-start | bytes 3145728 | tf_op jit(solution)/shard_map/all_to_all | solution.py:455
  60.2 0.1 eq.26
  60.3 0.0 copy-done.11
  60.3 0.1 copy.28.range_ref
  60.4 0.1 reduce_or.9
  60.5 0.6 convert_reduce_fusion.1
  61.1 0.1 convert_reduce_fusion
  61.3 0.1 select_reduce_fusion.source_ref
  61.4 0.7 broadcast_in_dim.24.count_ref
  62.0 2.0 %settle_edges.1 = (bf16[12,3,4096]{2,1,0:T(4,128)(2,1)}, f32[4,2]{1,0:T(4,128)S(1)}) custom-call(s32[12]{0:T(128)S(1)} %select_reduce_fusion.source_ref, s32[9]{0:T(128)S(1)} %broadcast_in_dim.24.count_ref, s32[4,2]{1,0:T(4,128)S(1)} %copy.28.range_ref, bf16[16,4,4096]{2,1,0:T(4,128)(2,1)} %all-to-all-done.2.got_ref), custom_call_target="tpu_custom_call" | custom-call | tf_op jit(solution)/shard_map/settle_edges/pallas_call | solution.py:381
  64.1 0.6 copy.29
  64.7 9.7 %settle_states.2.refs_0_ = bf16[12,16,4096]{2,1,0:T(8,128)(2,1)} custom-call(s32[12]{0:T(128)S(1)} %select_reduce_fusion.source_ref, s32[9]{0:T(128)S(1)} %broadcast_in_dim.24.count_ref, bf16[16,16,1024]{2,1,0:T(8,128)(2,1)} %all-to-all-done.1.got_ref), custom_call_target="tpu_custom_call" | custom-call | tf_op jit(solution)/shard_map/settle_states/pallas_call | solution.py:419
  74.4 21.9 %all-to-all-done.got_ref = bf16[16,16,3072]{2,1,0:T(8,128)(2,1)S(1)} async-done(((bf16[16,16,3072]{2,1,0:T(8,128)(2,1)}), bf16[16,16,3072]{2,1,0:T(8,128)(2,1)S(1)}, u32[]{:S(2)}, u32[]{:S(2)}) %all-to-all-start) | async-done | bytes 1572896 | tf_op jit(solution)/shard_map/all_to_all | solution.py:455
  96.4 1.6 %settle_states.3 = bf16[12,16,4096]{2,1,0:T(8,128)(2,1)} custom-call(s32[12]{0:T(128)S(1)} %select_reduce_fusion.source_ref, s32[9]{0:T(128)S(1)} %broadcast_in_dim.24.count_ref, bf16[16,16,3072]{2,1,0:T(8,128)(2,1)S(1)} %all-to-all-done.got_ref, bf16[12,16,4096]{2,1,0:T(8,128)(2,1)} %settle_states.2.refs_0_), custom_call_target="tpu_custom_call", output_to_operand_aliasing={{}: (3, {})} | custom-call | tf_op jit(solution)/shard_map/settle_states/pallas_call | solution.py:419
  (1 shorter events, 0.0 us)
Async XLA Ops:
  0.6 0.8 copy-start.1
  1.5 0.7 copy-start.2
  2.2 6.6 %copy-start.3 = (s32[8]{0:T(128)S(1)}, s32[8]{0:T(128)}, u32[]{:S(2)}) copy-start(s32[8]{0:T(128)} %length_ref.1) | copy-start | bytes 100
  2.2 6.6 %copy-start.4 = (s32[8]{0:T(128)S(1)}, s32[8]{0:T(128)}, u32[]{:S(2)}) copy-start(s32[8]{0:T(128)} %accepted_ref.1) | copy-start | bytes 100
  2.2 6.6 %copy-start.5 = (s32[128]{0:T(128)S(1)}, s32[128]{0:T(128)}, u32[]{:S(2)}) copy-start(s32[128]{0:T(128)} %owner_ref.1) | copy-start | bytes 1540
  7.4 12.0 %copy-start = (f32[128,288]{1,0:T(8,128)S(1)}, f32[128,288]{1,0:T(8,128)}, u32[]{:S(2)}) copy-start(f32[128,288]{1,0:T(8,128)} %get-tuple-element.12.refs_3_._) | copy-start | bytes 442372
  7.4 12.0 %copy-start.6 = (f32[4096]{0:T(1024)S(1)}, f32[4096]{0:T(1024)}, u32[]{:S(2)}) copy-start(f32[4096]{0:T(1024)} %param.28) | copy-start | bytes 49156
  7.4 12.0 %copy-start.7 = (f32[4096]{0:T(1024)S(1)}, f32[4096]{0:T(1024)}, u32[]{:S(2)}) copy-start(f32[4096]{0:T(1024)} %param.30) | copy-start | bytes 49156
  7.4 12.0 %copy-start.8 = (f32[256]{0:T(256)S(1)}, f32[256]{0:T(256)}, u32[]{:S(2)}) copy-start(f32[256]{0:T(256)} %param.24) | copy-start | bytes 3076
  7.5 12.0 %copy-start.9 = (f32[16]{0:T(128)S(1)}, f32[16]{0:T(128)}, u32[]{:S(2)}) copy-start(f32[16]{0:T(128)} %param.25) | copy-start | bytes 196
  7.5 12.0 %copy-start.10 = (f32[16]{0:T(128)S(1)}, f32[16]{0:T(128)}, u32[]{:S(2)}) copy-start(f32[16]{0:T(128)} %param.26) | copy-start | bytes 196
  7.5 11.9 %collective-permute-start = (f32[128,288]{1,0:T(8,128)}, f32[128,288]{1,0:T(8,128)S(1)}, u32[]{:S(2)}, u32[]{:S(2)}) collective-permute-start(f32[128,288]{1,0:T(8,128)} %get-tuple-element.12.refs_3_._), channel_id=1, source_target_pairs={{0,1},{1,0},{2,3},{3,2},{4,5},{5,4},{6,7},{7,6},{8,9},{9,8},{10,11... | collective-permute-start | bytes 442376 | tf_op jit(solution)/shard_map/ppermute | solution.py:450
  12.5 20.5 %all-to-all-start.2 = ((bf16[16,4,4096]{2,1,0:T(4,128)(2,1)}), bf16[16,4,4096]{2,1,0:T(4,128)(2,1)}, u32[]{:S(2)}, u32[]{:S(2)}) async-start(bf16[16,4,4096]{2,1,0:T(4,128)(2,1)} %kept_edges.1), calls=%async_computation.2 | async-start | bytes 1048576 | tf_op jit(solution)/shard_map/all_to_all | solution.py:455
  33.1 21.0 %all-to-all-start.1 = ((bf16[16,16,1024]{2,1,0:T(8,128)(2,1)}), bf16[16,16,1024]{2,1,0:T(8,128)(2,1)}, u32[]{:S(2)}, u32[]{:S(2)}) async-start(bf16[16,16,1024]{2,1,0:T(8,128)(2,1)} %bitcast.27), calls=%async_computation.1 | async-start | bytes 1048576 | tf_op jit(solution)/shard_map/all_to_all | solution.py:455
  54.1 6.2 %copy-start.11 = (s32[4,2]{0,1:T(2,128)S(1)}, s32[4,2]{0,1:T(2,128)}, u32[]{:S(2)}) copy-start(s32[4,2]{0,1:T(2,128)} %param.34) | copy-start | bytes 100
  54.1 42.2 %all-to-all-start = ((bf16[16,16,3072]{2,1,0:T(8,128)(2,1)}), bf16[16,16,3072]{2,1,0:T(8,128)(2,1)S(1)}, u32[]{:S(2)}, u32[]{:S(2)}) async-start(bf16[16,16,3072]{2,1,0:T(8,128)(2,1)} %bitcast.24), calls=%async_computation | async-start | bytes 3145728 | tf_op jit(solution)/shard_map/all_to_all | solution.py:455

commit v3 on v1

v3 whole, which is shorter than its diff:
```python
import functools

import jax
import jax.numpy as jnp
from jax import lax
from jax.experimental import pallas as pl
from jax.experimental.pallas import tpu as pltpu
from jax.sharding import PartitionSpec as P

EPSILON = 1e-06
SQUARE_FLOOR = 0.25
LOG2_E = 1.4426950408889634
LANES = 128
EDGE_ROWS = 4
DIGIT = 7
VMEM_BYTES = 48 * 1024 * 1024
ROUND = 4
VECTOR_WEIGHT = 30000


def iota(shape, axis):
    return lax.broadcasted_iota(jnp.int32, shape, axis)


def one_hot(condition):
    return jnp.where(condition, 1.0, 0.0).astype(jnp.bfloat16)


def dot(lhs, rhs):
    return jnp.dot(lhs, rhs, preferred_element_type=jnp.float32)


def in_hbm(array):
    return pltpu.with_memory_space_constraint(array, pltpu.HBM)


def silu(value):
    return value * (0.5 + 0.5 * jnp.tanh(0.5 * value))


def to_step_major(requests, steps):
    rows = requests * steps
    row, col = iota((rows, rows), 0), iota((rows, rows), 1)
    return one_hot(col == lax.rem(row, requests) * steps + lax.div(row, requests))


def to_request_major(requests, steps):
    rows = requests * steps
    row, col = iota((rows, rows), 0), iota((rows, rows), 1)
    return one_hot(row == lax.rem(col, requests) * steps + lax.div(col, requests))


def by_request(index, scalars):
    out = jnp.zeros_like(index)
    for request, scalar in enumerate(scalars):
        out = jnp.where(index == request, scalar, out)
    return out


def conv_kernel(
    place_ref, accepted_ref, length_ref, owner_ref, x_ref, edge_ref, weight_ref, bias_ref, proj_ref,
    conv_ref, partial_ref, slot_ref,
):
    lags, requests, block = edge_ref.shape
    taps = weight_ref.shape[0]
    steps = x_ref.shape[0] // requests
    slots = slot_ref.shape[0]
    stream = dot(to_step_major(requests, steps), x_ref[...])
    window = [edge_ref[k].astype(jnp.float32) for k in range(lags)]
    window += [stream[t * requests : (t + 1) * requests] for t in range(steps)]
    weight = [weight_ref[k : k + 1, :] for k in range(taps)]
    outs = []
    for t in range(steps):
        summed = bias_ref[...] + weight[0] * window[t]
        for k in range(1, taps):
            summed = summed + weight[k] * window[t + k]
        outs.append(silu(summed))
    conv_out = jnp.concatenate(outs, axis=0).astype(jnp.bfloat16)
    conv_ref[...] = conv_out
    partial = lax.dot_general(
        conv_out, proj_ref[...], (((1,), (1,)), ((), ())), preferred_element_type=jnp.float32
    )

    @pl.when(pl.program_id(0) == 0)
    def _():
        partial_ref[...] = partial

    @pl.when(pl.program_id(0) > 0)
    def _():
        partial_ref[...] += partial

    base = place_ref[0] * requests
    accepted = [accepted_ref[r] for r in range(requests)]
    lengths = [length_ref[r] + accepted[r] + 1 for r in range(requests)]
    owners = [owner_ref[base + r] for r in range(requests)]
    rows = jnp.concatenate(window, axis=0).astype(jnp.bfloat16)
    height, count = slots * EDGE_ROWS, rows.shape[0]
    row, col = iota((height, count), 0), iota((1, count), 1)
    request, lag = lax.rem(col, requests), lax.rem(row, EDGE_ROWS)
    pick = (
        (lax.div(row, EDGE_ROWS) == by_request(request, owners))
        & (lax.div(col, requests) - by_request(request, accepted) == lag)
        & (lag < lags)
    )
    picked = dot(one_hot(pick), rows)
    low = [length & ((1 << DIGIT) - 1) for length in lengths]
    high = [length >> DIGIT for length in lengths]
    numbers = by_request(iota((1, block), 1), accepted + low + high).astype(jnp.float32)
    last = lax.rem(iota((height, block), 0), EDGE_ROWS) == lags
    picked = jnp.where(last, jnp.broadcast_to(numbers, (height, block)), picked)
    for s in range(slots):
        slot_ref[s] = picked[s * EDGE_ROWS : (s + 1) * EDGE_ROWS].astype(jnp.bfloat16)


def conv_project(scalars, x_in, conv_edge, conv_weight, conv_bias, proj, slots):
    rows, channels = x_in.shape
    lags, requests, _ = conv_edge.shape
    taps, width = conv_weight.shape[0], proj.shape[0]
    block = min(1024, channels)
    return pl.pallas_call(
        conv_kernel,
        grid=(channels // block,),
        in_specs=[pl.BlockSpec(memory_space=pltpu.SMEM)] * len(scalars)
        + [
            pl.BlockSpec((rows, block), lambda j: (0, j)),
            pl.BlockSpec((lags, requests, block), lambda j: (0, 0, j)),
            pl.BlockSpec((taps, block), lambda j: (0, j)),
            pl.BlockSpec((1, block), lambda j: (0, j)),
            pl.BlockSpec((width, block), lambda j: (0, j)),
        ],
        out_specs=[
            pl.BlockSpec((rows, block), lambda j: (0, j)),
            pl.BlockSpec((rows, width), lambda j: (0, 0)),
            pl.BlockSpec((slots, EDGE_ROWS, block), lambda j: (0, 0, j)),
        ],
        out_shape=[
            pltpu.HBM((rows, channels), jnp.bfloat16),
            pltpu.HBM((rows, width), jnp.float32),
            pltpu.HBM((slots, EDGE_ROWS, channels), jnp.bfloat16),
        ],
        compiler_params=pltpu.CompilerParams(
            dimension_semantics=("arbitrary",), vmem_limit_bytes=VMEM_BYTES
        ),
        name="conv_project",
    )(*scalars, *(in_hbm(a) for a in (x_in, conv_edge, conv_weight, conv_bias, proj)))


def rms_scaled(values, gain, floor_value, eps_value):
    square = jnp.mean(values * values, axis=-1, keepdims=True)
    return (values * lax.rsqrt(jnp.maximum(square, floor_value) + eps_value) * gain).astype(jnp.bfloat16)


def summed(part_refs):
    total = part_refs[0][...]
    for part in part_refs[1:]:
        total = total + part[...]
    return total


def softplus(raw):
    return jnp.maximum(raw, 0.0) + jnp.log1p(jnp.exp(-jnp.abs(raw)))


def kept_kernel(parts, *refs):
    place_ref, accepted_ref, owner_ref = refs[:3]
    (
        dt_gain_ref, b_gain_ref, dt_weight_ref, dt_bias_ref, a_log_ref, conv_ref, state_ref,
        slot_ref, low_ref, in_ref, size_ref, drive_ref, rate_ref,
    ) = refs[3 + parts :]
    rank, states = dt_gain_ref.shape[1], b_gain_ref.shape[1]
    requests = accepted_ref.shape[0]
    rows, block = conv_ref.shape
    steps = rows // requests

    @pl.when(pl.program_id(0) == 0)
    def _():
        total = summed(refs[3 : 3 + parts])
        low_ref[...] = rms_scaled(total[:, :rank], dt_gain_ref[...], 0.0, EPSILON)
        in_map = rms_scaled(total[:, rank : rank + states], b_gain_ref[...], SQUARE_FLOOR, 0.0)
        turned = jnp.transpose(in_map.astype(jnp.float32))
        for row in range(rows):
            t, r = divmod(row, requests)
            in_ref[r * states : (r + 1) * states, t * LANES : (t + 1) * LANES] = (
                jnp.broadcast_to(turned[:, row : row + 1], (states, LANES))
            )

    row = iota((rows, 1), 0)
    live = lax.div(row, requests) < by_request(
        lax.rem(row, requests), [accepted_ref[r] for r in range(requests)]
    )
    size = softplus(dot(low_ref[...], dt_weight_ref[...]) + dt_bias_ref[...])
    size = jnp.where(live, size, 0.0)
    drive = size * conv_ref[...].astype(jnp.float32)
    for c in range(block // LANES):
        size_ref[c] = size[:, c * LANES : (c + 1) * LANES]
        drive_ref[c] = drive[:, c * LANES : (c + 1) * LANES]
    rate_ref[...] = jnp.exp(a_log_ref[...]) * (-LOG2_E)

    span = min(1024, block)
    halves = states // 8
    for r in range(requests):
        slot = owner_ref[place_ref[0] * requests + r]
        rounds = lax.div(accepted_ref[r] + (ROUND - 1), ROUND)
        for first in range(0, block, span):
            tiles = [slice(c, c + LANES) for c in range(first, first + span, LANES)]

            def one_round(i, hidden):
                hidden = [list(h) for h in hidden]
                for u in range(ROUND):
                    t = i * ROUND + u
                    at = pl.ds(t * requests + r, 8, stride=0)
                    b = [
                        in_ref[
                            r * states + 8 * h : r * states + 8 * (h + 1),
                            pl.ds(pl.multiple_of(t * LANES, LANES), LANES),
                        ]
                        for h in range(halves)
                    ]
                    for c, tile in enumerate(tiles):
                        place = first // LANES + c
                        now, drive = size_ref[place, at, :], drive_ref[place, at, :]
                        for h in range(halves):
                            decay = jnp.exp2(now * rate_ref[8 * h : 8 * (h + 1), tile])
                            hidden[h][c] = decay * hidden[h][c] + drive * b[h]
                return tuple(tuple(h) for h in hidden)

            old = state_ref[r * states : (r + 1) * states, first : first + span].astype(jnp.float32)
            start = tuple(
                tuple(
                    old[8 * h : 8 * (h + 1), c * LANES : (c + 1) * LANES] for c in range(len(tiles))
                )
                for h in range(halves)
            )
            done = lax.fori_loop(0, rounds, one_round, start)
            new = jnp.concatenate([jnp.concatenate(h, axis=1) for h in done], axis=0)
            slot_ref[slot, :, first : first + span] = new.astype(jnp.bfloat16)


def kept_states(scalars, partials, gains, dt_weight, dt_bias, a_log, conv, state, slots):
    rows, channels = conv.shape
    states, rank = a_log.shape[0], dt_weight.shape[0]
    requests = scalars[1].shape[0]
    block = min(1024, channels)

    def whole(array):
        return pl.BlockSpec(array.shape, lambda j: (0, 0))

    wide = [in_hbm(dt_weight), dt_bias, in_hbm(a_log), in_hbm(conv), in_hbm(state)]
    return pl.pallas_call(
        functools.partial(kept_kernel, len(partials)),
        grid=(channels // block,),
        in_specs=[pl.BlockSpec(memory_space=pltpu.SMEM)] * len(scalars)
        + [whole(a) for a in (*partials, *gains)]
        + [pl.BlockSpec((a.shape[0], block), lambda j: (0, j)) for a in wide],
        out_specs=pl.BlockSpec((slots, states, block), lambda j: (0, 0, j)),
        out_shape=pltpu.HBM((slots, states, channels), jnp.bfloat16),
        scratch_shapes=[
            pltpu.VMEM((rows, rank), jnp.bfloat16),
            pltpu.VMEM((requests * states, rows // requests * LANES), jnp.float32),
            pltpu.VMEM((block // LANES, rows, LANES), jnp.float32),
            pltpu.VMEM((block // LANES, rows, LANES), jnp.float32),
            pltpu.VMEM((states, block), jnp.float32),
        ],
        compiler_params=pltpu.CompilerParams(
            dimension_semantics=("arbitrary",), vmem_limit_bytes=VMEM_BYTES
        ),
        cost_estimate=pl.CostEstimate(
            flops=VECTOR_WEIGHT * 4 * rows * states * channels,
            transcendentals=rows * states * channels,
            bytes_accessed=2 * channels * (rows + rank + states * (requests + slots)),
        ),
        name="kept_states",
    )(*scalars, *partials, *gains, *wide)


def scan_kernel(parts, *refs):
    (
        dt_gain_ref, b_gain_ref, c_gain_ref, dt_weight_ref, dt_bias_ref, a_log_ref, skip_ref,
        conv_ref, state_ref, z_ref, mixed_ref,
        low_ref, in_ref, out_ref, size_ref, drive_ref, rate_ref, start_ref, sum_ref,
    ) = refs[parts:]
    rank, states = dt_gain_ref.shape[1], b_gain_ref.shape[1]
    rows, block = conv_ref.shape
    requests = state_ref.shape[0] // states
    steps = rows // requests

    @pl.when(pl.program_id(0) == 0)
    def _():
        total = summed(refs[:parts])
        low_ref[...] = rms_scaled(total[:, :rank], dt_gain_ref[...], 0.0, EPSILON)
        in_map = rms_scaled(total[:, rank : rank + states], b_gain_ref[...], SQUARE_FLOOR, 0.0)
        out_map = rms_scaled(total[:, rank + states :], c_gain_ref[...], SQUARE_FLOOR, 0.0)
        wide = states * LANES
        spread = one_hot(lax.div(iota((states, wide), 1), LANES) == iota((states, wide), 0))
        in_ref[...] = dot(in_map, spread)
        out_ref[...] = dot(out_map, spread)

    conv = conv_ref[...].astype(jnp.float32)
    size = softplus(dot(low_ref[...], dt_weight_ref[...]) + dt_bias_ref[...])
    size_ref[...] = size
    drive_ref[...] = size * conv
    start_ref[...] = dot(to_step_major(requests, states), state_ref[...])
    rate = jnp.exp(a_log_ref[...]) * (-LOG2_E)
    for n in range(states):
        rate_ref[n * requests : (n + 1) * requests, :] = jnp.broadcast_to(
            rate[n : n + 1, :], (requests, block)
        )

    pair = 2 if block % (2 * LANES) == 0 else 1

    def columns(c, carry):
        spans = [pl.ds(pl.multiple_of((c * pair + i) * LANES, LANES), LANES) for i in range(pair)]
        start = tuple(
            tuple(start_ref[n * requests : (n + 1) * requests, s] for s in spans)
            for n in range(states)
        )

        def step(t, hidden):
            at = pl.ds(pl.multiple_of(t * requests, requests), requests)
            sizes = [size_ref[at, s] for s in spans]
            drives = [drive_ref[at, s] for s in spans]
            sums = [None] * pair
            new = []
            for n in range(states):
                b = in_ref[at, n * LANES : (n + 1) * LANES]
                c_map = out_ref[at, n * LANES : (n + 1) * LANES]
                own = slice(n * requests, (n + 1) * requests)
                mine = []
                for i, s in enumerate(spans):
                    h = jnp.exp2(sizes[i] * rate_ref[own, s]) * hidden[n][i] + drives[i] * b
                    term = c_map * h
                    sums[i] = term if sums[i] is None else sums[i] + term
                    mine.append(h)
                new.append(tuple(mine))
            for i, s in enumerate(spans):
                sum_ref[at, s] = sums[i]
            return tuple(new)

        lax.fori_loop(0, steps, step, start, unroll=2)
        return carry

    lax.fori_loop(0, block // (pair * LANES), columns, 0)

    gate = silu(dot(to_step_major(requests, steps), z_ref[...]))
    mixed = ((sum_ref[...] + skip_ref[...] * conv) * gate).astype(jnp.bfloat16)
    mixed_ref[...] = dot(to_request_major(requests, steps), mixed).astype(jnp.bfloat16)


def scan(partials, gains, dt_weight, dt_bias, a_log, skip, conv, state, z_gate):
    rows, channels = conv.shape
    states, rank = a_log.shape[0], dt_weight.shape[0]
    block = min(512, channels)

    def whole(array):
        return pl.BlockSpec(array.shape, lambda j: (0, 0))

    wide = [in_hbm(dt_weight), dt_bias, in_hbm(a_log), skip, in_hbm(conv), in_hbm(state), in_hbm(z_gate)]
    tall = pltpu.VMEM((rows, block), jnp.float32)
    table = pltpu.VMEM((rows, states * LANES), jnp.float32)
    return pl.pallas_call(
        functools.partial(scan_kernel, len(partials)),
        grid=(channels // block,),
        in_specs=[whole(a) for a in (*partials, *gains)]
        + [pl.BlockSpec((a.shape[0], block), lambda j: (0, j)) for a in wide],
        out_specs=pl.BlockSpec((rows, block), lambda j: (0, j)),
        out_shape=jax.ShapeDtypeStruct((rows, channels), jnp.bfloat16),
        scratch_shapes=[
            pltpu.VMEM((rows, rank), jnp.bfloat16), table, table, tall, tall,
            pltpu.VMEM((state.shape[0], block), jnp.float32),
            pltpu.VMEM((state.shape[0], block), jnp.float32),
            tall,
        ],
        compiler_params=pltpu.CompilerParams(
            dimension_semantics=("arbitrary",), vmem_limit_bytes=VMEM_BYTES
        ),
        cost_estimate=pl.CostEstimate(
            flops=VECTOR_WEIGHT * 8 * rows * states * channels,
            transcendentals=rows * states * channels,
            bytes_accessed=2 * channels * (3 * rows + rank),
        ),
        name="scan",
    )(*partials, *gains, *wide)


def edge_kernel(steps, source_ref, count_ref, range_ref, got_ref, edge_ref, stats_ref):
    slots, _, channels = got_ref.shape
    own_most, lags, _ = edge_ref.shape
    for i in range(own_most):

        @pl.when(i < count_ref[0])
        def _():
            edge_ref[i] = got_ref[source_ref[i], :lags, :]

        @pl.when(i >= count_ref[0])
        def _():
            edge_ref[i] = jnp.zeros((lags, channels), jnp.bfloat16)

    requests = count_ref.shape[0] - 1
    numbers = got_ref[:, lags, :LANES].astype(jnp.float32)
    lane, slot = iota((slots, LANES), 1), iota((slots, LANES), 0)
    request = slot * requests + lax.rem(lane, requests)
    counts = jnp.where(lane < requests, numbers, 0.0)
    digit = lax.div(lane, requests)
    lengths = jnp.where(digit == 1, numbers, 0.0) + jnp.where(
        digit == 2, numbers * float(1 << DIGIT), 0.0
    )
    tenants = range_ref.shape[0]
    tiles = (tenants, 2)
    sums, loads, members = [], [], []
    for k in range(tenants):
        start, end = range_ref[k, 0], range_ref[k, 1]
        inside = (request >= start) & (request < end)
        sums.append(jnp.sum(jnp.where(inside, counts, 0.0), keepdims=True))
        loads.append(jnp.sum(jnp.where(inside, lengths, 0.0), keepdims=True))
        members.append(jnp.full((1, 1), 1, jnp.int32) * (end - start))
    members = [m.astype(jnp.float32) for m in members]
    mean = sum(loads[1:], loads[0]) / sum(members[1:], members[0])
    out = jnp.zeros(tiles, jnp.float32)
    row, col = iota(tiles, 0), iota(tiles, 1)
    for k in range(tenants):
        rate = sums[k] / (float(steps) * members[k])
        load = loads[k] / members[k] / mean
        out = jnp.where(row == k, jnp.where(col == 0, rate, load), out)
    stats_ref[...] = out


def settle_edges(source, count, tenant_range, got, own_most, lags, steps):
    smem = pl.BlockSpec(memory_space=pltpu.SMEM)
    vmem = pl.BlockSpec(memory_space=pltpu.VMEM)
    return pl.pallas_call(
        functools.partial(edge_kernel, steps),
        in_specs=[smem, smem, smem, vmem],
        out_specs=[vmem, vmem],
        out_shape=[
            jax.ShapeDtypeStruct((own_most, lags, got.shape[2]), jnp.bfloat16),
            jax.ShapeDtypeStruct((tenant_range.shape[0], 2), jnp.float32),
        ],
        compiler_params=pltpu.CompilerParams(vmem_limit_bytes=VMEM_BYTES),
        name="settle_edges",
    )(source, count, tenant_range, got)


def settle_kernel(source_ref, count_ref, got_ref, owned_ref, blank_ref, sems):
    own_most = owned_ref.shape[0]
    blank_ref[...] = jnp.zeros_like(blank_ref)

    def copy(i, filled):
        origin = got_ref.at[source_ref[i]] if filled else blank_ref
        return pltpu.make_async_copy(origin, owned_ref.at[i], sems.at[i])

    for act in ("start", "wait"):
        for i in range(own_most):
            for filled in (True, False):

                @pl.when((i < count_ref[0]) == filled)
                def _():
                    getattr(copy(i, filled), act)()


def settle_states(source, count, got, own_most):
    smem = pl.BlockSpec(memory_space=pltpu.SMEM)
    anywhere = pl.BlockSpec(memory_space=pl.ANY)
    return pl.pallas_call(
        settle_kernel,
        in_specs=[smem, smem, anywhere],
        out_specs=anywhere,
        out_shape=jax.ShapeDtypeStruct((own_most, *got.shape[1:]), got.dtype),
        scratch_shapes=[
            pltpu.VMEM(got.shape[1:], got.dtype),
            pltpu.SemaphoreType.DMA((own_most,)),
        ],
        compiler_params=pltpu.CompilerParams(vmem_limit_bytes=VMEM_BYTES),
        name="settle_states",
    )(source, count, in_hbm(got))


def per_device(
    x_in, z_gate, conv_edge, conv_weight, conv_bias, x_proj_weight, dt_gain, b_gain, c_gain,
    dt_proj_weight, dt_bias, a_log, skip, ssm_state, accepted, prompt_len, tenant_range, owner,
):
    requests, states, channels = ssm_state.shape
    lags = conv_edge.shape[1]
    owners = lax.axis_size("req")
    own_most = min(requests + requests // 2, owners)
    place = lax.axis_index("req").astype(jnp.int32).reshape(1)

    conv, partial, edge_slots = conv_project(
        (place, accepted, prompt_len, owner), x_in, jnp.transpose(conv_edge, (1, 0, 2)),
        conv_weight, conv_bias.reshape(1, -1), x_proj_weight.T, owners,
    )
    if lax.axis_size("tp") == 2:
        partials = (partial, lax.ppermute(partial, "tp", [(0, 1), (1, 0)]))
    else:
        partials = (lax.psum(partial, "tp"),)

    def exchange(slots):
        return lax.all_to_all(slots, "req", split_axis=0, concat_axis=0, tiled=True)

    got_edges = exchange(edge_slots)

    hits = jnp.any(owner.reshape(owners, requests) == place, axis=1)
    ids = jnp.arange(owners, dtype=jnp.int32)
    ranks = jnp.sum((hits[None, :] & (ids[None, :] < ids[:, None])).astype(jnp.int32), axis=1)
    at = hits[None, :] & (ranks[None, :] == jnp.arange(own_most, dtype=jnp.int32)[:, None])
    source = jnp.sum(jnp.where(at, ids[None, :], 0), axis=1)
    count = jnp.broadcast_to(jnp.sum(hits.astype(jnp.int32)), (requests + 1,))

    gains = (dt_gain.reshape(1, -1), b_gain.reshape(1, -1), c_gain.reshape(1, -1))
    bias = dt_bias.reshape(1, -1)
    state = ssm_state.reshape(requests * states, channels)
    slots = kept_states(
        (place, accepted, owner), partials, gains[:2], dt_proj_weight, bias, a_log, conv, state, owners
    )
    got = exchange(slots)
    mixed = scan(
        partials, gains, dt_proj_weight, bias, a_log, skip.reshape(1, -1), conv, state, z_gate
    )
    owned_edge, tenant_stats = settle_edges(
        source, count, tenant_range, got_edges, own_most, lags, x_in.shape[0] // requests
    )
    owned = settle_states(source, count, got, own_most)
    return (mixed, owned, owned_edge, tenant_stats)


def solution(mesh):
    placed = (
        P("req", "tp"),
        P("req", "tp"),
        P("req", None, "tp"),
        P(None, "tp"),
        P("tp"),
        P("tp", None),
        P(),
        P(),
        P(),
        P(None, "tp"),
        P("tp"),
        P(None, "tp"),
        P("tp"),
        P("req", None, "tp"),
        P("req"),
        P("req"),
        P(),
        P(),
    )
    return jax.shard_map(
        per_device,
        mesh=mesh,
        in_specs=placed,
        out_specs=(P("req", "tp"), P("req", None, "tp"), P("req", None, "tp"), P()),
        check_vma=False,
    )
```

time: 107 us -> 131 us (1.22)
  the two profiles are of different devices: /device:TPU:11 before, /device:TPU:1 now
where the time goes in v3:
time: 131 us; the launch traced here: 130 us
  Pallas kernels  83.5 us (64%)
  waiting for transfers between devices  23.3 us (18%)
  starting transfers between devices  17.2 us (13%)
  local copies, waits for them, and re-layouts  4.44 us (3%)
    pallas_call x1, Pallas kernels, settle_states(): pl.pallas_call(settle_kernel, in_specs=[smem, smem, anywhere], out_specs=...  49.4 us
    all_to_all x2, waiting for transfers between devices, exchange(): return lax.all_to_all(slots, 'req', split_axis=0, concat_axis=0, tiled=True)  19.2 us
    pallas_call x1, Pallas kernels, scan(): pl.pallas_call(functools.partial(scan_kernel, len(partials)), grid=(chann...  18.9 us
    all_to_all x2, starting transfers between devices, exchange(): return lax.all_to_all(slots, 'req', split_axis=0, concat_axis=0, tiled=True)  15.9 us
    pallas_call x1, Pallas kernels, kept_states(): pl.pallas_call(functools.partial(kept_kernel, len(partials)), grid=(chann...  7.22 us
    pallas_call x1, Pallas kernels, conv_project(): pl.pallas_call(conv_kernel, grid=(channels // block,), in_specs=[pl.Block...  5.92 us
    ppermute x1, waiting for transfers between devices, per_device(): partials = (partial, lax.ppermute(partial, 'tp', [(0, 1), (1, 0)]))  4.09 us
    unnamed x28, local copies, waits for them, and re-layouts  3.66 us
  transfers between devices with their start and end apart: 3, of which 2 were waited for; matrix products, arithmetic and copies ran while one was open for 2% of the time, Pallas kernels for 22%

profile of v3, /device:TPU:1, one launch (start us, length us, event | category | flops | bytes accessed | tf_op | source)
XLA Modules:
  0.0 130.3 jit_solution(9065820151360475865)
XLA Ops:
  0.6 0.0 copy-start
  0.7 0.6 copy-done
  1.3 0.0 copy-start.1
  1.3 0.7 copy-done.1
  2.0 0.0 copy-start.3
  2.0 0.7 copy-done.3
  2.6 0.0 copy-start.4
  2.6 0.0 copy-start.12
  2.6 0.0 copy-start.2
  2.6 0.0 copy-start.7
  2.6 0.0 copy-start.9
  2.6 0.0 copy-start.10
  2.6 5.9 %conv_project.1 = (bf16[128,4096]{1,0:T(8,128)(2,1)}, f32[128,288]{1,0:T(8,128)}, bf16[16,4,4096]{2,1,0:T(4,128)(2,1)}) custom-call(s32[1]{0:T(128)} %bitcast.place_ref.refs_0_, s32[8]{0:T(128)S(1)} %copy-done.1, s32[8]{0:T(128)S(1)} %copy-done, s32[128]{0:T(128)S(1)} %copy-done.3, bf16[128,4096]{1,0:T(8,128)(2,1)} %x_ref.1, bf16[3,8,4096]{2,1,0:T(8,128)(2,1)} %bitcast.19, ...), custom_call_target="tpu_custom_call" | custom-call | tf_op jit(solution)/shard_map/conv_project/pallas_call | solution.py:120
  8.6 7.3 %all-to-all-start.1 = ((bf16[16,4,4096]{2,1,0:T(4,128)(2,1)}), bf16[16,4,4096]{2,1,0:T(4,128)(2,1)}, u32[]{:S(2)}, u32[]{:S(2)}) async-start(bf16[16,4,4096]{2,1,0:T(4,128)(2,1)} %get-tuple-element.11), calls=%async_computation.1 | async-start | bytes 1048576 | tf_op jit(solution)/shard_map/all_to_all | solution.py:497
  15.9 1.2 collective-permute-start
  17.1 0.0 copy-done.4
  17.1 0.1 eq.26
  17.2 0.1 reduce_or.9
  17.3 0.1 convert_reduce_fusion
  17.5 0.7 convert_reduce_fusion.1
  18.2 0.0 copy-done.12
  18.2 0.1 copy.26.range_ref
  18.3 0.1 select_reduce_fusion.source_ref
  18.4 4.1 %collective-permute-done.refs_1_.refs_4_ = f32[128,288]{1,0:T(8,128)S(1)} collective-permute-done((f32[128,288]{1,0:T(8,128)}, f32[128,288]{1,0:T(8,128)S(1)}, u32[]{:S(2)}, u32[]{:S(2)}) %collective-permute-start) | collective-permute-done | bytes 147488 | tf_op jit(solution)/shard_map/ppermute | solution.py:492
  22.5 0.0 copy-done.2
  22.5 0.0 copy-done.7
  22.5 0.0 copy-done.9
  22.5 0.0 copy-done.10
  22.5 0.0 copy-start.5
  22.5 0.9 copy-done.5
  23.4 7.2 %kept_states.1 = bf16[16,16,4096]{2,1,0:T(8,128)(2,1)} custom-call(s32[1]{0:T(128)} %bitcast.place_ref.refs_0_, s32[8]{0:T(128)S(1)} %copy-done.2, s32[128]{0:T(128)S(1)} %copy-done.4, f32[128,288]{1,0:T(8,128)S(1)} %copy-done.5, f32[128,288]{1,0:T(8,128)S(1)} %collective-permute-done.refs_1_.refs_4_, f32[1,256]{1,0:T(1,128)S(1)} %bitcast.13, ...), custom_call_target="tpu_custom_call" | custom-call | flops 1006632960000 | bytes 6291456 | tf_op jit(solution)/shard_map/kept_states/pallas_call | solution.py:249
  30.7 0.0 copy-start.6
  30.7 0.0 copy-start.8
  30.7 0.0 copy-start.11
  30.7 0.0 all-to-all-done.1.got_ref
  30.7 8.6 %all-to-all-start = ((bf16[16,16,4096]{2,1,0:T(8,128)(2,1)}), bf16[16,16,4096]{2,1,0:T(8,128)(2,1)}, u32[]{:S(2)}, u32[]{:S(2)}) async-start(bf16[16,16,4096]{2,1,0:T(8,128)(2,1)} %kept_states.1), calls=%async_computation | async-start | bytes 4194304 | tf_op jit(solution)/shard_map/all_to_all | solution.py:497
  39.3 0.0 copy-done.6
  39.3 0.0 copy-done.8
  39.3 0.0 copy-done.11
  39.3 18.9 %scan.1 = bf16[128,4096]{1,0:T(8,128)(2,1)} custom-call(f32[128,288]{1,0:T(8,128)S(1)} %copy-done.6, f32[128,288]{1,0:T(8,128)S(1)} %collective-permute-done.refs_1_.refs_4_, f32[1,256]{1,0:T(1,128)S(1)} %bitcast.14, f32[1,16]{1,0:T(1,128)S(1)} %bitcast.16, f32[1,16]{1,0:T(1,128)S(1)} %bitcast.17, bf16[256,4096]{1,0:T(8,128)(2,1)} %refs_7_.3, ...), custom_call_target="tpu_custom_call" | custom-call | flops 2013265920000 | bytes 5242880 | tf_op jit(solution)/shard_map/scan/pallas_call | solution.py:360
  58.2 0.7 broadcast_in_dim.24.count_ref
  58.9 2.0 %settle_edges.1 = (bf16[12,3,4096]{2,1,0:T(4,128)(2,1)}, f32[4,2]{1,0:T(4,128)S(1)}) custom-call(s32[12]{0:T(128)S(1)} %select_reduce_fusion.source_ref, s32[9]{0:T(128)S(1)} %broadcast_in_dim.24.count_ref, s32[4,2]{1,0:T(4,128)S(1)} %copy.26.range_ref, bf16[16,4,4096]{2,1,0:T(4,128)(2,1)} %all-to-all-done.1.got_ref), custom_call_target="tpu_custom_call" | custom-call | tf_op jit(solution)/shard_map/settle_edges/pallas_call | solution.py:430
  61.0 0.6 copy.27
  61.6 19.2 %all-to-all-done.got_ref = bf16[16,16,4096]{2,1,0:T(8,128)(2,1)} async-done(((bf16[16,16,4096]{2,1,0:T(8,128)(2,1)}), bf16[16,16,4096]{2,1,0:T(8,128)(2,1)}, u32[]{:S(2)}, u32[]{:S(2)}) %all-to-all-start) | async-done | bytes 2097184 | tf_op jit(solution)/shard_map/all_to_all | solution.py:497
  80.9 49.4 %settle_states.1 = bf16[12,16,4096]{2,1,0:T(8,128)(2,1)} custom-call(s32[12]{0:T(128)S(1)} %select_reduce_fusion.source_ref, s32[9]{0:T(128)S(1)} %broadcast_in_dim.24.count_ref, bf16[16,16,4096]{2,1,0:T(8,128)(2,1)} %all-to-all-done.got_ref), custom_call_target="tpu_custom_call" | custom-call | tf_op jit(solution)/shard_map/settle_states/pallas_call | solution.py:463
  (1 shorter events, 0.0 us)
Async XLA Ops:
  0.6 0.7 copy-start
  1.3 0.7 copy-start.1
  2.0 0.7 copy-start.3
  2.6 14.5 %copy-start.4 = (s32[128]{0:T(128)S(1)}, s32[128]{0:T(128)}, u32[]{:S(2)}) copy-start(s32[128]{0:T(128)} %refs_2_.1) | copy-start | bytes 1540
  2.6 15.6 %copy-start.12 = (s32[4,2]{0,1:T(2,128)S(1)}, s32[4,2]{0,1:T(2,128)}, u32[]{:S(2)}) copy-start(s32[4,2]{0,1:T(2,128)} %param.34) | copy-start | bytes 100
  2.6 19.9 %copy-start.2 = (s32[8]{0:T(128)S(1)}, s32[8]{0:T(128)}, u32[]{:S(2)}) copy-start(s32[8]{0:T(128)} %refs_1_.1) | copy-start | bytes 100
  2.6 19.9 %copy-start.7 = (f32[4096]{0:T(1024)S(1)}, f32[4096]{0:T(1024)}, u32[]{:S(2)}) copy-start(f32[4096]{0:T(1024)} %param.28) | copy-start | bytes 49156
  2.6 19.9 %copy-start.9 = (f32[256]{0:T(256)S(1)}, f32[256]{0:T(256)}, u32[]{:S(2)}) copy-start(f32[256]{0:T(256)} %param.24) | copy-start | bytes 3076
  2.6 19.9 %copy-start.10 = (f32[16]{0:T(128)S(1)}, f32[16]{0:T(128)}, u32[]{:S(2)}) copy-start(f32[16]{0:T(128)} %param.25) | copy-start | bytes 196
  8.6 22.1 %all-to-all-start.1 = ((bf16[16,4,4096]{2,1,0:T(4,128)(2,1)}), bf16[16,4,4096]{2,1,0:T(4,128)(2,1)}, u32[]{:S(2)}, u32[]{:S(2)}) async-start(bf16[16,4,4096]{2,1,0:T(4,128)(2,1)} %get-tuple-element.11), calls=%async_computation.1 | async-start | bytes 1048576 | tf_op jit(solution)/shard_map/all_to_all | solution.py:497
  15.9 6.6 %collective-permute-start = (f32[128,288]{1,0:T(8,128)}, f32[128,288]{1,0:T(8,128)S(1)}, u32[]{:S(2)}, u32[]{:S(2)}) collective-permute-start(f32[128,288]{1,0:T(8,128)} %get-tuple-element.9.refs_0_.refs_3_), channel_id=1, source_target_pairs={{0,1},{1,0},{2,3},{3,2},{4,5},{5,4},{6,7},{7,6},{8,9},{9,8},{10,11... | collective-permute-start | bytes 442376 | tf_op jit(solution)/shard_map/ppermute | solution.py:492
  22.5 0.9 copy-start.5
  30.7 8.6 %copy-start.6 = (f32[128,288]{1,0:T(8,128)S(1)}, f32[128,288]{1,0:T(8,128)}, u32[]{:S(2)}) copy-start(f32[128,288]{1,0:T(8,128)} %get-tuple-element.9.refs_0_.refs_3_) | copy-start | bytes 442372
  30.7 8.6 %copy-start.8 = (f32[4096]{0:T(1024)S(1)}, f32[4096]{0:T(1024)}, u32[]{:S(2)}) copy-start(f32[4096]{0:T(1024)} %param.30) | copy-start | bytes 49156
  30.7 8.7 %copy-start.11 = (f32[16]{0:T(128)S(1)}, f32[16]{0:T(128)}, u32[]{:S(2)}) copy-start(f32[16]{0:T(128)} %param.26) | copy-start | bytes 196
  30.7 50.2 %all-to-all-start = ((bf16[16,16,4096]{2,1,0:T(8,128)(2,1)}), bf16[16,16,4096]{2,1,0:T(8,128)(2,1)}, u32[]{:S(2)}, u32[]{:S(2)}) async-start(bf16[16,16,4096]{2,1,0:T(8,128)(2,1)} %kept_states.1), calls=%async_computation | async-start | bytes 4194304 | tf_op jit(solution)/shard_map/all_to_all | solution.py:497

commit v4 on v3

--- a/solution.py
+++ b/solution.py
@@ -12,6 +12,7 @@
 LOG2_E = 1.4426950408889634
 LANES = 128
 EDGE_ROWS = 4
+PLANE = 4
 DIGIT = 7
 VMEM_BYTES = 48 * 1024 * 1024
 ROUND = 4
@@ -57,14 +58,10 @@
     return out
 
 
-def conv_kernel(
-    place_ref, accepted_ref, length_ref, owner_ref, x_ref, edge_ref, weight_ref, bias_ref, proj_ref,
-    conv_ref, partial_ref, slot_ref,
-):
-    lags, requests, block = edge_ref.shape
+def conv_kernel(x_ref, edge_ref, weight_ref, bias_ref, proj_ref, conv_ref, partial_ref):
+    lags, requests, _ = edge_ref.shape
     taps = weight_ref.shape[0]
     steps = x_ref.shape[0] // requests
-    slots = slot_ref.shape[0]
     stream = dot(to_step_major(requests, steps), x_ref[...])
     window = [edge_ref[k].astype(jnp.float32) for k in range(lags)]
     window += [stream[t * requests : (t + 1) * requests] for t in range(steps)]
@@ -89,30 +86,8 @@
     def _():
         partial_ref[...] += partial
 
-    base = place_ref[0] * requests
-    accepted = [accepted_ref[r] for r in range(requests)]
-    lengths = [length_ref[r] + accepted[r] + 1 for r in range(requests)]
-    owners = [owner_ref[base + r] for r in range(requests)]
-    rows = jnp.concatenate(window, axis=0).astype(jnp.bfloat16)
-    height, count = slots * EDGE_ROWS, rows.shape[0]
-    row, col = iota((height, count), 0), iota((1, count), 1)
-    request, lag = lax.rem(col, requests), lax.rem(row, EDGE_ROWS)
-    pick = (
-        (lax.div(row, EDGE_ROWS) == by_request(request, owners))
-        & (lax.div(col, requests) - by_request(request, accepted) == lag)
-        & (lag < lags)
-    )
-    picked = dot(one_hot(pick), rows)
-    low = [length & ((1 << DIGIT) - 1) for length in lengths]
-    high = [length >> DIGIT for length in lengths]
-    numbers = by_request(iota((1, block), 1), accepted + low + high).astype(jnp.float32)
-    last = lax.rem(iota((height, block), 0), EDGE_ROWS) == lags
-    picked = jnp.where(last, jnp.broadcast_to(numbers, (height, block)), picked)
-    for s in range(slots):
-        slot_ref[s] = picked[s * EDGE_ROWS : (s + 1) * EDGE_ROWS].astype(jnp.bfloat16)
-
-
-def conv_project(scalars, x_in, conv_edge, conv_weight, conv_bias, proj, slots):
+
+def conv_project(x_in, conv_edge, conv_weight, conv_bias, proj):
     rows, channels = x_in.shape
     lags, requests, _ = conv_edge.shape
     taps, width = conv_weight.shape[0], proj.shape[0]
@@ -120,8 +95,7 @@
     return pl.pallas_call(
         conv_kernel,
         grid=(channels // block,),
-        in_specs=[pl.BlockSpec(memory_space=pltpu.SMEM)] * len(scalars)
-        + [
+        in_specs=[
             pl.BlockSpec((rows, block), lambda j: (0, j)),
             pl.BlockSpec((lags, requests, block), lambda j: (0, 0, j)),
             pl.BlockSpec((taps, block), lambda j: (0, j)),
@@ -131,18 +105,101 @@
         out_specs=[
             pl.BlockSpec((rows, block), lambda j: (0, j)),
             pl.BlockSpec((rows, width), lambda j: (0, 0)),
-            pl.BlockSpec((slots, EDGE_ROWS, block), lambda j: (0, 0, j)),
         ],
         out_shape=[
             pltpu.HBM((rows, channels), jnp.bfloat16),
             pltpu.HBM((rows, width), jnp.float32),
-            pltpu.HBM((slots, EDGE_ROWS, channels), jnp.bfloat16),
         ],
         compiler_params=pltpu.CompilerParams(
             dimension_semantics=("arbitrary",), vmem_limit_bytes=VMEM_BYTES
         ),
         name="conv_project",
-    )(*scalars, *(in_hbm(a) for a in (x_in, conv_edge, conv_weight, conv_bias, proj)))
+    )(*(in_hbm(a) for a in (x_in, conv_edge, conv_weight, conv_bias, proj)))
+
+
+def kept_edge_kernel(
+    place_ref, accepted_ref, length_ref, owner_ref, x_ref, edge_ref, _, *group_refs
+):
+    lags, requests, block = edge_ref.shape
+    steps = x_ref.shape[0] // requests
+    place = place_ref[0]
+    accepted = [accepted_ref[r] for r in range(requests)]
+    lengths = [length_ref[r] + accepted[r] + 1 for r in range(requests)]
+    deltas = [owner_ref[place * requests + r] ^ place for r in range(requests)]
+    height = len(group_refs) * PLANE * EDGE_ROWS
+    slot = lax.div(iota((height, 1), 0), EDGE_ROWS)
+    lag = lax.rem(iota((height, 1), 0), EDGE_ROWS)
+
+    def pick(request, position):
+        return one_hot(
+            (slot == by_request(request, deltas))
+            & (position - by_request(request, accepted) == lag)
+            & (lag < lags)
+        )
+
+    col = iota((1, requests * steps), 1)
+    picked = dot(pick(lax.div(col, steps), lax.rem(col, steps) + lags), x_ref[...])
+    col = iota((1, lags * requests), 1)
+    edge = jnp.concatenate([edge_ref[k].astype(jnp.float32) for k in range(lags)], axis=0)
+    picked += dot(pick(lax.rem(col, requests), lax.div(col, requests)), edge.astype(jnp.bfloat16))
+    low = [length & ((1 << DIGIT) - 1) for length in lengths]
+    high = [length >> DIGIT for length in lengths]
+    numbers = by_request(iota((1, block), 1), accepted + low + high).astype(jnp.float32)
+    picked = jnp.where(lag == lags, numbers, picked).astype(jnp.bfloat16)
+    group = PLANE * EDGE_ROWS
+    for d, ref in enumerate(group_refs):
+        ref[...] = picked[d * group : (d + 1) * group]
+
+
+def kept_edges(scalars, x_in, conv_edge, after, owners):
+    rows, channels = x_in.shape
+    lags, requests, _ = conv_edge.shape
+    block = min(2048, channels)
+    groups = owners // PLANE
+    return pl.pallas_call(
+        kept_edge_kernel,
+        grid=(channels // block,),
+        in_specs=[pl.BlockSpec(memory_space=pltpu.SMEM)] * len(scalars)
+        + [
+            pl.BlockSpec((rows, block), lambda j: (0, j)),
+            pl.BlockSpec((lags, requests, block), lambda j: (0, 0, j)),
+            pl.BlockSpec(memory_space=pl.ANY),
+        ],
+        out_specs=[pl.BlockSpec((PLANE * EDGE_ROWS, block), lambda j: (0, j))] * groups,
+        out_shape=[pltpu.HBM((PLANE * EDGE_ROWS, channels), jnp.bfloat16)] * groups,
+        compiler_params=pltpu.CompilerParams(
+            dimension_semantics=("arbitrary",), vmem_limit_bytes=VMEM_BYTES
+        ),
+        name="kept_edges",
+    )(*scalars, in_hbm(x_in), in_hbm(conv_edge), in_hbm(after))
+
+
+def regroup_kernel(*refs):
+    groups = len(refs) - 1 - PLANE
+    rows = jnp.concatenate([ref[...].astype(jnp.float32) for ref in refs[:groups]], axis=0)
+    for p, out_ref in enumerate(refs[-PLANE:]):
+        parts = [
+            rows[(d * PLANE + p) * EDGE_ROWS : (d * PLANE + p + 1) * EDGE_ROWS] for d in range(groups)
+        ]
+        out_ref[...] = jnp.concatenate(parts, axis=0).astype(jnp.bfloat16)
+
+
+def regroup(arrived, after):
+    rows, channels = arrived[0].shape
+    block = min(1024, channels)
+    height = len(arrived) * EDGE_ROWS
+    return pl.pallas_call(
+        regroup_kernel,
+        grid=(channels // block,),
+        in_specs=[pl.BlockSpec((rows, block), lambda j: (0, j))] * len(arrived)
+        + [pl.BlockSpec(memory_space=pl.ANY)],
+        out_specs=[pl.BlockSpec((height, block), lambda j: (0, j))] * PLANE,
+        out_shape=[pltpu.HBM((height, channels), jnp.bfloat16)] * PLANE,
+        compiler_params=pltpu.CompilerParams(
+            dimension_semantics=("arbitrary",), vmem_limit_bytes=VMEM_BYTES
+        ),
+        name="regroup",
+    )(*arrived, in_hbm(after))
 
 
 def rms_scaled(values, gain, floor_value, eps_value):
@@ -382,62 +439,79 @@
     )(*partials, *gains, *wide)
 
 
-def edge_kernel(steps, source_ref, count_ref, range_ref, got_ref, edge_ref, stats_ref):
-    slots, _, channels = got_ref.shape
-    own_most, lags, _ = edge_ref.shape
+def edge_kernel(steps, requests, place_ref, source_ref, count_ref, range_ref, *refs):
+    group_refs, edge_ref, stats_ref = refs[:-2], refs[-2], refs[-1]
+    own_most, lags, block = edge_ref.shape
+    groups = group_refs[0].shape[0] // EDGE_ROWS
+    height = len(group_refs) * groups * EDGE_ROWS
+    place = place_ref[0]
+
+    def sender(index):
+        p, d = lax.div(index, groups * EDGE_ROWS), lax.rem(lax.div(index, EDGE_ROWS), groups)
+        return (d * PLANE + p) ^ place
+
+    got = jnp.concatenate([ref[...] for ref in group_refs], axis=0)
+    sources = [jnp.where(i < count_ref[0], source_ref[i], -1) for i in range(own_most)]
+    row, col = iota((own_most * 8, 1), 0), iota((1, height), 1)
+    wanted = jnp.full((own_most * 8, 1), -1, jnp.int32)
+    for i, source in enumerate(sources):
+        wanted = jnp.where(lax.div(row, 8) == i, source, wanted)
+    pick = (sender(col) == wanted) & (lax.rem(col, EDGE_ROWS) == lax.rem(row, 8))
+    picked = dot(one_hot(pick), got)
     for i in range(own_most):
-
-        @pl.when(i < count_ref[0])
-        def _():
-            edge_ref[i] = got_ref[source_ref[i], :lags, :]
-
-        @pl.when(i >= count_ref[0])
-        def _():
-            edge_ref[i] = jnp.zeros((lags, channels), jnp.bfloat16)
-
-    requests = count_ref.shape[0] - 1
-    numbers = got_ref[:, lags, :LANES].astype(jnp.float32)
-    lane, slot = iota((slots, LANES), 1), iota((slots, LANES), 0)
-    request = slot * requests + lax.rem(lane, requests)
-    counts = jnp.where(lane < requests, numbers, 0.0)
-    digit = lax.div(lane, requests)
-    lengths = jnp.where(digit == 1, numbers, 0.0) + jnp.where(
-        digit == 2, numbers * float(1 << DIGIT), 0.0
-    )
-    tenants = range_ref.shape[0]
-    tiles = (tenants, 2)
-    sums, loads, members = [], [], []
-    for k in range(tenants):
-        start, end = range_ref[k, 0], range_ref[k, 1]
-        inside = (request >= start) & (request < end)
-        sums.append(jnp.sum(jnp.where(inside, counts, 0.0), keepdims=True))
-        loads.append(jnp.sum(jnp.where(inside, lengths, 0.0), keepdims=True))
-        members.append(jnp.full((1, 1), 1, jnp.int32) * (end - start))
-    members = [m.astype(jnp.float32) for m in members]
-    mean = sum(loads[1:], loads[0]) / sum(members[1:], members[0])
-    out = jnp.zeros(tiles, jnp.float32)
-    row, col = iota(tiles, 0), iota(tiles, 1)
-    for k in range(tenants):
-        rate = sums[k] / (float(steps) * members[k])
-        load = loads[k] / members[k] / mean
-        out = jnp.where(row == k, jnp.where(col == 0, rate, load), out)
-    stats_ref[...] = out
-
-
-def settle_edges(source, count, tenant_range, got, own_most, lags, steps):
+        edge_ref[i] = picked[i * 8 : i * 8 + lags].astype(jnp.bfloat16)
+
+    @pl.when(pl.program_id(0) == 0)
+    def _():
+        numbers = got[:, :LANES].astype(jnp.float32)
+        row, lane = iota((height, LANES), 0), iota((height, LANES), 1)
+        mine = lax.rem(row, EDGE_ROWS) == lags
+        request = sender(row) * requests + lax.rem(lane, requests)
+        digit = lax.div(lane, requests)
+        counts = jnp.where(digit == 0, numbers, 0.0)
+        lengths = jnp.where(digit == 1, numbers, 0.0) + jnp.where(
+            digit == 2, numbers * float(1 << DIGIT), 0.0
+        )
+        tenants = range_ref.shape[0]
+        sums, loads, members = [], [], []
+        for k in range(tenants):
+            start, end = range_ref[k, 0], range_ref[k, 1]
+            inside = mine & (request >= start) & (request < end)
+            sums.append(jnp.sum(jnp.where(inside, counts, 0.0), keepdims=True))
+            loads.append(jnp.sum(jnp.where(inside, lengths, 0.0), keepdims=True))
+            members.append((jnp.zeros((1, 1), jnp.int32) + (end - start)).astype(jnp.float32))
+        mean = sum(loads[1:], loads[0]) / sum(members[1:], members[0])
+        out = jnp.zeros((tenants, 2), jnp.float32)
+        row, col = iota((tenants, 2), 0), iota((tenants, 2), 1)
+        for k in range(tenants):
+            rate = sums[k] / (float(steps) * members[k])
+            load = loads[k] / members[k] / mean
+            out = jnp.where(row == k, jnp.where(col == 0, rate, load), out)
+        stats_ref[...] = out
+
+
+def settle_edges(place, source, count, tenant_range, got, own_most, lags, steps, requests):
     smem = pl.BlockSpec(memory_space=pltpu.SMEM)
-    vmem = pl.BlockSpec(memory_space=pltpu.VMEM)
+    height, channels = got[0].shape
+    block = min(2048, channels)
+    stats = (tenant_range.shape[0], 2)
     return pl.pallas_call(
-        functools.partial(edge_kernel, steps),
-        in_specs=[smem, smem, smem, vmem],
-        out_specs=[vmem, vmem],
+        functools.partial(edge_kernel, steps, requests),
+        grid=(channels // block,),
+        in_specs=[smem] * 4 + [pl.BlockSpec((height, block), lambda j: (0, j))] * len(got),
+        out_specs=[
+            pl.BlockSpec((own_most, lags, block), lambda j: (0, 0, j)),
+            pl.BlockSpec(stats, lambda j: (0, 0)),
+        ],
         out_shape=[
-            jax.ShapeDtypeStruct((own_most, lags, got.shape[2]), jnp.bfloat16),
-            jax.ShapeDtypeStruct((tenant_range.shape[0], 2), jnp.float32),
-        ],
-        compiler_params=pltpu.CompilerParams(vmem_limit_bytes=VMEM_BYTES),
+            jax.ShapeDtypeStruct((own_most, lags, channels), jnp.bfloat16),
+            jax.ShapeDtypeStruct(stats, jnp.float32),
+        ],
+        compiler_params=pltpu.CompilerParams(
+            dimension_semantics=("arbitrary",), vmem_limit_bytes=VMEM_BYTES
+        ),
         name="settle_edges",
-    )(source, count, tenant_range, got)
+    )(place, source, count, tenant_range, *got)
 
 
 def settle_kernel(source_ref, count_ref, got_ref, owned_ref, blank_ref, sems):
@@ -462,7 +536,7 @@
     anywhere = pl.BlockSpec(memory_space=pl.ANY)
     return pl.pallas_call(
         settle_kernel,
-        in_specs=[smem, smem, anywhere],
+        in_specs=[smem, smem, pl.BlockSpec(memory_space=pltpu.VMEM)],
         out_specs=anywhere,
         out_shape=jax.ShapeDtypeStruct((own_most, *got.shape[1:]), got.dtype),
         scratch_shapes=[
@@ -471,7 +545,7 @@
         ],
         compiler_params=pltpu.CompilerParams(vmem_limit_bytes=VMEM_BYTES),
         name="settle_states",
-    )(source, count, in_hbm(got))
+    )(source, count, got)
 
 
 def per_device(
@@ -484,26 +558,27 @@
     own_most = min(requests + requests // 2, owners)
     place = lax.axis_index("req").astype(jnp.int32).reshape(1)
 
-    conv, partial, edge_slots = conv_project(
-        (place, accepted, prompt_len, owner), x_in, jnp.transpose(conv_edge, (1, 0, 2)),
-        conv_weight, conv_bias.reshape(1, -1), x_proj_weight.T, owners,
+    by_lag = jnp.transpose(conv_edge, (1, 0, 2))
+    conv, partial = conv_project(
+        x_in, by_lag, conv_weight, conv_bias.reshape(1, -1), x_proj_weight.T
     )
     if lax.axis_size("tp") == 2:
-        partials = (partial, lax.ppermute(partial, "tp", [(0, 1), (1, 0)]))
+        partials = (in_hbm(partial), lax.ppermute(partial, "tp", [(0, 1), (1, 0)]))
     else:
         partials = (lax.psum(partial, "tp"),)
 
-    def exchange(slots):
-        return lax.all_to_all(slots, "req", split_axis=0, concat_axis=0, tiled=True)
-
-    got_edges = exchange(edge_slots)
+    def swap(rows, delta):
+        return lax.ppermute(rows, "req", [(i, i ^ delta) for i in range(owners)]) if delta else rows
+
+    groups = kept_edges((place, accepted, prompt_len, owner), x_in, by_lag, partial, owners)
+    groups = [swap(rows, d * PLANE) for d, rows in enumerate(groups)]
 
     hits = jnp.any(owner.reshape(owners, requests) == place, axis=1)
     ids = jnp.arange(owners, dtype=jnp.int32)
     ranks = jnp.sum((hits[None, :] & (ids[None, :] < ids[:, None])).astype(jnp.int32), axis=1)
     at = hits[None, :] & (ranks[None, :] == jnp.arange(own_most, dtype=jnp.int32)[:, None])
     source = jnp.sum(jnp.where(at, ids[None, :], 0), axis=1)
-    count = jnp.broadcast_to(jnp.sum(hits.astype(jnp.int32)), (requests + 1,))
+    count = jnp.sum(hits.astype(jnp.int32)).reshape(1)
 
     gains = (dt_gain.reshape(1, -1), b_gain.reshape(1, -1), c_gain.reshape(1, -1))
     bias = dt_bias.reshape(1, -1)
@@ -511,12 +586,14 @@
     slots = kept_states(
         (place, accepted, owner), partials, gains[:2], dt_proj_weight, bias, a_log, conv, state, owners
     )
-    got = exchange(slots)
+    got = lax.all_to_all(slots, "req", split_axis=0, concat_axis=0, tiled=True)
     mixed = scan(
         partials, gains, dt_proj_weight, bias, a_log, skip.reshape(1, -1), conv, state, z_gate
     )
+    groups = [swap(rows, p) for p, rows in enumerate(regroup(groups, mixed))]
     owned_edge, tenant_stats = settle_edges(
-        source, count, tenant_range, got_edges, own_most, lags, x_in.shape[0] // requests
+        place, source, count, tenant_range, groups, own_most, lags, x_in.shape[0] // requests,
+        requests,
     )
     owned = settle_states(source, count, got, own_most)
     return (mixed, owned, owned_edge, tenant_stats)

time: 131 us -> 83.2 us (0.64)
  the two profiles are of different devices: /device:TPU:1 before, /device:TPU:11 now
where the time goes in v4:
time: 83.2 us; the launch traced here: 83.6 us
  Pallas kernels  44.2 us (53%)
  waiting for transfers between devices  18.1 us (22%)
  starting transfers between devices  17.2 us (21%)
  local copies, waits for them, and re-layouts  1.79 us (2%)
  other arithmetic  1.53 us (2%)
    pallas_call x1, Pallas kernels, scan(): pl.pallas_call(functools.partial(scan_kernel, len(partials)), grid=(chann...  19.1 us
    ppermute x6, waiting for transfers between devices, swap(): lax.ppermute(rows, 'req', [(i, i ^ delta) for i in range(owners)])  11.3 us
    all_to_all x1, starting transfers between devices, per_device(): got = lax.all_to_all(slots, 'req', split_axis=0, concat_axis=0, tiled=True)  11 us
    pallas_call x1, Pallas kernels, kept_states(): pl.pallas_call(functools.partial(kept_kernel, len(partials)), grid=(chann...  8.41 us
    all_to_all x1, waiting for transfers between devices, per_device(): got = lax.all_to_all(slots, 'req', split_axis=0, concat_axis=0, tiled=True)  6.82 us
    pallas_call x1, Pallas kernels, conv_project(): pl.pallas_call(conv_kernel, grid=(channels // block,), in_specs=[pl.Block...  5.2 us
    ppermute x6, starting transfers between devices, swap(): lax.ppermute(rows, 'req', [(i, i ^ delta) for i in range(owners)])  4.88 us
    pallas_call x1, Pallas kernels, settle_states(): pl.pallas_call(settle_kernel, in_specs=[smem, smem, pl.BlockSpec(memory_s...  3.47 us
  transfers between devices with their start and end apart: 8, of which 3 were waited for; matrix products, arithmetic and copies ran while one was open for 3% of the time, Pallas kernels for 42%

profile of v4, /device:TPU:11, one launch (start us, length us, event | category | flops | bytes accessed | tf_op | source)
XLA Modules:
  0.0 83.6 jit_solution(2749590308188095512)
XLA Ops:
  0.6 0.0 copy-start.3
  0.6 0.0 copy-start.4
  0.7 0.0 copy-start.2
  0.7 0.0 copy-start.5
  0.7 0.0 copy-start.7
  0.7 0.0 copy-start.8
  0.7 5.2 %conv_project.1 = (bf16[128,4096]{1,0:T(8,128)(2,1)}, f32[128,288]{1,0:T(8,128)}) custom-call(bf16[128,4096]{1,0:T(8,128)(2,1)} %x_ref.3, bf16[3,8,4096]{2,1,0:T(8,128)(2,1)} %bitcast.20, f32[4,4096]{1,0:T(4,128)} %weight_ref.1, f32[1,4096]{1,0:T(1,128)} %bitcast.22, bf16[288,4096]{1,0:T(8,128)(2,1)} %bitcast.19), custom_call_target="tpu_custom_call" | custom-call | tf_op jit(solution)/shard_map/conv_project/pallas_call | solution.py:95
  5.9 1.2 %collective-permute-start = (f32[128,288]{1,0:T(8,128)}, f32[128,288]{1,0:T(8,128)S(1)}, u32[]{:S(2)}, u32[]{:S(2)}) collective-permute-start(f32[128,288]{1,0:T(8,128)} %get-tuple-element.16.refs_0_.refs_3_._), channel_id=1, source_target_pairs={{0,1},{1,0},{2,3},{3,2},{4,5},{5,4},{6,7},{7,6},{8,9},{9,8},{10,11... | collective-permute-start | bytes 442376 | tf_op jit(solution)/shard_map/ppermute | solution.py:566
  7.1 0.0 copy-done.3
  7.1 0.0 copy-done.4
  7.1 0.0 copy-done.2
  7.1 2.4 %kept_edges.1 = (bf16[16,4096]{1,0:T(8,128)(2,1)}, bf16[16,4096]{1,0:T(8,128)(2,1)}, bf16[16,4096]{1,0:T(8,128)(2,1)}, bf16[16,4096]{1,0:T(8,128)(2,1)}) custom-call(s32[1]{0:T(128)} %bitcast.10.refs_0_.place_ref, s32[8]{0:T(128)S(1)} %copy-done.4, s32[8]{0:T(128)S(1)} %copy-done.2, s32[128]{0:T(128)S(1)} %copy-done.3, bf16[128,4096]{1,0:T(8,128)(2,1)} %x_ref.3, ...), custom_call_target="tpu_custom_call" | custom-call | tf_op jit(solution)/shard_map/kept_edges/pallas_call | solution.py:159
  9.6 0.2 collective-permute-start.1
  9.8 2.3 %collective-permute-start.2 = (bf16[16,4096]{1,0:T(8,128)(2,1)}, bf16[16,4096]{1,0:T(8,128)(2,1)}, u32[]{:S(2)}, u32[]{:S(2)}) collective-permute-start(bf16[16,4096]{1,0:T(8,128)(2,1)} %get-tuple-element.20), channel_id=1, source_target_pairs={{0,16},{2,18},{4,20},{6,22},{8,24},{10,26},{12,28},{14,30},{16,0},... | collective-permute-start | bytes 393224 | tf_op jit(solution)/shard_map/ppermute | solution.py:571
  12.1 0.2 collective-permute-start.3
  12.2 0.1 eq.26
  12.3 0.1 reduce_or.9
  12.5 0.0 copy-start.11
  12.5 0.6 convert_reduce_fusion
  13.1 0.0 collective-permute-done.refs_1_.refs_4_
  13.1 0.0 copy-done.11
  13.1 0.0 copy-done.5
  13.1 8.4 %kept_states.1 = bf16[16,16,4096]{2,1,0:T(8,128)(2,1)} custom-call(s32[1]{0:T(128)} %bitcast.10.refs_0_.place_ref, s32[8]{0:T(128)S(1)} %copy-done.4, s32[128]{0:T(128)S(1)} %copy-done.3, f32[128,288]{1,0:T(8,128)} %get-tuple-element.16.refs_0_.refs_3_._, f32[128,288]{1,0:T(8,128)S(1)} %collective-permute-done.refs_1_.refs_4_, f32[1,256]{1,0:T(1,128)S(1)} %bitcast.14, ...), custom_call_target="tpu_custom_call" | custom-call | flops 1006632960000 | bytes 6291456 | tf_op jit(solution)/shard_map/kept_states/pallas_call | solution.py:306
  21.5 11.0 %all-to-all-start = ((bf16[16,16,4096]{2,1,0:T(8,128)(2,1)}), bf16[16,16,4096]{2,1,0:T(8,128)(2,1)}, u32[]{:S(2)}, u32[]{:S(2)}) async-start(bf16[16,16,4096]{2,1,0:T(8,128)(2,1)} %kept_states.1), calls=%async_computation | async-start | bytes 4194304 | tf_op jit(solution)/shard_map/all_to_all | solution.py:589
  32.6 0.0 copy-done.9
  32.6 0.0 copy-start
  32.6 0.0 copy-start.12
  32.6 0.0 copy-start.10
  32.6 19.1 %scan.1.refs_4_ = bf16[128,4096]{1,0:T(8,128)(2,1)} custom-call(f32[128,288]{1,0:T(8,128)} %get-tuple-element.16.refs_0_.refs_3_._, f32[128,288]{1,0:T(8,128)S(1)} %collective-permute-done.refs_1_.refs_4_, f32[1,256]{1,0:T(1,128)S(1)} %bitcast.15, f32[1,16]{1,0:T(1,128)S(1)} %bitcast.17, f32[1,16]{1,0:T(1,128)S(1)} %bitcast.18, bf16[256,4096]{1,0:T(8,128)(2,1)} %refs_7_.3, ...), custom_call_target="tpu_custom_call" | custom-call | flops 2013265920000 | bytes 5242880 | tf_op jit(solution)/shard_map/scan/pallas_call | solution.py:417
  51.7 0.0 collective-permute-done.1.refs_1_
  51.7 0.0 collective-permute-done.2.refs_2_
  51.7 0.0 collective-permute-done.3.refs_3_
  51.8 0.0 copy-done
  51.8 2.9 %regroup.1 = (bf16[16,4096]{1,0:T(8,128)(2,1)}, bf16[16,4096]{1,0:T(8,128)(2,1)}, bf16[16,4096]{1,0:T(8,128)(2,1)}, bf16[16,4096]{1,0:T(8,128)(2,1)}) custom-call(bf16[16,4096]{1,0:T(8,128)(2,1)S(1)} %copy-done, bf16[16,4096]{1,0:T(8,128)(2,1)} %collective-permute-done.1.refs_1_, bf16[16,4096]{1,0:T(8,128)(2,1)} %collective-permute-done.2.refs_2_, ...), custom_call_target="tpu_custom_call" | custom-call | tf_op jit(solution)/shard_map/regroup/pallas_call | solution.py:191
  54.7 0.4 collective-permute-start.4
  55.1 0.3 collective-permute-start.5
  55.4 1.5 %collective-permute-start.6 = (bf16[16,4096]{1,0:T(8,128)(2,1)}, bf16[16,4096]{1,0:T(8,128)(2,1)S(1)}, u32[]{:S(2)}, u32[]{:S(2)}) collective-permute-start(bf16[16,4096]{1,0:T(8,128)(2,1)} %get-tuple-element.25), channel_id=1, source_target_pairs={{0,6},{2,4},{4,2},{6,0},{8,14},{10,12},{12,10},{14,8},{16,22},{18,... | collective-permute-start | bytes 393224 | tf_op jit(solution)/shard_map/ppermute | solution.py:571
  56.9 0.7 convert_reduce_fusion.1
  57.6 0.1 copy.26.range_ref
  57.7 0.1 select_reduce_fusion.source_ref
  57.8 0.0 collective-permute-done.4.refs_1_
  57.8 2.8 %collective-permute-done.5.refs_2_ = bf16[16,4096]{1,0:T(8,128)(2,1)S(1)} collective-permute-done((bf16[16,4096]{1,0:T(8,128)(2,1)}, bf16[16,4096]{1,0:T(8,128)(2,1)S(1)}, u32[]{:S(2)}, u32[]{:S(2)}) %collective-permute-start.5) | collective-permute-done | bytes 131104 | tf_op jit(solution)/shard_map/ppermute | solution.py:571
  60.6 8.5 %collective-permute-done.6.refs_3_ = bf16[16,4096]{1,0:T(8,128)(2,1)S(1)} collective-permute-done((bf16[16,4096]{1,0:T(8,128)(2,1)}, bf16[16,4096]{1,0:T(8,128)(2,1)S(1)}, u32[]{:S(2)}, u32[]{:S(2)}) %collective-permute-start.6) | collective-permute-done | bytes 131104 | tf_op jit(solution)/shard_map/ppermute | solution.py:571
  69.1 0.9 %copy-done.1 = bf16[16,4096]{1,0:T(8,128)(2,1)S(1)} copy-done((bf16[16,4096]{1,0:T(8,128)(2,1)S(1)}, bf16[16,4096]{1,0:T(8,128)(2,1)}, u32[]{:S(2)}) %copy-start.1) | copy-done | bytes 131096
  70.0 2.6 %settle_edges.1 = (bf16[12,3,4096]{2,1,0:T(4,128)(2,1)}, f32[4,2]{1,0:T(4,128)S(1)}) custom-call(s32[1]{0:T(128)} %bitcast.10.refs_0_.place_ref, s32[12]{0:T(128)S(1)} %select_reduce_fusion.source_ref, s32[1]{0:T(128)} %bitcast.9.count_ref, s32[4,2]{1,0:T(4,128)S(1)} %copy.26.range_ref, bf16[16,4096]{1,0:T(8,128)(2,1)S(1)} %copy-done.1, ...), custom_call_target="tpu_custom_call" | custom-call | tf_op jit(solution)/shard_map/settle_edges/pallas_call | solution.py:498
  72.6 0.6 copy.27
  73.3 6.8 %all-to-all-done.got_ref = bf16[16,16,4096]{2,1,0:T(8,128)(2,1)} async-done(((bf16[16,16,4096]{2,1,0:T(8,128)(2,1)}), bf16[16,16,4096]{2,1,0:T(8,128)(2,1)}, u32[]{:S(2)}, u32[]{:S(2)}) %all-to-all-start) | async-done | bytes 2097184 | tf_op jit(solution)/shard_map/all_to_all | solution.py:589
  80.1 3.5 %settle_states.1 = bf16[12,16,4096]{2,1,0:T(8,128)(2,1)} custom-call(s32[12]{0:T(128)S(1)} %select_reduce_fusion.source_ref, s32[1]{0:T(128)} %bitcast.9.count_ref, bf16[16,16,4096]{2,1,0:T(8,128)(2,1)} %all-to-all-done.got_ref), custom_call_target="tpu_custom_call" | custom-call | tf_op jit(solution)/shard_map/settle_states/pallas_call | solution.py:537
  (11 shorter events, 0.0 us)
Async XLA Ops:
  0.6 6.5 %copy-start.3 = (s32[128]{0:T(128)S(1)}, s32[128]{0:T(128)}, u32[]{:S(2)}) copy-start(s32[128]{0:T(128)} %owner_ref.1) | copy-start | bytes 1540
  0.6 6.5 %copy-start.4 = (s32[8]{0:T(128)S(1)}, s32[8]{0:T(128)}, u32[]{:S(2)}) copy-start(s32[8]{0:T(128)} %accepted_ref.1) | copy-start | bytes 100
  0.7 6.5 %copy-start.2 = (s32[8]{0:T(128)S(1)}, s32[8]{0:T(128)}, u32[]{:S(2)}) copy-start(s32[8]{0:T(128)} %length_ref.1) | copy-start | bytes 100
  0.7 12.4 %copy-start.5 = (f32[4096]{0:T(1024)S(1)}, f32[4096]{0:T(1024)}, u32[]{:S(2)}) copy-start(f32[4096]{0:T(1024)} %param.28) | copy-start | bytes 49156
  0.7 12.4 %copy-start.7 = (f32[256]{0:T(256)S(1)}, f32[256]{0:T(256)}, u32[]{:S(2)}) copy-start(f32[256]{0:T(256)} %param.24) | copy-start | bytes 3076
  0.7 12.4 %copy-start.8 = (f32[16]{0:T(128)S(1)}, f32[16]{0:T(128)}, u32[]{:S(2)}) copy-start(f32[16]{0:T(128)} %param.25) | copy-start | bytes 196
  5.9 7.2 %collective-permute-start = (f32[128,288]{1,0:T(8,128)}, f32[128,288]{1,0:T(8,128)S(1)}, u32[]{:S(2)}, u32[]{:S(2)}) collective-permute-start(f32[128,288]{1,0:T(8,128)} %get-tuple-element.16.refs_0_.refs_3_._), channel_id=1, source_target_pairs={{0,1},{1,0},{2,3},{3,2},{4,5},{5,4},{6,7},{7,6},{8,9},{9,8},{10,11... | collective-permute-start | bytes 442376 | tf_op jit(solution)/shard_map/ppermute | solution.py:566
  9.6 42.2 %collective-permute-start.1 = (bf16[16,4096]{1,0:T(8,128)(2,1)}, bf16[16,4096]{1,0:T(8,128)(2,1)}, u32[]{:S(2)}, u32[]{:S(2)}) collective-permute-start(bf16[16,4096]{1,0:T(8,128)(2,1)} %get-tuple-element.19), channel_id=1, source_target_pairs={{0,8},{2,10},{4,12},{6,14},{8,0},{10,2},{12,4},{14,6},{16,24},{18,... | collective-permute-start | bytes 393224 | tf_op jit(solution)/shard_map/ppermute | solution.py:571
  9.8 42.0 %collective-permute-start.2 = (bf16[16,4096]{1,0:T(8,128)(2,1)}, bf16[16,4096]{1,0:T(8,128)(2,1)}, u32[]{:S(2)}, u32[]{:S(2)}) collective-permute-start(bf16[16,4096]{1,0:T(8,128)(2,1)} %get-tuple-element.20), channel_id=1, source_target_pairs={{0,16},{2,18},{4,20},{6,22},{8,24},{10,26},{12,28},{14,30},{16,0},... | collective-permute-start | bytes 393224 | tf_op jit(solution)/shard_map/ppermute | solution.py:571
  12.1 39.7 %collective-permute-start.3 = (bf16[16,4096]{1,0:T(8,128)(2,1)}, bf16[16,4096]{1,0:T(8,128)(2,1)}, u32[]{:S(2)}, u32[]{:S(2)}) collective-permute-start(bf16[16,4096]{1,0:T(8,128)(2,1)} %get-tuple-element.21), channel_id=1, source_target_pairs={{0,24},{2,26},{4,28},{6,30},{8,16},{10,18},{12,20},{14,22},{16,8},... | collective-permute-start | bytes 393224 | tf_op jit(solution)/shard_map/ppermute | solution.py:571
  12.5 0.7 copy-start.11
  21.5 11.0 %copy-start.6 = (f32[4096]{0:T(1024)S(1)}, f32[4096]{0:T(1024)}, u32[]{:S(2)}) copy-start(f32[4096]{0:T(1024)} %param.30) | copy-start | bytes 49156
  21.5 11.0 %copy-start.9 = (f32[16]{0:T(128)S(1)}, f32[16]{0:T(128)}, u32[]{:S(2)}) copy-start(f32[16]{0:T(128)} %param.26) | copy-start | bytes 196
  21.5 58.6 %all-to-all-start = ((bf16[16,16,4096]{2,1,0:T(8,128)(2,1)}), bf16[16,16,4096]{2,1,0:T(8,128)(2,1)}, u32[]{:S(2)}, u32[]{:S(2)}) async-start(bf16[16,16,4096]{2,1,0:T(8,128)(2,1)} %kept_states.1), calls=%async_computation | async-start | bytes 4194304 | tf_op jit(solution)/shard_map/all_to_all | solution.py:589
  32.6 19.2 %copy-start = (bf16[16,4096]{1,0:T(8,128)(2,1)S(1)}, bf16[16,4096]{1,0:T(8,128)(2,1)}, u32[]{:S(2)}) copy-start(bf16[16,4096]{1,0:T(8,128)(2,1)} %get-tuple-element.18.refs_0_) | copy-start | bytes 393220
  32.6 24.3 %copy-start.12 = (pred[16]{0:T(512)(128)(4,1)S(1)}, pred[16]{0:T(512)(128)(4,1)}, u32[]{:S(2)}) copy-start(pred[16]{0:T(512)(128)(4,1)} %copy-done.11) | copy-start | bytes 52
  32.6 24.9 %copy-start.10 = (s32[4,2]{0,1:T(2,128)S(1)}, s32[4,2]{0,1:T(2,128)}, u32[]{:S(2)}) copy-start(s32[4,2]{0,1:T(2,128)} %param.34) | copy-start | bytes 100
  32.6 25.0 %copy-start.13 = (s32[16]{0:T(128)S(1)}, s32[16]{0:T(128)}, u32[]{:S(2)}) copy-start(s32[16]{0:T(128)} %convert_reduce_fusion) | copy-start | bytes 196
  54.7 3.1 %collective-permute-start.4 = (bf16[16,4096]{1,0:T(8,128)(2,1)}, bf16[16,4096]{1,0:T(8,128)(2,1)S(1)}, u32[]{:S(2)}, u32[]{:S(2)}) collective-permute-start(bf16[16,4096]{1,0:T(8,128)(2,1)} %get-tuple-element.23), channel_id=1, source_target_pairs={{0,2},{2,0},{4,6},{6,4},{8,10},{10,8},{12,14},{14,12},{16,18},{18,... | collective-permute-start | bytes 393224 | tf_op jit(solution)/shard_map/ppermute | solution.py:571
  55.1 5.5 %collective-permute-start.5 = (bf16[16,4096]{1,0:T(8,128)(2,1)}, bf16[16,4096]{1,0:T(8,128)(2,1)S(1)}, u32[]{:S(2)}, u32[]{:S(2)}) collective-permute-start(bf16[16,4096]{1,0:T(8,128)(2,1)} %get-tuple-element.24), channel_id=1, source_target_pairs={{0,4},{2,6},{4,0},{6,2},{8,12},{10,14},{12,8},{14,10},{16,20},{18,... | collective-permute-start | bytes 393224 | tf_op jit(solution)/shard_map/ppermute | solution.py:571
  55.4 13.7 %collective-permute-start.6 = (bf16[16,4096]{1,0:T(8,128)(2,1)}, bf16[16,4096]{1,0:T(8,128)(2,1)S(1)}, u32[]{:S(2)}, u32[]{:S(2)}) collective-permute-start(bf16[16,4096]{1,0:T(8,128)(2,1)} %get-tuple-element.25), channel_id=1, source_target_pairs={{0,6},{2,4},{4,2},{6,0},{8,14},{10,12},{12,10},{14,8},{16,22},{18,... | collective-permute-start | bytes 393224 | tf_op jit(solution)/shard_map/ppermute | solution.py:571
  69.1 0.9 %copy-start.1 = (bf16[16,4096]{1,0:T(8,128)(2,1)S(1)}, bf16[16,4096]{1,0:T(8,128)(2,1)}, u32[]{:S(2)}) copy-start(bf16[16,4096]{1,0:T(8,128)(2,1)} %get-tuple-element.22.refs_0_) | copy-start | bytes 393220

commit v5 on v4

--- a/solution.py
+++ b/solution.py
@@ -14,7 +14,7 @@
 EDGE_ROWS = 4
 PLANE = 4
 DIGIT = 7
-VMEM_BYTES = 48 * 1024 * 1024
+VMEM_BYTES = 24 * 1024 * 1024
 ROUND = 4
 VECTOR_WEIGHT = 30000
 
@@ -58,63 +58,77 @@
     return out
 
 
-def conv_kernel(x_ref, edge_ref, weight_ref, bias_ref, proj_ref, conv_ref, partial_ref):
-    lags, requests, _ = edge_ref.shape
+def conv_kernel(
+    x_hbm, edge_hbm, weight_hbm, bias_hbm, proj_hbm, conv_hbm, partial_ref,
+    x_ref, edge_ref, weight_ref, bias_ref, proj_ref, conv_ref, sems, out_sems,
+):
+    lags, requests, channels = edge_ref.shape
     taps = weight_ref.shape[0]
     steps = x_ref.shape[0] // requests
-    stream = dot(to_step_major(requests, steps), x_ref[...])
-    window = [edge_ref[k].astype(jnp.float32) for k in range(lags)]
-    window += [stream[t * requests : (t + 1) * requests] for t in range(steps)]
-    weight = [weight_ref[k : k + 1, :] for k in range(taps)]
-    outs = []
-    for t in range(steps):
-        summed = bias_ref[...] + weight[0] * window[t]
-        for k in range(1, taps):
-            summed = summed + weight[k] * window[t + k]
-        outs.append(silu(summed))
-    conv_out = jnp.concatenate(outs, axis=0).astype(jnp.bfloat16)
-    conv_ref[...] = conv_out
-    partial = lax.dot_general(
-        conv_out, proj_ref[...], (((1,), (1,)), ((), ())), preferred_element_type=jnp.float32
-    )
-
-    @pl.when(pl.program_id(0) == 0)
-    def _():
-        partial_ref[...] = partial
-
-    @pl.when(pl.program_id(0) > 0)
-    def _():
-        partial_ref[...] += partial
+    block = min(1024, channels)
+    pieces = [slice(c, c + block) for c in range(0, channels, block)]
+    small = [(weight_hbm, weight_ref), (bias_hbm, bias_ref), (edge_hbm, edge_ref)]
+    copies = [pltpu.make_async_copy(*pair, sems.at[i]) for i, pair in enumerate(small)]
+    for piece in pieces:
+        for pair in ((x_hbm, x_ref), (proj_hbm, proj_ref)):
+            copies.append(
+                pltpu.make_async_copy(*(ref.at[:, piece] for ref in pair), sems.at[len(copies)])
+            )
+    for copy in copies:
+        copy.start()
+    results = [
+        pltpu.make_async_copy(conv_ref.at[:, piece], conv_hbm.at[:, piece], out_sems.at[i])
+        for i, piece in enumerate(pieces)
+    ]
+    order = to_step_major(requests, steps)
+    for copy in copies[: len(small)]:
+        copy.wait()
+    for i, piece in enumerate(pieces):
+        copies[len(small) + 2 * i].wait()
+        stream = dot(order, x_ref[:, piece])
+        window = [edge_ref[k, :, piece].astype(jnp.float32) for k in range(lags)]
+        window += [stream[t * requests : (t + 1) * requests] for t in range(steps)]
+        weight = [weight_ref[k : k + 1, piece] for k in range(taps)]
+        outs = []
+        for t in range(steps):
+            added = bias_ref[:, piece] + weight[0] * window[t]
+            for k in range(1, taps):
+                added = added + weight[k] * window[t + k]
+            outs.append(silu(added))
+        conv_out = jnp.concatenate(outs, axis=0).astype(jnp.bfloat16)
+        conv_ref[:, piece] = conv_out
+        results[i].start()
+        copies[len(small) + 2 * i + 1].wait()
+        partial = lax.dot_general(
+            conv_out, proj_ref[:, piece], (((1,), (1,)), ((), ())),
+            preferred_element_type=jnp.float32,
+        )
+        partial_ref[...] = partial if i == 0 else partial_ref[...] + partial
+    for result in results:
+        result.wait()
 
 
 def conv_project(x_in, conv_edge, conv_weight, conv_bias, proj):
     rows, channels = x_in.shape
-    lags, requests, _ = conv_edge.shape
-    taps, width = conv_weight.shape[0], proj.shape[0]
-    block = min(1024, channels)
+    operands = (x_in, conv_edge, conv_weight, conv_bias, proj)
+    pieces = channels // min(1024, channels)
     return pl.pallas_call(
         conv_kernel,
-        grid=(channels // block,),
-        in_specs=[
-            pl.BlockSpec((rows, block), lambda j: (0, j)),
-            pl.BlockSpec((lags, requests, block), lambda j: (0, 0, j)),
-            pl.BlockSpec((taps, block), lambda j: (0, j)),
-            pl.BlockSpec((1, block), lambda j: (0, j)),
-            pl.BlockSpec((width, block), lambda j: (0, j)),
-        ],
-        out_specs=[
-            pl.BlockSpec((rows, block), lambda j: (0, j)),
-            pl.BlockSpec((rows, width), lambda j: (0, 0)),
-        ],
+        in_specs=[pl.BlockSpec(memory_space=pl.ANY)] * len(operands),
+        out_specs=[pl.BlockSpec(memory_space=pl.ANY), pl.BlockSpec(memory_space=pltpu.VMEM)],
         out_shape=[
             pltpu.HBM((rows, channels), jnp.bfloat16),
-            pltpu.HBM((rows, width), jnp.float32),
-        ],
-        compiler_params=pltpu.CompilerParams(
-            dimension_semantics=("arbitrary",), vmem_limit_bytes=VMEM_BYTES
-        ),
+            pltpu.HBM((rows, proj.shape[0]), jnp.float32),
+        ],
+        scratch_shapes=[pltpu.VMEM(a.shape, a.dtype) for a in operands]
+        + [
+            pltpu.VMEM((rows, channels), jnp.bfloat16),
+            pltpu.SemaphoreType.DMA((3 + 2 * pieces,)),
+            pltpu.SemaphoreType.DMA((pieces,)),
+        ],
+        compiler_params=pltpu.CompilerParams(vmem_limit_bytes=VMEM_BYTES),
         name="conv_project",
-    )(*(in_hbm(a) for a in (x_in, conv_edge, conv_weight, conv_bias, proj)))
+    )(*(in_hbm(a) for a in operands))
 
 
 def kept_edge_kernel(
@@ -221,67 +235,75 @@
 def kept_kernel(parts, *refs):
     place_ref, accepted_ref, owner_ref = refs[:3]
     (
-        dt_gain_ref, b_gain_ref, dt_weight_ref, dt_bias_ref, a_log_ref, conv_ref, state_ref,
-        slot_ref, low_ref, in_ref, size_ref, drive_ref, rate_ref,
+        dt_gain_ref, b_gain_ref, dt_weight_ref, dt_bias_ref, state_ref, a_log_hbm, conv_hbm,
+        slot_ref, part_ref, a_log_ref, conv_ref, in_ref, size_ref, drive_ref, rate_ref, new_ref,
+        in_sems, sems,
     ) = refs[3 + parts :]
+    pairs = ((refs[3], part_ref), (a_log_hbm, a_log_ref), (conv_hbm, conv_ref))
+    copies = [pltpu.make_async_copy(*pair, in_sems.at[i]) for i, pair in enumerate(pairs)]
+    for copy in copies:
+        copy.start()
     rank, states = dt_gain_ref.shape[1], b_gain_ref.shape[1]
     requests = accepted_ref.shape[0]
-    rows, block = conv_ref.shape
+    rows, channels = conv_ref.shape
     steps = rows // requests
-
-    @pl.when(pl.program_id(0) == 0)
-    def _():
-        total = summed(refs[3 : 3 + parts])
-        low_ref[...] = rms_scaled(total[:, :rank], dt_gain_ref[...], 0.0, EPSILON)
-        in_map = rms_scaled(total[:, rank : rank + states], b_gain_ref[...], SQUARE_FLOOR, 0.0)
-        turned = jnp.transpose(in_map.astype(jnp.float32))
-        for row in range(rows):
-            t, r = divmod(row, requests)
-            in_ref[r * states : (r + 1) * states, t * LANES : (t + 1) * LANES] = (
-                jnp.broadcast_to(turned[:, row : row + 1], (states, LANES))
-            )
+    span = min(1024, channels)
+    halves = states // 8
+
+    copies[0].wait()
+    total = part_ref[...]
+    for part in refs[4 : 3 + parts]:
+        total = total + part[...]
+    low = rms_scaled(total[:, :rank], dt_gain_ref[...], 0.0, EPSILON)
+    in_map = rms_scaled(total[:, rank : rank + states], b_gain_ref[...], SQUARE_FLOOR, 0.0)
+    turned = jnp.transpose(in_map.astype(jnp.float32))
+    for row in range(rows):
+        t, r = divmod(row, requests)
+        in_ref[r * states : (r + 1) * states, t * LANES : (t + 1) * LANES] = jnp.broadcast_to(
+            turned[:, row : row + 1], (states, LANES)
+        )
 
     row = iota((rows, 1), 0)
     live = lax.div(row, requests) < by_request(
         lax.rem(row, requests), [accepted_ref[r] for r in range(requests)]
     )
-    size = softplus(dot(low_ref[...], dt_weight_ref[...]) + dt_bias_ref[...])
-    size = jnp.where(live, size, 0.0)
-    drive = size * conv_ref[...].astype(jnp.float32)
-    for c in range(block // LANES):
-        size_ref[c] = size[:, c * LANES : (c + 1) * LANES]
-        drive_ref[c] = drive[:, c * LANES : (c + 1) * LANES]
-    rate_ref[...] = jnp.exp(a_log_ref[...]) * (-LOG2_E)
-
-    span = min(1024, block)
-    halves = states // 8
-    for r in range(requests):
-        slot = owner_ref[place_ref[0] * requests + r]
+    copies[1].wait()
+    copies[2].wait()
+    for first in range(0, channels, span):
+        piece = slice(first, first + span)
+        size = softplus(dot(low, dt_weight_ref[:, piece]) + dt_bias_ref[:, piece])
+        size = jnp.where(live, size, 0.0)
+        drive = size * conv_ref[:, piece].astype(jnp.float32)
+        for c in range(span // LANES):
+            tile = slice(c * LANES, (c + 1) * LANES)
+            size_ref[first // LANES + c, :rows, :] = size[:, tile]
+            drive_ref[first // LANES + c, :rows, :] = drive[:, tile]
+        rate_ref[:, piece] = jnp.exp(a_log_ref[:, piece]) * (-LOG2_E)
+
+    def one_request(r, carry):
+        own = pl.multiple_of(r * states, states)
         rounds = lax.div(accepted_ref[r] + (ROUND - 1), ROUND)
-        for first in range(0, block, span):
-            tiles = [slice(c, c + LANES) for c in range(first, first + span, LANES)]
+
+        def one_span(part, inner):
+            tiles = [pl.multiple_of(part * span + c, LANES) for c in range(0, span, LANES)]
 
             def one_round(i, hidden):
                 hidden = [list(h) for h in hidden]
                 for u in range(ROUND):
                     t = i * ROUND + u
                     at = pl.ds(t * requests + r, 8, stride=0)
-                    b = [
-                        in_ref[
-                            r * states + 8 * h : r * states + 8 * (h + 1),
-                            pl.ds(pl.multiple_of(t * LANES, LANES), LANES),
-                        ]
-                        for h in range(halves)
-                    ]
+                    lanes = pl.ds(pl.multiple_of(t * LANES, LANES), LANES)
+                    b = [in_ref[pl.ds(own + 8 * h, 8), lanes] for h in range(halves)]
                     for c, tile in enumerate(tiles):
-                        place = first // LANES + c
+                        place = part * (span // LANES) + c
                         now, drive = size_ref[place, at, :], drive_ref[place, at, :]
                         for h in range(halves):
-                            decay = jnp.exp2(now * rate_ref[8 * h : 8 * (h + 1), tile])
-                            hidden[h][c] = decay * hidden[h][c] + drive * b[h]
+                            rate = rate_ref[8 * h : 8 * (h + 1), pl.ds(tile, LANES)]
+                            hidden[h][c] = jnp.exp2(now * rate) * hidden[h][c] + drive * b[h]
                 return tuple(tuple(h) for h in hidden)
 
-            old = state_ref[r * states : (r + 1) * states, first : first + span].astype(jnp.float32)
+            lanes = pl.ds(pl.multiple_of(part * span, span), span)
+            old = state_ref[pl.ds(own, states), lanes].astype(jnp.float32)
             start = tuple(
                 tuple(
                     old[8 * h : 8 * (h + 1), c * LANES : (c + 1) * LANES] for c in range(len(tiles))
@@ -290,44 +312,55 @@
             )
             done = lax.fori_loop(0, rounds, one_round, start)
             new = jnp.concatenate([jnp.concatenate(h, axis=1) for h in done], axis=0)
-            slot_ref[slot, :, first : first + span] = new.astype(jnp.bfloat16)
+            new_ref[r, :, lanes] = new.astype(jnp.bfloat16)
+            return inner
+
+        lax.fori_loop(0, channels // span, one_span, 0)
+        slot = owner_ref[place_ref[0] * requests + r]
+        pltpu.make_async_copy(new_ref.at[r], slot_ref.at[slot], sems.at[r]).start()
+        return carry
+
+    lax.fori_loop(0, requests, one_request, 0)
+    for r in range(requests):
+        slot = owner_ref[place_ref[0] * requests + r]
+        pltpu.make_async_copy(new_ref.at[r], slot_ref.at[slot], sems.at[r]).wait()
 
 
 def kept_states(scalars, partials, gains, dt_weight, dt_bias, a_log, conv, state, slots):
     rows, channels = conv.shape
     states, rank = a_log.shape[0], dt_weight.shape[0]
     requests = scalars[1].shape[0]
-    block = min(1024, channels)
-
-    def whole(array):
-        return pl.BlockSpec(array.shape, lambda j: (0, 0))
-
-    wide = [in_hbm(dt_weight), dt_bias, in_hbm(a_log), in_hbm(conv), in_hbm(state)]
+    near = [*partials[1:], *gains, dt_weight, dt_bias, state]
+    far = [in_hbm(a_log), in_hbm(conv)]
+    anywhere = pl.BlockSpec(memory_space=pl.ANY)
     return pl.pallas_call(
         functools.partial(kept_kernel, len(partials)),
-        grid=(channels // block,),
         in_specs=[pl.BlockSpec(memory_space=pltpu.SMEM)] * len(scalars)
-        + [whole(a) for a in (*partials, *gains)]
-        + [pl.BlockSpec((a.shape[0], block), lambda j: (0, j)) for a in wide],
-        out_specs=pl.BlockSpec((slots, states, block), lambda j: (0, 0, j)),
+        + [anywhere]
+        + [pl.BlockSpec(memory_space=pltpu.VMEM)] * len(near)
+        + [anywhere] * len(far),
+        out_specs=anywhere,
         out_shape=pltpu.HBM((slots, states, channels), jnp.bfloat16),
         scratch_shapes=[
-            pltpu.VMEM((rows, rank), jnp.bfloat16),
+            pltpu.VMEM(partials[0].shape, jnp.float32),
+            pltpu.VMEM(a_log.shape, jnp.float32),
+            pltpu.VMEM(conv.shape, jnp.bfloat16),
             pltpu.VMEM((requests * states, rows // requests * LANES), jnp.float32),
-            pltpu.VMEM((block // LANES, rows, LANES), jnp.float32),
-            pltpu.VMEM((block // LANES, rows, LANES), jnp.float32),
-            pltpu.VMEM((states, block), jnp.float32),
-        ],
-        compiler_params=pltpu.CompilerParams(
-            dimension_semantics=("arbitrary",), vmem_limit_bytes=VMEM_BYTES
-        ),
+            pltpu.VMEM((channels // LANES, rows + 8, LANES), jnp.float32),
+            pltpu.VMEM((channels // LANES, rows + 8, LANES), jnp.float32),
+            pltpu.VMEM((states, channels), jnp.float32),
+            pltpu.VMEM((requests, states, channels), jnp.bfloat16),
+            pltpu.SemaphoreType.DMA((1 + len(far),)),
+            pltpu.SemaphoreType.DMA((requests,)),
+        ],
+        compiler_params=pltpu.CompilerParams(vmem_limit_bytes=VMEM_BYTES),
         cost_estimate=pl.CostEstimate(
             flops=VECTOR_WEIGHT * 4 * rows * states * channels,
             transcendentals=rows * states * channels,
             bytes_accessed=2 * channels * (rows + rank + states * (requests + slots)),
         ),
         name="kept_states",
-    )(*scalars, *partials, *gains, *wide)
+    )(*scalars, in_hbm(partials[0]), *near, *far)
 
 
 def scan_kernel(parts, *refs):
@@ -514,33 +547,48 @@
     )(place, source, count, tenant_range, *got)
 
 
-def settle_kernel(source_ref, count_ref, got_ref, owned_ref, blank_ref, sems):
+def settle_kernel(source_ref, count_ref, got_ref, owned_ref, rows_ref, in_sems, out_sems):
     own_most = owned_ref.shape[0]
-    blank_ref[...] = jnp.zeros_like(blank_ref)
-
-    def copy(i, filled):
-        origin = got_ref.at[source_ref[i]] if filled else blank_ref
-        return pltpu.make_async_copy(origin, owned_ref.at[i], sems.at[i])
-
-    for act in ("start", "wait"):
-        for i in range(own_most):
-            for filled in (True, False):
-
-                @pl.when((i < count_ref[0]) == filled)
-                def _():
-                    getattr(copy(i, filled), act)()
+
+    def fetch(i):
+        return pltpu.make_async_copy(got_ref.at[source_ref[i]], rows_ref.at[i], in_sems.at[i])
+
+    def put(i):
+        return pltpu.make_async_copy(rows_ref.at[i], owned_ref.at[i], out_sems.at[i])
+
+    for i in range(own_most):
+
+        @pl.when(i < count_ref[0])
+        def _():
+            fetch(i).start()
+
+    for i in range(own_most):
+
+        @pl.when(i < count_ref[0])
+        def _():
+            fetch(i).wait()
+
+        @pl.when(i >= count_ref[0])
+        def _():
+            rows_ref[i] = jnp.zeros(rows_ref.shape[1:], rows_ref.dtype)
+
+        put(i).start()
+    for i in range(own_most):
+        put(i).wait()
 
 
 def settle_states(source, count, got, own_most):
     smem = pl.BlockSpec(memory_space=pltpu.SMEM)
     anywhere = pl.BlockSpec(memory_space=pl.ANY)
+    shape = (own_most, *got.shape[1:])
     return pl.pallas_call(
         settle_kernel,
-        in_specs=[smem, smem, pl.BlockSpec(memory_space=pltpu.VMEM)],
+        in_specs=[smem, smem, anywhere],
         out_specs=anywhere,
-        out_shape=jax.ShapeDtypeStruct((own_most, *got.shape[1:]), got.dtype),
+        out_shape=pltpu.HBM(shape, got.dtype),
         scratch_shapes=[
-            pltpu.VMEM(got.shape[1:], got.dtype),
+            pltpu.VMEM(shape, got.dtype),
+            pltpu.SemaphoreType.DMA((own_most,)),
             pltpu.SemaphoreType.DMA((own_most,)),
         ],
         compiler_params=pltpu.CompilerParams(vmem_limit_bytes=VMEM_BYTES),
@@ -563,7 +611,7 @@
         x_in, by_lag, conv_weight, conv_bias.reshape(1, -1), x_proj_weight.T
     )
     if lax.axis_size("tp") == 2:
-        partials = (in_hbm(partial), lax.ppermute(partial, "tp", [(0, 1), (1, 0)]))
+        partials = (partial, lax.ppermute(partial, "tp", [(0, 1), (1, 0)]))
     else:
         partials = (lax.psum(partial, "tp"),)
 

time: 83.2 us -> 82.6 us (level)
  starting transfers between devices: 17.2 us -> 16 us
    all_to_all x1, starting transfers between devices: 11 us -> 9.82 us  [per_device(): got = lax.all_to_all(slots, 'req', split_axis=0, concat_axis=0, tiled=True)]
    unnamed x30 -> x40, local copies, waits for them, and re-layouts: 1.7 us -> 1.74 us
where the time goes in v5:
time: 82.6 us; the launch traced here: 82.1 us
  Pallas kernels  43.6 us (53%)
  waiting for transfers between devices  18.2 us (22%)
  starting transfers between devices  16 us (19%)
  local copies, waits for them, and re-layouts  1.83 us (2%)
  other arithmetic  1.59 us (2%)
  between operations  0.9 us (1%)
    pallas_call x1, Pallas kernels, scan(): pl.pallas_call(functools.partial(scan_kernel, len(partials)), grid=(chann...  18.9 us
    ppermute x6, waiting for transfers between devices, swap(): lax.ppermute(rows, 'req', [(i, i ^ delta) for i in range(owners)])  11.1 us
    all_to_all x1, starting transfers between devices, per_device(): got = lax.all_to_all(slots, 'req', split_axis=0, concat_axis=0, tiled=True)  9.82 us
    pallas_call x1, Pallas kernels, kept_states(): pl.pallas_call(functools.partial(kept_kernel, len(partials)), in_specs=[p...  7.64 us
    all_to_all x1, waiting for transfers between devices, per_device(): got = lax.all_to_all(slots, 'req', split_axis=0, concat_axis=0, tiled=True)  7.16 us
    pallas_call x1, Pallas kernels, conv_project(): pl.pallas_call(conv_kernel, in_specs=[pl.BlockSpec(memory_space=pl.ANY)]...  5.52 us
    ppermute x6, starting transfers between devices, swap(): lax.ppermute(rows, 'req', [(i, i ^ delta) for i in range(owners)])  4.89 us
    pallas_call x1, Pallas kernels, settle_states(): pl.pallas_call(settle_kernel, in_specs=[smem, smem, anywhere], out_specs=...  3.51 us
  transfers between devices with their start and end apart: 8, of which 3 were waited for; matrix products, arithmetic and copies ran while one was open for 3% of the time, Pallas kernels for 42%

profile of v5, /device:TPU:11, one launch (start us, length us, event | category | flops | bytes accessed | tf_op | source)
XLA Modules:
  0.0 82.1 jit_solution(765377507551506361)
XLA Ops:
  0.6 0.0 copy-start.4
  0.6 0.0 copy-start.5
  0.7 0.0 copy-start.3
  0.7 0.0 copy-start.6
  0.7 0.0 copy-start.7
  0.7 0.0 copy-start.10
  0.7 0.0 copy-start.12
  0.7 5.5 %conv_project.1 = (bf16[128,4096]{1,0:T(8,128)(2,1)}, f32[128,288]{1,0:T(8,128)}) custom-call(bf16[128,4096]{1,0:T(8,128)(2,1)} %x_ref.1, bf16[3,8,4096]{2,1,0:T(8,128)(2,1)} %bitcast.22, f32[4,4096]{1,0:T(4,128)} %weight_hbm.1, f32[1,4096]{1,0:T(1,128)} %bitcast.24, bf16[288,4096]{1,0:T(8,128)(2,1)} %bitcast.21), custom_call_target="tpu_custom_call" | custom-call | tf_op jit(solution)/shard_map/conv_project/pallas_call | solution.py:115
  6.2 1.3 %collective-permute-start = (f32[128,288]{1,0:T(8,128)}, f32[128,288]{1,0:T(8,128)S(1)}, u32[]{:S(2)}, u32[]{:S(2)}) collective-permute-start(f32[128,288]{1,0:T(8,128)} %get-tuple-element.16.refs_0_.refs_3_._), channel_id=1, source_target_pairs={{0,1},{1,0},{2,3},{3,2},{4,5},{5,4},{6,7},{7,6},{8,9},{9,8},{10,11... | collective-permute-start | bytes 442376 | tf_op jit(solution)/shard_map/ppermute | solution.py:614
  7.6 0.0 copy-done.4
  7.6 0.0 copy-done.3
  7.6 2.4 %kept_edges.1 = (bf16[16,4096]{1,0:T(8,128)(2,1)}, bf16[16,4096]{1,0:T(8,128)(2,1)}, bf16[16,4096]{1,0:T(8,128)(2,1)}, bf16[16,4096]{1,0:T(8,128)(2,1)}) custom-call(s32[1]{0:T(128)} %bitcast.10.refs_0_.place_ref, s32[8]{0:T(128)S(1)} %copy-done.5, s32[8]{0:T(128)S(1)} %copy-done.3, s32[128]{0:T(128)S(1)} %copy-done.4, bf16[128,4096]{1,0:T(8,128)(2,1)} %x_ref.1, ...), custom_call_target="tpu_custom_call" | custom-call | tf_op jit(solution)/shard_map/kept_edges/pallas_call | solution.py:173
  10.0 0.2 collective-permute-start.1
  10.2 2.3 %collective-permute-start.2 = (bf16[16,4096]{1,0:T(8,128)(2,1)}, bf16[16,4096]{1,0:T(8,128)(2,1)}, u32[]{:S(2)}, u32[]{:S(2)}) collective-permute-start(bf16[16,4096]{1,0:T(8,128)(2,1)} %get-tuple-element.20), channel_id=1, source_target_pairs={{0,16},{2,18},{4,20},{6,22},{8,24},{10,26},{12,28},{14,30},{16,0},... | collective-permute-start | bytes 393224 | tf_op jit(solution)/shard_map/ppermute | solution.py:619
  12.5 0.2 collective-permute-start.3
  12.7 0.1 eq.26
  12.8 0.1 reduce_or.9
  12.9 0.7 convert_reduce_fusion
  13.5 0.0 collective-permute-done.refs_1_.refs_4_
  13.6 7.6 %kept_states.1 = bf16[16,16,4096]{2,1,0:T(8,128)(2,1)} custom-call(s32[1]{0:T(128)} %bitcast.10.refs_0_.place_ref, s32[8]{0:T(128)S(1)} %copy-done.5, s32[128]{0:T(128)S(1)} %copy-done.4, f32[128,288]{1,0:T(8,128)} %get-tuple-element.16.refs_0_.refs_3_._, f32[128,288]{1,0:T(8,128)S(1)} %collective-permute-done.refs_1_.refs_4_, f32[1,256]{1,0:T(1,128)S(1)} %bitcast.16, ...), custom_call_target="tpu_custom_call" | custom-call | flops 1006632960000 | bytes 6291456 | tf_op jit(solution)/shard_map/kept_states/pallas_call | solution.py:336
  21.2 0.0 copy-start
  21.3 0.0 copy-start.9
  21.3 0.0 copy-start.11
  21.3 0.0 copy-start.13
  21.3 0.0 copy-start.14
  21.3 9.8 %all-to-all-start = ((bf16[16,16,4096]{2,1,0:T(8,128)(2,1)}), bf16[16,16,4096]{2,1,0:T(8,128)(2,1)}, u32[]{:S(2)}, u32[]{:S(2)}) async-start(bf16[16,16,4096]{2,1,0:T(8,128)(2,1)} %kept_states.1), calls=%async_computation | async-start | bytes 4194304 | tf_op jit(solution)/shard_map/all_to_all | solution.py:637
  31.1 0.0 copy-done.9
  31.1 0.0 copy-done.11
  31.2 0.0 copy-start.15
  31.2 18.9 %scan.1.refs_4_ = bf16[128,4096]{1,0:T(8,128)(2,1)} custom-call(f32[128,288]{1,0:T(8,128)S(1)} %copy-done, f32[128,288]{1,0:T(8,128)S(1)} %collective-permute-done.refs_1_.refs_4_, f32[1,256]{1,0:T(1,128)S(1)} %bitcast.17, f32[1,16]{1,0:T(1,128)S(1)} %bitcast.19, f32[1,16]{1,0:T(1,128)S(1)} %bitcast.20, bf16[256,4096]{1,0:T(8,128)(2,1)} %refs_7_.3, ...), custom_call_target="tpu_custom_call" | custom-call | flops 2013265920000 | bytes 5242880 | tf_op jit(solution)/shard_map/scan/pallas_call | solution.py:450
  50.1 0.0 collective-permute-done.1.refs_1_
  50.1 0.0 collective-permute-done.2.refs_2_
  50.1 0.0 collective-permute-done.3.refs_3_
  50.2 2.9 %regroup.1 = (bf16[16,4096]{1,0:T(8,128)(2,1)}, bf16[16,4096]{1,0:T(8,128)(2,1)}, bf16[16,4096]{1,0:T(8,128)(2,1)}, bf16[16,4096]{1,0:T(8,128)(2,1)}) custom-call(bf16[16,4096]{1,0:T(8,128)(2,1)S(1)} %copy-done.1, bf16[16,4096]{1,0:T(8,128)(2,1)} %collective-permute-done.1.refs_1_, bf16[16,4096]{1,0:T(8,128)(2,1)} %collective-permute-done.2.refs_2_, ...), custom_call_target="tpu_custom_call" | custom-call | tf_op jit(solution)/shard_map/regroup/pallas_call | solution.py:205
  53.1 0.4 collective-permute-start.4
  53.5 0.3 collective-permute-start.5
  53.8 1.5 %collective-permute-start.6 = (bf16[16,4096]{1,0:T(8,128)(2,1)}, bf16[16,4096]{1,0:T(8,128)(2,1)S(1)}, u32[]{:S(2)}, u32[]{:S(2)}) collective-permute-start(bf16[16,4096]{1,0:T(8,128)(2,1)} %get-tuple-element.25), channel_id=1, source_target_pairs={{0,6},{2,4},{4,2},{6,0},{8,14},{10,12},{12,10},{14,8},{16,22},{18,... | collective-permute-start | bytes 393224 | tf_op jit(solution)/shard_map/ppermute | solution.py:619
  55.3 0.7 convert_reduce_fusion.1
  56.0 0.1 copy.26.range_ref
  56.1 0.1 select_reduce_fusion.source_ref
  56.2 0.0 collective-permute-done.4.refs_1_
  56.2 2.9 %collective-permute-done.5.refs_2_ = bf16[16,4096]{1,0:T(8,128)(2,1)S(1)} collective-permute-done((bf16[16,4096]{1,0:T(8,128)(2,1)}, bf16[16,4096]{1,0:T(8,128)(2,1)S(1)}, u32[]{:S(2)}, u32[]{:S(2)}) %collective-permute-start.5) | collective-permute-done | bytes 131104 | tf_op jit(solution)/shard_map/ppermute | solution.py:619
  59.1 8.2 %collective-permute-done.6.refs_3_ = bf16[16,4096]{1,0:T(8,128)(2,1)S(1)} collective-permute-done((bf16[16,4096]{1,0:T(8,128)(2,1)}, bf16[16,4096]{1,0:T(8,128)(2,1)S(1)}, u32[]{:S(2)}, u32[]{:S(2)}) %collective-permute-start.6) | collective-permute-done | bytes 131104 | tf_op jit(solution)/shard_map/ppermute | solution.py:619
  67.3 0.9 %copy-done.2 = bf16[16,4096]{1,0:T(8,128)(2,1)S(1)} copy-done((bf16[16,4096]{1,0:T(8,128)(2,1)S(1)}, bf16[16,4096]{1,0:T(8,128)(2,1)}, u32[]{:S(2)}) %copy-start.2) | copy-done | bytes 131096
  68.2 2.6 %settle_edges.1 = (bf16[12,3,4096]{2,1,0:T(4,128)(2,1)}, f32[4,2]{1,0:T(4,128)S(1)}) custom-call(s32[1]{0:T(128)} %bitcast.10.refs_0_.place_ref, s32[12]{0:T(128)S(1)} %select_reduce_fusion.source_ref, s32[1]{0:T(128)} %bitcast.9.count_ref, s32[4,2]{1,0:T(4,128)S(1)} %copy.26.range_ref, bf16[16,4096]{1,0:T(8,128)(2,1)S(1)} %copy-done.2, ...), custom_call_target="tpu_custom_call" | custom-call | tf_op jit(solution)/shard_map/settle_edges/pallas_call | solution.py:531
  70.8 0.6 copy.27
  71.5 7.2 %all-to-all-done.got_ref = bf16[16,16,4096]{2,1,0:T(8,128)(2,1)} async-done(((bf16[16,16,4096]{2,1,0:T(8,128)(2,1)}), bf16[16,16,4096]{2,1,0:T(8,128)(2,1)}, u32[]{:S(2)}, u32[]{:S(2)}) %all-to-all-start) | async-done | bytes 2097184 | tf_op jit(solution)/shard_map/all_to_all | solution.py:637
  78.6 3.5 %settle_states.1 = bf16[12,16,4096]{2,1,0:T(8,128)(2,1)} custom-call(s32[12]{0:T(128)S(1)} %select_reduce_fusion.source_ref, s32[1]{0:T(128)} %bitcast.9.count_ref, bf16[16,16,4096]{2,1,0:T(8,128)(2,1)} %all-to-all-done.got_ref), custom_call_target="tpu_custom_call" | custom-call | tf_op jit(solution)/shard_map/settle_states/pallas_call | solution.py:584
  (21 shorter events, 0.0 us)
Async XLA Ops:
  0.6 6.9 %copy-start.4 = (s32[128]{0:T(128)S(1)}, s32[128]{0:T(128)}, u32[]{:S(2)}) copy-start(s32[128]{0:T(128)} %owner_ref.1) | copy-start | bytes 1540
  0.6 6.9 %copy-start.5 = (s32[8]{0:T(128)S(1)}, s32[8]{0:T(128)}, u32[]{:S(2)}) copy-start(s32[8]{0:T(128)} %accepted_ref.1) | copy-start | bytes 100
  0.7 6.9 %copy-start.3 = (s32[8]{0:T(128)S(1)}, s32[8]{0:T(128)}, u32[]{:S(2)}) copy-start(s32[8]{0:T(128)} %length_ref.1) | copy-start | bytes 100
  0.7 12.9 %copy-start.6 = (bf16[256,4096]{1,0:T(8,128)(2,1)S(1)}, bf16[256,4096]{1,0:T(8,128)(2,1)}, u32[]{:S(2)}) copy-start(bf16[256,4096]{1,0:T(8,128)(2,1)} %refs_7_.3) | copy-start | bytes 6291460
  0.7 12.9 %copy-start.7 = (bf16[8,16,4096]{2,1,0:T(8,128)(2,1)S(1)}, bf16[8,16,4096]{2,1,0:T(8,128)(2,1)}, u32[]{:S(2)}) copy-start(bf16[8,16,4096]{2,1,0:T(8,128)(2,1)} %param.31) | copy-start | bytes 3145732
  0.7 12.9 %copy-start.8 = (f32[4096]{0:T(1024)S(1)}, f32[4096]{0:T(1024)}, u32[]{:S(2)}) copy-start(f32[4096]{0:T(1024)} %param.28) | copy-start | bytes 49156
  0.7 12.9 %copy-start.10 = (f32[256]{0:T(256)S(1)}, f32[256]{0:T(256)}, u32[]{:S(2)}) copy-start(f32[256]{0:T(256)} %param.24) | copy-start | bytes 3076
  0.7 12.9 %copy-start.12 = (f32[16]{0:T(128)S(1)}, f32[16]{0:T(128)}, u32[]{:S(2)}) copy-start(f32[16]{0:T(128)} %param.25) | copy-start | bytes 196
  6.2 7.3 %collective-permute-start = (f32[128,288]{1,0:T(8,128)}, f32[128,288]{1,0:T(8,128)S(1)}, u32[]{:S(2)}, u32[]{:S(2)}) collective-permute-start(f32[128,288]{1,0:T(8,128)} %get-tuple-element.16.refs_0_.refs_3_._), channel_id=1, source_target_pairs={{0,1},{1,0},{2,3},{3,2},{4,5},{5,4},{6,7},{7,6},{8,9},{9,8},{10,11... | collective-permute-start | bytes 442376 | tf_op jit(solution)/shard_map/ppermute | solution.py:614
  10.0 40.2 %collective-permute-start.1 = (bf16[16,4096]{1,0:T(8,128)(2,1)}, bf16[16,4096]{1,0:T(8,128)(2,1)}, u32[]{:S(2)}, u32[]{:S(2)}) collective-permute-start(bf16[16,4096]{1,0:T(8,128)(2,1)} %get-tuple-element.19), channel_id=1, source_target_pairs={{0,8},{2,10},{4,12},{6,14},{8,0},{10,2},{12,4},{14,6},{16,24},{18,... | collective-permute-start | bytes 393224 | tf_op jit(solution)/shard_map/ppermute | solution.py:619
  10.2 40.0 %collective-permute-start.2 = (bf16[16,4096]{1,0:T(8,128)(2,1)}, bf16[16,4096]{1,0:T(8,128)(2,1)}, u32[]{:S(2)}, u32[]{:S(2)}) collective-permute-start(bf16[16,4096]{1,0:T(8,128)(2,1)} %get-tuple-element.20), channel_id=1, source_target_pairs={{0,16},{2,18},{4,20},{6,22},{8,24},{10,26},{12,28},{14,30},{16,0},... | collective-permute-start | bytes 393224 | tf_op jit(solution)/shard_map/ppermute | solution.py:619
  12.5 37.7 %collective-permute-start.3 = (bf16[16,4096]{1,0:T(8,128)(2,1)}, bf16[16,4096]{1,0:T(8,128)(2,1)}, u32[]{:S(2)}, u32[]{:S(2)}) collective-permute-start(bf16[16,4096]{1,0:T(8,128)(2,1)} %get-tuple-element.21), channel_id=1, source_target_pairs={{0,24},{2,26},{4,28},{6,30},{8,16},{10,18},{12,20},{14,22},{16,8},... | collective-permute-start | bytes 393224 | tf_op jit(solution)/shard_map/ppermute | solution.py:619
  12.9 8.3 %copy-start.16 = (pred[16]{0:T(512)(128)(4,1)}, pred[16]{0:T(512)(128)(4,1)S(1)}, u32[]{:S(2)}) copy-start(pred[16]{0:T(512)(128)(4,1)S(1)} %reduce_or.9) | copy-start | bytes 52
  21.2 9.9 %copy-start = (f32[128,288]{1,0:T(8,128)S(1)}, f32[128,288]{1,0:T(8,128)}, u32[]{:S(2)}) copy-start(f32[128,288]{1,0:T(8,128)} %get-tuple-element.16.refs_0_.refs_3_._) | copy-start | bytes 442372
  21.3 9.9 %copy-start.9 = (f32[4096]{0:T(1024)S(1)}, f32[4096]{0:T(1024)}, u32[]{:S(2)}) copy-start(f32[4096]{0:T(1024)} %param.30) | copy-start | bytes 49156
  21.3 9.9 %copy-start.11 = (f32[256]{0:T(256)S(1)}, f32[256]{0:T(256)}, u32[]{:S(2)}) copy-start(f32[256]{0:T(256)} %param.24) | copy-start | bytes 3076
  21.3 9.9 %copy-start.13 = (f32[16]{0:T(128)S(1)}, f32[16]{0:T(128)}, u32[]{:S(2)}) copy-start(f32[16]{0:T(128)} %param.25) | copy-start | bytes 196
  21.3 9.9 %copy-start.14 = (f32[16]{0:T(128)S(1)}, f32[16]{0:T(128)}, u32[]{:S(2)}) copy-start(f32[16]{0:T(128)} %param.26) | copy-start | bytes 196
  21.3 57.3 %all-to-all-start = ((bf16[16,16,4096]{2,1,0:T(8,128)(2,1)}), bf16[16,16,4096]{2,1,0:T(8,128)(2,1)}, u32[]{:S(2)}, u32[]{:S(2)}) async-start(bf16[16,16,4096]{2,1,0:T(8,128)(2,1)} %kept_states.1), calls=%async_computation | async-start | bytes 4194304 | tf_op jit(solution)/shard_map/all_to_all | solution.py:637
  31.2 19.0 %copy-start.1 = (bf16[16,4096]{1,0:T(8,128)(2,1)S(1)}, bf16[16,4096]{1,0:T(8,128)(2,1)}, u32[]{:S(2)}) copy-start(bf16[16,4096]{1,0:T(8,128)(2,1)} %get-tuple-element.18.refs_0_) | copy-start | bytes 393220
  31.2 24.1 %copy-start.17 = (pred[16]{0:T(512)(128)(4,1)S(1)}, pred[16]{0:T(512)(128)(4,1)}, u32[]{:S(2)}) copy-start(pred[16]{0:T(512)(128)(4,1)} %copy-done.16) | copy-start | bytes 52
  31.2 24.8 %copy-start.15 = (s32[4,2]{0,1:T(2,128)S(1)}, s32[4,2]{0,1:T(2,128)}, u32[]{:S(2)}) copy-start(s32[4,2]{0,1:T(2,128)} %param.34) | copy-start | bytes 100
  31.2 24.9 %copy-start.18 = (s32[16]{0:T(128)S(1)}, s32[16]{0:T(128)}, u32[]{:S(2)}) copy-start(s32[16]{0:T(128)} %convert_reduce_fusion) | copy-start | bytes 196
  53.1 3.1 %collective-permute-start.4 = (bf16[16,4096]{1,0:T(8,128)(2,1)}, bf16[16,4096]{1,0:T(8,128)(2,1)S(1)}, u32[]{:S(2)}, u32[]{:S(2)}) collective-permute-start(bf16[16,4096]{1,0:T(8,128)(2,1)} %get-tuple-element.23), channel_id=1, source_target_pairs={{0,2},{2,0},{4,6},{6,4},{8,10},{10,8},{12,14},{14,12},{16,18},{18,... | collective-permute-start | bytes 393224 | tf_op jit(solution)/shard_map/ppermute | solution.py:619
  53.5 5.6 %collective-permute-start.5 = (bf16[16,4096]{1,0:T(8,128)(2,1)}, bf16[16,4096]{1,0:T(8,128)(2,1)S(1)}, u32[]{:S(2)}, u32[]{:S(2)}) collective-permute-start(bf16[16,4096]{1,0:T(8,128)(2,1)} %get-tuple-element.24), channel_id=1, source_target_pairs={{0,4},{2,6},{4,0},{6,2},{8,12},{10,14},{12,8},{14,10},{16,20},{18,... | collective-permute-start | bytes 393224 | tf_op jit(solution)/shard_map/ppermute | solution.py:619
  53.8 13.5 %collective-permute-start.6 = (bf16[16,4096]{1,0:T(8,128)(2,1)}, bf16[16,4096]{1,0:T(8,128)(2,1)S(1)}, u32[]{:S(2)}, u32[]{:S(2)}) collective-permute-start(bf16[16,4096]{1,0:T(8,128)(2,1)} %get-tuple-element.25), channel_id=1, source_target_pairs={{0,6},{2,4},{4,2},{6,0},{8,14},{10,12},{12,10},{14,8},{16,22},{18,... | collective-permute-start | bytes 393224 | tf_op jit(solution)/shard_map/ppermute | solution.py:619
  67.3 0.9 %copy-start.2 = (bf16[16,4096]{1,0:T(8,128)(2,1)S(1)}, bf16[16,4096]{1,0:T(8,128)(2,1)}, u32[]{:S(2)}) copy-start(bf16[16,4096]{1,0:T(8,128)(2,1)} %get-tuple-element.22.refs_0_) | copy-start | bytes 393220

commit v6 on v5

--- a/solution.py
+++ b/solution.py
@@ -15,6 +15,7 @@
 PLANE = 4
 DIGIT = 7
 VMEM_BYTES = 24 * 1024 * 1024
+BLOCK = 2048
 ROUND = 4
 VECTOR_WEIGHT = 30000
 
@@ -60,31 +61,24 @@
 
 def conv_kernel(
     x_hbm, edge_hbm, weight_hbm, bias_hbm, proj_hbm, conv_hbm, partial_ref,
-    x_ref, edge_ref, weight_ref, bias_ref, proj_ref, conv_ref, sems, out_sems,
+    x_ref, edge_ref, weight_ref, bias_ref, proj_ref, conv_ref, sems, out_sem,
 ):
     lags, requests, channels = edge_ref.shape
     taps = weight_ref.shape[0]
     steps = x_ref.shape[0] // requests
-    block = min(1024, channels)
+    block = min(BLOCK, channels)
     pieces = [slice(c, c + block) for c in range(0, channels, block)]
-    small = [(weight_hbm, weight_ref), (bias_hbm, bias_ref), (edge_hbm, edge_ref)]
-    copies = [pltpu.make_async_copy(*pair, sems.at[i]) for i, pair in enumerate(small)]
-    for piece in pieces:
-        for pair in ((x_hbm, x_ref), (proj_hbm, proj_ref)):
-            copies.append(
-                pltpu.make_async_copy(*(ref.at[:, piece] for ref in pair), sems.at[len(copies)])
-            )
+    pairs = [(weight_hbm, weight_ref), (bias_hbm, bias_ref), (edge_hbm, edge_ref)]
+    pairs += [(x_hbm.at[:, piece], x_ref.at[:, piece]) for piece in pieces]
+    pairs.append((proj_hbm, proj_ref))
+    copies = [pltpu.make_async_copy(*pair, sems.at[i]) for i, pair in enumerate(pairs)]
     for copy in copies:
         copy.start()
-    results = [
-        pltpu.make_async_copy(conv_ref.at[:, piece], conv_hbm.at[:, piece], out_sems.at[i])
-        for i, piece in enumerate(pieces)
-    ]
     order = to_step_major(requests, steps)
-    for copy in copies[: len(small)]:
+    for copy in copies[:3]:
         copy.wait()
     for i, piece in enumerate(pieces):
-        copies[len(small) + 2 * i].wait()
+        copies[3 + i].wait()
         stream = dot(order, x_ref[:, piece])
         window = [edge_ref[k, :, piece].astype(jnp.float32) for k in range(lags)]
         window += [stream[t * requests : (t + 1) * requests] for t in range(steps)]
@@ -95,36 +89,33 @@
             for k in range(1, taps):
                 added = added + weight[k] * window[t + k]
             outs.append(silu(added))
-        conv_out = jnp.concatenate(outs, axis=0).astype(jnp.bfloat16)
-        conv_ref[:, piece] = conv_out
-        results[i].start()
-        copies[len(small) + 2 * i + 1].wait()
-        partial = lax.dot_general(
-            conv_out, proj_ref[:, piece], (((1,), (1,)), ((), ())),
-            preferred_element_type=jnp.float32,
-        )
-        partial_ref[...] = partial if i == 0 else partial_ref[...] + partial
-    for result in results:
-        result.wait()
+        conv_ref[:, piece] = jnp.concatenate(outs, axis=0).astype(jnp.bfloat16)
+    result = pltpu.make_async_copy(conv_ref, conv_hbm, out_sem)
+    result.start()
+    copies[-1].wait()
+    partial_ref[...] = lax.dot_general(
+        proj_ref[...], conv_ref[...], (((1,), (1,)), ((), ())), preferred_element_type=jnp.float32
+    )
+    result.wait()
 
 
 def conv_project(x_in, conv_edge, conv_weight, conv_bias, proj):
     rows, channels = x_in.shape
     operands = (x_in, conv_edge, conv_weight, conv_bias, proj)
-    pieces = channels // min(1024, channels)
+    pieces = channels // min(BLOCK, channels)
     return pl.pallas_call(
         conv_kernel,
         in_specs=[pl.BlockSpec(memory_space=pl.ANY)] * len(operands),
         out_specs=[pl.BlockSpec(memory_space=pl.ANY), pl.BlockSpec(memory_space=pltpu.VMEM)],
         out_shape=[
             pltpu.HBM((rows, channels), jnp.bfloat16),
-            pltpu.HBM((rows, proj.shape[0]), jnp.float32),
+            pltpu.HBM((proj.shape[0], rows), jnp.float32),
         ],
         scratch_shapes=[pltpu.VMEM(a.shape, a.dtype) for a in operands]
         + [
             pltpu.VMEM((rows, channels), jnp.bfloat16),
-            pltpu.SemaphoreType.DMA((3 + 2 * pieces,)),
-            pltpu.SemaphoreType.DMA((pieces,)),
+            pltpu.SemaphoreType.DMA((4 + pieces,)),
+            pltpu.SemaphoreType.DMA,
         ],
         compiler_params=pltpu.CompilerParams(vmem_limit_bytes=VMEM_BYTES),
         name="conv_project",
@@ -216,9 +207,24 @@
     )(*arrived, in_hbm(after))
 
 
-def rms_scaled(values, gain, floor_value, eps_value):
-    square = jnp.mean(values * values, axis=-1, keepdims=True)
-    return (values * lax.rsqrt(jnp.maximum(square, floor_value) + eps_value) * gain).astype(jnp.bfloat16)
+def column(row):
+    count = row.shape[1]
+    same = iota((count, count), 0) == iota((count, count), 1)
+    return jnp.sum(jnp.where(same, row, 0.0), axis=1, keepdims=True)
+
+
+def normal(values, floor_value, eps_value):
+    square = jnp.mean(values * values, axis=0, keepdims=True)
+    return values * lax.rsqrt(jnp.maximum(square, floor_value) + eps_value)
+
+
+def low_rank(total, gain):
+    low = jnp.transpose(normal(total[: gain.shape[1]], 0.0, EPSILON))
+    return (low * gain).astype(jnp.bfloat16)
+
+
+def state_map(values, gain):
+    return (normal(values, SQUARE_FLOOR, 0.0) * column(gain)).astype(jnp.bfloat16)
 
 
 def summed(part_refs):
@@ -247,22 +253,21 @@
     requests = accepted_ref.shape[0]
     rows, channels = conv_ref.shape
     steps = rows // requests
-    span = min(1024, channels)
+    span = min(2048, channels)
     halves = states // 8
 
     copies[0].wait()
     total = part_ref[...]
     for part in refs[4 : 3 + parts]:
         total = total + part[...]
-    low = rms_scaled(total[:, :rank], dt_gain_ref[...], 0.0, EPSILON)
-    in_map = rms_scaled(total[:, rank : rank + states], b_gain_ref[...], SQUARE_FLOOR, 0.0)
-    turned = jnp.transpose(in_map.astype(jnp.float32))
+    turned = state_map(total[rank : rank + states], b_gain_ref[...]).astype(jnp.float32)
     for row in range(rows):
         t, r = divmod(row, requests)
         in_ref[r * states : (r + 1) * states, t * LANES : (t + 1) * LANES] = jnp.broadcast_to(
             turned[:, row : row + 1], (states, LANES)
         )
 
+    low = low_rank(total, dt_gain_ref[...])
     row = iota((rows, 1), 0)
     live = lax.div(row, requests) < by_request(
         lax.rem(row, requests), [accepted_ref[r] for r in range(requests)]
@@ -377,13 +382,14 @@
     @pl.when(pl.program_id(0) == 0)
     def _():
         total = summed(refs[:parts])
-        low_ref[...] = rms_scaled(total[:, :rank], dt_gain_ref[...], 0.0, EPSILON)
-        in_map = rms_scaled(total[:, rank : rank + states], b_gain_ref[...], SQUARE_FLOOR, 0.0)
-        out_map = rms_scaled(total[:, rank + states :], c_gain_ref[...], SQUARE_FLOOR, 0.0)
+        low_ref[...] = low_rank(total, dt_gain_ref[...])
+        in_map = state_map(total[rank : rank + states], b_gain_ref[...])
+        out_map = state_map(total[rank + states :], c_gain_ref[...])
         wide = states * LANES
         spread = one_hot(lax.div(iota((states, wide), 1), LANES) == iota((states, wide), 0))
-        in_ref[...] = dot(in_map, spread)
-        out_ref[...] = dot(out_map, spread)
+        turn = (((0,), (0,)), ((), ()))
+        in_ref[...] = lax.dot_general(in_map, spread, turn, preferred_element_type=jnp.float32)
+        out_ref[...] = lax.dot_general(out_map, spread, turn, preferred_element_type=jnp.float32)
 
     conv = conv_ref[...].astype(jnp.float32)
     size = softplus(dot(low_ref[...], dt_weight_ref[...]) + dt_bias_ref[...])
@@ -472,7 +478,7 @@
     )(*partials, *gains, *wide)
 
 
-def edge_kernel(steps, requests, place_ref, source_ref, count_ref, range_ref, *refs):
+def edge_kernel(steps, requests, place_ref, source_ref, range_ref, *refs):
     group_refs, edge_ref, stats_ref = refs[:-2], refs[-2], refs[-1]
     own_most, lags, block = edge_ref.shape
     groups = group_refs[0].shape[0] // EDGE_ROWS
@@ -484,11 +490,10 @@
         return (d * PLANE + p) ^ place
 
     got = jnp.concatenate([ref[...] for ref in group_refs], axis=0)
-    sources = [jnp.where(i < count_ref[0], source_ref[i], -1) for i in range(own_most)]
     row, col = iota((own_most * 8, 1), 0), iota((1, height), 1)
     wanted = jnp.full((own_most * 8, 1), -1, jnp.int32)
-    for i, source in enumerate(sources):
-        wanted = jnp.where(lax.div(row, 8) == i, source, wanted)
+    for i in range(own_most):
+        wanted = jnp.where(lax.div(row, 8) == i, source_ref[i], wanted)
     pick = (sender(col) == wanted) & (lax.rem(col, EDGE_ROWS) == lax.rem(row, 8))
     picked = dot(one_hot(pick), got)
     for i in range(own_most):
@@ -523,7 +528,7 @@
         stats_ref[...] = out
 
 
-def settle_edges(place, source, count, tenant_range, got, own_most, lags, steps, requests):
+def settle_edges(place, source, tenant_range, got, own_most, lags, steps, requests):
     smem = pl.BlockSpec(memory_space=pltpu.SMEM)
     height, channels = got[0].shape
     block = min(2048, channels)
@@ -531,7 +536,7 @@
     return pl.pallas_call(
         functools.partial(edge_kernel, steps, requests),
         grid=(channels // block,),
-        in_specs=[smem] * 4 + [pl.BlockSpec((height, block), lambda j: (0, j))] * len(got),
+        in_specs=[smem] * 3 + [pl.BlockSpec((height, block), lambda j: (0, j))] * len(got),
         out_specs=[
             pl.BlockSpec((own_most, lags, block), lambda j: (0, 0, j)),
             pl.BlockSpec(stats, lambda j: (0, 0)),
@@ -544,56 +549,41 @@
             dimension_semantics=("arbitrary",), vmem_limit_bytes=VMEM_BYTES
         ),
         name="settle_edges",
-    )(place, source, count, tenant_range, *got)
-
-
-def settle_kernel(source_ref, count_ref, got_ref, owned_ref, rows_ref, in_sems, out_sems):
-    own_most = owned_ref.shape[0]
-
-    def fetch(i):
-        return pltpu.make_async_copy(got_ref.at[source_ref[i]], rows_ref.at[i], in_sems.at[i])
-
-    def put(i):
-        return pltpu.make_async_copy(rows_ref.at[i], owned_ref.at[i], out_sems.at[i])
-
-    for i in range(own_most):
-
-        @pl.when(i < count_ref[0])
-        def _():
-            fetch(i).start()
-
-    for i in range(own_most):
-
-        @pl.when(i < count_ref[0])
-        def _():
-            fetch(i).wait()
-
-        @pl.when(i >= count_ref[0])
-        def _():
-            rows_ref[i] = jnp.zeros(rows_ref.shape[1:], rows_ref.dtype)
-
-        put(i).start()
-    for i in range(own_most):
-        put(i).wait()
-
-
-def settle_states(source, count, got, own_most):
-    smem = pl.BlockSpec(memory_space=pltpu.SMEM)
+    )(place, source, tenant_range, *got)
+
+
+def settle_kernel(source_ref, got_hbm, owned_hbm, rows_ref, in_sem, sems):
+    slots = got_hbm.shape[0]
+    fetch = pltpu.make_async_copy(got_hbm, rows_ref.at[:slots], in_sem)
+    fetch.start()
+    rows_ref[slots] = jnp.zeros(rows_ref.shape[1:], rows_ref.dtype)
+    fetch.wait()
+    puts = [
+        pltpu.make_async_copy(rows_ref.at[source_ref[i]], owned_hbm.at[i], sems.at[i])
+        for i in range(owned_hbm.shape[0])
+    ]
+    for put in puts:
+        put.start()
+    for put in puts:
+        put.wait()
+
+
+def settle_states(source, got, own_most):
     anywhere = pl.BlockSpec(memory_space=pl.ANY)
-    shape = (own_most, *got.shape[1:])
+    slots, *rest = got.shape
     return pl.pallas_call(
         settle_kernel,
-        in_specs=[smem, smem, anywhere],
+        in_specs=[pl.BlockSpec(memory_space=pltpu.SMEM), anywhere],
         out_specs=anywhere,
-        out_shape=pltpu.HBM(shape, got.dtype),
+        out_shape=pltpu.HBM((own_most, *rest), got.dtype),
         scratch_shapes=[
-            pltpu.VMEM(shape, got.dtype),
-            pltpu.SemaphoreType.DMA((own_most,)),
+            pltpu.VMEM((slots + 1, *rest), got.dtype),
+            pltpu.SemaphoreType.DMA,
             pltpu.SemaphoreType.DMA((own_most,)),
         ],
         compiler_params=pltpu.CompilerParams(vmem_limit_bytes=VMEM_BYTES),
         name="settle_states",
-    )(source, count, got)
+    )(source, in_hbm(got))
 
 
 def per_device(
@@ -625,8 +615,7 @@
     ids = jnp.arange(owners, dtype=jnp.int32)
     ranks = jnp.sum((hits[None, :] & (ids[None, :] < ids[:, None])).astype(jnp.int32), axis=1)
     at = hits[None, :] & (ranks[None, :] == jnp.arange(own_most, dtype=jnp.int32)[:, None])
-    source = jnp.sum(jnp.where(at, ids[None, :], 0), axis=1)
-    count = jnp.sum(hits.astype(jnp.int32)).reshape(1)
+    source = owners - jnp.sum(jnp.where(at, owners - ids[None, :], 0), axis=1)
 
     gains = (dt_gain.reshape(1, -1), b_gain.reshape(1, -1), c_gain.reshape(1, -1))
     bias = dt_bias.reshape(1, -1)
@@ -640,10 +629,10 @@
     )
     groups = [swap(rows, p) for p, rows in enumerate(regroup(groups, mixed))]
     owned_edge, tenant_stats = settle_edges(
-        place, source, count, tenant_range, groups, own_most, lags, x_in.shape[0] // requests,
+        place, source, tenant_range, groups, own_most, lags, x_in.shape[0] // requests,
         requests,
     )
-    owned = settle_states(source, count, got, own_most)
+    owned = settle_states(source, got, own_most)
     return (mixed, owned, owned_edge, tenant_stats)
 
 

time: 82.6 us -> 81.5 us (0.987)
  Pallas kernels: 43.6 us -> 41.2 us
  waiting for transfers between devices: 18.2 us -> 19.9 us
    all_to_all x1, waiting for transfers between devices: 7.16 us -> 9.71 us  [per_device(): got = lax.all_to_all(slots, 'req', split_axis=0, concat_axis=0, tiled=True)]
    pallas_call x1, Pallas kernels: 5.52 us -> 4.25 us  [conv_project(): pl.pallas_call(conv_kernel, in_specs=[pl.BlockSpec(memory_space=pl.ANY)]...]
    ppermute x6, waiting for transfers between devices: 11.1 us -> 10.1 us  [swap(): lax.ppermute(rows, 'req', [(i, i ^ delta) for i in range(owners)])]
    unnamed x40 -> x32, local copies, waits for them, and re-layouts: 1.74 us -> 1.71 us
  transfers between devices with their start and end apart: 8 -> 8, of which waited for: 3 -> 3; matrix products, arithmetic and copies ran while one was open for 3% -> 2% of each run, Pallas kernels for 42% -> 42%
where the time goes in v6:
time: 81.5 us; the launch traced here: 80.7 us
  Pallas kernels  41.2 us (51%)
  waiting for transfers between devices  19.9 us (24%)
  starting transfers between devices  16.1 us (20%)
  local copies, waits for them, and re-layouts  1.81 us (2%)
  other arithmetic  0.94 us (1%)
  between operations  0.86 us (1%)
    pallas_call x1, Pallas kernels, scan(): pl.pallas_call(functools.partial(scan_kernel, len(partials)), grid=(chann...  18.9 us
    ppermute x6, waiting for transfers between devices, swap(): lax.ppermute(rows, 'req', [(i, i ^ delta) for i in range(owners)])  10.1 us
    all_to_all x1, starting transfers between devices, per_device(): got = lax.all_to_all(slots, 'req', split_axis=0, concat_axis=0, tiled=True)  9.89 us
    all_to_all x1, waiting for transfers between devices, per_device(): got = lax.all_to_all(slots, 'req', split_axis=0, concat_axis=0, tiled=True)  9.71 us
    pallas_call x1, Pallas kernels, kept_states(): pl.pallas_call(functools.partial(kept_kernel, len(partials)), in_specs=[p...  7.28 us
    ppermute x6, starting transfers between devices, swap(): lax.ppermute(rows, 'req', [(i, i ^ delta) for i in range(owners)])  4.88 us
    pallas_call x1, Pallas kernels, conv_project(): pl.pallas_call(conv_kernel, in_specs=[pl.BlockSpec(memory_space=pl.ANY)]...  4.25 us
    pallas_call x1, Pallas kernels, settle_states(): pl.pallas_call(settle_kernel, in_specs=[pl.BlockSpec(memory_space=pltpu.S...  3.37 us
  transfers between devices with their start and end apart: 8, of which 3 were waited for; matrix products, arithmetic and copies ran while one was open for 2% of the time, Pallas kernels for 42%

profile of v6, /device:TPU:11, one launch (start us, length us, event | category | flops | bytes accessed | tf_op | source)
XLA Modules:
  0.0 80.7 jit_solution(10938764941568941997)
XLA Ops:
  0.6 0.0 copy-start.4
  0.6 0.0 copy-start.5
  0.7 0.0 copy-start.3
  0.7 0.0 copy-start.13
  0.7 0.0 copy-start.6
  0.7 0.0 copy-start.7
  0.7 0.0 copy-start.8
  0.7 0.0 copy-start.10
  0.7 0.0 copy-start.11
  0.7 4.3 %conv_project.1 = (bf16[128,4096]{1,0:T(8,128)(2,1)}, f32[288,128]{1,0:T(8,128)}) custom-call(bf16[128,4096]{1,0:T(8,128)(2,1)} %x_ref.1, bf16[3,8,4096]{2,1,0:T(8,128)(2,1)} %bitcast.21, f32[4,4096]{1,0:T(4,128)} %weight_hbm.1, f32[1,4096]{1,0:T(1,128)} %bitcast.23, bf16[288,4096]{1,0:T(8,128)(2,1)} %bitcast.20), custom_call_target="tpu_custom_call" | custom-call | tf_op jit(solution)/shard_map/conv_project/pallas_call | solution.py:106
  5.0 1.3 %collective-permute-start = (f32[288,128]{1,0:T(8,128)}, f32[288,128]{1,0:T(8,128)S(1)}, u32[]{:S(2)}, u32[]{:S(2)}) collective-permute-start(f32[288,128]{1,0:T(8,128)} %get-tuple-element.16.refs_0_.refs_3_._), channel_id=1, source_target_pairs={{0,1},{1,0},{2,3},{3,2},{4,5},{5,4},{6,7},{7,6},{8,9},{9,8},{10,11... | collective-permute-start | bytes 442376 | tf_op jit(solution)/shard_map/ppermute | solution.py:604
  6.3 0.0 copy-done.4
  6.3 0.0 copy-done.5
  6.3 0.0 copy-done.3
  6.3 2.4 %kept_edges.1 = (bf16[16,4096]{1,0:T(8,128)(2,1)}, bf16[16,4096]{1,0:T(8,128)(2,1)}, bf16[16,4096]{1,0:T(8,128)(2,1)}, bf16[16,4096]{1,0:T(8,128)(2,1)}) custom-call(s32[1]{0:T(128)} %bitcast.9.refs_0_.place_ref, s32[8]{0:T(128)S(1)} %copy-done.5, s32[8]{0:T(128)S(1)} %copy-done.3, s32[128]{0:T(128)S(1)} %copy-done.4, bf16[128,4096]{1,0:T(8,128)(2,1)} %x_ref.1, ...), custom_call_target="tpu_custom_call" | custom-call | tf_op jit(solution)/shard_map/kept_edges/pallas_call | solution.py:164
  8.7 0.2 collective-permute-start.1
  8.9 2.3 %collective-permute-start.2 = (bf16[16,4096]{1,0:T(8,128)(2,1)}, bf16[16,4096]{1,0:T(8,128)(2,1)}, u32[]{:S(2)}, u32[]{:S(2)}) collective-permute-start(bf16[16,4096]{1,0:T(8,128)(2,1)} %get-tuple-element.20), channel_id=1, source_target_pairs={{0,16},{2,18},{4,20},{6,22},{8,24},{10,26},{12,28},{14,30},{16,0},... | collective-permute-start | bytes 393224 | tf_op jit(solution)/shard_map/ppermute | solution.py:609
  11.2 0.2 collective-permute-start.3
  11.4 0.1 eq.26
  11.5 0.1 reduce_or.9
  11.6 0.1 convert_reduce_fusion
  11.8 0.0 copy-done.13
  11.8 0.1 copy.26.range_ref
  11.9 0.7 select_reduce_fusion
  12.6 0.0 collective-permute-done.refs_1_.refs_4_
  12.6 0.0 copy-done.6
  12.6 7.3 %kept_states.1 = bf16[16,16,4096]{2,1,0:T(8,128)(2,1)} custom-call(s32[1]{0:T(128)} %bitcast.9.refs_0_.place_ref, s32[8]{0:T(128)S(1)} %copy-done.5, s32[128]{0:T(128)S(1)} %copy-done.4, f32[288,128]{1,0:T(8,128)} %get-tuple-element.16.refs_0_.refs_3_._, f32[288,128]{1,0:T(8,128)S(1)} %collective-permute-done.refs_1_.refs_4_, f32[1,256]{1,0:T(1,128)S(1)} %bitcast.15, ...), custom_call_target="tpu_custom_call" | custom-call | flops 1006632960000 | bytes 6291456 | tf_op jit(solution)/shard_map/kept_states/pallas_call | solution.py:341
  19.9 0.0 copy-start
  19.9 0.0 copy-start.9
  19.9 0.0 copy-start.12
  19.9 9.9 %all-to-all-start = ((bf16[16,16,4096]{2,1,0:T(8,128)(2,1)}), bf16[16,16,4096]{2,1,0:T(8,128)(2,1)}, u32[]{:S(2)}, u32[]{:S(2)}) async-start(bf16[16,16,4096]{2,1,0:T(8,128)(2,1)} %kept_states.1), calls=%async_computation | async-start | bytes 4194304 | tf_op jit(solution)/shard_map/all_to_all | solution.py:626
  29.8 18.9 %scan.1.refs_4_ = bf16[128,4096]{1,0:T(8,128)(2,1)} custom-call(f32[288,128]{1,0:T(8,128)S(1)} %copy-done, f32[288,128]{1,0:T(8,128)S(1)} %collective-permute-done.refs_1_.refs_4_, f32[1,256]{1,0:T(1,128)S(1)} %bitcast.16, f32[1,16]{1,0:T(1,128)S(1)} %bitcast.18, f32[1,16]{1,0:T(1,128)S(1)} %bitcast.19, bf16[256,4096]{1,0:T(8,128)(2,1)} %refs_7_.3, ...), custom_call_target="tpu_custom_call" | custom-call | flops 2013265920000 | bytes 5242880 | tf_op jit(solution)/shard_map/scan/pallas_call | solution.py:456
  48.8 0.0 collective-permute-done.1.refs_1_
  48.8 0.0 collective-permute-done.2.refs_2_
  48.8 0.0 collective-permute-done.3.refs_3_
  48.8 0.0 copy-done.1
  48.8 2.9 %regroup.1 = (bf16[16,4096]{1,0:T(8,128)(2,1)}, bf16[16,4096]{1,0:T(8,128)(2,1)}, bf16[16,4096]{1,0:T(8,128)(2,1)}, bf16[16,4096]{1,0:T(8,128)(2,1)}) custom-call(bf16[16,4096]{1,0:T(8,128)(2,1)S(1)} %copy-done.1, bf16[16,4096]{1,0:T(8,128)(2,1)} %collective-permute-done.1.refs_1_, bf16[16,4096]{1,0:T(8,128)(2,1)} %collective-permute-done.2.refs_2_, ...), custom_call_target="tpu_custom_call" | custom-call | tf_op jit(solution)/shard_map/regroup/pallas_call | solution.py:196
  51.7 0.4 collective-permute-start.4
  52.1 0.3 collective-permute-start.5
  52.4 1.5 %collective-permute-start.6 = (bf16[16,4096]{1,0:T(8,128)(2,1)}, bf16[16,4096]{1,0:T(8,128)(2,1)S(1)}, u32[]{:S(2)}, u32[]{:S(2)}) collective-permute-start(bf16[16,4096]{1,0:T(8,128)(2,1)} %get-tuple-element.25), channel_id=1, source_target_pairs={{0,6},{2,4},{4,2},{6,0},{8,14},{10,12},{12,10},{14,8},{16,22},{18,... | collective-permute-start | bytes 393224 | tf_op jit(solution)/shard_map/ppermute | solution.py:609
  53.9 0.0 collective-permute-done.4.refs_1_
  53.9 3.9 %collective-permute-done.5.refs_2_ = bf16[16,4096]{1,0:T(8,128)(2,1)S(1)} collective-permute-done((bf16[16,4096]{1,0:T(8,128)(2,1)}, bf16[16,4096]{1,0:T(8,128)(2,1)S(1)}, u32[]{:S(2)}, u32[]{:S(2)}) %collective-permute-start.5) | collective-permute-done | bytes 131104 | tf_op jit(solution)/shard_map/ppermute | solution.py:609
  57.8 6.3 %collective-permute-done.6.refs_3_ = bf16[16,4096]{1,0:T(8,128)(2,1)S(1)} collective-permute-done((bf16[16,4096]{1,0:T(8,128)(2,1)}, bf16[16,4096]{1,0:T(8,128)(2,1)S(1)}, u32[]{:S(2)}, u32[]{:S(2)}) %collective-permute-start.6) | collective-permute-done | bytes 131104 | tf_op jit(solution)/shard_map/ppermute | solution.py:609
  64.1 0.9 %copy-done.2 = bf16[16,4096]{1,0:T(8,128)(2,1)S(1)} copy-done((bf16[16,4096]{1,0:T(8,128)(2,1)S(1)}, bf16[16,4096]{1,0:T(8,128)(2,1)}, u32[]{:S(2)}) %copy-start.2) | copy-done | bytes 131096
  65.0 2.0 %settle_edges.1 = (bf16[12,3,4096]{2,1,0:T(4,128)(2,1)}, f32[4,2]{1,0:T(4,128)S(1)}) custom-call(s32[1]{0:T(128)} %bitcast.9.refs_0_.place_ref, s32[12]{0:T(128)S(1)} %broadcast_subtract_fusion.source_ref, s32[4,2]{1,0:T(4,128)S(1)} %copy.26.range_ref, bf16[16,4096]{1,0:T(8,128)(2,1)S(1)} %copy-done.2, bf16[16,4096]{1,0:T(8,128)(2,1)S(1)} %collective-permute-done.4.refs_1_, ...), custom_call_target="tpu_custom_call" | custom-call | tf_op jit(solution)/shard_map/settle_edges/pallas_call | solution.py:536
  67.0 0.6 copy.27
  67.6 9.7 %all-to-all-done.got_hbm = bf16[16,16,4096]{2,1,0:T(8,128)(2,1)} async-done(((bf16[16,16,4096]{2,1,0:T(8,128)(2,1)}), bf16[16,16,4096]{2,1,0:T(8,128)(2,1)}, u32[]{:S(2)}, u32[]{:S(2)}) %all-to-all-start) | async-done | bytes 2097184 | tf_op jit(solution)/shard_map/all_to_all | solution.py:626
  77.3 3.4 %settle_states.1 = bf16[12,16,4096]{2,1,0:T(8,128)(2,1)} custom-call(s32[12]{0:T(128)S(1)} %broadcast_subtract_fusion.source_ref, bf16[16,16,4096]{2,1,0:T(8,128)(2,1)} %all-to-all-done.got_hbm), custom_call_target="tpu_custom_call" | custom-call | tf_op jit(solution)/shard_map/settle_states/pallas_call | solution.py:574
  (14 shorter events, 0.0 us)
Async XLA Ops:
  0.6 5.7 %copy-start.4 = (s32[128]{0:T(128)S(1)}, s32[128]{0:T(128)}, u32[]{:S(2)}) copy-start(s32[128]{0:T(128)} %owner_ref.1) | copy-start | bytes 1540
  0.6 5.7 %copy-start.5 = (s32[8]{0:T(128)S(1)}, s32[8]{0:T(128)}, u32[]{:S(2)}) copy-start(s32[8]{0:T(128)} %accepted_ref.1) | copy-start | bytes 100
  0.7 5.7 %copy-start.3 = (s32[8]{0:T(128)S(1)}, s32[8]{0:T(128)}, u32[]{:S(2)}) copy-start(s32[8]{0:T(128)} %length_ref.1) | copy-start | bytes 100
  0.7 11.1 %copy-start.13 = (s32[4,2]{0,1:T(2,128)S(1)}, s32[4,2]{0,1:T(2,128)}, u32[]{:S(2)}) copy-start(s32[4,2]{0,1:T(2,128)} %param.34) | copy-start | bytes 100
  0.7 11.9 %copy-start.6 = (bf16[256,4096]{1,0:T(8,128)(2,1)S(1)}, bf16[256,4096]{1,0:T(8,128)(2,1)}, u32[]{:S(2)}) copy-start(bf16[256,4096]{1,0:T(8,128)(2,1)} %refs_7_.3) | copy-start | bytes 6291460
  0.7 11.9 %copy-start.7 = (bf16[8,16,4096]{2,1,0:T(8,128)(2,1)S(1)}, bf16[8,16,4096]{2,1,0:T(8,128)(2,1)}, u32[]{:S(2)}) copy-start(bf16[8,16,4096]{2,1,0:T(8,128)(2,1)} %param.31) | copy-start | bytes 3145732
  0.7 11.9 %copy-start.8 = (f32[4096]{0:T(1024)S(1)}, f32[4096]{0:T(1024)}, u32[]{:S(2)}) copy-start(f32[4096]{0:T(1024)} %param.28) | copy-start | bytes 49156
  0.7 11.9 %copy-start.10 = (f32[256]{0:T(256)S(1)}, f32[256]{0:T(256)}, u32[]{:S(2)}) copy-start(f32[256]{0:T(256)} %param.24) | copy-start | bytes 3076
  0.7 11.9 %copy-start.11 = (f32[16]{0:T(128)S(1)}, f32[16]{0:T(128)}, u32[]{:S(2)}) copy-start(f32[16]{0:T(128)} %param.25) | copy-start | bytes 196
  5.0 7.6 %collective-permute-start = (f32[288,128]{1,0:T(8,128)}, f32[288,128]{1,0:T(8,128)S(1)}, u32[]{:S(2)}, u32[]{:S(2)}) collective-permute-start(f32[288,128]{1,0:T(8,128)} %get-tuple-element.16.refs_0_.refs_3_._), channel_id=1, source_target_pairs={{0,1},{1,0},{2,3},{3,2},{4,5},{5,4},{6,7},{7,6},{8,9},{9,8},{10,11... | collective-permute-start | bytes 442376 | tf_op jit(solution)/shard_map/ppermute | solution.py:604
  8.7 40.0 %collective-permute-start.1 = (bf16[16,4096]{1,0:T(8,128)(2,1)}, bf16[16,4096]{1,0:T(8,128)(2,1)}, u32[]{:S(2)}, u32[]{:S(2)}) collective-permute-start(bf16[16,4096]{1,0:T(8,128)(2,1)} %get-tuple-element.19), channel_id=1, source_target_pairs={{0,8},{2,10},{4,12},{6,14},{8,0},{10,2},{12,4},{14,6},{16,24},{18,... | collective-permute-start | bytes 393224 | tf_op jit(solution)/shard_map/ppermute | solution.py:609
  8.9 39.9 %collective-permute-start.2 = (bf16[16,4096]{1,0:T(8,128)(2,1)}, bf16[16,4096]{1,0:T(8,128)(2,1)}, u32[]{:S(2)}, u32[]{:S(2)}) collective-permute-start(bf16[16,4096]{1,0:T(8,128)(2,1)} %get-tuple-element.20), channel_id=1, source_target_pairs={{0,16},{2,18},{4,20},{6,22},{8,24},{10,26},{12,28},{14,30},{16,0},... | collective-permute-start | bytes 393224 | tf_op jit(solution)/shard_map/ppermute | solution.py:609
  11.2 37.5 %collective-permute-start.3 = (bf16[16,4096]{1,0:T(8,128)(2,1)}, bf16[16,4096]{1,0:T(8,128)(2,1)}, u32[]{:S(2)}, u32[]{:S(2)}) collective-permute-start(bf16[16,4096]{1,0:T(8,128)(2,1)} %get-tuple-element.21), channel_id=1, source_target_pairs={{0,24},{2,26},{4,28},{6,30},{8,16},{10,18},{12,20},{14,22},{16,8},... | collective-permute-start | bytes 393224 | tf_op jit(solution)/shard_map/ppermute | solution.py:609
  19.9 9.9 %copy-start = (f32[288,128]{1,0:T(8,128)S(1)}, f32[288,128]{1,0:T(8,128)}, u32[]{:S(2)}) copy-start(f32[288,128]{1,0:T(8,128)} %get-tuple-element.16.refs_0_.refs_3_._) | copy-start | bytes 442372
  19.9 9.9 %copy-start.9 = (f32[4096]{0:T(1024)S(1)}, f32[4096]{0:T(1024)}, u32[]{:S(2)}) copy-start(f32[4096]{0:T(1024)} %param.30) | copy-start | bytes 49156
  19.9 9.9 %copy-start.12 = (f32[16]{0:T(128)S(1)}, f32[16]{0:T(128)}, u32[]{:S(2)}) copy-start(f32[16]{0:T(128)} %param.26) | copy-start | bytes 196
  19.9 57.4 %all-to-all-start = ((bf16[16,16,4096]{2,1,0:T(8,128)(2,1)}), bf16[16,16,4096]{2,1,0:T(8,128)(2,1)}, u32[]{:S(2)}, u32[]{:S(2)}) async-start(bf16[16,16,4096]{2,1,0:T(8,128)(2,1)} %kept_states.1), calls=%async_computation | async-start | bytes 4194304 | tf_op jit(solution)/shard_map/all_to_all | solution.py:626
  29.8 19.0 %copy-start.1 = (bf16[16,4096]{1,0:T(8,128)(2,1)S(1)}, bf16[16,4096]{1,0:T(8,128)(2,1)}, u32[]{:S(2)}) copy-start(bf16[16,4096]{1,0:T(8,128)(2,1)} %get-tuple-element.18.refs_0_) | copy-start | bytes 393220
  29.8 24.1 %copy-start.14 = (s32[12]{0:T(128)S(1)}, s32[12]{0:T(128)}, u32[]{:S(2)}) copy-start(s32[12]{0:T(128)} %select_reduce_fusion) | copy-start | bytes 148
  51.7 2.2 %collective-permute-start.4 = (bf16[16,4096]{1,0:T(8,128)(2,1)}, bf16[16,4096]{1,0:T(8,128)(2,1)S(1)}, u32[]{:S(2)}, u32[]{:S(2)}) collective-permute-start(bf16[16,4096]{1,0:T(8,128)(2,1)} %get-tuple-element.23), channel_id=1, source_target_pairs={{0,2},{2,0},{4,6},{6,4},{8,10},{10,8},{12,14},{14,12},{16,18},{18,... | collective-permute-start | bytes 393224 | tf_op jit(solution)/shard_map/ppermute | solution.py:609
  52.1 5.7 %collective-permute-start.5 = (bf16[16,4096]{1,0:T(8,128)(2,1)}, bf16[16,4096]{1,0:T(8,128)(2,1)S(1)}, u32[]{:S(2)}, u32[]{:S(2)}) collective-permute-start(bf16[16,4096]{1,0:T(8,128)(2,1)} %get-tuple-element.24), channel_id=1, source_target_pairs={{0,4},{2,6},{4,0},{6,2},{8,12},{10,14},{12,8},{14,10},{16,20},{18,... | collective-permute-start | bytes 393224 | tf_op jit(solution)/shard_map/ppermute | solution.py:609
  52.4 11.7 %collective-permute-start.6 = (bf16[16,4096]{1,0:T(8,128)(2,1)}, bf16[16,4096]{1,0:T(8,128)(2,1)S(1)}, u32[]{:S(2)}, u32[]{:S(2)}) collective-permute-start(bf16[16,4096]{1,0:T(8,128)(2,1)} %get-tuple-element.25), channel_id=1, source_target_pairs={{0,6},{2,4},{4,2},{6,0},{8,14},{10,12},{12,10},{14,8},{16,22},{18,... | collective-permute-start | bytes 393224 | tf_op jit(solution)/shard_map/ppermute | solution.py:609
  64.1 0.9 %copy-start.2 = (bf16[16,4096]{1,0:T(8,128)(2,1)S(1)}, bf16[16,4096]{1,0:T(8,128)(2,1)}, u32[]{:S(2)}) copy-start(bf16[16,4096]{1,0:T(8,128)(2,1)} %get-tuple-element.22.refs_0_) | copy-start | bytes 393220

commit v7 on v6

--- a/solution.py
+++ b/solution.py
@@ -157,26 +157,18 @@
 
 
 def kept_edges(scalars, x_in, conv_edge, after, owners):
-    rows, channels = x_in.shape
-    lags, requests, _ = conv_edge.shape
-    block = min(2048, channels)
+    channels = x_in.shape[1]
     groups = owners // PLANE
+    vmem = pl.BlockSpec(memory_space=pltpu.VMEM)
     return pl.pallas_call(
         kept_edge_kernel,
-        grid=(channels // block,),
         in_specs=[pl.BlockSpec(memory_space=pltpu.SMEM)] * len(scalars)
-        + [
-            pl.BlockSpec((rows, block), lambda j: (0, j)),
-            pl.BlockSpec((lags, requests, block), lambda j: (0, 0, j)),
-            pl.BlockSpec(memory_space=pl.ANY),
-        ],
-        out_specs=[pl.BlockSpec((PLANE * EDGE_ROWS, block), lambda j: (0, j))] * groups,
+        + [vmem, vmem, pl.BlockSpec(memory_space=pl.ANY)],
+        out_specs=[vmem] * groups,
         out_shape=[pltpu.HBM((PLANE * EDGE_ROWS, channels), jnp.bfloat16)] * groups,
-        compiler_params=pltpu.CompilerParams(
-            dimension_semantics=("arbitrary",), vmem_limit_bytes=VMEM_BYTES
-        ),
+        compiler_params=pltpu.CompilerParams(vmem_limit_bytes=VMEM_BYTES),
         name="kept_edges",
-    )(*scalars, in_hbm(x_in), in_hbm(conv_edge), in_hbm(after))
+    )(*scalars, x_in, conv_edge, in_hbm(after))
 
 
 def regroup_kernel(*refs):
@@ -241,11 +233,11 @@
 def kept_kernel(parts, *refs):
     place_ref, accepted_ref, owner_ref = refs[:3]
     (
-        dt_gain_ref, b_gain_ref, dt_weight_ref, dt_bias_ref, state_ref, a_log_hbm, conv_hbm,
-        slot_ref, part_ref, a_log_ref, conv_ref, in_ref, size_ref, drive_ref, rate_ref, new_ref,
+        dt_gain_ref, b_gain_ref, dt_weight_ref, dt_bias_ref, a_log_hbm, conv_hbm, state_hbm,
+        slot_ref, part_ref, a_log_ref, conv_ref, state_ref, in_ref, size_ref, drive_ref, rate_ref, new_ref,
         in_sems, sems,
     ) = refs[3 + parts :]
-    pairs = ((refs[3], part_ref), (a_log_hbm, a_log_ref), (conv_hbm, conv_ref))
+    pairs = ((refs[3], part_ref), (a_log_hbm, a_log_ref), (conv_hbm, conv_ref), (state_hbm, state_ref))
     copies = [pltpu.make_async_copy(*pair, in_sems.at[i]) for i, pair in enumerate(pairs)]
     for copy in copies:
         copy.start()
@@ -292,6 +284,11 @@
         def one_span(part, inner):
             tiles = [pl.multiple_of(part * span + c, LANES) for c in range(0, span, LANES)]
 
+            rates = [
+                [rate_ref[8 * h : 8 * (h + 1), pl.ds(tile, LANES)] for tile in tiles]
+                for h in range(halves)
+            ]
+
             def one_round(i, hidden):
                 hidden = [list(h) for h in hidden]
                 for u in range(ROUND):
@@ -303,8 +300,8 @@
                         place = part * (span // LANES) + c
                         now, drive = size_ref[place, at, :], drive_ref[place, at, :]
                         for h in range(halves):
-                            rate = rate_ref[8 * h : 8 * (h + 1), pl.ds(tile, LANES)]
-                            hidden[h][c] = jnp.exp2(now * rate) * hidden[h][c] + drive * b[h]
+                            decay = jnp.exp2(now * rates[h][c])
+                            hidden[h][c] = decay * hidden[h][c] + drive * b[h]
                 return tuple(tuple(h) for h in hidden)
 
             lanes = pl.ds(pl.multiple_of(part * span, span), span)
@@ -325,6 +322,7 @@
         pltpu.make_async_copy(new_ref.at[r], slot_ref.at[slot], sems.at[r]).start()
         return carry
 
+    copies[3].wait()
     lax.fori_loop(0, requests, one_request, 0)
     for r in range(requests):
         slot = owner_ref[place_ref[0] * requests + r]
@@ -335,8 +333,8 @@
     rows, channels = conv.shape
     states, rank = a_log.shape[0], dt_weight.shape[0]
     requests = scalars[1].shape[0]
-    near = [*partials[1:], *gains, dt_weight, dt_bias, state]
-    far = [in_hbm(a_log), in_hbm(conv)]
+    near = [*partials[1:], *gains, dt_weight, dt_bias]
+    far = [in_hbm(a_log), in_hbm(conv), in_hbm(state)]
     anywhere = pl.BlockSpec(memory_space=pl.ANY)
     return pl.pallas_call(
         functools.partial(kept_kernel, len(partials)),
@@ -350,6 +348,7 @@
             pltpu.VMEM(partials[0].shape, jnp.float32),
             pltpu.VMEM(a_log.shape, jnp.float32),
             pltpu.VMEM(conv.shape, jnp.bfloat16),
+            pltpu.VMEM(state.shape, jnp.bfloat16),
             pltpu.VMEM((requests * states, rows // requests * LANES), jnp.float32),
             pltpu.VMEM((channels // LANES, rows + 8, LANES), jnp.float32),
             pltpu.VMEM((channels // LANES, rows + 8, LANES), jnp.float32),
@@ -611,22 +610,22 @@
     groups = kept_edges((place, accepted, prompt_len, owner), x_in, by_lag, partial, owners)
     groups = [swap(rows, d * PLANE) for d, rows in enumerate(groups)]
 
+    gains = (dt_gain.reshape(1, -1), b_gain.reshape(1, -1), c_gain.reshape(1, -1))
+    bias = dt_bias.reshape(1, -1)
+    state = ssm_state.reshape(requests * states, channels)
+    slots = kept_states(
+        (place, accepted, owner), partials, gains[:2], dt_proj_weight, bias, a_log, conv, state, owners
+    )
+    got = lax.all_to_all(slots, "req", split_axis=0, concat_axis=0, tiled=True)
+    mixed = scan(
+        partials, gains, dt_proj_weight, bias, a_log, skip.reshape(1, -1), conv, state, z_gate
+    )
+    mixed, owner = lax.optimization_barrier((mixed, owner))
     hits = jnp.any(owner.reshape(owners, requests) == place, axis=1)
     ids = jnp.arange(owners, dtype=jnp.int32)
     ranks = jnp.sum((hits[None, :] & (ids[None, :] < ids[:, None])).astype(jnp.int32), axis=1)
     at = hits[None, :] & (ranks[None, :] == jnp.arange(own_most, dtype=jnp.int32)[:, None])
     source = owners - jnp.sum(jnp.where(at, owners - ids[None, :], 0), axis=1)
-
-    gains = (dt_gain.reshape(1, -1), b_gain.reshape(1, -1), c_gain.reshape(1, -1))
-    bias = dt_bias.reshape(1, -1)
-    state = ssm_state.reshape(requests * states, channels)
-    slots = kept_states(
-        (place, accepted, owner), partials, gains[:2], dt_proj_weight, bias, a_log, conv, state, owners
-    )
-    got = lax.all_to_all(slots, "req", split_axis=0, concat_axis=0, tiled=True)
-    mixed = scan(
-        partials, gains, dt_proj_weight, bias, a_log, skip.reshape(1, -1), conv, state, z_gate
-    )
     groups = [swap(rows, p) for p, rows in enumerate(regroup(groups, mixed))]
     owned_edge, tenant_stats = settle_edges(
         place, source, tenant_range, groups, own_most, lags, x_in.shape[0] // requests,

time: 81.5 us -> 80.2 us (0.984)
    all_to_all x1, waiting for transfers between devices: 9.71 us -> 7.72 us  [per_device(): got = lax.all_to_all(slots, 'req', split_axis=0, concat_axis=0, tiled=True)]
    ppermute x6, waiting for transfers between devices: 10.1 us -> 11.7 us  [swap(): lax.ppermute(rows, 'req', [(i, i ^ delta) for i in range(owners)])]
    unnamed x32 -> x34, local copies, waits for them, and re-layouts: 1.71 us -> 1.72 us
  transfers between devices with their start and end apart: 8 -> 8, of which waited for: 3 -> 3; matrix products, arithmetic and copies ran while one was open for 2% -> 2% of each run, Pallas kernels for 42% -> 41%
where the time goes in v7:
time: 80.2 us; the launch traced here: 79.4 us
  Pallas kernels  40.4 us (50%)
  waiting for transfers between devices  19.4 us (24%)
  starting transfers between devices  16 us (20%)
  local copies, waits for them, and re-layouts  1.81 us (2%)
  other arithmetic  0.88 us (1%)
  between operations  0.88 us (1%)
    pallas_call x1, Pallas kernels, scan(): pl.pallas_call(functools.partial(scan_kernel, len(partials)), grid=(chann...  18.9 us
    ppermute x6, waiting for transfers between devices, swap(): lax.ppermute(rows, 'req', [(i, i ^ delta) for i in range(owners)])  11.7 us
    all_to_all x1, starting transfers between devices, per_device(): got = lax.all_to_all(slots, 'req', split_axis=0, concat_axis=0, tiled=True)  9.85 us
    all_to_all x1, waiting for transfers between devices, per_device(): got = lax.all_to_all(slots, 'req', split_axis=0, concat_axis=0, tiled=True)  7.72 us
    pallas_call x1, Pallas kernels, kept_states(): pl.pallas_call(functools.partial(kept_kernel, len(partials)), in_specs=[p...  7.24 us
    ppermute x6, starting transfers between devices, swap(): lax.ppermute(rows, 'req', [(i, i ^ delta) for i in range(owners)])  4.86 us
    pallas_call x1, Pallas kernels, conv_project(): pl.pallas_call(conv_kernel, in_specs=[pl.BlockSpec(memory_space=pl.ANY)]...  4.25 us
    pallas_call x1, Pallas kernels, settle_states(): pl.pallas_call(settle_kernel, in_specs=[pl.BlockSpec(memory_space=pltpu.S...  3.37 us
  transfers between devices with their start and end apart: 8, of which 3 were waited for; matrix products, arithmetic and copies ran while one was open for 2% of the time, Pallas kernels for 41%

profile of v7, /device:TPU:11, one launch (start us, length us, event | category | flops | bytes accessed | tf_op | source)
XLA Modules:
  0.0 79.4 jit_solution(10237626246463687046)
XLA Ops:
  0.6 0.0 copy-start
  0.6 0.0 copy-start.1
  0.7 0.0 copy-start.7
  0.7 0.0 copy-start.6
  0.7 0.0 copy-start.5
  0.7 0.0 copy-start.14
  0.7 0.0 copy-start.8
  0.7 0.0 copy-start.9
  0.7 0.0 copy-start.11
  0.7 0.0 copy-start.12
  0.7 4.2 %conv_project.1 = (bf16[128,4096]{1,0:T(8,128)(2,1)}, f32[288,128]{1,0:T(8,128)}) custom-call(bf16[128,4096]{1,0:T(8,128)(2,1)} %x_ref.1, bf16[3,8,4096]{2,1,0:T(8,128)(2,1)} %bitcast.10, f32[4,4096]{1,0:T(4,128)} %weight_hbm.1, f32[1,4096]{1,0:T(1,128)} %bitcast.21, bf16[288,4096]{1,0:T(8,128)(2,1)} %bitcast.20), custom_call_target="tpu_custom_call" | custom-call | tf_op jit(solution)/shard_map/conv_project/pallas_call | solution.py:106
  5.0 1.3 %collective-permute-start = (f32[288,128]{1,0:T(8,128)}, f32[288,128]{1,0:T(8,128)S(1)}, u32[]{:S(2)}, u32[]{:S(2)}) collective-permute-start(f32[288,128]{1,0:T(8,128)} %get-tuple-element.18.refs_0_.refs_3_._), channel_id=1, source_target_pairs={{0,1},{1,0},{2,3},{3,2},{4,5},{5,4},{6,7},{7,6},{8,9},{9,8},{10,11... | collective-permute-start | bytes 442376 | tf_op jit(solution)/shard_map/ppermute | solution.py:603
  6.3 0.0 copy-done
  6.3 0.0 copy-done.1
  6.3 1.8 %kept_edges.1 = (bf16[16,4096]{1,0:T(8,128)(2,1)}, bf16[16,4096]{1,0:T(8,128)(2,1)}, bf16[16,4096]{1,0:T(8,128)(2,1)}, bf16[16,4096]{1,0:T(8,128)(2,1)}) custom-call(s32[1]{0:T(128)} %bitcast.9.refs_0_.place_ref, s32[8]{0:T(128)S(1)} %copy-done.6, s32[8]{0:T(128)S(1)} %copy-done.5, s32[128]{0:T(128)S(1)} %copy-done.7, bf16[128,4096]{1,0:T(8,128)(2,1)S(1)} %copy-done, ...), custom_call_target="tpu_custom_call" | custom-call | tf_op jit(solution)/shard_map/kept_edges/pallas_call | solution.py:163
  8.1 0.2 collective-permute-start.1
  8.2 2.3 %collective-permute-start.2 = (bf16[16,4096]{1,0:T(8,128)(2,1)}, bf16[16,4096]{1,0:T(8,128)(2,1)}, u32[]{:S(2)}, u32[]{:S(2)}) collective-permute-start(bf16[16,4096]{1,0:T(8,128)(2,1)} %get-tuple-element.24), channel_id=1, source_target_pairs={{0,16},{2,18},{4,20},{6,22},{8,24},{10,26},{12,28},{14,30},{16,0},... | collective-permute-start | bytes 393224 | tf_op jit(solution)/shard_map/ppermute | solution.py:608
  10.6 0.2 collective-permute-start.3
  10.7 0.1 copy.26.range_ref
  10.8 0.5 iota_subtract_fusion
  11.3 0.0 collective-permute-done.refs_1_.refs_4_
  11.4 7.2 %kept_states.1 = bf16[16,16,4096]{2,1,0:T(8,128)(2,1)} custom-call(s32[1]{0:T(128)} %bitcast.9.refs_0_.place_ref, s32[8]{0:T(128)S(1)} %copy-done.6, s32[128]{0:T(128)S(1)} %copy-done.7, f32[288,128]{1,0:T(8,128)} %get-tuple-element.18.refs_0_.refs_3_._, f32[288,128]{1,0:T(8,128)S(1)} %collective-permute-done.refs_1_.refs_4_, f32[1,256]{1,0:T(1,128)S(1)} %bitcast.15, ...), custom_call_target="tpu_custom_call" | custom-call | flops 1006632960000 | bytes 6291456 | tf_op jit(solution)/shard_map/kept_states/pallas_call | solution.py:339
  18.6 0.0 copy-start.2
  18.6 0.0 copy-start.10
  18.6 0.0 copy-start.13
  18.6 9.9 %all-to-all-start = ((bf16[16,16,4096]{2,1,0:T(8,128)(2,1)}), bf16[16,16,4096]{2,1,0:T(8,128)(2,1)}, u32[]{:S(2)}, u32[]{:S(2)}) async-start(bf16[16,16,4096]{2,1,0:T(8,128)(2,1)} %kept_states.1), calls=%async_computation | async-start | bytes 4194304 | tf_op jit(solution)/shard_map/all_to_all | solution.py:619
  28.5 0.0 copy-done.2
  28.5 0.0 copy-start.15
  28.5 18.9 %scan.1.refs_4_ = bf16[128,4096]{1,0:T(8,128)(2,1)} custom-call(f32[288,128]{1,0:T(8,128)S(1)} %copy-done.2, f32[288,128]{1,0:T(8,128)S(1)} %collective-permute-done.refs_1_.refs_4_, f32[1,256]{1,0:T(1,128)S(1)} %bitcast.16, f32[1,16]{1,0:T(1,128)S(1)} %bitcast.18, f32[1,16]{1,0:T(1,128)S(1)} %bitcast.19, bf16[256,4096]{1,0:T(8,128)(2,1)} %refs_7_.3, ...), custom_call_target="tpu_custom_call" | custom-call | flops 2013265920000 | bytes 5242880 | tf_op jit(solution)/shard_map/scan/pallas_call | solution.py:455
  47.4 0.1 eq.26
  47.5 0.0 collective-permute-done.1.refs_1_
  47.5 0.0 collective-permute-done.2.refs_2_
  47.5 0.0 collective-permute-done.3.refs_3_
  47.6 2.9 %regroup.1 = (bf16[16,4096]{1,0:T(8,128)(2,1)}, bf16[16,4096]{1,0:T(8,128)(2,1)}, bf16[16,4096]{1,0:T(8,128)(2,1)}, bf16[16,4096]{1,0:T(8,128)(2,1)}) custom-call(bf16[16,4096]{1,0:T(8,128)(2,1)S(1)} %copy-done.3, bf16[16,4096]{1,0:T(8,128)(2,1)} %collective-permute-done.1.refs_1_, bf16[16,4096]{1,0:T(8,128)(2,1)} %collective-permute-done.2.refs_2_, ...), custom_call_target="tpu_custom_call" | custom-call | tf_op jit(solution)/shard_map/regroup/pallas_call | solution.py:188
  50.5 0.4 collective-permute-start.4
  50.9 0.3 collective-permute-start.5
  51.2 1.5 %collective-permute-start.6 = (bf16[16,4096]{1,0:T(8,128)(2,1)}, bf16[16,4096]{1,0:T(8,128)(2,1)S(1)}, u32[]{:S(2)}, u32[]{:S(2)}) collective-permute-start(bf16[16,4096]{1,0:T(8,128)(2,1)} %get-tuple-element.29), channel_id=1, source_target_pairs={{0,6},{2,4},{4,2},{6,0},{8,14},{10,12},{12,10},{14,8},{16,22},{18,... | collective-permute-start | bytes 393224 | tf_op jit(solution)/shard_map/ppermute | solution.py:608
  52.7 0.1 reduce_or.9
  52.8 0.1 convert_reduce_fusion
  52.9 0.1 select_reduce_fusion
  53.1 0.0 collective-permute-done.4.refs_1_
  53.1 3.4 %collective-permute-done.5.refs_2_ = bf16[16,4096]{1,0:T(8,128)(2,1)S(1)} collective-permute-done((bf16[16,4096]{1,0:T(8,128)(2,1)}, bf16[16,4096]{1,0:T(8,128)(2,1)S(1)}, u32[]{:S(2)}, u32[]{:S(2)}) %collective-permute-start.5) | collective-permute-done | bytes 131104 | tf_op jit(solution)/shard_map/ppermute | solution.py:608
  56.5 8.3 %collective-permute-done.6.refs_3_ = bf16[16,4096]{1,0:T(8,128)(2,1)S(1)} collective-permute-done((bf16[16,4096]{1,0:T(8,128)(2,1)}, bf16[16,4096]{1,0:T(8,128)(2,1)S(1)}, u32[]{:S(2)}, u32[]{:S(2)}) %collective-permute-start.6) | collective-permute-done | bytes 131104 | tf_op jit(solution)/shard_map/ppermute | solution.py:608
  64.8 0.9 %copy-done.4 = bf16[16,4096]{1,0:T(8,128)(2,1)S(1)} copy-done((bf16[16,4096]{1,0:T(8,128)(2,1)S(1)}, bf16[16,4096]{1,0:T(8,128)(2,1)}, u32[]{:S(2)}) %copy-start.4) | copy-done | bytes 131096
  65.7 2.0 %settle_edges.1 = (bf16[12,3,4096]{2,1,0:T(4,128)(2,1)}, f32[4,2]{1,0:T(4,128)S(1)}) custom-call(s32[1]{0:T(128)} %bitcast.9.refs_0_.place_ref, s32[12]{0:T(128)S(1)} %broadcast_subtract_fusion.source_ref, s32[4,2]{1,0:T(4,128)S(1)} %copy.26.range_ref, bf16[16,4096]{1,0:T(8,128)(2,1)S(1)} %copy-done.4, bf16[16,4096]{1,0:T(8,128)(2,1)S(1)} %collective-permute-done.4.refs_1_, ...), custom_call_target="tpu_custom_call" | custom-call | tf_op jit(solution)/shard_map/settle_edges/pallas_call | solution.py:535
  67.7 0.6 copy.27
  68.3 7.7 %all-to-all-done.got_hbm = bf16[16,16,4096]{2,1,0:T(8,128)(2,1)} async-done(((bf16[16,16,4096]{2,1,0:T(8,128)(2,1)}), bf16[16,16,4096]{2,1,0:T(8,128)(2,1)}, u32[]{:S(2)}, u32[]{:S(2)}) %all-to-all-start) | async-done | bytes 2097184 | tf_op jit(solution)/shard_map/all_to_all | solution.py:619
  76.0 3.4 %settle_states.1 = bf16[12,16,4096]{2,1,0:T(8,128)(2,1)} custom-call(s32[12]{0:T(128)S(1)} %broadcast_subtract_fusion.source_ref, bf16[16,16,4096]{2,1,0:T(8,128)(2,1)} %all-to-all-done.got_hbm), custom_call_target="tpu_custom_call" | custom-call | tf_op jit(solution)/shard_map/settle_states/pallas_call | solution.py:573
  (16 shorter events, 0.0 us)
Async XLA Ops:
  0.6 5.7 %copy-start = (bf16[128,4096]{1,0:T(8,128)(2,1)S(1)}, bf16[128,4096]{1,0:T(8,128)(2,1)}, u32[]{:S(2)}) copy-start(bf16[128,4096]{1,0:T(8,128)(2,1)} %x_ref.1) | copy-start | bytes 3145732
  0.6 5.7 %copy-start.1 = (bf16[8,3,4096]{2,0,1:T(8,128)(2,1)S(1)}, bf16[8,3,4096]{2,0,1:T(8,128)(2,1)}, u32[]{:S(2)}) copy-start(bf16[8,3,4096]{2,0,1:T(8,128)(2,1)} %param.20) | copy-start | bytes 589828
  0.7 5.6 %copy-start.7 = (s32[128]{0:T(128)S(1)}, s32[128]{0:T(128)}, u32[]{:S(2)}) copy-start(s32[128]{0:T(128)} %owner_ref.1) | copy-start | bytes 1540
  0.7 5.6 %copy-start.6 = (s32[8]{0:T(128)S(1)}, s32[8]{0:T(128)}, u32[]{:S(2)}) copy-start(s32[8]{0:T(128)} %accepted_ref.1) | copy-start | bytes 100
  0.7 5.6 %copy-start.5 = (s32[8]{0:T(128)S(1)}, s32[8]{0:T(128)}, u32[]{:S(2)}) copy-start(s32[8]{0:T(128)} %length_ref.1) | copy-start | bytes 100
  0.7 10.0 %copy-start.14 = (s32[4,2]{0,1:T(2,128)S(1)}, s32[4,2]{0,1:T(2,128)}, u32[]{:S(2)}) copy-start(s32[4,2]{0,1:T(2,128)} %param.34) | copy-start | bytes 100
  0.7 10.6 %copy-start.8 = (bf16[256,4096]{1,0:T(8,128)(2,1)S(1)}, bf16[256,4096]{1,0:T(8,128)(2,1)}, u32[]{:S(2)}) copy-start(bf16[256,4096]{1,0:T(8,128)(2,1)} %refs_7_.3) | copy-start | bytes 6291460
  0.7 10.6 %copy-start.9 = (f32[4096]{0:T(1024)S(1)}, f32[4096]{0:T(1024)}, u32[]{:S(2)}) copy-start(f32[4096]{0:T(1024)} %param.28) | copy-start | bytes 49156
  0.7 10.6 %copy-start.11 = (f32[256]{0:T(256)S(1)}, f32[256]{0:T(256)}, u32[]{:S(2)}) copy-start(f32[256]{0:T(256)} %param.24) | copy-start | bytes 3076
  0.7 10.6 %copy-start.12 = (f32[16]{0:T(128)S(1)}, f32[16]{0:T(128)}, u32[]{:S(2)}) copy-start(f32[16]{0:T(128)} %param.25) | copy-start | bytes 196
  5.0 6.3 %collective-permute-start = (f32[288,128]{1,0:T(8,128)}, f32[288,128]{1,0:T(8,128)S(1)}, u32[]{:S(2)}, u32[]{:S(2)}) collective-permute-start(f32[288,128]{1,0:T(8,128)} %get-tuple-element.18.refs_0_.refs_3_._), channel_id=1, source_target_pairs={{0,1},{1,0},{2,3},{3,2},{4,5},{5,4},{6,7},{7,6},{8,9},{9,8},{10,11... | collective-permute-start | bytes 442376 | tf_op jit(solution)/shard_map/ppermute | solution.py:603
  8.1 39.4 %collective-permute-start.1 = (bf16[16,4096]{1,0:T(8,128)(2,1)}, bf16[16,4096]{1,0:T(8,128)(2,1)}, u32[]{:S(2)}, u32[]{:S(2)}) collective-permute-start(bf16[16,4096]{1,0:T(8,128)(2,1)} %get-tuple-element.23), channel_id=1, source_target_pairs={{0,8},{2,10},{4,12},{6,14},{8,0},{10,2},{12,4},{14,6},{16,24},{18,... | collective-permute-start | bytes 393224 | tf_op jit(solution)/shard_map/ppermute | solution.py:608
  8.2 39.3 %collective-permute-start.2 = (bf16[16,4096]{1,0:T(8,128)(2,1)}, bf16[16,4096]{1,0:T(8,128)(2,1)}, u32[]{:S(2)}, u32[]{:S(2)}) collective-permute-start(bf16[16,4096]{1,0:T(8,128)(2,1)} %get-tuple-element.24), channel_id=1, source_target_pairs={{0,16},{2,18},{4,20},{6,22},{8,24},{10,26},{12,28},{14,30},{16,0},... | collective-permute-start | bytes 393224 | tf_op jit(solution)/shard_map/ppermute | solution.py:608
  10.6 37.0 %collective-permute-start.3 = (bf16[16,4096]{1,0:T(8,128)(2,1)}, bf16[16,4096]{1,0:T(8,128)(2,1)}, u32[]{:S(2)}, u32[]{:S(2)}) collective-permute-start(bf16[16,4096]{1,0:T(8,128)(2,1)} %get-tuple-element.25), channel_id=1, source_target_pairs={{0,24},{2,26},{4,28},{6,30},{8,16},{10,18},{12,20},{14,22},{16,8},... | collective-permute-start | bytes 393224 | tf_op jit(solution)/shard_map/ppermute | solution.py:608
  18.6 9.9 %copy-start.2 = (f32[288,128]{1,0:T(8,128)S(1)}, f32[288,128]{1,0:T(8,128)}, u32[]{:S(2)}) copy-start(f32[288,128]{1,0:T(8,128)} %get-tuple-element.18.refs_0_.refs_3_._) | copy-start | bytes 442372
  18.6 9.9 %copy-start.10 = (f32[4096]{0:T(1024)S(1)}, f32[4096]{0:T(1024)}, u32[]{:S(2)}) copy-start(f32[4096]{0:T(1024)} %param.30) | copy-start | bytes 49156
  18.6 9.9 %copy-start.13 = (f32[16]{0:T(128)S(1)}, f32[16]{0:T(128)}, u32[]{:S(2)}) copy-start(f32[16]{0:T(128)} %param.26) | copy-start | bytes 196
  18.6 57.4 %all-to-all-start = ((bf16[16,16,4096]{2,1,0:T(8,128)(2,1)}), bf16[16,16,4096]{2,1,0:T(8,128)(2,1)}, u32[]{:S(2)}, u32[]{:S(2)}) async-start(bf16[16,16,4096]{2,1,0:T(8,128)(2,1)} %kept_states.1), calls=%async_computation | async-start | bytes 4194304 | tf_op jit(solution)/shard_map/all_to_all | solution.py:619
  28.5 19.0 %copy-start.3 = (bf16[16,4096]{1,0:T(8,128)(2,1)S(1)}, bf16[16,4096]{1,0:T(8,128)(2,1)}, u32[]{:S(2)}) copy-start(bf16[16,4096]{1,0:T(8,128)(2,1)} %get-tuple-element.22.refs_0_) | copy-start | bytes 393220
  28.5 24.4 %copy-start.15 = (s32[16]{0:T(128)S(1)}, s32[16]{0:T(128)}, u32[]{:S(2)}) copy-start(s32[16]{0:T(128)} %iota_subtract_fusion) | copy-start | bytes 196
  50.5 2.6 %collective-permute-start.4 = (bf16[16,4096]{1,0:T(8,128)(2,1)}, bf16[16,4096]{1,0:T(8,128)(2,1)S(1)}, u32[]{:S(2)}, u32[]{:S(2)}) collective-permute-start(bf16[16,4096]{1,0:T(8,128)(2,1)} %get-tuple-element.27), channel_id=1, source_target_pairs={{0,2},{2,0},{4,6},{6,4},{8,10},{10,8},{12,14},{14,12},{16,18},{18,... | collective-permute-start | bytes 393224 | tf_op jit(solution)/shard_map/ppermute | solution.py:608
  50.9 5.6 %collective-permute-start.5 = (bf16[16,4096]{1,0:T(8,128)(2,1)}, bf16[16,4096]{1,0:T(8,128)(2,1)S(1)}, u32[]{:S(2)}, u32[]{:S(2)}) collective-permute-start(bf16[16,4096]{1,0:T(8,128)(2,1)} %get-tuple-element.28), channel_id=1, source_target_pairs={{0,4},{2,6},{4,0},{6,2},{8,12},{10,14},{12,8},{14,10},{16,20},{18,... | collective-permute-start | bytes 393224 | tf_op jit(solution)/shard_map/ppermute | solution.py:608
  51.2 13.6 %collective-permute-start.6 = (bf16[16,4096]{1,0:T(8,128)(2,1)}, bf16[16,4096]{1,0:T(8,128)(2,1)S(1)}, u32[]{:S(2)}, u32[]{:S(2)}) collective-permute-start(bf16[16,4096]{1,0:T(8,128)(2,1)} %get-tuple-element.29), channel_id=1, source_target_pairs={{0,6},{2,4},{4,2},{6,0},{8,14},{10,12},{12,10},{14,8},{16,22},{18,... | collective-permute-start | bytes 393224 | tf_op jit(solution)/shard_map/ppermute | solution.py:608
  64.8 0.9 %copy-start.4 = (bf16[16,4096]{1,0:T(8,128)(2,1)S(1)}, bf16[16,4096]{1,0:T(8,128)(2,1)}, u32[]{:S(2)}) copy-start(bf16[16,4096]{1,0:T(8,128)(2,1)} %get-tuple-element.26.refs_0_) | copy-start | bytes 393220

commit v8 on v7

--- a/solution.py
+++ b/solution.py
@@ -2,6 +2,7 @@
 
 import jax
 import jax.numpy as jnp
+import numpy as np
 from jax import lax
 from jax.experimental import pallas as pl
 from jax.experimental.pallas import tpu as pltpu
@@ -60,8 +61,8 @@
 
 
 def conv_kernel(
-    x_hbm, edge_hbm, weight_hbm, bias_hbm, proj_hbm, conv_hbm, partial_ref,
-    x_ref, edge_ref, weight_ref, bias_ref, proj_ref, conv_ref, sems, out_sem,
+    x_hbm, edge_hbm, weight_hbm, bias_hbm, proj_hbm, conv_hbm, partial_ref, sent_ref,
+    x_ref, edge_ref, weight_ref, bias_ref, proj_ref, conv_ref, sems, out_sems,
 ):
     lags, requests, channels = edge_ref.shape
     taps = weight_ref.shape[0]
@@ -74,6 +75,10 @@
     copies = [pltpu.make_async_copy(*pair, sems.at[i]) for i, pair in enumerate(pairs)]
     for copy in copies:
         copy.start()
+    results = [
+        pltpu.make_async_copy(conv_ref.at[:, piece], conv_hbm.at[:, piece], out_sems.at[i])
+        for i, piece in enumerate(pieces)
+    ]
     order = to_step_major(requests, steps)
     for copy in copies[:3]:
         copy.wait()
@@ -90,13 +95,15 @@
                 added = added + weight[k] * window[t + k]
             outs.append(silu(added))
         conv_ref[:, piece] = jnp.concatenate(outs, axis=0).astype(jnp.bfloat16)
-    result = pltpu.make_async_copy(conv_ref, conv_hbm, out_sem)
-    result.start()
+        results[i].start()
     copies[-1].wait()
-    partial_ref[...] = lax.dot_general(
+    partial = lax.dot_general(
         proj_ref[...], conv_ref[...], (((1,), (1,)), ((), ())), preferred_element_type=jnp.float32
     )
-    result.wait()
+    partial_ref[...] = partial
+    sent_ref[...] = partial.astype(jnp.bfloat16)
+    for result in results:
+        result.wait()
 
 
 def conv_project(x_in, conv_edge, conv_weight, conv_bias, proj):
@@ -106,16 +113,17 @@
     return pl.pallas_call(
         conv_kernel,
         in_specs=[pl.BlockSpec(memory_space=pl.ANY)] * len(operands),
-        out_specs=[pl.BlockSpec(memory_space=pl.ANY), pl.BlockSpec(memory_space=pltpu.VMEM)],
+        out_specs=[pl.BlockSpec(memory_space=pl.ANY)] + [pl.BlockSpec(memory_space=pltpu.VMEM)] * 2,
         out_shape=[
             pltpu.HBM((rows, channels), jnp.bfloat16),
             pltpu.HBM((proj.shape[0], rows), jnp.float32),
+            pltpu.HBM((proj.shape[0], rows), jnp.bfloat16),
         ],
         scratch_shapes=[pltpu.VMEM(a.shape, a.dtype) for a in operands]
         + [
             pltpu.VMEM((rows, channels), jnp.bfloat16),
             pltpu.SemaphoreType.DMA((4 + pieces,)),
-            pltpu.SemaphoreType.DMA,
+            pltpu.SemaphoreType.DMA((pieces,)),
         ],
         compiler_params=pltpu.CompilerParams(vmem_limit_bytes=VMEM_BYTES),
         name="conv_project",
@@ -222,7 +230,7 @@
 def summed(part_refs):
     total = part_refs[0][...]
     for part in part_refs[1:]:
-        total = total + part[...]
+        total = total + part[...].astype(jnp.float32)
     return total
 
 
@@ -251,7 +259,7 @@
     copies[0].wait()
     total = part_ref[...]
     for part in refs[4 : 3 + parts]:
-        total = total + part[...]
+        total = total + part[...].astype(jnp.float32)
     turned = state_map(total[rank : rank + states], b_gain_ref[...]).astype(jnp.float32)
     for row in range(rows):
         t, r = divmod(row, requests)
@@ -596,11 +604,11 @@
     place = lax.axis_index("req").astype(jnp.int32).reshape(1)
 
     by_lag = jnp.transpose(conv_edge, (1, 0, 2))
-    conv, partial = conv_project(
+    conv, partial, sent = conv_project(
         x_in, by_lag, conv_weight, conv_bias.reshape(1, -1), x_proj_weight.T
     )
     if lax.axis_size("tp") == 2:
-        partials = (partial, lax.ppermute(partial, "tp", [(0, 1), (1, 0)]))
+        partials = (partial, lax.ppermute(sent, "tp", [(0, 1), (1, 0)]))
     else:
         partials = (lax.psum(partial, "tp"),)
 
@@ -622,7 +630,7 @@
     )
     mixed, owner = lax.optimization_barrier((mixed, owner))
     hits = jnp.any(owner.reshape(owners, requests) == place, axis=1)
-    ids = jnp.arange(owners, dtype=jnp.int32)
+    ids = np.arange(owners, dtype=np.int32)
     ranks = jnp.sum((hits[None, :] & (ids[None, :] < ids[:, None])).astype(jnp.int32), axis=1)
     at = hits[None, :] & (ranks[None, :] == jnp.arange(own_most, dtype=jnp.int32)[:, None])
     source = owners - jnp.sum(jnp.where(at, owners - ids[None, :], 0), axis=1)

time: 80.2 us -> 79.8 us (level)
    unnamed x34 -> x36, local copies, waits for them, and re-layouts: 1.72 us -> 1.72 us
  transfers between devices with their start and end apart: 8 -> 8, of which waited for: 3 -> 3; matrix products, arithmetic and copies ran while one was open for 2% -> 1% of each run, Pallas kernels for 41% -> 41%
where the time goes in v8:
time: 79.8 us; the launch traced here: 79.6 us
  Pallas kernels  40.4 us (51%)
  waiting for transfers between devices  19.4 us (24%)
  starting transfers between devices  16.7 us (21%)
  local copies, waits for them, and re-layouts  1.82 us (2%)
  between operations  0.88 us (1%)
    pallas_call x1, Pallas kernels, scan(): pl.pallas_call(functools.partial(scan_kernel, len(partials)), grid=(chann...  18.9 us
    ppermute x6, waiting for transfers between devices, swap(): lax.ppermute(rows, 'req', [(i, i ^ delta) for i in range(owners)])  12.5 us
    all_to_all x1, starting transfers between devices, per_device(): got = lax.all_to_all(slots, 'req', split_axis=0, concat_axis=0, tiled=True)  10.5 us
    pallas_call x1, Pallas kernels, kept_states(): pl.pallas_call(functools.partial(kept_kernel, len(partials)), in_specs=[p...  7.44 us
    all_to_all x1, waiting for transfers between devices, per_device(): got = lax.all_to_all(slots, 'req', split_axis=0, concat_axis=0, tiled=True)  6.95 us
    ppermute x6, starting transfers between devices, swap(): lax.ppermute(rows, 'req', [(i, i ^ delta) for i in range(owners)])  4.86 us
    pallas_call x1, Pallas kernels, conv_project(): pl.pallas_call(conv_kernel, in_specs=[pl.BlockSpec(memory_space=pl.ANY)]...  4.1 us
    pallas_call x1, Pallas kernels, settle_states(): pl.pallas_call(settle_kernel, in_specs=[pl.BlockSpec(memory_space=pltpu.S...  3.37 us
  transfers between devices with their start and end apart: 8, of which 3 were waited for; matrix products, arithmetic and copies ran while one was open for 1% of the time, Pallas kernels for 41%

profile of v8, /device:TPU:11, one launch (start us, length us, event | category | flops | bytes accessed | tf_op | source)
XLA Modules:
  0.0 79.6 jit_solution(9635083392735016564)
XLA Ops:
  0.6 0.0 copy-start
  0.6 0.0 copy-start.1
  0.7 0.0 copy-start.7
  0.7 0.0 copy-start.6
  0.7 0.0 copy-start.5
  0.7 0.0 copy-start.15
  0.7 0.0 copy-start.8
  0.7 0.0 copy-start.9
  0.7 0.0 copy-start.11
  0.7 4.1 %conv_project.1 = (bf16[128,4096]{1,0:T(8,128)(2,1)}, f32[288,128]{1,0:T(8,128)}, bf16[288,128]{1,0:T(8,128)(2,1)}) custom-call(bf16[128,4096]{1,0:T(8,128)(2,1)} %x_ref.1, bf16[3,8,4096]{2,1,0:T(8,128)(2,1)} %bitcast.10, f32[4,4096]{1,0:T(4,128)} %weight_hbm.1, f32[1,4096]{1,0:T(1,128)} %bitcast.21, bf16[288,4096]{1,0:T(8,128)(2,1)} %bitcast.20), custom_call_target="tpu_custom_call" | custom-call | tf_op jit(solution)/shard_map/conv_project/pallas_call | solution.py:113
  4.8 1.3 %collective-permute-start = (bf16[288,128]{1,0:T(8,128)(2,1)}, bf16[288,128]{1,0:T(8,128)(2,1)S(1)}, u32[]{:S(2)}, u32[]{:S(2)}) collective-permute-start(bf16[288,128]{1,0:T(8,128)(2,1)} %get-tuple-element.20), channel_id=1, source_target_pairs={{0,1},{1,0},{2,3},{3,2},{4,5},{5,4},{6,7},{7,6},{8,9},{9,8},{10,11... | collective-permute-start | bytes 221192 | tf_op jit(solution)/shard_map/ppermute | solution.py:611
  6.2 0.0 copy-done.1
  6.2 0.0 copy-done.6
  6.2 1.7 %kept_edges.1 = (bf16[16,4096]{1,0:T(8,128)(2,1)}, bf16[16,4096]{1,0:T(8,128)(2,1)}, bf16[16,4096]{1,0:T(8,128)(2,1)}, bf16[16,4096]{1,0:T(8,128)(2,1)}) custom-call(s32[1]{0:T(128)} %bitcast.9.refs_0_.place_ref, s32[8]{0:T(128)S(1)} %copy-done.6, s32[8]{0:T(128)S(1)} %copy-done.5, s32[128]{0:T(128)S(1)} %copy-done.7, bf16[128,4096]{1,0:T(8,128)(2,1)S(1)} %copy-done, ...), custom_call_target="tpu_custom_call" | custom-call | tf_op jit(solution)/shard_map/kept_edges/pallas_call | solution.py:171
  7.9 0.2 collective-permute-start.1
  8.1 2.3 %collective-permute-start.2 = (bf16[16,4096]{1,0:T(8,128)(2,1)}, bf16[16,4096]{1,0:T(8,128)(2,1)}, u32[]{:S(2)}, u32[]{:S(2)}) collective-permute-start(bf16[16,4096]{1,0:T(8,128)(2,1)} %get-tuple-element.26), channel_id=1, source_target_pairs={{0,16},{2,18},{4,20},{6,22},{8,24},{10,26},{12,28},{14,30},{16,0},... | collective-permute-start | bytes 393224 | tf_op jit(solution)/shard_map/ppermute | solution.py:616
  10.4 0.2 collective-permute-start.3
  10.6 0.0 copy-done.15
  10.6 0.1 copy.28.range_ref
  10.7 0.0 collective-permute-done.refs_1_.refs_4_
  10.7 0.0 copy-done.8
  10.7 7.4 %kept_states.1 = bf16[16,16,4096]{2,1,0:T(8,128)(2,1)} custom-call(s32[1]{0:T(128)} %bitcast.9.refs_0_.place_ref, s32[8]{0:T(128)S(1)} %copy-done.6, s32[128]{0:T(128)S(1)} %copy-done.7, f32[288,128]{1,0:T(8,128)} %get-tuple-element.19.refs_0_.refs_3_._, bf16[288,128]{1,0:T(8,128)(2,1)S(1)} %collective-permute-done.refs_1_.refs_4_, f32[1,256]{1,0:T(1,128)S(1)} %bitcast.15, ...), custom_call_target="tpu_custom_call" | custom-call | flops 1006632960000 | bytes 6291456 | tf_op jit(solution)/shard_map/kept_states/pallas_call | solution.py:347
  18.1 0.0 copy-start.2
  18.1 0.0 copy-start.10
  18.2 0.0 copy-start.13
  18.2 10.5 %all-to-all-start = ((bf16[16,16,4096]{2,1,0:T(8,128)(2,1)}), bf16[16,16,4096]{2,1,0:T(8,128)(2,1)}, u32[]{:S(2)}, u32[]{:S(2)}) async-start(bf16[16,16,4096]{2,1,0:T(8,128)(2,1)} %kept_states.1), calls=%async_computation | async-start | bytes 4194304 | tf_op jit(solution)/shard_map/all_to_all | solution.py:627
  28.7 0.0 copy-start.14
  28.7 0.0 copy-start.16
  28.8 18.9 %scan.1.refs_4_ = bf16[128,4096]{1,0:T(8,128)(2,1)} custom-call(f32[288,128]{1,0:T(8,128)S(1)} %copy-done.2, bf16[288,128]{1,0:T(8,128)(2,1)S(1)} %collective-permute-done.refs_1_.refs_4_, f32[1,256]{1,0:T(1,128)S(1)} %bitcast.16, f32[1,16]{1,0:T(1,128)S(1)} %bitcast.18, f32[1,16]{1,0:T(1,128)S(1)} %bitcast.19, bf16[256,4096]{1,0:T(8,128)(2,1)} %refs_7_.3, ...), custom_call_target="tpu_custom_call" | custom-call | flops 2013265920000 | bytes 5242880 | tf_op jit(solution)/shard_map/scan/pallas_call | solution.py:463
  47.6 0.1 eq.26
  47.7 0.1 reduce_or.9
  47.9 0.1 convert_reduce_fusion
  48.0 0.1 select_reduce_fusion
  48.1 0.0 collective-permute-done.1.refs_1_
  48.1 0.0 collective-permute-done.2.refs_2_
  48.1 0.0 collective-permute-done.3.refs_3_
  48.1 2.9 %regroup.1 = (bf16[16,4096]{1,0:T(8,128)(2,1)}, bf16[16,4096]{1,0:T(8,128)(2,1)}, bf16[16,4096]{1,0:T(8,128)(2,1)}, bf16[16,4096]{1,0:T(8,128)(2,1)}) custom-call(bf16[16,4096]{1,0:T(8,128)(2,1)S(1)} %copy-done.3, bf16[16,4096]{1,0:T(8,128)(2,1)} %collective-permute-done.1.refs_1_, bf16[16,4096]{1,0:T(8,128)(2,1)} %collective-permute-done.2.refs_2_, ...), custom_call_target="tpu_custom_call" | custom-call | tf_op jit(solution)/shard_map/regroup/pallas_call | solution.py:196
  51.1 0.4 collective-permute-start.4
  51.5 0.3 collective-permute-start.5
  51.8 1.5 %collective-permute-start.6 = (bf16[16,4096]{1,0:T(8,128)(2,1)}, bf16[16,4096]{1,0:T(8,128)(2,1)S(1)}, u32[]{:S(2)}, u32[]{:S(2)}) collective-permute-start(bf16[16,4096]{1,0:T(8,128)(2,1)} %get-tuple-element.31), channel_id=1, source_target_pairs={{0,6},{2,4},{4,2},{6,0},{8,14},{10,12},{12,10},{14,8},{16,22},{18,... | collective-permute-start | bytes 393224 | tf_op jit(solution)/shard_map/ppermute | solution.py:616
  53.3 0.0 collective-permute-done.4.refs_1_
  53.3 3.5 %collective-permute-done.5.refs_2_ = bf16[16,4096]{1,0:T(8,128)(2,1)S(1)} collective-permute-done((bf16[16,4096]{1,0:T(8,128)(2,1)}, bf16[16,4096]{1,0:T(8,128)(2,1)S(1)}, u32[]{:S(2)}, u32[]{:S(2)}) %collective-permute-start.5) | collective-permute-done | bytes 131104 | tf_op jit(solution)/shard_map/ppermute | solution.py:616
  56.8 9.0 %collective-permute-done.6.refs_3_ = bf16[16,4096]{1,0:T(8,128)(2,1)S(1)} collective-permute-done((bf16[16,4096]{1,0:T(8,128)(2,1)}, bf16[16,4096]{1,0:T(8,128)(2,1)S(1)}, u32[]{:S(2)}, u32[]{:S(2)}) %collective-permute-start.6) | collective-permute-done | bytes 131104 | tf_op jit(solution)/shard_map/ppermute | solution.py:616
  65.7 0.9 %copy-done.4 = bf16[16,4096]{1,0:T(8,128)(2,1)S(1)} copy-done((bf16[16,4096]{1,0:T(8,128)(2,1)S(1)}, bf16[16,4096]{1,0:T(8,128)(2,1)}, u32[]{:S(2)}) %copy-start.4) | copy-done | bytes 131096
  66.6 2.0 %settle_edges.1 = (bf16[12,3,4096]{2,1,0:T(4,128)(2,1)}, f32[4,2]{1,0:T(4,128)S(1)}) custom-call(s32[1]{0:T(128)} %bitcast.9.refs_0_.place_ref, s32[12]{0:T(128)S(1)} %broadcast_subtract_fusion.source_ref, s32[4,2]{1,0:T(4,128)S(1)} %copy.28.range_ref, bf16[16,4096]{1,0:T(8,128)(2,1)S(1)} %copy-done.4, bf16[16,4096]{1,0:T(8,128)(2,1)S(1)} %collective-permute-done.4.refs_1_, ...), custom_call_target="tpu_custom_call" | custom-call | tf_op jit(solution)/shard_map/settle_edges/pallas_call | solution.py:543
  68.6 0.6 copy.29
  69.3 6.9 %all-to-all-done.got_hbm = bf16[16,16,4096]{2,1,0:T(8,128)(2,1)} async-done(((bf16[16,16,4096]{2,1,0:T(8,128)(2,1)}), bf16[16,16,4096]{2,1,0:T(8,128)(2,1)}, u32[]{:S(2)}, u32[]{:S(2)}) %all-to-all-start) | async-done | bytes 2097184 | tf_op jit(solution)/shard_map/all_to_all | solution.py:627
  76.2 3.4 %settle_states.1 = bf16[12,16,4096]{2,1,0:T(8,128)(2,1)} custom-call(s32[12]{0:T(128)S(1)} %broadcast_subtract_fusion.source_ref, bf16[16,16,4096]{2,1,0:T(8,128)(2,1)} %all-to-all-done.got_hbm), custom_call_target="tpu_custom_call" | custom-call | tf_op jit(solution)/shard_map/settle_states/pallas_call | solution.py:581
  (17 shorter events, 0.0 us)
Async XLA Ops:
  0.6 5.5 %copy-start = (bf16[128,4096]{1,0:T(8,128)(2,1)S(1)}, bf16[128,4096]{1,0:T(8,128)(2,1)}, u32[]{:S(2)}) copy-start(bf16[128,4096]{1,0:T(8,128)(2,1)} %x_ref.1) | copy-start | bytes 3145732
  0.6 5.5 %copy-start.1 = (bf16[8,3,4096]{2,0,1:T(8,128)(2,1)S(1)}, bf16[8,3,4096]{2,0,1:T(8,128)(2,1)}, u32[]{:S(2)}) copy-start(bf16[8,3,4096]{2,0,1:T(8,128)(2,1)} %param.22) | copy-start | bytes 589828
  0.7 5.5 %copy-start.7 = (s32[128]{0:T(128)S(1)}, s32[128]{0:T(128)}, u32[]{:S(2)}) copy-start(s32[128]{0:T(128)} %owner_ref.1) | copy-start | bytes 1540
  0.7 5.5 %copy-start.6 = (s32[8]{0:T(128)S(1)}, s32[8]{0:T(128)}, u32[]{:S(2)}) copy-start(s32[8]{0:T(128)} %accepted_ref.1) | copy-start | bytes 100
  0.7 5.5 %copy-start.5 = (s32[8]{0:T(128)S(1)}, s32[8]{0:T(128)}, u32[]{:S(2)}) copy-start(s32[8]{0:T(128)} %length_ref.1) | copy-start | bytes 100
  0.7 9.9 %copy-start.15 = (s32[4,2]{0,1:T(2,128)S(1)}, s32[4,2]{0,1:T(2,128)}, u32[]{:S(2)}) copy-start(s32[4,2]{0,1:T(2,128)} %param.36) | copy-start | bytes 100
  0.7 10.0 %copy-start.8 = (bf16[256,4096]{1,0:T(8,128)(2,1)S(1)}, bf16[256,4096]{1,0:T(8,128)(2,1)}, u32[]{:S(2)}) copy-start(bf16[256,4096]{1,0:T(8,128)(2,1)} %refs_7_.3) | copy-start | bytes 6291460
  0.7 10.0 %copy-start.9 = (f32[4096]{0:T(1024)S(1)}, f32[4096]{0:T(1024)}, u32[]{:S(2)}) copy-start(f32[4096]{0:T(1024)} %param.30) | copy-start | bytes 49156
  0.7 10.0 %copy-start.11 = (f32[256]{0:T(256)S(1)}, f32[256]{0:T(256)}, u32[]{:S(2)}) copy-start(f32[256]{0:T(256)} %param.26) | copy-start | bytes 3076
  0.7 10.0 %copy-start.12 = (f32[16]{0:T(128)S(1)}, f32[16]{0:T(128)}, u32[]{:S(2)}) copy-start(f32[16]{0:T(128)} %param.27) | copy-start | bytes 196
  4.8 5.8 %collective-permute-start = (bf16[288,128]{1,0:T(8,128)(2,1)}, bf16[288,128]{1,0:T(8,128)(2,1)S(1)}, u32[]{:S(2)}, u32[]{:S(2)}) collective-permute-start(bf16[288,128]{1,0:T(8,128)(2,1)} %get-tuple-element.20), channel_id=1, source_target_pairs={{0,1},{1,0},{2,3},{3,2},{4,5},{5,4},{6,7},{7,6},{8,9},{9,8},{10,11... | collective-permute-start | bytes 221192 | tf_op jit(solution)/shard_map/ppermute | solution.py:611
  7.9 40.2 %collective-permute-start.1 = (bf16[16,4096]{1,0:T(8,128)(2,1)}, bf16[16,4096]{1,0:T(8,128)(2,1)}, u32[]{:S(2)}, u32[]{:S(2)}) collective-permute-start(bf16[16,4096]{1,0:T(8,128)(2,1)} %get-tuple-element.25), channel_id=1, source_target_pairs={{0,8},{2,10},{4,12},{6,14},{8,0},{10,2},{12,4},{14,6},{16,24},{18,... | collective-permute-start | bytes 393224 | tf_op jit(solution)/shard_map/ppermute | solution.py:616
  8.1 40.0 %collective-permute-start.2 = (bf16[16,4096]{1,0:T(8,128)(2,1)}, bf16[16,4096]{1,0:T(8,128)(2,1)}, u32[]{:S(2)}, u32[]{:S(2)}) collective-permute-start(bf16[16,4096]{1,0:T(8,128)(2,1)} %get-tuple-element.26), channel_id=1, source_target_pairs={{0,16},{2,18},{4,20},{6,22},{8,24},{10,26},{12,28},{14,30},{16,0},... | collective-permute-start | bytes 393224 | tf_op jit(solution)/shard_map/ppermute | solution.py:616
  10.4 37.7 %collective-permute-start.3 = (bf16[16,4096]{1,0:T(8,128)(2,1)}, bf16[16,4096]{1,0:T(8,128)(2,1)}, u32[]{:S(2)}, u32[]{:S(2)}) collective-permute-start(bf16[16,4096]{1,0:T(8,128)(2,1)} %get-tuple-element.27), channel_id=1, source_target_pairs={{0,24},{2,26},{4,28},{6,30},{8,16},{10,18},{12,20},{14,22},{16,8},... | collective-permute-start | bytes 393224 | tf_op jit(solution)/shard_map/ppermute | solution.py:616
  18.1 10.6 %copy-start.2 = (f32[288,128]{1,0:T(8,128)S(1)}, f32[288,128]{1,0:T(8,128)}, u32[]{:S(2)}) copy-start(f32[288,128]{1,0:T(8,128)} %get-tuple-element.19.refs_0_.refs_3_._) | copy-start | bytes 442372
  18.1 10.6 %copy-start.10 = (f32[4096]{0:T(1024)S(1)}, f32[4096]{0:T(1024)}, u32[]{:S(2)}) copy-start(f32[4096]{0:T(1024)} %param.32) | copy-start | bytes 49156
  18.2 10.6 %copy-start.13 = (f32[16]{0:T(128)S(1)}, f32[16]{0:T(128)}, u32[]{:S(2)}) copy-start(f32[16]{0:T(128)} %param.28) | copy-start | bytes 196
  18.2 58.1 %all-to-all-start = ((bf16[16,16,4096]{2,1,0:T(8,128)(2,1)}), bf16[16,16,4096]{2,1,0:T(8,128)(2,1)}, u32[]{:S(2)}, u32[]{:S(2)}) async-start(bf16[16,16,4096]{2,1,0:T(8,128)(2,1)} %kept_states.1), calls=%async_computation | async-start | bytes 4194304 | tf_op jit(solution)/shard_map/all_to_all | solution.py:627
  28.7 19.1 %copy-start.14 = (pred[16,16]{1,0:T(8,128)(4,1)S(1)}, pred[16,16]{1,0:T(8,128)(4,1)}, u32[]{:S(2)}) copy-start(pred[16,16]{1,0:T(8,128)(4,1)} %constant.16.clone) | copy-start | bytes 772
  28.7 19.2 %copy-start.16 = (s32[16]{0:T(128)S(1)}, s32[16]{0:T(128)}, u32[]{:S(2)}) copy-start(s32[16]{0:T(128)} %constant.22) | copy-start | bytes 196
  28.8 19.4 %copy-start.3 = (bf16[16,4096]{1,0:T(8,128)(2,1)S(1)}, bf16[16,4096]{1,0:T(8,128)(2,1)}, u32[]{:S(2)}) copy-start(bf16[16,4096]{1,0:T(8,128)(2,1)} %get-tuple-element.24.refs_0_) | copy-start | bytes 393220
  51.1 2.2 %collective-permute-start.4 = (bf16[16,4096]{1,0:T(8,128)(2,1)}, bf16[16,4096]{1,0:T(8,128)(2,1)S(1)}, u32[]{:S(2)}, u32[]{:S(2)}) collective-permute-start(bf16[16,4096]{1,0:T(8,128)(2,1)} %get-tuple-element.29), channel_id=1, source_target_pairs={{0,2},{2,0},{4,6},{6,4},{8,10},{10,8},{12,14},{14,12},{16,18},{18,... | collective-permute-start | bytes 393224 | tf_op jit(solution)/shard_map/ppermute | solution.py:616
  51.5 5.3 %collective-permute-start.5 = (bf16[16,4096]{1,0:T(8,128)(2,1)}, bf16[16,4096]{1,0:T(8,128)(2,1)S(1)}, u32[]{:S(2)}, u32[]{:S(2)}) collective-permute-start(bf16[16,4096]{1,0:T(8,128)(2,1)} %get-tuple-element.30), channel_id=1, source_target_pairs={{0,4},{2,6},{4,0},{6,2},{8,12},{10,14},{12,8},{14,10},{16,20},{18,... | collective-permute-start | bytes 393224 | tf_op jit(solution)/shard_map/ppermute | solution.py:616
  51.8 14.0 %collective-permute-start.6 = (bf16[16,4096]{1,0:T(8,128)(2,1)}, bf16[16,4096]{1,0:T(8,128)(2,1)S(1)}, u32[]{:S(2)}, u32[]{:S(2)}) collective-permute-start(bf16[16,4096]{1,0:T(8,128)(2,1)} %get-tuple-element.31), channel_id=1, source_target_pairs={{0,6},{2,4},{4,2},{6,0},{8,14},{10,12},{12,10},{14,8},{16,22},{18,... | collective-permute-start | bytes 393224 | tf_op jit(solution)/shard_map/ppermute | solution.py:616
  65.7 0.9 %copy-start.4 = (bf16[16,4096]{1,0:T(8,128)(2,1)S(1)}, bf16[16,4096]{1,0:T(8,128)(2,1)}, u32[]{:S(2)}) copy-start(bf16[16,4096]{1,0:T(8,128)(2,1)} %get-tuple-element.28.refs_0_) | copy-start | bytes 393220

commit v9 on v8

--- a/solution.py
+++ b/solution.py
@@ -17,6 +17,7 @@
 DIGIT = 7
 VMEM_BYTES = 24 * 1024 * 1024
 BLOCK = 2048
+PARTS = 4
 ROUND = 4
 VECTOR_WEIGHT = 30000
 
@@ -61,7 +62,7 @@
 
 
 def conv_kernel(
-    x_hbm, edge_hbm, weight_hbm, bias_hbm, proj_hbm, conv_hbm, partial_ref, sent_ref,
+    x_hbm, edge_hbm, weight_hbm, bias_hbm, proj_hbm, conv_hbm, partial_ref,
     x_ref, edge_ref, weight_ref, bias_ref, proj_ref, conv_ref, sems, out_sems,
 ):
     lags, requests, channels = edge_ref.shape
@@ -97,11 +98,9 @@
         conv_ref[:, piece] = jnp.concatenate(outs, axis=0).astype(jnp.bfloat16)
         results[i].start()
     copies[-1].wait()
-    partial = lax.dot_general(
+    partial_ref[...] = lax.dot_general(
         proj_ref[...], conv_ref[...], (((1,), (1,)), ((), ())), preferred_element_type=jnp.float32
     )
-    partial_ref[...] = partial
-    sent_ref[...] = partial.astype(jnp.bfloat16)
     for result in results:
         result.wait()
 
@@ -113,11 +112,10 @@
     return pl.pallas_call(
         conv_kernel,
         in_specs=[pl.BlockSpec(memory_space=pl.ANY)] * len(operands),
-        out_specs=[pl.BlockSpec(memory_space=pl.ANY)] + [pl.BlockSpec(memory_space=pltpu.VMEM)] * 2,
+        out_specs=[pl.BlockSpec(memory_space=pl.ANY), pl.BlockSpec(memory_space=pltpu.VMEM)],
         out_shape=[
             pltpu.HBM((rows, channels), jnp.bfloat16),
             pltpu.HBM((proj.shape[0], rows), jnp.float32),
-            pltpu.HBM((proj.shape[0], rows), jnp.bfloat16),
         ],
         scratch_shapes=[pltpu.VMEM(a.shape, a.dtype) for a in operands]
         + [
@@ -230,7 +228,7 @@
 def summed(part_refs):
     total = part_refs[0][...]
     for part in part_refs[1:]:
-        total = total + part[...].astype(jnp.float32)
+        total = total + part[...]
     return total
 
 
@@ -259,7 +257,7 @@
     copies[0].wait()
     total = part_ref[...]
     for part in refs[4 : 3 + parts]:
-        total = total + part[...].astype(jnp.float32)
+        total = total + part[...]
     turned = state_map(total[rank : rank + states], b_gain_ref[...]).astype(jnp.float32)
     for row in range(rows):
         t, r = divmod(row, requests)
@@ -559,38 +557,50 @@
     )(place, source, tenant_range, *got)
 
 
-def settle_kernel(source_ref, got_hbm, owned_hbm, rows_ref, in_sem, sems):
-    slots = got_hbm.shape[0]
-    fetch = pltpu.make_async_copy(got_hbm, rows_ref.at[:slots], in_sem)
-    fetch.start()
+def settle_kernel(source_ref, bound_ref, got_hbm, owned_hbm, rows_ref, in_sems, sems):
+    slots, own_most = got_hbm.shape[0], owned_hbm.shape[0]
+    size = slots // PARTS
+    parts = [slice(q * size, (q + 1) * size) for q in range(PARTS)]
+    fetches = [
+        pltpu.make_async_copy(got_hbm.at[part], rows_ref.at[part], in_sems.at[q])
+        for q, part in enumerate(parts)
+    ]
+    for fetch in fetches:
+        fetch.start()
     rows_ref[slots] = jnp.zeros(rows_ref.shape[1:], rows_ref.dtype)
-    fetch.wait()
-    puts = [
-        pltpu.make_async_copy(rows_ref.at[source_ref[i]], owned_hbm.at[i], sems.at[i])
-        for i in range(owned_hbm.shape[0])
-    ]
-    for put in puts:
-        put.start()
-    for put in puts:
-        put.wait()
-
-
-def settle_states(source, got, own_most):
+
+    def put(i):
+        return pltpu.make_async_copy(rows_ref.at[source_ref[i]], owned_hbm.at[i], sems.at[i])
+
+    def start(i, carry):
+        put(i).start()
+        return carry
+
+    lax.fori_loop(bound_ref[PARTS], own_most, start, 0)
+    for q, fetch in enumerate(fetches):
+        fetch.wait()
+        lax.fori_loop(bound_ref[q], bound_ref[q + 1], start, 0)
+    for i in range(own_most):
+        put(i).wait()
+
+
+def settle_states(source, bounds, got, own_most):
+    smem = pl.BlockSpec(memory_space=pltpu.SMEM)
     anywhere = pl.BlockSpec(memory_space=pl.ANY)
     slots, *rest = got.shape
     return pl.pallas_call(
         settle_kernel,
-        in_specs=[pl.BlockSpec(memory_space=pltpu.SMEM), anywhere],
+        in_specs=[smem, smem, anywhere],
         out_specs=anywhere,
         out_shape=pltpu.HBM((own_most, *rest), got.dtype),
         scratch_shapes=[
             pltpu.VMEM((slots + 1, *rest), got.dtype),
-            pltpu.SemaphoreType.DMA,
+            pltpu.SemaphoreType.DMA((PARTS,)),
             pltpu.SemaphoreType.DMA((own_most,)),
         ],
         compiler_params=pltpu.CompilerParams(vmem_limit_bytes=VMEM_BYTES),
         name="settle_states",
-    )(source, in_hbm(got))
+    )(source, bounds, in_hbm(got))
 
 
 def per_device(
@@ -604,11 +614,11 @@
     place = lax.axis_index("req").astype(jnp.int32).reshape(1)
 
     by_lag = jnp.transpose(conv_edge, (1, 0, 2))
-    conv, partial, sent = conv_project(
+    conv, partial = conv_project(
         x_in, by_lag, conv_weight, conv_bias.reshape(1, -1), x_proj_weight.T
     )
     if lax.axis_size("tp") == 2:
-        partials = (partial, lax.ppermute(sent, "tp", [(0, 1), (1, 0)]))
+        partials = (partial, lax.ppermute(partial, "tp", [(0, 1), (1, 0)]))
     else:
         partials = (lax.psum(partial, "tp"),)
 
@@ -616,7 +626,8 @@
         return lax.ppermute(rows, "req", [(i, i ^ delta) for i in range(owners)]) if delta else rows
 
     groups = kept_edges((place, accepted, prompt_len, owner), x_in, by_lag, partial, owners)
-    groups = [swap(rows, d * PLANE) for d, rows in enumerate(groups)]
+    half = len(groups) // 2
+    far = [swap(rows, d * PLANE) for d, rows in enumerate(groups) if d >= half]
 
     gains = (dt_gain.reshape(1, -1), b_gain.reshape(1, -1), c_gain.reshape(1, -1))
     bias = dt_bias.reshape(1, -1)
@@ -628,10 +639,13 @@
     mixed = scan(
         partials, gains, dt_proj_weight, bias, a_log, skip.reshape(1, -1), conv, state, z_gate
     )
-    mixed, owner = lax.optimization_barrier((mixed, owner))
+    mixed, owner, *near = lax.optimization_barrier((mixed, owner, *groups[:half]))
+    groups = [swap(rows, d * PLANE) for d, rows in enumerate(near)] + far
     hits = jnp.any(owner.reshape(owners, requests) == place, axis=1)
     ids = np.arange(owners, dtype=np.int32)
     ranks = jnp.sum((hits[None, :] & (ids[None, :] < ids[:, None])).astype(jnp.int32), axis=1)
+    starts = np.arange(PARTS + 1, dtype=np.int32) * (owners // PARTS)
+    bounds = jnp.sum((hits[None, :] & (ids[None, :] < starts[:, None])).astype(jnp.int32), axis=1)
     at = hits[None, :] & (ranks[None, :] == jnp.arange(own_most, dtype=jnp.int32)[:, None])
     source = owners - jnp.sum(jnp.where(at, owners - ids[None, :], 0), axis=1)
     groups = [swap(rows, p) for p, rows in enumerate(regroup(groups, mixed))]
@@ -639,7 +653,7 @@
         place, source, tenant_range, groups, own_most, lags, x_in.shape[0] // requests,
         requests,
     )
-    owned = settle_states(source, got, own_most)
+    owned = settle_states(source, bounds, got, own_most)
     return (mixed, owned, owned_edge, tenant_stats)
 
 

time: 79.8 us -> 87.1 us (1.091); the launches traced: 79.6 us -> 85.6 us
  waiting for transfers between devices: 19.4 us -> 27.4 us
  starting transfers between devices: 16.7 us -> 14.1 us
    ppermute x6, waiting for transfers between devices: 12.5 us -> 27.4 us  [swap(): lax.ppermute(rows, 'req', [(i, i ^ delta) for i in range(owners)])]
    all_to_all x1, waiting for transfers between devices: 6.95 us -> 0.01 us  [per_device(): got = lax.all_to_all(slots, 'req', split_axis=0, concat_axis=0, tiled=True)]
    all_to_all x1, starting transfers between devices: 10.5 us -> 7.49 us  [per_device(): got = lax.all_to_all(slots, 'req', split_axis=0, concat_axis=0, tiled=True)]
    pallas_call x1, Pallas kernels: 7.44 us -> 8.36 us  [kept_states(): pl.pallas_call(functools.partial(kept_kernel, len(partials)), in_specs=[p...]
  transfers between devices with their start and end apart: 8 -> 8, of which waited for: 3 -> 3; matrix products, arithmetic and copies ran while one was open for 1% -> 2% of each run, Pallas kernels for 41% -> 40%
where the time goes in v9:
time: 87.1 us; the launch traced here: 85.6 us
  Pallas kernels  40.9 us (47%)
  waiting for transfers between devices  27.4 us (31%)
  starting transfers between devices  14.1 us (16%)
  local copies, waits for them, and re-layouts  1.83 us (2%)
  between operations  0.88 us (1%)
    ppermute x6, waiting for transfers between devices, swap(): lax.ppermute(rows, 'req', [(i, i ^ delta) for i in range(owners)])  27.4 us
    pallas_call x1, Pallas kernels, scan(): pl.pallas_call(functools.partial(scan_kernel, len(partials)), grid=(chann...  18.9 us
    pallas_call x1, Pallas kernels, kept_states(): pl.pallas_call(functools.partial(kept_kernel, len(partials)), in_specs=[p...  8.36 us
    all_to_all x1, starting transfers between devices, per_device(): got = lax.all_to_all(slots, 'req', split_axis=0, concat_axis=0, tiled=True)  7.49 us
    ppermute x6, starting transfers between devices, swap(): lax.ppermute(rows, 'req', [(i, i ^ delta) for i in range(owners)])  5.28 us
    pallas_call x1, Pallas kernels, conv_project(): pl.pallas_call(conv_kernel, in_specs=[pl.BlockSpec(memory_space=pl.ANY)]...  4.09 us
    pallas_call x1, Pallas kernels, settle_states(): pl.pallas_call(settle_kernel, in_specs=[smem, smem, anywhere], out_specs=...  2.9 us
    pallas_call x1, Pallas kernels, regroup(): pl.pallas_call(regroup_kernel, grid=(channels // block,), in_specs=[pl.Bl...  2.89 us
  transfers between devices with their start and end apart: 8, of which 3 were waited for; matrix products, arithmetic and copies ran while one was open for 2% of the time, Pallas kernels for 40%

profile of v9, /device:TPU:11, one launch (start us, length us, event | category | flops | bytes accessed | tf_op | source)
XLA Modules:
  0.0 85.6 jit_solution(8418646457614798223)
XLA Ops:
  0.6 0.0 copy-start
  0.6 0.0 copy-start.1
  0.7 0.0 copy-start.7
  0.7 0.0 copy-start.6
  0.7 0.0 copy-start.8
  0.7 4.1 %conv_project.1 = (bf16[128,4096]{1,0:T(8,128)(2,1)}, f32[288,128]{1,0:T(8,128)}) custom-call(bf16[128,4096]{1,0:T(8,128)(2,1)} %x_ref.1, bf16[3,8,4096]{2,1,0:T(8,128)(2,1)} %bitcast.10, f32[4,4096]{1,0:T(4,128)} %weight_hbm.1, f32[1,4096]{1,0:T(1,128)} %bitcast.21, bf16[288,4096]{1,0:T(8,128)(2,1)} %bitcast.20), custom_call_target="tpu_custom_call" | custom-call | tf_op jit(solution)/shard_map/conv_project/pallas_call | solution.py:112
  4.8 1.3 %collective-permute-start = (f32[288,128]{1,0:T(8,128)}, f32[288,128]{1,0:T(8,128)S(1)}, u32[]{:S(2)}, u32[]{:S(2)}) collective-permute-start(f32[288,128]{1,0:T(8,128)} %get-tuple-element.20.refs_0_._.refs_3_), channel_id=1, source_target_pairs={{0,1},{1,0},{2,3},{3,2},{4,5},{5,4},{6,7},{7,6},{8,9},{9,8},{10,11... | collective-permute-start | bytes 442376 | tf_op jit(solution)/shard_map/ppermute | solution.py:621
  6.1 0.0 copy-done.7
  6.1 1.8 %kept_edges.1 = (bf16[16,4096]{1,0:T(8,128)(2,1)}, bf16[16,4096]{1,0:T(8,128)(2,1)}, bf16[16,4096]{1,0:T(8,128)(2,1)}, bf16[16,4096]{1,0:T(8,128)(2,1)}) custom-call(s32[1]{0:T(128)} %bitcast.9.place_ref.refs_0_, s32[8]{0:T(128)S(1)} %copy-done.6, s32[8]{0:T(128)S(1)} %copy-done.5, s32[128]{0:T(128)S(1)} %copy-done.7, bf16[128,4096]{1,0:T(8,128)(2,1)S(1)} %copy-done, ...), custom_call_target="tpu_custom_call" | custom-call | tf_op jit(solution)/shard_map/kept_edges/pallas_call | solution.py:169
  7.9 2.3 %collective-permute-start.2 = (bf16[16,4096]{1,0:T(8,128)(2,1)}, bf16[16,4096]{1,0:T(8,128)(2,1)}, u32[]{:S(2)}, u32[]{:S(2)}) collective-permute-start(bf16[16,4096]{1,0:T(8,128)(2,1)} %get-tuple-element.28), channel_id=1, source_target_pairs={{0,16},{2,18},{4,20},{6,22},{8,24},{10,26},{12,28},{14,30},{16,0},... | collective-permute-start | bytes 393224 | tf_op jit(solution)/shard_map/ppermute | solution.py:626
  10.2 0.0 collective-permute-start.3
  10.2 0.1 copy.29.range_ref
  10.3 0.0 collective-permute-done.refs_1_.refs_4_
  10.3 0.0 copy-done.11
  10.4 8.4 %kept_states.1 = bf16[16,16,4096]{2,1,0:T(8,128)(2,1)} custom-call(s32[1]{0:T(128)} %bitcast.9.place_ref.refs_0_, s32[8]{0:T(128)S(1)} %copy-done.6, s32[128]{0:T(128)S(1)} %copy-done.7, f32[288,128]{1,0:T(8,128)} %get-tuple-element.20.refs_0_._.refs_3_, f32[288,128]{1,0:T(8,128)S(1)} %collective-permute-done.refs_1_.refs_4_, f32[1,256]{1,0:T(1,128)S(1)} %bitcast.15, ...), custom_call_target="tpu_custom_call" | custom-call | flops 1006632960000 | bytes 6291456 | tf_op jit(solution)/shard_map/kept_states/pallas_call | solution.py:345
  18.7 0.0 copy-start.2
  18.7 0.0 copy-start.10
  18.7 0.0 copy-start.13
  18.8 7.5 %all-to-all-start = ((bf16[16,16,4096]{2,1,0:T(8,128)(2,1)}), bf16[16,16,4096]{2,1,0:T(8,128)(2,1)}, u32[]{:S(2)}, u32[]{:S(2)}) async-start(bf16[16,16,4096]{2,1,0:T(8,128)(2,1)} %kept_states.1), calls=%async_computation | async-start | bytes 4194304 | tf_op jit(solution)/shard_map/all_to_all | solution.py:638
  26.3 0.0 copy-start.14
  26.3 0.0 copy-start.17
  26.3 0.0 copy-start.3
  26.3 0.0 copy-start.16
  26.3 18.9 %scan.1.refs_4_ = bf16[128,4096]{1,0:T(8,128)(2,1)} custom-call(f32[288,128]{1,0:T(8,128)S(1)} %copy-done.2, f32[288,128]{1,0:T(8,128)S(1)} %collective-permute-done.refs_1_.refs_4_, f32[1,256]{1,0:T(1,128)S(1)} %bitcast.16, f32[1,16]{1,0:T(1,128)S(1)} %bitcast.18, f32[1,16]{1,0:T(1,128)S(1)} %bitcast.19, bf16[256,4096]{1,0:T(8,128)(2,1)} %refs_7_.3, ...), custom_call_target="tpu_custom_call" | custom-call | flops 2013265920000 | bytes 5242880 | tf_op jit(solution)/shard_map/scan/pallas_call | solution.py:461
  45.3 0.1 eq.26
  45.4 0.3 collective-permute-start.1
  45.7 0.1 reduce_or.9
  45.8 0.1 convert_reduce_fusion
  45.9 0.0 copy-done.17
  46.0 0.1 select_reduce_fusion
  46.1 0.0 collective-permute-done.2.refs_2_
  46.1 0.0 collective-permute-done.3.refs_3_
  46.1 18.5 %collective-permute-done.1.refs_1_ = bf16[16,4096]{1,0:T(8,128)(2,1)S(1)} collective-permute-done((bf16[16,4096]{1,0:T(8,128)(2,1)S(1)}, bf16[16,4096]{1,0:T(8,128)(2,1)S(1)}, u32[]{:S(2)}, u32[]{:S(2)}) %collective-permute-start.1) | collective-permute-done | bytes 131104 | tf_op jit(solution)/shard_map/ppermute | solution.py:626
  64.5 0.0 copy-done.3
  64.5 2.9 %regroup.1 = (bf16[16,4096]{1,0:T(8,128)(2,1)}, bf16[16,4096]{1,0:T(8,128)(2,1)}, bf16[16,4096]{1,0:T(8,128)(2,1)}, bf16[16,4096]{1,0:T(8,128)(2,1)}) custom-call(bf16[16,4096]{1,0:T(8,128)(2,1)S(1)} %copy-done.3, bf16[16,4096]{1,0:T(8,128)(2,1)S(1)} %collective-permute-done.1.refs_1_, bf16[16,4096]{1,0:T(8,128)(2,1)} %collective-permute-done.2.refs_2_, ...), custom_call_target="tpu_custom_call" | custom-call | tf_op jit(solution)/shard_map/regroup/pallas_call | solution.py:194
  67.4 0.9 %collective-permute-start.4 = (bf16[16,4096]{1,0:T(8,128)(2,1)}, bf16[16,4096]{1,0:T(8,128)(2,1)S(1)}, u32[]{:S(2)}, u32[]{:S(2)}) collective-permute-start(bf16[16,4096]{1,0:T(8,128)(2,1)} %get-tuple-element.31), channel_id=1, source_target_pairs={{0,2},{2,0},{4,6},{6,4},{8,10},{10,8},{12,14},{14,12},{16,18},{18,... | collective-permute-start | bytes 393224 | tf_op jit(solution)/shard_map/ppermute | solution.py:626
  68.4 0.0 collective-permute-start.5
  68.4 1.7 %collective-permute-start.6 = (bf16[16,4096]{1,0:T(8,128)(2,1)}, bf16[16,4096]{1,0:T(8,128)(2,1)S(1)}, u32[]{:S(2)}, u32[]{:S(2)}) collective-permute-start(bf16[16,4096]{1,0:T(8,128)(2,1)} %get-tuple-element.33), channel_id=1, source_target_pairs={{0,6},{2,4},{4,2},{6,0},{8,14},{10,12},{12,10},{14,8},{16,22},{18,... | collective-permute-start | bytes 393224 | tf_op jit(solution)/shard_map/ppermute | solution.py:626
  70.1 0.0 copy-done.16
  70.1 0.1 convert_reduce_fusion.1.bound_ref
  70.2 0.0 collective-permute-done.4.refs_1_
  70.2 6.1 %collective-permute-done.5.refs_2_ = bf16[16,4096]{1,0:T(8,128)(2,1)S(1)} collective-permute-done((bf16[16,4096]{1,0:T(8,128)(2,1)}, bf16[16,4096]{1,0:T(8,128)(2,1)S(1)}, u32[]{:S(2)}, u32[]{:S(2)}) %collective-permute-start.5) | collective-permute-done | bytes 131104 | tf_op jit(solution)/shard_map/ppermute | solution.py:626
  76.3 2.8 %collective-permute-done.6.refs_3_ = bf16[16,4096]{1,0:T(8,128)(2,1)S(1)} collective-permute-done((bf16[16,4096]{1,0:T(8,128)(2,1)}, bf16[16,4096]{1,0:T(8,128)(2,1)S(1)}, u32[]{:S(2)}, u32[]{:S(2)}) %collective-permute-start.6) | collective-permute-done | bytes 131104 | tf_op jit(solution)/shard_map/ppermute | solution.py:626
  79.2 0.9 %copy-done.4 = bf16[16,4096]{1,0:T(8,128)(2,1)S(1)} copy-done((bf16[16,4096]{1,0:T(8,128)(2,1)S(1)}, bf16[16,4096]{1,0:T(8,128)(2,1)}, u32[]{:S(2)}) %copy-start.4) | copy-done | bytes 131096
  80.1 2.0 %settle_edges.1 = (bf16[12,3,4096]{2,1,0:T(4,128)(2,1)}, f32[4,2]{1,0:T(4,128)S(1)}) custom-call(s32[1]{0:T(128)} %bitcast.9.place_ref.refs_0_, s32[12]{0:T(128)S(1)} %broadcast_subtract_fusion.source_ref, s32[4,2]{1,0:T(4,128)S(1)} %copy.29.range_ref, bf16[16,4096]{1,0:T(8,128)(2,1)S(1)} %copy-done.4, bf16[16,4096]{1,0:T(8,128)(2,1)S(1)} %collective-permute-done.4.refs_1_, ...), custom_call_target="tpu_custom_call" | custom-call | tf_op jit(solution)/shard_map/settle_edges/pallas_call | solution.py:541
  82.0 0.6 copy.30
  82.7 0.0 all-to-all-done.got_hbm
  82.7 2.9 %settle_states.1 = bf16[12,16,4096]{2,1,0:T(8,128)(2,1)} custom-call(s32[12]{0:T(128)S(1)} %broadcast_subtract_fusion.source_ref, s32[5]{0:T(128)S(1)} %convert_reduce_fusion.1.bound_ref, bf16[16,16,4096]{2,1,0:T(8,128)(2,1)} %all-to-all-done.got_hbm), custom_call_target="tpu_custom_call" | custom-call | tf_op jit(solution)/shard_map/settle_states/pallas_call | solution.py:591
  (22 shorter events, 0.0 us)
Async XLA Ops:
  0.6 5.5 %copy-start = (bf16[128,4096]{1,0:T(8,128)(2,1)S(1)}, bf16[128,4096]{1,0:T(8,128)(2,1)}, u32[]{:S(2)}) copy-start(bf16[128,4096]{1,0:T(8,128)(2,1)} %x_ref.1) | copy-start | bytes 3145732
  0.6 5.5 %copy-start.1 = (bf16[8,3,4096]{2,0,1:T(8,128)(2,1)S(1)}, bf16[8,3,4096]{2,0,1:T(8,128)(2,1)}, u32[]{:S(2)}) copy-start(bf16[8,3,4096]{2,0,1:T(8,128)(2,1)} %param.23) | copy-start | bytes 589828
  0.7 5.5 %copy-start.7 = (s32[128]{0:T(128)S(1)}, s32[128]{0:T(128)}, u32[]{:S(2)}) copy-start(s32[128]{0:T(128)} %refs_2_.1) | copy-start | bytes 1540
  0.7 5.5 %copy-start.6 = (s32[8]{0:T(128)S(1)}, s32[8]{0:T(128)}, u32[]{:S(2)}) copy-start(s32[8]{0:T(128)} %refs_1_.1) | copy-start | bytes 100
  0.7 5.5 %copy-start.5 = (s32[8]{0:T(128)S(1)}, s32[8]{0:T(128)}, u32[]{:S(2)}) copy-start(s32[8]{0:T(128)} %length_ref.1) | copy-start | bytes 100
  0.7 9.6 %copy-start.15 = (s32[4,2]{0,1:T(2,128)S(1)}, s32[4,2]{0,1:T(2,128)}, u32[]{:S(2)}) copy-start(s32[4,2]{0,1:T(2,128)} %param.37) | copy-start | bytes 100
  0.7 9.6 %copy-start.8 = (bf16[256,4096]{1,0:T(8,128)(2,1)S(1)}, bf16[256,4096]{1,0:T(8,128)(2,1)}, u32[]{:S(2)}) copy-start(bf16[256,4096]{1,0:T(8,128)(2,1)} %refs_7_.3) | copy-start | bytes 6291460
  0.7 9.6 %copy-start.9 = (f32[4096]{0:T(1024)S(1)}, f32[4096]{0:T(1024)}, u32[]{:S(2)}) copy-start(f32[4096]{0:T(1024)} %param.31) | copy-start | bytes 49156
  0.7 9.6 %copy-start.11 = (f32[256]{0:T(256)S(1)}, f32[256]{0:T(256)}, u32[]{:S(2)}) copy-start(f32[256]{0:T(256)} %param.27) | copy-start | bytes 3076
  0.7 9.6 %copy-start.12 = (f32[16]{0:T(128)S(1)}, f32[16]{0:T(128)}, u32[]{:S(2)}) copy-start(f32[16]{0:T(128)} %param.28) | copy-start | bytes 196
  4.8 5.5 %collective-permute-start = (f32[288,128]{1,0:T(8,128)}, f32[288,128]{1,0:T(8,128)S(1)}, u32[]{:S(2)}, u32[]{:S(2)}) collective-permute-start(f32[288,128]{1,0:T(8,128)} %get-tuple-element.20.refs_0_._.refs_3_), channel_id=1, source_target_pairs={{0,1},{1,0},{2,3},{3,2},{4,5},{5,4},{6,7},{7,6},{8,9},{9,8},{10,11... | collective-permute-start | bytes 442376 | tf_op jit(solution)/shard_map/ppermute | solution.py:621
  7.9 38.1 %collective-permute-start.2 = (bf16[16,4096]{1,0:T(8,128)(2,1)}, bf16[16,4096]{1,0:T(8,128)(2,1)}, u32[]{:S(2)}, u32[]{:S(2)}) collective-permute-start(bf16[16,4096]{1,0:T(8,128)(2,1)} %get-tuple-element.28), channel_id=1, source_target_pairs={{0,16},{2,18},{4,20},{6,22},{8,24},{10,26},{12,28},{14,30},{16,0},... | collective-permute-start | bytes 393224 | tf_op jit(solution)/shard_map/ppermute | solution.py:626
  10.2 35.8 %collective-permute-start.3 = (bf16[16,4096]{1,0:T(8,128)(2,1)}, bf16[16,4096]{1,0:T(8,128)(2,1)}, u32[]{:S(2)}, u32[]{:S(2)}) collective-permute-start(bf16[16,4096]{1,0:T(8,128)(2,1)} %get-tuple-element.29), channel_id=1, source_target_pairs={{0,24},{2,26},{4,28},{6,30},{8,16},{10,18},{12,20},{14,22},{16,8},... | collective-permute-start | bytes 393224 | tf_op jit(solution)/shard_map/ppermute | solution.py:626
  18.7 7.5 %copy-start.2 = (f32[288,128]{1,0:T(8,128)S(1)}, f32[288,128]{1,0:T(8,128)}, u32[]{:S(2)}) copy-start(f32[288,128]{1,0:T(8,128)} %get-tuple-element.20.refs_0_._.refs_3_) | copy-start | bytes 442372
  18.7 7.5 %copy-start.10 = (f32[4096]{0:T(1024)S(1)}, f32[4096]{0:T(1024)}, u32[]{:S(2)}) copy-start(f32[4096]{0:T(1024)} %param.33) | copy-start | bytes 49156
  18.7 7.5 %copy-start.13 = (f32[16]{0:T(128)S(1)}, f32[16]{0:T(128)}, u32[]{:S(2)}) copy-start(f32[16]{0:T(128)} %param.29) | copy-start | bytes 196
  18.8 63.9 %all-to-all-start = ((bf16[16,16,4096]{2,1,0:T(8,128)(2,1)}), bf16[16,16,4096]{2,1,0:T(8,128)(2,1)}, u32[]{:S(2)}, u32[]{:S(2)}) async-start(bf16[16,16,4096]{2,1,0:T(8,128)(2,1)} %kept_states.1), calls=%async_computation | async-start | bytes 4194304 | tf_op jit(solution)/shard_map/all_to_all | solution.py:638
  26.3 19.1 %copy-start.18 = (bf16[16,4096]{1,0:T(8,128)(2,1)S(1)}, bf16[16,4096]{1,0:T(8,128)(2,1)}, u32[]{:S(2)}) copy-start(bf16[16,4096]{1,0:T(8,128)(2,1)} %get-tuple-element.27) | copy-start | bytes 393220
  26.3 19.5 %copy-start.14 = (pred[16,16]{1,0:T(8,128)(4,1)S(1)}, pred[16,16]{1,0:T(8,128)(4,1)}, u32[]{:S(2)}) copy-start(pred[16,16]{1,0:T(8,128)(4,1)} %constant.18.clone) | copy-start | bytes 772
  26.3 19.7 %copy-start.17 = (s32[16]{0:T(128)S(1)}, s32[16]{0:T(128)}, u32[]{:S(2)}) copy-start(s32[16]{0:T(128)} %constant.25) | copy-start | bytes 196
  26.3 38.2 %copy-start.3 = (bf16[16,4096]{1,0:T(8,128)(2,1)S(1)}, bf16[16,4096]{1,0:T(8,128)(2,1)}, u32[]{:S(2)}) copy-start(bf16[16,4096]{1,0:T(8,128)(2,1)} %get-tuple-element.26.refs_0_) | copy-start | bytes 393220
  26.3 43.8 %copy-start.16 = (pred[5,16]{1,0:T(8,128)(4,1)S(1)}, pred[5,16]{1,0:T(8,128)(4,1)}, u32[]{:S(2)}) copy-start(pred[5,16]{1,0:T(8,128)(4,1)} %constant.19.clone) | copy-start | bytes 244
  45.4 19.2 %collective-permute-start.1 = (bf16[16,4096]{1,0:T(8,128)(2,1)S(1)}, bf16[16,4096]{1,0:T(8,128)(2,1)S(1)}, u32[]{:S(2)}, u32[]{:S(2)}) collective-permute-start(bf16[16,4096]{1,0:T(8,128)(2,1)S(1)} %copy-done.18), channel_id=1, source_target_pairs={{0,8},{2,10},{4,12},{6,14},{8,0},{10,2},{12,4},{14,6},{16,24},{18,... | collective-permute-start | bytes 393224 | tf_op jit(solution)/shard_map/ppermute | solution.py:626
  67.4 2.8 %collective-permute-start.4 = (bf16[16,4096]{1,0:T(8,128)(2,1)}, bf16[16,4096]{1,0:T(8,128)(2,1)S(1)}, u32[]{:S(2)}, u32[]{:S(2)}) collective-permute-start(bf16[16,4096]{1,0:T(8,128)(2,1)} %get-tuple-element.31), channel_id=1, source_target_pairs={{0,2},{2,0},{4,6},{6,4},{8,10},{10,8},{12,14},{14,12},{16,18},{18,... | collective-permute-start | bytes 393224 | tf_op jit(solution)/shard_map/ppermute | solution.py:626
  68.4 8.0 %collective-permute-start.5 = (bf16[16,4096]{1,0:T(8,128)(2,1)}, bf16[16,4096]{1,0:T(8,128)(2,1)S(1)}, u32[]{:S(2)}, u32[]{:S(2)}) collective-permute-start(bf16[16,4096]{1,0:T(8,128)(2,1)} %get-tuple-element.32), channel_id=1, source_target_pairs={{0,4},{2,6},{4,0},{6,2},{8,12},{10,14},{12,8},{14,10},{16,20},{18,... | collective-permute-start | bytes 393224 | tf_op jit(solution)/shard_map/ppermute | solution.py:626
  68.4 10.8 %collective-permute-start.6 = (bf16[16,4096]{1,0:T(8,128)(2,1)}, bf16[16,4096]{1,0:T(8,128)(2,1)S(1)}, u32[]{:S(2)}, u32[]{:S(2)}) collective-permute-start(bf16[16,4096]{1,0:T(8,128)(2,1)} %get-tuple-element.33), channel_id=1, source_target_pairs={{0,6},{2,4},{4,2},{6,0},{8,14},{10,12},{12,10},{14,8},{16,22},{18,... | collective-permute-start | bytes 393224 | tf_op jit(solution)/shard_map/ppermute | solution.py:626
  79.1 0.9 %copy-start.4 = (bf16[16,4096]{1,0:T(8,128)(2,1)S(1)}, bf16[16,4096]{1,0:T(8,128)(2,1)}, u32[]{:S(2)}) copy-start(bf16[16,4096]{1,0:T(8,128)(2,1)} %get-tuple-element.30.refs_0_) | copy-start | bytes 393220

commit v10 on v9

--- a/solution.py
+++ b/solution.py
@@ -177,6 +177,22 @@
     )(*scalars, x_in, conv_edge, in_hbm(after))
 
 
+def hold_kernel(rows_ref, _, out_ref):
+    out_ref[...] = rows_ref[...]
+
+
+def hold(rows, after):
+    vmem = pl.BlockSpec(memory_space=pltpu.VMEM)
+    return pl.pallas_call(
+        hold_kernel,
+        in_specs=[vmem, pl.BlockSpec(memory_space=pl.ANY)],
+        out_specs=vmem,
+        out_shape=pltpu.HBM(rows.shape, rows.dtype),
+        compiler_params=pltpu.CompilerParams(vmem_limit_bytes=VMEM_BYTES),
+        name="hold",
+    )(rows, in_hbm(after))
+
+
 def regroup_kernel(*refs):
     groups = len(refs) - 1 - PLANE
     rows = jnp.concatenate([ref[...].astype(jnp.float32) for ref in refs[:groups]], axis=0)
@@ -635,12 +651,13 @@
     slots = kept_states(
         (place, accepted, owner), partials, gains[:2], dt_proj_weight, bias, a_log, conv, state, owners
     )
+    near = [hold(rows, slots) if d else rows for d, rows in enumerate(groups[:half])]
     got = lax.all_to_all(slots, "req", split_axis=0, concat_axis=0, tiled=True)
+    groups = [swap(rows, d * PLANE) for d, rows in enumerate(near)] + far
     mixed = scan(
         partials, gains, dt_proj_weight, bias, a_log, skip.reshape(1, -1), conv, state, z_gate
     )
-    mixed, owner, *near = lax.optimization_barrier((mixed, owner, *groups[:half]))
-    groups = [swap(rows, d * PLANE) for d, rows in enumerate(near)] + far
+    mixed, owner = lax.optimization_barrier((mixed, owner))
     hits = jnp.any(owner.reshape(owners, requests) == place, axis=1)
     ids = np.arange(owners, dtype=np.int32)
     ranks = jnp.sum((hits[None, :] & (ids[None, :] < ids[:, None])).astype(jnp.int32), axis=1)

time: 87.1 us -> 86 us (0.987); the launches traced: 85.6 us -> 85.4 us
  no operation moved by 1% of the time
where the time goes in v10:
time: 86 us; the launch traced here: 85.4 us
  Pallas kernels  41.4 us (48%)
  waiting for transfers between devices  26.9 us (31%)
  starting transfers between devices  14 us (16%)
  local copies, waits for them, and re-layouts  1.82 us (2%)
  between operations  0.87 us (1%)
    ppermute x6, waiting for transfers between devices, swap(): lax.ppermute(rows, 'req', [(i, i ^ delta) for i in range(owners)])  26.9 us
    pallas_call x1, Pallas kernels, scan(): pl.pallas_call(functools.partial(scan_kernel, len(partials)), grid=(chann...  18.9 us
    pallas_call x1, Pallas kernels, kept_states(): pl.pallas_call(functools.partial(kept_kernel, len(partials)), in_specs=[p...  7.87 us
    all_to_all x1, starting transfers between devices, per_device(): got = lax.all_to_all(slots, 'req', split_axis=0, concat_axis=0, tiled=True)  7.47 us
    ppermute x6, starting transfers between devices, swap(): lax.ppermute(rows, 'req', [(i, i ^ delta) for i in range(owners)])  5.22 us
    pallas_call x1, Pallas kernels, conv_project(): pl.pallas_call(conv_kernel, in_specs=[pl.BlockSpec(memory_space=pl.ANY)]...  4.09 us
    pallas_call x1, Pallas kernels, settle_states(): pl.pallas_call(settle_kernel, in_specs=[smem, smem, anywhere], out_specs=...  3.14 us
    pallas_call x1, Pallas kernels, regroup(): pl.pallas_call(regroup_kernel, grid=(channels // block,), in_specs=[pl.Bl...  2.92 us
  transfers between devices with their start and end apart: 8, of which 3 were waited for; matrix products, arithmetic and copies ran while one was open for 2% of the time, Pallas kernels for 40%

profile of v10, /device:TPU:11, one launch (start us, length us, event | category | flops | bytes accessed | tf_op | source)
XLA Modules:
  0.0 85.4 jit_solution(14675203325307060002)
XLA Ops:
  0.6 0.0 copy-start.1
  0.6 0.0 copy-start
  0.7 0.0 copy-start.7
  0.7 0.0 copy-start.8
  0.7 0.0 copy-start.6
  0.7 0.0 copy-start.16
  0.7 0.0 copy-start.9
  0.7 0.0 copy-start.10
  0.7 0.0 copy-start.12
  0.7 0.0 copy-start.13
  0.7 4.1 %conv_project.1 = (bf16[128,4096]{1,0:T(8,128)(2,1)}, f32[288,128]{1,0:T(8,128)}) custom-call(bf16[128,4096]{1,0:T(8,128)(2,1)} %x_ref.1, bf16[3,8,4096]{2,1,0:T(8,128)(2,1)} %bitcast.10, f32[4,4096]{1,0:T(4,128)} %weight_hbm.1, f32[1,4096]{1,0:T(1,128)} %bitcast.21, bf16[288,4096]{1,0:T(8,128)(2,1)} %bitcast.20), custom_call_target="tpu_custom_call" | custom-call | tf_op jit(solution)/shard_map/conv_project/pallas_call | solution.py:112
  4.8 1.3 %collective-permute-start = (f32[288,128]{1,0:T(8,128)}, f32[288,128]{1,0:T(8,128)S(1)}, u32[]{:S(2)}, u32[]{:S(2)}) collective-permute-start(f32[288,128]{1,0:T(8,128)} %get-tuple-element.18.refs_0_.refs_3_._), channel_id=1, source_target_pairs={{0,1},{1,0},{2,3},{3,2},{4,5},{5,4},{6,7},{7,6},{8,9},{9,8},{10,11... | collective-permute-start | bytes 442376 | tf_op jit(solution)/shard_map/ppermute | solution.py:637
  6.1 1.8 %kept_edges.1 = (bf16[16,4096]{1,0:T(8,128)(2,1)}, bf16[16,4096]{1,0:T(8,128)(2,1)}, bf16[16,4096]{1,0:T(8,128)(2,1)}, bf16[16,4096]{1,0:T(8,128)(2,1)}) custom-call(s32[1]{0:T(128)} %bitcast.9.refs_0_.place_ref, s32[8]{0:T(128)S(1)} %copy-done.7, s32[8]{0:T(128)S(1)} %copy-done.6, s32[128]{0:T(128)S(1)} %copy-done.8, bf16[128,4096]{1,0:T(8,128)(2,1)S(1)} %copy-done, ...), custom_call_target="tpu_custom_call" | custom-call | tf_op jit(solution)/shard_map/kept_edges/pallas_call | solution.py:169
  7.9 2.3 %collective-permute-start.2 = (bf16[16,4096]{1,0:T(8,128)(2,1)}, bf16[16,4096]{1,0:T(8,128)(2,1)}, u32[]{:S(2)}, u32[]{:S(2)}) collective-permute-start(bf16[16,4096]{1,0:T(8,128)(2,1)} %get-tuple-element.24), channel_id=1, source_target_pairs={{0,16},{2,18},{4,20},{6,22},{8,24},{10,26},{12,28},{14,30},{16,0},... | collective-permute-start | bytes 393224 | tf_op jit(solution)/shard_map/ppermute | solution.py:642
  10.2 0.0 collective-permute-start.3
  10.2 0.1 copy.29.range_ref
  10.3 0.0 collective-permute-done.refs_1_.refs_4_
  10.3 7.9 %kept_states.1._ = bf16[16,16,4096]{2,1,0:T(8,128)(2,1)} custom-call(s32[1]{0:T(128)} %bitcast.9.refs_0_.place_ref, s32[8]{0:T(128)S(1)} %copy-done.7, s32[128]{0:T(128)S(1)} %copy-done.8, f32[288,128]{1,0:T(8,128)} %get-tuple-element.18.refs_0_.refs_3_._, f32[288,128]{1,0:T(8,128)S(1)} %collective-permute-done.refs_1_.refs_4_, f32[1,256]{1,0:T(1,128)S(1)} %bitcast.15, ...), custom_call_target="tpu_custom_call" | custom-call | flops 1006632960000 | bytes 6291456 | tf_op jit(solution)/shard_map/kept_states/pallas_call | solution.py:361
  18.2 0.0 copy-start.4
  18.2 7.5 %all-to-all-start = ((bf16[16,16,4096]{2,1,0:T(8,128)(2,1)}), bf16[16,16,4096]{2,1,0:T(8,128)(2,1)}, u32[]{:S(2)}, u32[]{:S(2)}) async-start(bf16[16,16,4096]{2,1,0:T(8,128)(2,1)} %kept_states.1._), calls=%async_computation | async-start | bytes 4194304 | tf_op jit(solution)/shard_map/all_to_all | solution.py:655
  25.7 0.0 copy-start.11
  25.7 0.0 copy-start.14
  25.7 0.7 hold.1
  26.4 0.3 collective-permute-start.1
  26.7 0.0 copy-start.18
  26.7 0.0 copy-start.17
  26.7 18.9 %scan.1.refs_4_ = bf16[128,4096]{1,0:T(8,128)(2,1)} custom-call(f32[288,128]{1,0:T(8,128)S(1)} %copy-done.2, f32[288,128]{1,0:T(8,128)S(1)} %collective-permute-done.refs_1_.refs_4_, f32[1,256]{1,0:T(1,128)S(1)} %bitcast.16, f32[1,16]{1,0:T(1,128)S(1)} %bitcast.18, f32[1,16]{1,0:T(1,128)S(1)} %bitcast.19, bf16[256,4096]{1,0:T(8,128)(2,1)} %refs_7_.3, ...), custom_call_target="tpu_custom_call" | custom-call | flops 2013265920000 | bytes 5242880 | tf_op jit(solution)/shard_map/scan/pallas_call | solution.py:477
  45.7 0.1 eq.26
  45.8 0.1 reduce_or.9
  45.9 0.1 convert_reduce_fusion
  46.0 0.1 select_reduce_fusion
  46.2 0.0 collective-permute-done.2.refs_2_
  46.2 0.0 collective-permute-done.3.refs_3_
  46.2 17.9 %collective-permute-done.1.refs_1_ = bf16[16,4096]{1,0:T(8,128)(2,1)} collective-permute-done((bf16[16,4096]{1,0:T(8,128)(2,1)}, bf16[16,4096]{1,0:T(8,128)(2,1)}, u32[]{:S(2)}, u32[]{:S(2)}) %collective-permute-start.1) | collective-permute-done | bytes 131104 | tf_op jit(solution)/shard_map/ppermute | solution.py:642
  64.1 2.9 %regroup.1 = (bf16[16,4096]{1,0:T(8,128)(2,1)}, bf16[16,4096]{1,0:T(8,128)(2,1)}, bf16[16,4096]{1,0:T(8,128)(2,1)}, bf16[16,4096]{1,0:T(8,128)(2,1)}) custom-call(bf16[16,4096]{1,0:T(8,128)(2,1)S(1)} %copy-done.3, bf16[16,4096]{1,0:T(8,128)(2,1)} %collective-permute-done.1.refs_1_, bf16[16,4096]{1,0:T(8,128)(2,1)} %collective-permute-done.2.refs_2_, ...), custom_call_target="tpu_custom_call" | custom-call | tf_op jit(solution)/shard_map/regroup/pallas_call | solution.py:210
  67.0 0.9 %collective-permute-start.4 = (bf16[16,4096]{1,0:T(8,128)(2,1)}, bf16[16,4096]{1,0:T(8,128)(2,1)S(1)}, u32[]{:S(2)}, u32[]{:S(2)}) collective-permute-start(bf16[16,4096]{1,0:T(8,128)(2,1)} %get-tuple-element.27), channel_id=1, source_target_pairs={{0,2},{2,0},{4,6},{6,4},{8,10},{10,8},{12,14},{14,12},{16,18},{18,... | collective-permute-start | bytes 393224 | tf_op jit(solution)/shard_map/ppermute | solution.py:642
  68.0 0.0 collective-permute-start.5
  68.0 1.7 %collective-permute-start.6 = (bf16[16,4096]{1,0:T(8,128)(2,1)}, bf16[16,4096]{1,0:T(8,128)(2,1)S(1)}, u32[]{:S(2)}, u32[]{:S(2)}) collective-permute-start(bf16[16,4096]{1,0:T(8,128)(2,1)} %get-tuple-element.29), channel_id=1, source_target_pairs={{0,6},{2,4},{4,2},{6,0},{8,14},{10,12},{12,10},{14,8},{16,22},{18,... | collective-permute-start | bytes 393224 | tf_op jit(solution)/shard_map/ppermute | solution.py:642
  69.7 0.0 copy-done.17
  69.7 0.1 convert_reduce_fusion.1.bound_ref
  69.8 0.0 collective-permute-done.4.refs_1_
  69.8 6.1 %collective-permute-done.5.refs_2_ = bf16[16,4096]{1,0:T(8,128)(2,1)S(1)} collective-permute-done((bf16[16,4096]{1,0:T(8,128)(2,1)}, bf16[16,4096]{1,0:T(8,128)(2,1)S(1)}, u32[]{:S(2)}, u32[]{:S(2)}) %collective-permute-start.5) | collective-permute-done | bytes 131104 | tf_op jit(solution)/shard_map/ppermute | solution.py:642
  75.9 2.8 %collective-permute-done.6.refs_3_ = bf16[16,4096]{1,0:T(8,128)(2,1)S(1)} collective-permute-done((bf16[16,4096]{1,0:T(8,128)(2,1)}, bf16[16,4096]{1,0:T(8,128)(2,1)S(1)}, u32[]{:S(2)}, u32[]{:S(2)}) %collective-permute-start.6) | collective-permute-done | bytes 131104 | tf_op jit(solution)/shard_map/ppermute | solution.py:642
  78.7 0.9 %copy-done.5 = bf16[16,4096]{1,0:T(8,128)(2,1)S(1)} copy-done((bf16[16,4096]{1,0:T(8,128)(2,1)S(1)}, bf16[16,4096]{1,0:T(8,128)(2,1)}, u32[]{:S(2)}) %copy-start.5) | copy-done | bytes 131096
  79.6 2.0 %settle_edges.1 = (bf16[12,3,4096]{2,1,0:T(4,128)(2,1)}, f32[4,2]{1,0:T(4,128)S(1)}) custom-call(s32[1]{0:T(128)} %bitcast.9.refs_0_.place_ref, s32[12]{0:T(128)S(1)} %broadcast_subtract_fusion.source_ref, s32[4,2]{1,0:T(4,128)S(1)} %copy.29.range_ref, bf16[16,4096]{1,0:T(8,128)(2,1)S(1)} %copy-done.5, bf16[16,4096]{1,0:T(8,128)(2,1)S(1)} %collective-permute-done.4.refs_1_, ...), custom_call_target="tpu_custom_call" | custom-call | tf_op jit(solution)/shard_map/settle_edges/pallas_call | solution.py:557
  81.6 0.6 copy.30
  82.3 0.0 all-to-all-done.got_hbm
  82.3 3.1 %settle_states.1 = bf16[12,16,4096]{2,1,0:T(8,128)(2,1)} custom-call(s32[12]{0:T(128)S(1)} %broadcast_subtract_fusion.source_ref, s32[5]{0:T(128)S(1)} %convert_reduce_fusion.1.bound_ref, bf16[16,16,4096]{2,1,0:T(8,128)(2,1)} %all-to-all-done.got_hbm), custom_call_target="tpu_custom_call" | custom-call | tf_op jit(solution)/shard_map/settle_states/pallas_call | solution.py:607
  (23 shorter events, 0.1 us)
Async XLA Ops:
  0.6 5.5 %copy-start.1 = (bf16[8,3,4096]{2,0,1:T(8,128)(2,1)S(1)}, bf16[8,3,4096]{2,0,1:T(8,128)(2,1)}, u32[]{:S(2)}) copy-start(bf16[8,3,4096]{2,0,1:T(8,128)(2,1)} %param.23) | copy-start | bytes 589828
  0.6 5.5 %copy-start = (bf16[128,4096]{1,0:T(8,128)(2,1)S(1)}, bf16[128,4096]{1,0:T(8,128)(2,1)}, u32[]{:S(2)}) copy-start(bf16[128,4096]{1,0:T(8,128)(2,1)} %x_ref.1) | copy-start | bytes 3145732
  0.7 5.5 %copy-start.7 = (s32[8]{0:T(128)S(1)}, s32[8]{0:T(128)}, u32[]{:S(2)}) copy-start(s32[8]{0:T(128)} %accepted_ref.1) | copy-start | bytes 100
  0.7 5.5 %copy-start.8 = (s32[128]{0:T(128)S(1)}, s32[128]{0:T(128)}, u32[]{:S(2)}) copy-start(s32[128]{0:T(128)} %owner_ref.1) | copy-start | bytes 1540
  0.7 5.5 %copy-start.6 = (s32[8]{0:T(128)S(1)}, s32[8]{0:T(128)}, u32[]{:S(2)}) copy-start(s32[8]{0:T(128)} %length_ref.1) | copy-start | bytes 100
  0.7 9.5 %copy-start.16 = (s32[4,2]{0,1:T(2,128)S(1)}, s32[4,2]{0,1:T(2,128)}, u32[]{:S(2)}) copy-start(s32[4,2]{0,1:T(2,128)} %param.37) | copy-start | bytes 100
  0.7 9.6 %copy-start.9 = (bf16[256,4096]{1,0:T(8,128)(2,1)S(1)}, bf16[256,4096]{1,0:T(8,128)(2,1)}, u32[]{:S(2)}) copy-start(bf16[256,4096]{1,0:T(8,128)(2,1)} %refs_7_.3) | copy-start | bytes 6291460
  0.7 9.6 %copy-start.10 = (f32[4096]{0:T(1024)S(1)}, f32[4096]{0:T(1024)}, u32[]{:S(2)}) copy-start(f32[4096]{0:T(1024)} %param.31) | copy-start | bytes 49156
  0.7 9.6 %copy-start.12 = (f32[256]{0:T(256)S(1)}, f32[256]{0:T(256)}, u32[]{:S(2)}) copy-start(f32[256]{0:T(256)} %param.27) | copy-start | bytes 3076
  0.7 9.6 %copy-start.13 = (f32[16]{0:T(128)S(1)}, f32[16]{0:T(128)}, u32[]{:S(2)}) copy-start(f32[16]{0:T(128)} %param.28) | copy-start | bytes 196
  4.8 5.5 %collective-permute-start = (f32[288,128]{1,0:T(8,128)}, f32[288,128]{1,0:T(8,128)S(1)}, u32[]{:S(2)}, u32[]{:S(2)}) collective-permute-start(f32[288,128]{1,0:T(8,128)} %get-tuple-element.18.refs_0_.refs_3_._), channel_id=1, source_target_pairs={{0,1},{1,0},{2,3},{3,2},{4,5},{5,4},{6,7},{7,6},{8,9},{9,8},{10,11... | collective-permute-start | bytes 442376 | tf_op jit(solution)/shard_map/ppermute | solution.py:637
  7.9 38.3 %collective-permute-start.2 = (bf16[16,4096]{1,0:T(8,128)(2,1)}, bf16[16,4096]{1,0:T(8,128)(2,1)}, u32[]{:S(2)}, u32[]{:S(2)}) collective-permute-start(bf16[16,4096]{1,0:T(8,128)(2,1)} %get-tuple-element.24), channel_id=1, source_target_pairs={{0,16},{2,18},{4,20},{6,22},{8,24},{10,26},{12,28},{14,30},{16,0},... | collective-permute-start | bytes 393224 | tf_op jit(solution)/shard_map/ppermute | solution.py:642
  10.2 36.0 %collective-permute-start.3 = (bf16[16,4096]{1,0:T(8,128)(2,1)}, bf16[16,4096]{1,0:T(8,128)(2,1)}, u32[]{:S(2)}, u32[]{:S(2)}) collective-permute-start(bf16[16,4096]{1,0:T(8,128)(2,1)} %get-tuple-element.25), channel_id=1, source_target_pairs={{0,24},{2,26},{4,28},{6,30},{8,16},{10,18},{12,20},{14,22},{16,8},... | collective-permute-start | bytes 393224 | tf_op jit(solution)/shard_map/ppermute | solution.py:642
  18.2 7.5 %copy-start.4 = (bf16[16,4096]{1,0:T(8,128)(2,1)S(1)}, bf16[16,4096]{1,0:T(8,128)(2,1)}, u32[]{:S(2)}) copy-start(bf16[16,4096]{1,0:T(8,128)(2,1)} %get-tuple-element.23.rows_ref) | copy-start | bytes 393220
  18.2 64.0 %all-to-all-start = ((bf16[16,16,4096]{2,1,0:T(8,128)(2,1)}), bf16[16,16,4096]{2,1,0:T(8,128)(2,1)}, u32[]{:S(2)}, u32[]{:S(2)}) async-start(bf16[16,16,4096]{2,1,0:T(8,128)(2,1)} %kept_states.1._), calls=%async_computation | async-start | bytes 4194304 | tf_op jit(solution)/shard_map/all_to_all | solution.py:655
  25.7 1.0 %copy-start.2 = (f32[288,128]{1,0:T(8,128)S(1)}, f32[288,128]{1,0:T(8,128)}, u32[]{:S(2)}) copy-start(f32[288,128]{1,0:T(8,128)} %get-tuple-element.18.refs_0_.refs_3_._) | copy-start | bytes 442372
  25.7 1.0 %copy-start.11 = (f32[4096]{0:T(1024)S(1)}, f32[4096]{0:T(1024)}, u32[]{:S(2)}) copy-start(f32[4096]{0:T(1024)} %param.33) | copy-start | bytes 49156
  25.7 1.0 %copy-start.14 = (f32[16]{0:T(128)S(1)}, f32[16]{0:T(128)}, u32[]{:S(2)}) copy-start(f32[16]{0:T(128)} %param.29) | copy-start | bytes 196
  26.4 37.7 %collective-permute-start.1 = (bf16[16,4096]{1,0:T(8,128)(2,1)}, bf16[16,4096]{1,0:T(8,128)(2,1)}, u32[]{:S(2)}, u32[]{:S(2)}) collective-permute-start(bf16[16,4096]{1,0:T(8,128)(2,1)} %hold.1), channel_id=1, source_target_pairs={{0,8},{2,10},{4,12},{6,14},{8,0},{10,2},{12,4},{14,6},{16,24},{18,... | collective-permute-start | bytes 393224 | tf_op jit(solution)/shard_map/ppermute | solution.py:642
  26.7 19.2 %copy-start.15 = (pred[16,16]{1,0:T(8,128)(4,1)S(1)}, pred[16,16]{1,0:T(8,128)(4,1)}, u32[]{:S(2)}) copy-start(pred[16,16]{1,0:T(8,128)(4,1)} %constant.18.clone) | copy-start | bytes 772
  26.7 19.3 %copy-start.18 = (s32[16]{0:T(128)S(1)}, s32[16]{0:T(128)}, u32[]{:S(2)}) copy-start(s32[16]{0:T(128)} %constant.25) | copy-start | bytes 196
  26.7 37.4 %copy-start.3 = (bf16[16,4096]{1,0:T(8,128)(2,1)S(1)}, bf16[16,4096]{1,0:T(8,128)(2,1)}, u32[]{:S(2)}) copy-start(bf16[16,4096]{1,0:T(8,128)(2,1)} %get-tuple-element.22.refs_0_) | copy-start | bytes 393220
  26.7 42.9 %copy-start.17 = (pred[5,16]{1,0:T(8,128)(4,1)S(1)}, pred[5,16]{1,0:T(8,128)(4,1)}, u32[]{:S(2)}) copy-start(pred[5,16]{1,0:T(8,128)(4,1)} %constant.19.clone) | copy-start | bytes 244
  67.0 2.8 %collective-permute-start.4 = (bf16[16,4096]{1,0:T(8,128)(2,1)}, bf16[16,4096]{1,0:T(8,128)(2,1)S(1)}, u32[]{:S(2)}, u32[]{:S(2)}) collective-permute-start(bf16[16,4096]{1,0:T(8,128)(2,1)} %get-tuple-element.27), channel_id=1, source_target_pairs={{0,2},{2,0},{4,6},{6,4},{8,10},{10,8},{12,14},{14,12},{16,18},{18,... | collective-permute-start | bytes 393224 | tf_op jit(solution)/shard_map/ppermute | solution.py:642
  68.0 8.0 %collective-permute-start.5 = (bf16[16,4096]{1,0:T(8,128)(2,1)}, bf16[16,4096]{1,0:T(8,128)(2,1)S(1)}, u32[]{:S(2)}, u32[]{:S(2)}) collective-permute-start(bf16[16,4096]{1,0:T(8,128)(2,1)} %get-tuple-element.28), channel_id=1, source_target_pairs={{0,4},{2,6},{4,0},{6,2},{8,12},{10,14},{12,8},{14,10},{16,20},{18,... | collective-permute-start | bytes 393224 | tf_op jit(solution)/shard_map/ppermute | solution.py:642
  68.0 10.8 %collective-permute-start.6 = (bf16[16,4096]{1,0:T(8,128)(2,1)}, bf16[16,4096]{1,0:T(8,128)(2,1)S(1)}, u32[]{:S(2)}, u32[]{:S(2)}) collective-permute-start(bf16[16,4096]{1,0:T(8,128)(2,1)} %get-tuple-element.29), channel_id=1, source_target_pairs={{0,6},{2,4},{4,2},{6,0},{8,14},{10,12},{12,10},{14,8},{16,22},{18,... | collective-permute-start | bytes 393224 | tf_op jit(solution)/shard_map/ppermute | solution.py:642
  78.7 0.9 %copy-start.5 = (bf16[16,4096]{1,0:T(8,128)(2,1)S(1)}, bf16[16,4096]{1,0:T(8,128)(2,1)}, u32[]{:S(2)}) copy-start(bf16[16,4096]{1,0:T(8,128)(2,1)} %get-tuple-element.26.refs_0_) | copy-start | bytes 393220

commit v11 on v9

--- a/solution.py
+++ b/solution.py
@@ -635,12 +635,13 @@
     slots = kept_states(
         (place, accepted, owner), partials, gains[:2], dt_proj_weight, bias, a_log, conv, state, owners
     )
+    slots, *near = lax.optimization_barrier((slots, *groups[:half]))
     got = lax.all_to_all(slots, "req", split_axis=0, concat_axis=0, tiled=True)
+    groups = [swap(rows, d * PLANE) for d, rows in enumerate(near)] + far
     mixed = scan(
         partials, gains, dt_proj_weight, bias, a_log, skip.reshape(1, -1), conv, state, z_gate
     )
-    mixed, owner, *near = lax.optimization_barrier((mixed, owner, *groups[:half]))
-    groups = [swap(rows, d * PLANE) for d, rows in enumerate(near)] + far
+    mixed, owner = lax.optimization_barrier((mixed, owner))
     hits = jnp.any(owner.reshape(owners, requests) == place, axis=1)
     ids = np.arange(owners, dtype=np.int32)
     ranks = jnp.sum((hits[None, :] & (ids[None, :] < ids[:, None])).astype(jnp.int32), axis=1)

time: 87.1 us -> 78.9 us (0.906); the launches traced: 85.6 us -> 78.7 us
  waiting for transfers between devices: 27.4 us -> 19.3 us
  starting transfers between devices: 14.1 us -> 15.6 us
    ppermute x6, waiting for transfers between devices: 27.4 us -> 12.3 us  [swap(): lax.ppermute(rows, 'req', [(i, i ^ delta) for i in range(owners)])]
    all_to_all x1, waiting for transfers between devices: 0.01 us -> 6.94 us  [per_device(): got = lax.all_to_all(slots, 'req', split_axis=0, concat_axis=0, tiled=True)]
    all_to_all x1, starting transfers between devices: 7.49 us -> 8.48 us  [per_device(): got = lax.all_to_all(slots, 'req', split_axis=0, concat_axis=0, tiled=True)]
  transfers between devices with their start and end apart: 8 -> 8, of which waited for: 3 -> 3; matrix products, arithmetic and copies ran while one was open for 2% -> 2% of each run, Pallas kernels for 40% -> 42%
where the time goes in v11:
time: 78.9 us; the launch traced here: 78.7 us
  Pallas kernels  40.6 us (51%)
  waiting for transfers between devices  19.3 us (24%)
  starting transfers between devices  15.6 us (20%)
  local copies, waits for them, and re-layouts  1.82 us (2%)
  between operations  0.89 us (1%)
    pallas_call x1, Pallas kernels, scan(): pl.pallas_call(functools.partial(scan_kernel, len(partials)), grid=(chann...  18.9 us
    ppermute x6, waiting for transfers between devices, swap(): lax.ppermute(rows, 'req', [(i, i ^ delta) for i in range(owners)])  12.3 us
    all_to_all x1, starting transfers between devices, per_device(): got = lax.all_to_all(slots, 'req', split_axis=0, concat_axis=0, tiled=True)  8.48 us
    pallas_call x1, Pallas kernels, kept_states(): pl.pallas_call(functools.partial(kept_kernel, len(partials)), in_specs=[p...  7.91 us
    all_to_all x1, waiting for transfers between devices, per_device(): got = lax.all_to_all(slots, 'req', split_axis=0, concat_axis=0, tiled=True)  6.94 us
    ppermute x6, starting transfers between devices, swap(): lax.ppermute(rows, 'req', [(i, i ^ delta) for i in range(owners)])  5.82 us
    pallas_call x1, Pallas kernels, conv_project(): pl.pallas_call(conv_kernel, in_specs=[pl.BlockSpec(memory_space=pl.ANY)]...  4.09 us
    pallas_call x1, Pallas kernels, settle_states(): pl.pallas_call(settle_kernel, in_specs=[smem, smem, anywhere], out_specs=...  3.06 us
  transfers between devices with their start and end apart: 8, of which 3 were waited for; matrix products, arithmetic and copies ran while one was open for 2% of the time, Pallas kernels for 42%

profile of v11, /device:TPU:11, one launch (start us, length us, event | category | flops | bytes accessed | tf_op | source)
XLA Modules:
  0.0 78.7 jit_solution(10101011244774747132)
XLA Ops:
  0.6 0.0 copy-start.1
  0.6 0.0 copy-start
  0.7 0.0 copy-start.6
  0.7 0.0 copy-start.7
  0.7 0.0 copy-start.5
  0.7 0.0 copy-start.15
  0.7 0.0 copy-start.8
  0.7 0.0 copy-start.9
  0.7 0.0 copy-start.11
  0.7 4.1 %conv_project.1 = (bf16[128,4096]{1,0:T(8,128)(2,1)}, f32[288,128]{1,0:T(8,128)}) custom-call(bf16[128,4096]{1,0:T(8,128)(2,1)} %x_ref.1, bf16[3,8,4096]{2,1,0:T(8,128)(2,1)} %bitcast.10, f32[4,4096]{1,0:T(4,128)} %weight_hbm.1, f32[1,4096]{1,0:T(1,128)} %bitcast.21, bf16[288,4096]{1,0:T(8,128)(2,1)} %bitcast.20), custom_call_target="tpu_custom_call" | custom-call | tf_op jit(solution)/shard_map/conv_project/pallas_call | solution.py:112
  4.8 1.3 %collective-permute-start = (f32[288,128]{1,0:T(8,128)}, f32[288,128]{1,0:T(8,128)S(1)}, u32[]{:S(2)}, u32[]{:S(2)}) collective-permute-start(f32[288,128]{1,0:T(8,128)} %get-tuple-element.21.refs_0_.refs_3_._), channel_id=1, source_target_pairs={{0,1},{1,0},{2,3},{3,2},{4,5},{5,4},{6,7},{7,6},{8,9},{9,8},{10,11... | collective-permute-start | bytes 442376 | tf_op jit(solution)/shard_map/ppermute | solution.py:621
  6.1 1.8 %kept_edges.1 = (bf16[16,4096]{1,0:T(8,128)(2,1)}, bf16[16,4096]{1,0:T(8,128)(2,1)}, bf16[16,4096]{1,0:T(8,128)(2,1)}, bf16[16,4096]{1,0:T(8,128)(2,1)}) custom-call(s32[1]{0:T(128)} %bitcast.9.refs_0_.place_ref, s32[8]{0:T(128)S(1)} %copy-done.6, s32[8]{0:T(128)S(1)} %copy-done.5, s32[128]{0:T(128)S(1)} %copy-done.7, bf16[128,4096]{1,0:T(8,128)(2,1)S(1)} %copy-done, ...), custom_call_target="tpu_custom_call" | custom-call | tf_op jit(solution)/shard_map/kept_edges/pallas_call | solution.py:169
  7.9 2.3 %collective-permute-start.2 = (bf16[16,4096]{1,0:T(8,128)(2,1)}, bf16[16,4096]{1,0:T(8,128)(2,1)}, u32[]{:S(2)}, u32[]{:S(2)}) collective-permute-start(bf16[16,4096]{1,0:T(8,128)(2,1)} %get-tuple-element.30), channel_id=1, source_target_pairs={{0,16},{2,18},{4,20},{6,22},{8,24},{10,26},{12,28},{14,30},{16,0},... | collective-permute-start | bytes 393224 | tf_op jit(solution)/shard_map/ppermute | solution.py:626
  10.2 0.0 collective-permute-start.3
  10.2 0.1 copy.29.range_ref
  10.3 0.0 collective-permute-done.refs_1_.refs_4_
  10.3 7.9 %kept_states.1 = bf16[16,16,4096]{2,1,0:T(8,128)(2,1)} custom-call(s32[1]{0:T(128)} %bitcast.9.refs_0_.place_ref, s32[8]{0:T(128)S(1)} %copy-done.6, s32[128]{0:T(128)S(1)} %copy-done.7, f32[288,128]{1,0:T(8,128)} %get-tuple-element.21.refs_0_.refs_3_._, f32[288,128]{1,0:T(8,128)S(1)} %collective-permute-done.refs_1_.refs_4_, f32[1,256]{1,0:T(1,128)S(1)} %bitcast.15, ...), custom_call_target="tpu_custom_call" | custom-call | flops 1006632960000 | bytes 6291456 | tf_op jit(solution)/shard_map/kept_states/pallas_call | solution.py:345
  18.3 0.0 copy-start.2
  18.3 0.0 copy-start.10
  18.3 0.0 copy-start.13
  18.3 1.3 %collective-permute-start.1 = (bf16[16,4096]{1,0:T(8,128)(2,1)}, bf16[16,4096]{1,0:T(8,128)(2,1)}, u32[]{:S(2)}, u32[]{:S(2)}) collective-permute-start(bf16[16,4096]{1,0:T(8,128)(2,1)} %get-tuple-element.29), channel_id=1, source_target_pairs={{0,8},{2,10},{4,12},{6,14},{8,0},{10,2},{12,4},{14,6},{16,24},{18,... | collective-permute-start | bytes 393224 | tf_op jit(solution)/shard_map/ppermute | solution.py:626
  19.6 8.5 %all-to-all-start = ((bf16[16,16,4096]{2,1,0:T(8,128)(2,1)}), bf16[16,16,4096]{2,1,0:T(8,128)(2,1)}, u32[]{:S(2)}, u32[]{:S(2)}) async-start(bf16[16,16,4096]{2,1,0:T(8,128)(2,1)} %kept_states.1), calls=%async_computation | async-start | bytes 4194304 | tf_op jit(solution)/shard_map/all_to_all | solution.py:639
  28.1 0.0 copy-done.10
  28.1 0.0 copy-done.13
  28.1 0.0 copy-start.14
  28.1 0.0 copy-start.17
  28.1 0.0 copy-start.16
  28.2 18.9 %scan.1.refs_4_ = bf16[128,4096]{1,0:T(8,128)(2,1)} custom-call(f32[288,128]{1,0:T(8,128)S(1)} %copy-done.2, f32[288,128]{1,0:T(8,128)S(1)} %collective-permute-done.refs_1_.refs_4_, f32[1,256]{1,0:T(1,128)S(1)} %bitcast.16, f32[1,16]{1,0:T(1,128)S(1)} %bitcast.18, f32[1,16]{1,0:T(1,128)S(1)} %bitcast.19, bf16[256,4096]{1,0:T(8,128)(2,1)} %refs_7_.3, ...), custom_call_target="tpu_custom_call" | custom-call | flops 2013265920000 | bytes 5242880 | tf_op jit(solution)/shard_map/scan/pallas_call | solution.py:461
  47.0 0.1 eq.26
  47.1 0.1 reduce_or.9
  47.3 0.1 convert_reduce_fusion
  47.4 0.1 select_reduce_fusion
  47.5 0.0 collective-permute-done.2.refs_2_
  47.5 0.0 collective-permute-done.3.refs_3_
  47.5 0.0 collective-permute-done.1.refs_1_
  47.5 2.9 %regroup.1 = (bf16[16,4096]{1,0:T(8,128)(2,1)}, bf16[16,4096]{1,0:T(8,128)(2,1)}, bf16[16,4096]{1,0:T(8,128)(2,1)}, bf16[16,4096]{1,0:T(8,128)(2,1)}) custom-call(bf16[16,4096]{1,0:T(8,128)(2,1)S(1)} %copy-done.3, bf16[16,4096]{1,0:T(8,128)(2,1)} %collective-permute-done.1.refs_1_, bf16[16,4096]{1,0:T(8,128)(2,1)} %collective-permute-done.2.refs_2_, ...), custom_call_target="tpu_custom_call" | custom-call | tf_op jit(solution)/shard_map/regroup/pallas_call | solution.py:194
  50.5 0.4 collective-permute-start.4
  50.9 0.3 collective-permute-start.5
  51.2 1.5 %collective-permute-start.6 = (bf16[16,4096]{1,0:T(8,128)(2,1)}, bf16[16,4096]{1,0:T(8,128)(2,1)S(1)}, u32[]{:S(2)}, u32[]{:S(2)}) collective-permute-start(bf16[16,4096]{1,0:T(8,128)(2,1)} %get-tuple-element.35), channel_id=1, source_target_pairs={{0,6},{2,4},{4,2},{6,0},{8,14},{10,12},{12,10},{14,8},{16,22},{18,... | collective-permute-start | bytes 393224 | tf_op jit(solution)/shard_map/ppermute | solution.py:626
  52.7 0.1 convert_reduce_fusion.1.bound_ref
  52.8 0.0 collective-permute-done.4.refs_1_
  52.8 3.3 %collective-permute-done.5.refs_2_ = bf16[16,4096]{1,0:T(8,128)(2,1)S(1)} collective-permute-done((bf16[16,4096]{1,0:T(8,128)(2,1)}, bf16[16,4096]{1,0:T(8,128)(2,1)S(1)}, u32[]{:S(2)}, u32[]{:S(2)}) %collective-permute-start.5) | collective-permute-done | bytes 131104 | tf_op jit(solution)/shard_map/ppermute | solution.py:626
  56.1 9.0 %collective-permute-done.6.refs_3_ = bf16[16,4096]{1,0:T(8,128)(2,1)S(1)} collective-permute-done((bf16[16,4096]{1,0:T(8,128)(2,1)}, bf16[16,4096]{1,0:T(8,128)(2,1)S(1)}, u32[]{:S(2)}, u32[]{:S(2)}) %collective-permute-start.6) | collective-permute-done | bytes 131104 | tf_op jit(solution)/shard_map/ppermute | solution.py:626
  65.1 0.9 %copy-done.4 = bf16[16,4096]{1,0:T(8,128)(2,1)S(1)} copy-done((bf16[16,4096]{1,0:T(8,128)(2,1)S(1)}, bf16[16,4096]{1,0:T(8,128)(2,1)}, u32[]{:S(2)}) %copy-start.4) | copy-done | bytes 131096
  66.0 2.0 %settle_edges.1 = (bf16[12,3,4096]{2,1,0:T(4,128)(2,1)}, f32[4,2]{1,0:T(4,128)S(1)}) custom-call(s32[1]{0:T(128)} %bitcast.9.refs_0_.place_ref, s32[12]{0:T(128)S(1)} %broadcast_subtract_fusion.source_ref, s32[4,2]{1,0:T(4,128)S(1)} %copy.29.range_ref, bf16[16,4096]{1,0:T(8,128)(2,1)S(1)} %copy-done.4, bf16[16,4096]{1,0:T(8,128)(2,1)S(1)} %collective-permute-done.4.refs_1_, ...), custom_call_target="tpu_custom_call" | custom-call | tf_op jit(solution)/shard_map/settle_edges/pallas_call | solution.py:541
  68.0 0.6 copy.30
  68.7 6.9 %all-to-all-done.got_hbm = bf16[16,16,4096]{2,1,0:T(8,128)(2,1)} async-done(((bf16[16,16,4096]{2,1,0:T(8,128)(2,1)}), bf16[16,16,4096]{2,1,0:T(8,128)(2,1)}, u32[]{:S(2)}, u32[]{:S(2)}) %all-to-all-start) | async-done | bytes 2097184 | tf_op jit(solution)/shard_map/all_to_all | solution.py:639
  75.6 3.1 %settle_states.1 = bf16[12,16,4096]{2,1,0:T(8,128)(2,1)} custom-call(s32[12]{0:T(128)S(1)} %broadcast_subtract_fusion.source_ref, s32[5]{0:T(128)S(1)} %convert_reduce_fusion.1.bound_ref, bf16[16,16,4096]{2,1,0:T(8,128)(2,1)} %all-to-all-done.got_hbm), custom_call_target="tpu_custom_call" | custom-call | tf_op jit(solution)/shard_map/settle_states/pallas_call | solution.py:591
  (20 shorter events, 0.0 us)
Async XLA Ops:
  0.6 5.5 %copy-start.1 = (bf16[8,3,4096]{2,0,1:T(8,128)(2,1)S(1)}, bf16[8,3,4096]{2,0,1:T(8,128)(2,1)}, u32[]{:S(2)}) copy-start(bf16[8,3,4096]{2,0,1:T(8,128)(2,1)} %param.23) | copy-start | bytes 589828
  0.6 5.5 %copy-start = (bf16[128,4096]{1,0:T(8,128)(2,1)S(1)}, bf16[128,4096]{1,0:T(8,128)(2,1)}, u32[]{:S(2)}) copy-start(bf16[128,4096]{1,0:T(8,128)(2,1)} %x_ref.1) | copy-start | bytes 3145732
  0.7 5.5 %copy-start.6 = (s32[8]{0:T(128)S(1)}, s32[8]{0:T(128)}, u32[]{:S(2)}) copy-start(s32[8]{0:T(128)} %accepted_ref.1) | copy-start | bytes 100
  0.7 5.5 %copy-start.7 = (s32[128]{0:T(128)S(1)}, s32[128]{0:T(128)}, u32[]{:S(2)}) copy-start(s32[128]{0:T(128)} %owner_ref.1) | copy-start | bytes 1540
  0.7 5.5 %copy-start.5 = (s32[8]{0:T(128)S(1)}, s32[8]{0:T(128)}, u32[]{:S(2)}) copy-start(s32[8]{0:T(128)} %length_ref.1) | copy-start | bytes 100
  0.7 9.5 %copy-start.15 = (s32[4,2]{0,1:T(2,128)S(1)}, s32[4,2]{0,1:T(2,128)}, u32[]{:S(2)}) copy-start(s32[4,2]{0,1:T(2,128)} %param.37) | copy-start | bytes 100
  0.7 9.6 %copy-start.8 = (bf16[256,4096]{1,0:T(8,128)(2,1)S(1)}, bf16[256,4096]{1,0:T(8,128)(2,1)}, u32[]{:S(2)}) copy-start(bf16[256,4096]{1,0:T(8,128)(2,1)} %refs_7_.3) | copy-start | bytes 6291460
  0.7 9.6 %copy-start.9 = (f32[4096]{0:T(1024)S(1)}, f32[4096]{0:T(1024)}, u32[]{:S(2)}) copy-start(f32[4096]{0:T(1024)} %param.31) | copy-start | bytes 49156
  0.7 9.6 %copy-start.11 = (f32[256]{0:T(256)S(1)}, f32[256]{0:T(256)}, u32[]{:S(2)}) copy-start(f32[256]{0:T(256)} %param.27) | copy-start | bytes 3076
  0.7 9.6 %copy-start.12 = (f32[16]{0:T(128)S(1)}, f32[16]{0:T(128)}, u32[]{:S(2)}) copy-start(f32[16]{0:T(128)} %param.28) | copy-start | bytes 196
  4.8 5.5 %collective-permute-start = (f32[288,128]{1,0:T(8,128)}, f32[288,128]{1,0:T(8,128)S(1)}, u32[]{:S(2)}, u32[]{:S(2)}) collective-permute-start(f32[288,128]{1,0:T(8,128)} %get-tuple-element.21.refs_0_.refs_3_._), channel_id=1, source_target_pairs={{0,1},{1,0},{2,3},{3,2},{4,5},{5,4},{6,7},{7,6},{8,9},{9,8},{10,11... | collective-permute-start | bytes 442376 | tf_op jit(solution)/shard_map/ppermute | solution.py:621
  7.9 39.6 %collective-permute-start.2 = (bf16[16,4096]{1,0:T(8,128)(2,1)}, bf16[16,4096]{1,0:T(8,128)(2,1)}, u32[]{:S(2)}, u32[]{:S(2)}) collective-permute-start(bf16[16,4096]{1,0:T(8,128)(2,1)} %get-tuple-element.30), channel_id=1, source_target_pairs={{0,16},{2,18},{4,20},{6,22},{8,24},{10,26},{12,28},{14,30},{16,0},... | collective-permute-start | bytes 393224 | tf_op jit(solution)/shard_map/ppermute | solution.py:626
  10.2 37.3 %collective-permute-start.3 = (bf16[16,4096]{1,0:T(8,128)(2,1)}, bf16[16,4096]{1,0:T(8,128)(2,1)}, u32[]{:S(2)}, u32[]{:S(2)}) collective-permute-start(bf16[16,4096]{1,0:T(8,128)(2,1)} %get-tuple-element.31), channel_id=1, source_target_pairs={{0,24},{2,26},{4,28},{6,30},{8,16},{10,18},{12,20},{14,22},{16,8},... | collective-permute-start | bytes 393224 | tf_op jit(solution)/shard_map/ppermute | solution.py:626
  18.3 9.8 %copy-start.2 = (f32[288,128]{1,0:T(8,128)S(1)}, f32[288,128]{1,0:T(8,128)}, u32[]{:S(2)}) copy-start(f32[288,128]{1,0:T(8,128)} %get-tuple-element.21.refs_0_.refs_3_._) | copy-start | bytes 442372
  18.3 9.8 %copy-start.10 = (f32[4096]{0:T(1024)S(1)}, f32[4096]{0:T(1024)}, u32[]{:S(2)}) copy-start(f32[4096]{0:T(1024)} %param.33) | copy-start | bytes 49156
  18.3 9.8 %copy-start.13 = (f32[16]{0:T(128)S(1)}, f32[16]{0:T(128)}, u32[]{:S(2)}) copy-start(f32[16]{0:T(128)} %param.29) | copy-start | bytes 196
  18.3 29.2 %collective-permute-start.1 = (bf16[16,4096]{1,0:T(8,128)(2,1)}, bf16[16,4096]{1,0:T(8,128)(2,1)}, u32[]{:S(2)}, u32[]{:S(2)}) collective-permute-start(bf16[16,4096]{1,0:T(8,128)(2,1)} %get-tuple-element.29), channel_id=1, source_target_pairs={{0,8},{2,10},{4,12},{6,14},{8,0},{10,2},{12,4},{14,6},{16,24},{18,... | collective-permute-start | bytes 393224 | tf_op jit(solution)/shard_map/ppermute | solution.py:626
  19.6 56.0 %all-to-all-start = ((bf16[16,16,4096]{2,1,0:T(8,128)(2,1)}), bf16[16,16,4096]{2,1,0:T(8,128)(2,1)}, u32[]{:S(2)}, u32[]{:S(2)}) async-start(bf16[16,16,4096]{2,1,0:T(8,128)(2,1)} %kept_states.1), calls=%async_computation | async-start | bytes 4194304 | tf_op jit(solution)/shard_map/all_to_all | solution.py:639
  28.1 19.1 %copy-start.14 = (pred[16,16]{1,0:T(8,128)(4,1)S(1)}, pred[16,16]{1,0:T(8,128)(4,1)}, u32[]{:S(2)}) copy-start(pred[16,16]{1,0:T(8,128)(4,1)} %constant.18.clone) | copy-start | bytes 772
  28.1 19.3 %copy-start.17 = (s32[16]{0:T(128)S(1)}, s32[16]{0:T(128)}, u32[]{:S(2)}) copy-start(s32[16]{0:T(128)} %constant.25) | copy-start | bytes 196
  28.1 19.4 %copy-start.3 = (bf16[16,4096]{1,0:T(8,128)(2,1)S(1)}, bf16[16,4096]{1,0:T(8,128)(2,1)}, u32[]{:S(2)}) copy-start(bf16[16,4096]{1,0:T(8,128)(2,1)} %get-tuple-element.28.refs_0_) | copy-start | bytes 393220
  28.1 24.5 %copy-start.16 = (pred[5,16]{1,0:T(8,128)(4,1)S(1)}, pred[5,16]{1,0:T(8,128)(4,1)}, u32[]{:S(2)}) copy-start(pred[5,16]{1,0:T(8,128)(4,1)} %constant.19.clone) | copy-start | bytes 244
  50.5 2.3 %collective-permute-start.4 = (bf16[16,4096]{1,0:T(8,128)(2,1)}, bf16[16,4096]{1,0:T(8,128)(2,1)S(1)}, u32[]{:S(2)}, u32[]{:S(2)}) collective-permute-start(bf16[16,4096]{1,0:T(8,128)(2,1)} %get-tuple-element.33), channel_id=1, source_target_pairs={{0,2},{2,0},{4,6},{6,4},{8,10},{10,8},{12,14},{14,12},{16,18},{18,... | collective-permute-start | bytes 393224 | tf_op jit(solution)/shard_map/ppermute | solution.py:626
  50.9 5.3 %collective-permute-start.5 = (bf16[16,4096]{1,0:T(8,128)(2,1)}, bf16[16,4096]{1,0:T(8,128)(2,1)S(1)}, u32[]{:S(2)}, u32[]{:S(2)}) collective-permute-start(bf16[16,4096]{1,0:T(8,128)(2,1)} %get-tuple-element.34), channel_id=1, source_target_pairs={{0,4},{2,6},{4,0},{6,2},{8,12},{10,14},{12,8},{14,10},{16,20},{18,... | collective-permute-start | bytes 393224 | tf_op jit(solution)/shard_map/ppermute | solution.py:626
  51.2 14.0 %collective-permute-start.6 = (bf16[16,4096]{1,0:T(8,128)(2,1)}, bf16[16,4096]{1,0:T(8,128)(2,1)S(1)}, u32[]{:S(2)}, u32[]{:S(2)}) collective-permute-start(bf16[16,4096]{1,0:T(8,128)(2,1)} %get-tuple-element.35), channel_id=1, source_target_pairs={{0,6},{2,4},{4,2},{6,0},{8,14},{10,12},{12,10},{14,8},{16,22},{18,... | collective-permute-start | bytes 393224 | tf_op jit(solution)/shard_map/ppermute | solution.py:626
  65.1 0.9 %copy-start.4 = (bf16[16,4096]{1,0:T(8,128)(2,1)S(1)}, bf16[16,4096]{1,0:T(8,128)(2,1)}, u32[]{:S(2)}) copy-start(bf16[16,4096]{1,0:T(8,128)(2,1)} %get-tuple-element.32.refs_0_) | copy-start | bytes 393220

commit v12 on v11

--- a/solution.py
+++ b/solution.py
@@ -254,6 +254,8 @@
     span = min(2048, channels)
     halves = states // 8
 
+    copies[1].wait()
+    rate_ref[...] = jnp.exp(a_log_ref[...]) * (-LOG2_E)
     copies[0].wait()
     total = part_ref[...]
     for part in refs[4 : 3 + parts]:
@@ -270,7 +272,6 @@
     live = lax.div(row, requests) < by_request(
         lax.rem(row, requests), [accepted_ref[r] for r in range(requests)]
     )
-    copies[1].wait()
     copies[2].wait()
     for first in range(0, channels, span):
         piece = slice(first, first + span)
@@ -281,7 +282,6 @@
             tile = slice(c * LANES, (c + 1) * LANES)
             size_ref[first // LANES + c, :rows, :] = size[:, tile]
             drive_ref[first // LANES + c, :rows, :] = drive[:, tile]
-        rate_ref[:, piece] = jnp.exp(a_log_ref[:, piece]) * (-LOG2_E)
 
     def one_request(r, carry):
         own = pl.multiple_of(r * states, states)

time: 78.9 us -> 79.3 us (level)
    all_to_all x1, starting transfers between devices: 8.48 us -> 9.93 us  [per_device(): got = lax.all_to_all(slots, 'req', split_axis=0, concat_axis=0, tiled=True)]
    ppermute x6, starting transfers between devices: 5.82 us -> 4.59 us  [swap(): lax.ppermute(rows, 'req', [(i, i ^ delta) for i in range(owners)])]
  transfers between devices with their start and end apart: 8 -> 8, of which waited for: 3 -> 3; matrix products, arithmetic and copies ran while one was open for 2% -> 2% of each run, Pallas kernels for 42% -> 43%
where the time goes in v12:
time: 79.3 us; the launch traced here: 79.5 us
  Pallas kernels  41.2 us (52%)
  waiting for transfers between devices  19.3 us (24%)
  starting transfers between devices  15.8 us (20%)
  local copies, waits for them, and re-layouts  1.82 us (2%)
  between operations  0.9 us (1%)
    pallas_call x1, Pallas kernels, scan(): pl.pallas_call(functools.partial(scan_kernel, len(partials)), grid=(chann...  18.9 us
    ppermute x6, waiting for transfers between devices, swap(): lax.ppermute(rows, 'req', [(i, i ^ delta) for i in range(owners)])  12.3 us
    all_to_all x1, starting transfers between devices, per_device(): got = lax.all_to_all(slots, 'req', split_axis=0, concat_axis=0, tiled=True)  9.93 us
    pallas_call x1, Pallas kernels, kept_states(): pl.pallas_call(functools.partial(kept_kernel, len(partials)), in_specs=[p...  8.68 us
    all_to_all x1, waiting for transfers between devices, per_device(): got = lax.all_to_all(slots, 'req', split_axis=0, concat_axis=0, tiled=True)  6.94 us
    ppermute x6, starting transfers between devices, swap(): lax.ppermute(rows, 'req', [(i, i ^ delta) for i in range(owners)])  4.59 us
    pallas_call x1, Pallas kernels, conv_project(): pl.pallas_call(conv_kernel, in_specs=[pl.BlockSpec(memory_space=pl.ANY)]...  4.09 us
    pallas_call x1, Pallas kernels, regroup(): pl.pallas_call(regroup_kernel, grid=(channels // block,), in_specs=[pl.Bl...  2.92 us
  transfers between devices with their start and end apart: 8, of which 3 were waited for; matrix products, arithmetic and copies ran while one was open for 2% of the time, Pallas kernels for 43%

profile of v12, /device:TPU:11, one launch (start us, length us, event | category | flops | bytes accessed | tf_op | source)
XLA Modules:
  0.0 79.5 jit_solution(4702412633491354671)
XLA Ops:
  0.6 0.0 copy-start.1
  0.6 0.0 copy-start
  0.7 0.0 copy-start.6
  0.7 0.0 copy-start.7
  0.7 0.0 copy-start.5
  0.7 0.0 copy-start.8
  0.7 4.1 %conv_project.1 = (bf16[128,4096]{1,0:T(8,128)(2,1)}, f32[288,128]{1,0:T(8,128)}) custom-call(bf16[128,4096]{1,0:T(8,128)(2,1)} %x_ref.1, bf16[3,8,4096]{2,1,0:T(8,128)(2,1)} %bitcast.10, f32[4,4096]{1,0:T(4,128)} %weight_hbm.1, f32[1,4096]{1,0:T(1,128)} %bitcast.21, bf16[288,4096]{1,0:T(8,128)(2,1)} %bitcast.20), custom_call_target="tpu_custom_call" | custom-call | tf_op jit(solution)/shard_map/conv_project/pallas_call | solution.py:112
  4.8 1.3 %collective-permute-start = (f32[288,128]{1,0:T(8,128)}, f32[288,128]{1,0:T(8,128)S(1)}, u32[]{:S(2)}, u32[]{:S(2)}) collective-permute-start(f32[288,128]{1,0:T(8,128)} %get-tuple-element.21.refs_0_.refs_3_._), channel_id=1, source_target_pairs={{0,1},{1,0},{2,3},{3,2},{4,5},{5,4},{6,7},{7,6},{8,9},{9,8},{10,11... | collective-permute-start | bytes 442376 | tf_op jit(solution)/shard_map/ppermute | solution.py:621
  6.1 0.0 copy-done.6
  6.1 1.8 %kept_edges.1 = (bf16[16,4096]{1,0:T(8,128)(2,1)}, bf16[16,4096]{1,0:T(8,128)(2,1)}, bf16[16,4096]{1,0:T(8,128)(2,1)}, bf16[16,4096]{1,0:T(8,128)(2,1)}) custom-call(s32[1]{0:T(128)} %bitcast.9.refs_0_.place_ref, s32[8]{0:T(128)S(1)} %copy-done.6, s32[8]{0:T(128)S(1)} %copy-done.5, s32[128]{0:T(128)S(1)} %copy-done.7, bf16[128,4096]{1,0:T(8,128)(2,1)S(1)} %copy-done, ...), custom_call_target="tpu_custom_call" | custom-call | tf_op jit(solution)/shard_map/kept_edges/pallas_call | solution.py:169
  7.9 2.3 %collective-permute-start.2 = (bf16[16,4096]{1,0:T(8,128)(2,1)}, bf16[16,4096]{1,0:T(8,128)(2,1)}, u32[]{:S(2)}, u32[]{:S(2)}) collective-permute-start(bf16[16,4096]{1,0:T(8,128)(2,1)} %get-tuple-element.30), channel_id=1, source_target_pairs={{0,16},{2,18},{4,20},{6,22},{8,24},{10,26},{12,28},{14,30},{16,0},... | collective-permute-start | bytes 393224 | tf_op jit(solution)/shard_map/ppermute | solution.py:626
  10.2 0.0 collective-permute-start.3
  10.2 0.1 copy.29.range_ref
  10.3 0.0 collective-permute-done.refs_1_.refs_4_
  10.3 0.0 copy-done.9
  10.3 0.0 copy-done.12
  10.3 8.7 %kept_states.1 = bf16[16,16,4096]{2,1,0:T(8,128)(2,1)} custom-call(s32[1]{0:T(128)} %bitcast.9.refs_0_.place_ref, s32[8]{0:T(128)S(1)} %copy-done.6, s32[128]{0:T(128)S(1)} %copy-done.7, f32[288,128]{1,0:T(8,128)} %get-tuple-element.21.refs_0_.refs_3_._, f32[288,128]{1,0:T(8,128)S(1)} %collective-permute-done.refs_1_.refs_4_, f32[1,256]{1,0:T(1,128)S(1)} %bitcast.15, ...), custom_call_target="tpu_custom_call" | custom-call | flops 1006632960000 | bytes 6291456 | tf_op jit(solution)/shard_map/kept_states/pallas_call | solution.py:345
  19.0 0.0 copy-start.2
  19.0 0.0 copy-start.10
  19.1 0.0 copy-start.13
  19.1 0.1 collective-permute-start.1
  19.1 9.9 %all-to-all-start = ((bf16[16,16,4096]{2,1,0:T(8,128)(2,1)}), bf16[16,16,4096]{2,1,0:T(8,128)(2,1)}, u32[]{:S(2)}, u32[]{:S(2)}) async-start(bf16[16,16,4096]{2,1,0:T(8,128)(2,1)} %kept_states.1), calls=%async_computation | async-start | bytes 4194304 | tf_op jit(solution)/shard_map/all_to_all | solution.py:639
  29.1 0.0 copy-done.2
  29.1 0.0 copy-start.14
  29.1 0.0 copy-start.17
  29.1 0.0 copy-start.16
  29.2 18.9 %scan.1.refs_4_ = bf16[128,4096]{1,0:T(8,128)(2,1)} custom-call(f32[288,128]{1,0:T(8,128)S(1)} %copy-done.2, f32[288,128]{1,0:T(8,128)S(1)} %collective-permute-done.refs_1_.refs_4_, f32[1,256]{1,0:T(1,128)S(1)} %bitcast.16, f32[1,16]{1,0:T(1,128)S(1)} %bitcast.18, f32[1,16]{1,0:T(1,128)S(1)} %bitcast.19, bf16[256,4096]{1,0:T(8,128)(2,1)} %refs_7_.3, ...), custom_call_target="tpu_custom_call" | custom-call | flops 2013265920000 | bytes 5242880 | tf_op jit(solution)/shard_map/scan/pallas_call | solution.py:461
  48.0 0.1 eq.26
  48.1 0.1 reduce_or.9
  48.3 0.1 convert_reduce_fusion
  48.4 0.1 select_reduce_fusion
  48.5 0.0 collective-permute-done.2.refs_2_
  48.5 0.0 collective-permute-done.3.refs_3_
  48.5 0.0 collective-permute-done.1.refs_1_
  48.5 2.9 %regroup.1 = (bf16[16,4096]{1,0:T(8,128)(2,1)}, bf16[16,4096]{1,0:T(8,128)(2,1)}, bf16[16,4096]{1,0:T(8,128)(2,1)}, bf16[16,4096]{1,0:T(8,128)(2,1)}) custom-call(bf16[16,4096]{1,0:T(8,128)(2,1)S(1)} %copy-done.3, bf16[16,4096]{1,0:T(8,128)(2,1)} %collective-permute-done.1.refs_1_, bf16[16,4096]{1,0:T(8,128)(2,1)} %collective-permute-done.2.refs_2_, ...), custom_call_target="tpu_custom_call" | custom-call | tf_op jit(solution)/shard_map/regroup/pallas_call | solution.py:194
  51.5 0.4 collective-permute-start.4
  51.9 0.3 collective-permute-start.5
  52.2 1.5 %collective-permute-start.6 = (bf16[16,4096]{1,0:T(8,128)(2,1)}, bf16[16,4096]{1,0:T(8,128)(2,1)S(1)}, u32[]{:S(2)}, u32[]{:S(2)}) collective-permute-start(bf16[16,4096]{1,0:T(8,128)(2,1)} %get-tuple-element.35), channel_id=1, source_target_pairs={{0,6},{2,4},{4,2},{6,0},{8,14},{10,12},{12,10},{14,8},{16,22},{18,... | collective-permute-start | bytes 393224 | tf_op jit(solution)/shard_map/ppermute | solution.py:626
  53.7 0.0 copy-done.16
  53.7 0.1 convert_reduce_fusion.1.bound_ref
  53.8 0.0 collective-permute-done.4.refs_1_
  53.8 3.3 %collective-permute-done.5.refs_2_ = bf16[16,4096]{1,0:T(8,128)(2,1)S(1)} collective-permute-done((bf16[16,4096]{1,0:T(8,128)(2,1)}, bf16[16,4096]{1,0:T(8,128)(2,1)S(1)}, u32[]{:S(2)}, u32[]{:S(2)}) %collective-permute-start.5) | collective-permute-done | bytes 131104 | tf_op jit(solution)/shard_map/ppermute | solution.py:626
  57.1 9.0 %collective-permute-done.6.refs_3_ = bf16[16,4096]{1,0:T(8,128)(2,1)S(1)} collective-permute-done((bf16[16,4096]{1,0:T(8,128)(2,1)}, bf16[16,4096]{1,0:T(8,128)(2,1)S(1)}, u32[]{:S(2)}, u32[]{:S(2)}) %collective-permute-start.6) | collective-permute-done | bytes 131104 | tf_op jit(solution)/shard_map/ppermute | solution.py:626
  66.1 0.9 %copy-done.4 = bf16[16,4096]{1,0:T(8,128)(2,1)S(1)} copy-done((bf16[16,4096]{1,0:T(8,128)(2,1)S(1)}, bf16[16,4096]{1,0:T(8,128)(2,1)}, u32[]{:S(2)}) %copy-start.4) | copy-done | bytes 131096
  67.0 2.0 %settle_edges.1 = (bf16[12,3,4096]{2,1,0:T(4,128)(2,1)}, f32[4,2]{1,0:T(4,128)S(1)}) custom-call(s32[1]{0:T(128)} %bitcast.9.refs_0_.place_ref, s32[12]{0:T(128)S(1)} %broadcast_subtract_fusion.source_ref, s32[4,2]{1,0:T(4,128)S(1)} %copy.29.range_ref, bf16[16,4096]{1,0:T(8,128)(2,1)S(1)} %copy-done.4, bf16[16,4096]{1,0:T(8,128)(2,1)S(1)} %collective-permute-done.4.refs_1_, ...), custom_call_target="tpu_custom_call" | custom-call | tf_op jit(solution)/shard_map/settle_edges/pallas_call | solution.py:541
  69.0 0.6 copy.30
  69.7 6.9 %all-to-all-done.got_hbm = bf16[16,16,4096]{2,1,0:T(8,128)(2,1)} async-done(((bf16[16,16,4096]{2,1,0:T(8,128)(2,1)}), bf16[16,16,4096]{2,1,0:T(8,128)(2,1)}, u32[]{:S(2)}, u32[]{:S(2)}) %all-to-all-start) | async-done | bytes 2097184 | tf_op jit(solution)/shard_map/all_to_all | solution.py:639
  76.6 2.9 %settle_states.1 = bf16[12,16,4096]{2,1,0:T(8,128)(2,1)} custom-call(s32[12]{0:T(128)S(1)} %broadcast_subtract_fusion.source_ref, s32[5]{0:T(128)S(1)} %convert_reduce_fusion.1.bound_ref, bf16[16,16,4096]{2,1,0:T(8,128)(2,1)} %all-to-all-done.got_hbm), custom_call_target="tpu_custom_call" | custom-call | tf_op jit(solution)/shard_map/settle_states/pallas_call | solution.py:591
  (20 shorter events, 0.0 us)
Async XLA Ops:
  0.6 5.5 %copy-start.1 = (bf16[8,3,4096]{2,0,1:T(8,128)(2,1)S(1)}, bf16[8,3,4096]{2,0,1:T(8,128)(2,1)}, u32[]{:S(2)}) copy-start(bf16[8,3,4096]{2,0,1:T(8,128)(2,1)} %param.23) | copy-start | bytes 589828
  0.6 5.5 %copy-start = (bf16[128,4096]{1,0:T(8,128)(2,1)S(1)}, bf16[128,4096]{1,0:T(8,128)(2,1)}, u32[]{:S(2)}) copy-start(bf16[128,4096]{1,0:T(8,128)(2,1)} %x_ref.1) | copy-start | bytes 3145732
  0.7 5.5 %copy-start.6 = (s32[8]{0:T(128)S(1)}, s32[8]{0:T(128)}, u32[]{:S(2)}) copy-start(s32[8]{0:T(128)} %accepted_ref.1) | copy-start | bytes 100
  0.7 5.5 %copy-start.7 = (s32[128]{0:T(128)S(1)}, s32[128]{0:T(128)}, u32[]{:S(2)}) copy-start(s32[128]{0:T(128)} %owner_ref.1) | copy-start | bytes 1540
  0.7 5.5 %copy-start.5 = (s32[8]{0:T(128)S(1)}, s32[8]{0:T(128)}, u32[]{:S(2)}) copy-start(s32[8]{0:T(128)} %length_ref.1) | copy-start | bytes 100
  0.7 9.5 %copy-start.15 = (s32[4,2]{0,1:T(2,128)S(1)}, s32[4,2]{0,1:T(2,128)}, u32[]{:S(2)}) copy-start(s32[4,2]{0,1:T(2,128)} %param.37) | copy-start | bytes 100
  0.7 9.6 %copy-start.8 = (bf16[256,4096]{1,0:T(8,128)(2,1)S(1)}, bf16[256,4096]{1,0:T(8,128)(2,1)}, u32[]{:S(2)}) copy-start(bf16[256,4096]{1,0:T(8,128)(2,1)} %refs_7_.3) | copy-start | bytes 6291460
  0.7 9.6 %copy-start.9 = (f32[4096]{0:T(1024)S(1)}, f32[4096]{0:T(1024)}, u32[]{:S(2)}) copy-start(f32[4096]{0:T(1024)} %param.31) | copy-start | bytes 49156
  0.7 9.6 %copy-start.11 = (f32[256]{0:T(256)S(1)}, f32[256]{0:T(256)}, u32[]{:S(2)}) copy-start(f32[256]{0:T(256)} %param.27) | copy-start | bytes 3076
  0.7 9.6 %copy-start.12 = (f32[16]{0:T(128)S(1)}, f32[16]{0:T(128)}, u32[]{:S(2)}) copy-start(f32[16]{0:T(128)} %param.28) | copy-start | bytes 196
  4.8 5.5 %collective-permute-start = (f32[288,128]{1,0:T(8,128)}, f32[288,128]{1,0:T(8,128)S(1)}, u32[]{:S(2)}, u32[]{:S(2)}) collective-permute-start(f32[288,128]{1,0:T(8,128)} %get-tuple-element.21.refs_0_.refs_3_._), channel_id=1, source_target_pairs={{0,1},{1,0},{2,3},{3,2},{4,5},{5,4},{6,7},{7,6},{8,9},{9,8},{10,11... | collective-permute-start | bytes 442376 | tf_op jit(solution)/shard_map/ppermute | solution.py:621
  7.9 40.6 %collective-permute-start.2 = (bf16[16,4096]{1,0:T(8,128)(2,1)}, bf16[16,4096]{1,0:T(8,128)(2,1)}, u32[]{:S(2)}, u32[]{:S(2)}) collective-permute-start(bf16[16,4096]{1,0:T(8,128)(2,1)} %get-tuple-element.30), channel_id=1, source_target_pairs={{0,16},{2,18},{4,20},{6,22},{8,24},{10,26},{12,28},{14,30},{16,0},... | collective-permute-start | bytes 393224 | tf_op jit(solution)/shard_map/ppermute | solution.py:626
  10.2 38.3 %collective-permute-start.3 = (bf16[16,4096]{1,0:T(8,128)(2,1)}, bf16[16,4096]{1,0:T(8,128)(2,1)}, u32[]{:S(2)}, u32[]{:S(2)}) collective-permute-start(bf16[16,4096]{1,0:T(8,128)(2,1)} %get-tuple-element.31), channel_id=1, source_target_pairs={{0,24},{2,26},{4,28},{6,30},{8,16},{10,18},{12,20},{14,22},{16,8},... | collective-permute-start | bytes 393224 | tf_op jit(solution)/shard_map/ppermute | solution.py:626
  19.0 10.1 %copy-start.2 = (f32[288,128]{1,0:T(8,128)S(1)}, f32[288,128]{1,0:T(8,128)}, u32[]{:S(2)}) copy-start(f32[288,128]{1,0:T(8,128)} %get-tuple-element.21.refs_0_.refs_3_._) | copy-start | bytes 442372
  19.0 10.0 %copy-start.10 = (f32[4096]{0:T(1024)S(1)}, f32[4096]{0:T(1024)}, u32[]{:S(2)}) copy-start(f32[4096]{0:T(1024)} %param.33) | copy-start | bytes 49156
  19.1 10.0 %copy-start.13 = (f32[16]{0:T(128)S(1)}, f32[16]{0:T(128)}, u32[]{:S(2)}) copy-start(f32[16]{0:T(128)} %param.29) | copy-start | bytes 196
  19.1 29.5 %collective-permute-start.1 = (bf16[16,4096]{1,0:T(8,128)(2,1)}, bf16[16,4096]{1,0:T(8,128)(2,1)}, u32[]{:S(2)}, u32[]{:S(2)}) collective-permute-start(bf16[16,4096]{1,0:T(8,128)(2,1)} %get-tuple-element.29), channel_id=1, source_target_pairs={{0,8},{2,10},{4,12},{6,14},{8,0},{10,2},{12,4},{14,6},{16,24},{18,... | collective-permute-start | bytes 393224 | tf_op jit(solution)/shard_map/ppermute | solution.py:626
  19.1 57.5 %all-to-all-start = ((bf16[16,16,4096]{2,1,0:T(8,128)(2,1)}), bf16[16,16,4096]{2,1,0:T(8,128)(2,1)}, u32[]{:S(2)}, u32[]{:S(2)}) async-start(bf16[16,16,4096]{2,1,0:T(8,128)(2,1)} %kept_states.1), calls=%async_computation | async-start | bytes 4194304 | tf_op jit(solution)/shard_map/all_to_all | solution.py:639
  29.1 19.1 %copy-start.14 = (pred[16,16]{1,0:T(8,128)(4,1)S(1)}, pred[16,16]{1,0:T(8,128)(4,1)}, u32[]{:S(2)}) copy-start(pred[16,16]{1,0:T(8,128)(4,1)} %constant.18.clone) | copy-start | bytes 772
  29.1 19.3 %copy-start.17 = (s32[16]{0:T(128)S(1)}, s32[16]{0:T(128)}, u32[]{:S(2)}) copy-start(s32[16]{0:T(128)} %constant.25) | copy-start | bytes 196
  29.1 19.4 %copy-start.3 = (bf16[16,4096]{1,0:T(8,128)(2,1)S(1)}, bf16[16,4096]{1,0:T(8,128)(2,1)}, u32[]{:S(2)}) copy-start(bf16[16,4096]{1,0:T(8,128)(2,1)} %get-tuple-element.28.refs_0_) | copy-start | bytes 393220
  29.1 24.5 %copy-start.16 = (pred[5,16]{1,0:T(8,128)(4,1)S(1)}, pred[5,16]{1,0:T(8,128)(4,1)}, u32[]{:S(2)}) copy-start(pred[5,16]{1,0:T(8,128)(4,1)} %constant.19.clone) | copy-start | bytes 244
  51.5 2.3 %collective-permute-start.4 = (bf16[16,4096]{1,0:T(8,128)(2,1)}, bf16[16,4096]{1,0:T(8,128)(2,1)S(1)}, u32[]{:S(2)}, u32[]{:S(2)}) collective-permute-start(bf16[16,4096]{1,0:T(8,128)(2,1)} %get-tuple-element.33), channel_id=1, source_target_pairs={{0,2},{2,0},{4,6},{6,4},{8,10},{10,8},{12,14},{14,12},{16,18},{18,... | collective-permute-start | bytes 393224 | tf_op jit(solution)/shard_map/ppermute | solution.py:626
  51.9 5.3 %collective-permute-start.5 = (bf16[16,4096]{1,0:T(8,128)(2,1)}, bf16[16,4096]{1,0:T(8,128)(2,1)S(1)}, u32[]{:S(2)}, u32[]{:S(2)}) collective-permute-start(bf16[16,4096]{1,0:T(8,128)(2,1)} %get-tuple-element.34), channel_id=1, source_target_pairs={{0,4},{2,6},{4,0},{6,2},{8,12},{10,14},{12,8},{14,10},{16,20},{18,... | collective-permute-start | bytes 393224 | tf_op jit(solution)/shard_map/ppermute | solution.py:626
  52.2 14.0 %collective-permute-start.6 = (bf16[16,4096]{1,0:T(8,128)(2,1)}, bf16[16,4096]{1,0:T(8,128)(2,1)S(1)}, u32[]{:S(2)}, u32[]{:S(2)}) collective-permute-start(bf16[16,4096]{1,0:T(8,128)(2,1)} %get-tuple-element.35), channel_id=1, source_target_pairs={{0,6},{2,4},{4,2},{6,0},{8,14},{10,12},{12,10},{14,8},{16,22},{18,... | collective-permute-start | bytes 393224 | tf_op jit(solution)/shard_map/ppermute | solution.py:626
  66.1 0.9 %copy-start.4 = (bf16[16,4096]{1,0:T(8,128)(2,1)S(1)}, bf16[16,4096]{1,0:T(8,128)(2,1)}, u32[]{:S(2)}) copy-start(bf16[16,4096]{1,0:T(8,128)(2,1)} %get-tuple-element.32.refs_0_) | copy-start | bytes 393220

commit v13 on v12

--- a/solution.py
+++ b/solution.py
@@ -17,7 +17,7 @@
 DIGIT = 7
 VMEM_BYTES = 24 * 1024 * 1024
 BLOCK = 2048
-PARTS = 4
+PARTS = 8
 ROUND = 4
 VECTOR_WEIGHT = 30000
 

time: 79.3 us -> 78.2 us (0.986); the launches traced: 79.5 us -> 77.4 us
  starting transfers between devices: 15.8 us -> 14.4 us
    all_to_all x1, starting transfers between devices: 9.93 us -> 8.56 us  [per_device(): got = lax.all_to_all(slots, 'req', split_axis=0, concat_axis=0, tiled=True)]
where the time goes in v13:
time: 78.2 us; the launch traced here: 77.4 us
  Pallas kernels  40.5 us (52%)
  waiting for transfers between devices  19.3 us (25%)
  starting transfers between devices  14.4 us (18%)
  local copies, waits for them, and re-layouts  1.82 us (2%)
  between operations  0.9 us (1%)
    pallas_call x1, Pallas kernels, scan(): pl.pallas_call(functools.partial(scan_kernel, len(partials)), grid=(chann...  18.9 us
    ppermute x6, waiting for transfers between devices, swap(): lax.ppermute(rows, 'req', [(i, i ^ delta) for i in range(owners)])  12.3 us
    all_to_all x1, starting transfers between devices, per_device(): got = lax.all_to_all(slots, 'req', split_axis=0, concat_axis=0, tiled=True)  8.56 us
    pallas_call x1, Pallas kernels, kept_states(): pl.pallas_call(functools.partial(kept_kernel, len(partials)), in_specs=[p...  8.02 us
    all_to_all x1, waiting for transfers between devices, per_device(): got = lax.all_to_all(slots, 'req', split_axis=0, concat_axis=0, tiled=True)  6.94 us
    ppermute x6, starting transfers between devices, swap(): lax.ppermute(rows, 'req', [(i, i ^ delta) for i in range(owners)])  4.59 us
    pallas_call x1, Pallas kernels, conv_project(): pl.pallas_call(conv_kernel, in_specs=[pl.BlockSpec(memory_space=pl.ANY)]...  4.09 us
    pallas_call x1, Pallas kernels, regroup(): pl.pallas_call(regroup_kernel, grid=(channels // block,), in_specs=[pl.Bl...  2.92 us
  transfers between devices with their start and end apart: 8, of which 3 were waited for; matrix products, arithmetic and copies ran while one was open for 2% of the time, Pallas kernels for 43%

profile of v13, /device:TPU:11, one launch (start us, length us, event | category | flops | bytes accessed | tf_op | source)
XLA Modules:
  0.0 77.4 jit_solution(1388603981890551000)
XLA Ops:
  0.6 0.0 copy-start.1
  0.7 0.0 copy-start.8
  0.7 0.0 copy-start.9
  0.7 0.0 copy-start.11
  0.7 0.0 copy-start.12
  0.7 4.1 %conv_project.1 = (bf16[128,4096]{1,0:T(8,128)(2,1)}, f32[288,128]{1,0:T(8,128)}) custom-call(bf16[128,4096]{1,0:T(8,128)(2,1)} %x_ref.1, bf16[3,8,4096]{2,1,0:T(8,128)(2,1)} %bitcast.10, f32[4,4096]{1,0:T(4,128)} %weight_hbm.1, f32[1,4096]{1,0:T(1,128)} %bitcast.21, bf16[288,4096]{1,0:T(8,128)(2,1)} %bitcast.20), custom_call_target="tpu_custom_call" | custom-call | tf_op jit(solution)/shard_map/conv_project/pallas_call | solution.py:112
  4.8 1.3 %collective-permute-start = (f32[288,128]{1,0:T(8,128)}, f32[288,128]{1,0:T(8,128)S(1)}, u32[]{:S(2)}, u32[]{:S(2)}) collective-permute-start(f32[288,128]{1,0:T(8,128)} %get-tuple-element.21.refs_0_.refs_3_._), channel_id=1, source_target_pairs={{0,1},{1,0},{2,3},{3,2},{4,5},{5,4},{6,7},{7,6},{8,9},{9,8},{10,11... | collective-permute-start | bytes 442376 | tf_op jit(solution)/shard_map/ppermute | solution.py:621
  6.1 0.0 copy-done.1
  6.1 0.0 copy-done.5
  6.1 1.8 %kept_edges.1 = (bf16[16,4096]{1,0:T(8,128)(2,1)}, bf16[16,4096]{1,0:T(8,128)(2,1)}, bf16[16,4096]{1,0:T(8,128)(2,1)}, bf16[16,4096]{1,0:T(8,128)(2,1)}) custom-call(s32[1]{0:T(128)} %bitcast.9.refs_0_.place_ref, s32[8]{0:T(128)S(1)} %copy-done.6, s32[8]{0:T(128)S(1)} %copy-done.5, s32[128]{0:T(128)S(1)} %copy-done.7, bf16[128,4096]{1,0:T(8,128)(2,1)S(1)} %copy-done, ...), custom_call_target="tpu_custom_call" | custom-call | tf_op jit(solution)/shard_map/kept_edges/pallas_call | solution.py:169
  7.9 2.3 %collective-permute-start.2 = (bf16[16,4096]{1,0:T(8,128)(2,1)}, bf16[16,4096]{1,0:T(8,128)(2,1)}, u32[]{:S(2)}, u32[]{:S(2)}) collective-permute-start(bf16[16,4096]{1,0:T(8,128)(2,1)} %get-tuple-element.30), channel_id=1, source_target_pairs={{0,16},{2,18},{4,20},{6,22},{8,24},{10,26},{12,28},{14,30},{16,0},... | collective-permute-start | bytes 393224 | tf_op jit(solution)/shard_map/ppermute | solution.py:626
  10.2 0.0 collective-permute-start.3
  10.2 0.1 copy.29.range_ref
  10.3 0.0 collective-permute-done.refs_1_.refs_4_
  10.3 8.0 %kept_states.1 = bf16[16,16,4096]{2,1,0:T(8,128)(2,1)} custom-call(s32[1]{0:T(128)} %bitcast.9.refs_0_.place_ref, s32[8]{0:T(128)S(1)} %copy-done.6, s32[128]{0:T(128)S(1)} %copy-done.7, f32[288,128]{1,0:T(8,128)} %get-tuple-element.21.refs_0_.refs_3_._, f32[288,128]{1,0:T(8,128)S(1)} %collective-permute-done.refs_1_.refs_4_, f32[1,256]{1,0:T(1,128)S(1)} %bitcast.15, ...), custom_call_target="tpu_custom_call" | custom-call | flops 1006632960000 | bytes 6291456 | tf_op jit(solution)/shard_map/kept_states/pallas_call | solution.py:345
  18.4 0.0 copy-start.2
  18.4 0.0 copy-start.10
  18.4 0.0 copy-start.13
  18.4 0.1 collective-permute-start.1
  18.5 8.6 %all-to-all-start = ((bf16[16,16,4096]{2,1,0:T(8,128)(2,1)}), bf16[16,16,4096]{2,1,0:T(8,128)(2,1)}, u32[]{:S(2)}, u32[]{:S(2)}) async-start(bf16[16,16,4096]{2,1,0:T(8,128)(2,1)} %kept_states.1), calls=%async_computation | async-start | bytes 4194304 | tf_op jit(solution)/shard_map/all_to_all | solution.py:639
  27.0 0.0 copy-done.10
  27.1 0.0 copy-done.13
  27.1 0.0 copy-start.15
  27.1 0.0 copy-start.17
  27.1 0.0 copy-start.3
  27.1 0.0 copy-start.14
  27.1 18.9 %scan.1.refs_4_ = bf16[128,4096]{1,0:T(8,128)(2,1)} custom-call(f32[288,128]{1,0:T(8,128)S(1)} %copy-done.2, f32[288,128]{1,0:T(8,128)S(1)} %collective-permute-done.refs_1_.refs_4_, f32[1,256]{1,0:T(1,128)S(1)} %bitcast.16, f32[1,16]{1,0:T(1,128)S(1)} %bitcast.18, f32[1,16]{1,0:T(1,128)S(1)} %bitcast.19, bf16[256,4096]{1,0:T(8,128)(2,1)} %refs_7_.3, ...), custom_call_target="tpu_custom_call" | custom-call | flops 2013265920000 | bytes 5242880 | tf_op jit(solution)/shard_map/scan/pallas_call | solution.py:461
  46.0 0.1 eq.26
  46.1 0.1 reduce_or.9
  46.2 0.0 copy-done.15
  46.2 0.1 convert_reduce_fusion.1
  46.3 0.1 select_reduce_fusion
  46.5 0.0 collective-permute-done.2.refs_2_
  46.5 0.0 collective-permute-done.3.refs_3_
  46.5 0.0 collective-permute-done.1.refs_1_
  46.5 2.9 %regroup.1 = (bf16[16,4096]{1,0:T(8,128)(2,1)}, bf16[16,4096]{1,0:T(8,128)(2,1)}, bf16[16,4096]{1,0:T(8,128)(2,1)}, bf16[16,4096]{1,0:T(8,128)(2,1)}) custom-call(bf16[16,4096]{1,0:T(8,128)(2,1)S(1)} %copy-done.3, bf16[16,4096]{1,0:T(8,128)(2,1)} %collective-permute-done.1.refs_1_, bf16[16,4096]{1,0:T(8,128)(2,1)} %collective-permute-done.2.refs_2_, ...), custom_call_target="tpu_custom_call" | custom-call | tf_op jit(solution)/shard_map/regroup/pallas_call | solution.py:194
  49.4 0.4 collective-permute-start.4
  49.8 0.3 collective-permute-start.5
  50.1 1.5 %collective-permute-start.6 = (bf16[16,4096]{1,0:T(8,128)(2,1)}, bf16[16,4096]{1,0:T(8,128)(2,1)S(1)}, u32[]{:S(2)}, u32[]{:S(2)}) collective-permute-start(bf16[16,4096]{1,0:T(8,128)(2,1)} %get-tuple-element.35), channel_id=1, source_target_pairs={{0,6},{2,4},{4,2},{6,0},{8,14},{10,12},{12,10},{14,8},{16,22},{18,... | collective-permute-start | bytes 393224 | tf_op jit(solution)/shard_map/ppermute | solution.py:626
  51.6 0.1 convert_reduce_fusion.bound_ref
  51.8 0.0 collective-permute-done.4.refs_1_
  51.8 3.3 %collective-permute-done.5.refs_2_ = bf16[16,4096]{1,0:T(8,128)(2,1)S(1)} collective-permute-done((bf16[16,4096]{1,0:T(8,128)(2,1)}, bf16[16,4096]{1,0:T(8,128)(2,1)S(1)}, u32[]{:S(2)}, u32[]{:S(2)}) %collective-permute-start.5) | collective-permute-done | bytes 131104 | tf_op jit(solution)/shard_map/ppermute | solution.py:626
  55.1 9.0 %collective-permute-done.6.refs_3_ = bf16[16,4096]{1,0:T(8,128)(2,1)S(1)} collective-permute-done((bf16[16,4096]{1,0:T(8,128)(2,1)}, bf16[16,4096]{1,0:T(8,128)(2,1)S(1)}, u32[]{:S(2)}, u32[]{:S(2)}) %collective-permute-start.6) | collective-permute-done | bytes 131104 | tf_op jit(solution)/shard_map/ppermute | solution.py:626
  64.1 0.9 %copy-done.4 = bf16[16,4096]{1,0:T(8,128)(2,1)S(1)} copy-done((bf16[16,4096]{1,0:T(8,128)(2,1)S(1)}, bf16[16,4096]{1,0:T(8,128)(2,1)}, u32[]{:S(2)}) %copy-start.4) | copy-done | bytes 131096
  65.0 2.0 %settle_edges.1 = (bf16[12,3,4096]{2,1,0:T(4,128)(2,1)}, f32[4,2]{1,0:T(4,128)S(1)}) custom-call(s32[1]{0:T(128)} %bitcast.9.refs_0_.place_ref, s32[12]{0:T(128)S(1)} %broadcast_subtract_fusion.source_ref, s32[4,2]{1,0:T(4,128)S(1)} %copy.29.range_ref, bf16[16,4096]{1,0:T(8,128)(2,1)S(1)} %copy-done.4, bf16[16,4096]{1,0:T(8,128)(2,1)S(1)} %collective-permute-done.4.refs_1_, ...), custom_call_target="tpu_custom_call" | custom-call | tf_op jit(solution)/shard_map/settle_edges/pallas_call | solution.py:541
  67.0 0.6 copy.30
  67.6 6.9 %all-to-all-done.got_hbm = bf16[16,16,4096]{2,1,0:T(8,128)(2,1)} async-done(((bf16[16,16,4096]{2,1,0:T(8,128)(2,1)}), bf16[16,16,4096]{2,1,0:T(8,128)(2,1)}, u32[]{:S(2)}, u32[]{:S(2)}) %all-to-all-start) | async-done | bytes 2097184 | tf_op jit(solution)/shard_map/all_to_all | solution.py:639
  74.6 2.8 %settle_states.1 = bf16[12,16,4096]{2,1,0:T(8,128)(2,1)} custom-call(s32[12]{0:T(128)S(1)} %broadcast_subtract_fusion.source_ref, s32[9]{0:T(128)S(1)} %convert_reduce_fusion.bound_ref, bf16[16,16,4096]{2,1,0:T(8,128)(2,1)} %all-to-all-done.got_hbm), custom_call_target="tpu_custom_call" | custom-call | tf_op jit(solution)/shard_map/settle_states/pallas_call | solution.py:591
  (20 shorter events, 0.0 us)
Async XLA Ops:
  0.6 5.5 %copy-start.1 = (bf16[8,3,4096]{2,0,1:T(8,128)(2,1)S(1)}, bf16[8,3,4096]{2,0,1:T(8,128)(2,1)}, u32[]{:S(2)}) copy-start(bf16[8,3,4096]{2,0,1:T(8,128)(2,1)} %param.23) | copy-start | bytes 589828
  0.6 5.5 %copy-start = (bf16[128,4096]{1,0:T(8,128)(2,1)S(1)}, bf16[128,4096]{1,0:T(8,128)(2,1)}, u32[]{:S(2)}) copy-start(bf16[128,4096]{1,0:T(8,128)(2,1)} %x_ref.1) | copy-start | bytes 3145732
  0.7 5.5 %copy-start.6 = (s32[8]{0:T(128)S(1)}, s32[8]{0:T(128)}, u32[]{:S(2)}) copy-start(s32[8]{0:T(128)} %accepted_ref.1) | copy-start | bytes 100
  0.7 5.5 %copy-start.7 = (s32[128]{0:T(128)S(1)}, s32[128]{0:T(128)}, u32[]{:S(2)}) copy-start(s32[128]{0:T(128)} %owner_ref.1) | copy-start | bytes 1540
  0.7 5.5 %copy-start.5 = (s32[8]{0:T(128)S(1)}, s32[8]{0:T(128)}, u32[]{:S(2)}) copy-start(s32[8]{0:T(128)} %length_ref.1) | copy-start | bytes 100
  0.7 9.5 %copy-start.16 = (s32[4,2]{0,1:T(2,128)S(1)}, s32[4,2]{0,1:T(2,128)}, u32[]{:S(2)}) copy-start(s32[4,2]{0,1:T(2,128)} %param.37) | copy-start | bytes 100
  0.7 9.6 %copy-start.8 = (bf16[256,4096]{1,0:T(8,128)(2,1)S(1)}, bf16[256,4096]{1,0:T(8,128)(2,1)}, u32[]{:S(2)}) copy-start(bf16[256,4096]{1,0:T(8,128)(2,1)} %refs_7_.3) | copy-start | bytes 6291460
  0.7 9.6 %copy-start.9 = (f32[4096]{0:T(1024)S(1)}, f32[4096]{0:T(1024)}, u32[]{:S(2)}) copy-start(f32[4096]{0:T(1024)} %param.31) | copy-start | bytes 49156
  0.7 9.6 %copy-start.11 = (f32[256]{0:T(256)S(1)}, f32[256]{0:T(256)}, u32[]{:S(2)}) copy-start(f32[256]{0:T(256)} %param.27) | copy-start | bytes 3076
  0.7 9.6 %copy-start.12 = (f32[16]{0:T(128)S(1)}, f32[16]{0:T(128)}, u32[]{:S(2)}) copy-start(f32[16]{0:T(128)} %param.28) | copy-start | bytes 196
  4.8 5.5 %collective-permute-start = (f32[288,128]{1,0:T(8,128)}, f32[288,128]{1,0:T(8,128)S(1)}, u32[]{:S(2)}, u32[]{:S(2)}) collective-permute-start(f32[288,128]{1,0:T(8,128)} %get-tuple-element.21.refs_0_.refs_3_._), channel_id=1, source_target_pairs={{0,1},{1,0},{2,3},{3,2},{4,5},{5,4},{6,7},{7,6},{8,9},{9,8},{10,11... | collective-permute-start | bytes 442376 | tf_op jit(solution)/shard_map/ppermute | solution.py:621
  7.9 38.6 %collective-permute-start.2 = (bf16[16,4096]{1,0:T(8,128)(2,1)}, bf16[16,4096]{1,0:T(8,128)(2,1)}, u32[]{:S(2)}, u32[]{:S(2)}) collective-permute-start(bf16[16,4096]{1,0:T(8,128)(2,1)} %get-tuple-element.30), channel_id=1, source_target_pairs={{0,16},{2,18},{4,20},{6,22},{8,24},{10,26},{12,28},{14,30},{16,0},... | collective-permute-start | bytes 393224 | tf_op jit(solution)/shard_map/ppermute | solution.py:626
  10.2 36.3 %collective-permute-start.3 = (bf16[16,4096]{1,0:T(8,128)(2,1)}, bf16[16,4096]{1,0:T(8,128)(2,1)}, u32[]{:S(2)}, u32[]{:S(2)}) collective-permute-start(bf16[16,4096]{1,0:T(8,128)(2,1)} %get-tuple-element.31), channel_id=1, source_target_pairs={{0,24},{2,26},{4,28},{6,30},{8,16},{10,18},{12,20},{14,22},{16,8},... | collective-permute-start | bytes 393224 | tf_op jit(solution)/shard_map/ppermute | solution.py:626
  18.4 8.7 %copy-start.2 = (f32[288,128]{1,0:T(8,128)S(1)}, f32[288,128]{1,0:T(8,128)}, u32[]{:S(2)}) copy-start(f32[288,128]{1,0:T(8,128)} %get-tuple-element.21.refs_0_.refs_3_._) | copy-start | bytes 442372
  18.4 8.7 %copy-start.10 = (f32[4096]{0:T(1024)S(1)}, f32[4096]{0:T(1024)}, u32[]{:S(2)}) copy-start(f32[4096]{0:T(1024)} %param.33) | copy-start | bytes 49156
  18.4 8.7 %copy-start.13 = (f32[16]{0:T(128)S(1)}, f32[16]{0:T(128)}, u32[]{:S(2)}) copy-start(f32[16]{0:T(128)} %param.29) | copy-start | bytes 196
  18.4 28.1 %collective-permute-start.1 = (bf16[16,4096]{1,0:T(8,128)(2,1)}, bf16[16,4096]{1,0:T(8,128)(2,1)}, u32[]{:S(2)}, u32[]{:S(2)}) collective-permute-start(bf16[16,4096]{1,0:T(8,128)(2,1)} %get-tuple-element.29), channel_id=1, source_target_pairs={{0,8},{2,10},{4,12},{6,14},{8,0},{10,2},{12,4},{14,6},{16,24},{18,... | collective-permute-start | bytes 393224 | tf_op jit(solution)/shard_map/ppermute | solution.py:626
  18.5 56.1 %all-to-all-start = ((bf16[16,16,4096]{2,1,0:T(8,128)(2,1)}), bf16[16,16,4096]{2,1,0:T(8,128)(2,1)}, u32[]{:S(2)}, u32[]{:S(2)}) async-start(bf16[16,16,4096]{2,1,0:T(8,128)(2,1)} %kept_states.1), calls=%async_computation | async-start | bytes 4194304 | tf_op jit(solution)/shard_map/all_to_all | solution.py:639
  27.1 19.1 %copy-start.15 = (pred[16,16]{1,0:T(8,128)(4,1)S(1)}, pred[16,16]{1,0:T(8,128)(4,1)}, u32[]{:S(2)}) copy-start(pred[16,16]{1,0:T(8,128)(4,1)} %constant.18.clone) | copy-start | bytes 772
  27.1 19.3 %copy-start.17 = (s32[16]{0:T(128)S(1)}, s32[16]{0:T(128)}, u32[]{:S(2)}) copy-start(s32[16]{0:T(128)} %constant.25) | copy-start | bytes 196
  27.1 19.4 %copy-start.3 = (bf16[16,4096]{1,0:T(8,128)(2,1)S(1)}, bf16[16,4096]{1,0:T(8,128)(2,1)}, u32[]{:S(2)}) copy-start(bf16[16,4096]{1,0:T(8,128)(2,1)} %get-tuple-element.28.refs_0_) | copy-start | bytes 393220
  27.1 24.5 %copy-start.14 = (pred[9,16]{1,0:T(8,128)(4,1)S(1)}, pred[9,16]{1,0:T(8,128)(4,1)}, u32[]{:S(2)}) copy-start(pred[9,16]{1,0:T(8,128)(4,1)} %constant.19.clone) | copy-start | bytes 436
  49.4 2.3 %collective-permute-start.4 = (bf16[16,4096]{1,0:T(8,128)(2,1)}, bf16[16,4096]{1,0:T(8,128)(2,1)S(1)}, u32[]{:S(2)}, u32[]{:S(2)}) collective-permute-start(bf16[16,4096]{1,0:T(8,128)(2,1)} %get-tuple-element.33), channel_id=1, source_target_pairs={{0,2},{2,0},{4,6},{6,4},{8,10},{10,8},{12,14},{14,12},{16,18},{18,... | collective-permute-start | bytes 393224 | tf_op jit(solution)/shard_map/ppermute | solution.py:626
  49.8 5.3 %collective-permute-start.5 = (bf16[16,4096]{1,0:T(8,128)(2,1)}, bf16[16,4096]{1,0:T(8,128)(2,1)S(1)}, u32[]{:S(2)}, u32[]{:S(2)}) collective-permute-start(bf16[16,4096]{1,0:T(8,128)(2,1)} %get-tuple-element.34), channel_id=1, source_target_pairs={{0,4},{2,6},{4,0},{6,2},{8,12},{10,14},{12,8},{14,10},{16,20},{18,... | collective-permute-start | bytes 393224 | tf_op jit(solution)/shard_map/ppermute | solution.py:626
  50.1 14.0 %collective-permute-start.6 = (bf16[16,4096]{1,0:T(8,128)(2,1)}, bf16[16,4096]{1,0:T(8,128)(2,1)S(1)}, u32[]{:S(2)}, u32[]{:S(2)}) collective-permute-start(bf16[16,4096]{1,0:T(8,128)(2,1)} %get-tuple-element.35), channel_id=1, source_target_pairs={{0,6},{2,4},{4,2},{6,0},{8,14},{10,12},{12,10},{14,8},{16,22},{18,... | collective-permute-start | bytes 393224 | tf_op jit(solution)/shard_map/ppermute | solution.py:626
  64.1 0.9 %copy-start.4 = (bf16[16,4096]{1,0:T(8,128)(2,1)S(1)}, bf16[16,4096]{1,0:T(8,128)(2,1)}, u32[]{:S(2)}) copy-start(bf16[16,4096]{1,0:T(8,128)(2,1)} %get-tuple-element.32.refs_0_) | copy-start | bytes 393220
